TPU v7x, 256 devices: a whole 4x4x8 slice. The times are simulated.
256 devices in a mesh: section: 2 (over x_hi), fsdp: 64 (over y, z, x_lo), dp: 2 (over core).
Axes of the slice: x: 4 (x_hi: 2, x_lo: 2; x = x_hi * 2 + x_lo), y: 4, z: 8, core: 2. Of those that a mesh axis runs over, the one named last changes fastest.
Arguments:
- hidden: bfloat16 [4, 512, 8192], P(('section', 'dp'), 'fsdp'), may hold values from -7 to 7
- cotangent: bfloat16 [4, 512, 8192], P(('section', 'dp'), None, 'fsdp'), may hold values from -6 to 6
- seg_ids: int32 [4, 512], P(('section', 'dp')), may hold values from 0 to 8, as said below
- advantage: float32 [4, 8], P(('section', 'dp')), may hold values from -4 to 4
- w_query: bfloat16 [8192, 8192], P('fsdp'), may hold values from -6 to 6
- w_key: bfloat16 [8192, 1024], P('fsdp'), may hold values from -6 to 6
- w_value: bfloat16 [8192, 1024], P('fsdp'), may hold values from -6 to 6
Outputs:
- rollout_query: bfloat16 [8192, 8192], P(None, 'fsdp')
- rollout_key: bfloat16 [8192, 8192], P(None, 'fsdp')
- rollout_value: bfloat16 [8192, 8192], P(None, 'fsdp')
Inputs may be any that keep to these rules, and one draw needn't show every extreme that they name: `seg_ids`: in each block ids never fall; each id below 8 covers 1 to 64 positions, one of them exactly 64, and every id below 8 appears; id 8 marks padding at the block's end.
All inputs are finite; a program needn't handle non-finite values.
Results may differ from a plain program's by a relative error of at most 0.015.
The roundings to bfloat16 on the way count: a program that leaves them out, or rounds other values in their place, can miss the bound.
Values may be sent and summed in bfloat16 or wider, within the bound.
No kernel may reach another device: no remote copies, remote signals or barrier semaphores. Data moves between devices by JAX's collectives and lax.ppermute only.
A program may use at most 64 MiB of HBM per device.

v0:
```python
import jax
import jax.numpy as jnp
from jax import lax
from jax.experimental import pallas as pl
from jax.experimental.pallas import tpu as pltpu
from jax.sharding import Mesh, PartitionSpec as P

D = 8192
HD = 128
RESP = 8

step_rate = 200.0
rope_base = 1000000.0
norm_eps = 1e-06
masked_score = -1e30

YZ = ("y", "zh", "zl")
MEM = ("zl", "core")
X = ("xh", "xl")
FS = ("y", "zh", "zl", "xl")


def rotate(field, cosine_table, sine_table):
    half_width = field.shape[-1] // 2
    lead_half = field[..., :half_width]
    tail_half = field[..., half_width:]
    return jnp.concatenate(
        [
            lead_half * cosine_table - tail_half * sine_table,
            tail_half * cosine_table + lead_half * sine_table,
        ],
        -1,
    )


def angles(seg_row):
    span_count = seg_row.shape[0]
    earlier = jnp.sum((seg_row[None, :] < seg_row[:, None]).astype(jnp.int32), axis=1)
    positions = jnp.arange(span_count, dtype=jnp.int32) - earlier
    frequency = rope_base ** (-jnp.arange(HD // 2, dtype=jnp.float32) * 2.0 / HD)
    phase_grid = positions.astype(jnp.float32)[:, None] * frequency[None, :]
    return jnp.cos(phase_grid), jnp.sin(phase_grid)


def token_weights(seg_row, advantage_row):
    id_range = jnp.arange(RESP + 1, dtype=jnp.int32)
    onehot = (seg_row[:, None] == id_range[None, :]).astype(jnp.float32)
    counts = jnp.sum(onehot, axis=0)[:RESP]
    per_token = -advantage_row / counts
    return jnp.sum(onehot[:, :RESP] * per_token[None, :], axis=1)


def attend_back(q_rot, k_rot, v_bf, grad_context, allowed):
    score_scale = HD ** (-0.5)
    f32 = jnp.float32
    scores = jnp.einsum("td,ud->tu", q_rot, k_rot, preferred_element_type=f32) * score_scale
    scores = jnp.where(allowed, scores, masked_score)
    row_top = jnp.max(scores, axis=-1, keepdims=True)
    exponent = jnp.exp(scores - row_top)
    attention = exponent / jnp.sum(exponent, axis=-1, keepdims=True)
    attention_bf = attention.astype(jnp.bfloat16)
    grad_prob = jnp.einsum("td,ud->tu", grad_context, v_bf, preferred_element_type=f32)
    inner_sum = jnp.sum(attention * grad_prob, axis=-1, keepdims=True)
    dscore = (attention * (grad_prob - inner_sum)).astype(jnp.bfloat16)
    grad_query = jnp.einsum("tu,ud->td", dscore, k_rot, preferred_element_type=f32) * score_scale
    grad_key = jnp.einsum("tu,td->ud", dscore, q_rot, preferred_element_type=f32) * score_scale
    grad_value = jnp.einsum("tu,td->ud", attention_bf, grad_context, preferred_element_type=f32)
    return grad_query, grad_key, grad_value


def swap(x):
    return lax.ppermute(x, ("xl", "core"), [(0, 0), (1, 2), (2, 1), (3, 3)])


def flip(x, axes):
    n = 2 ** len(axes)
    return lax.ppermute(x, axes, [(i, n - 1 - i) for i in range(n)])


def exchange(x, axes):
    return lax.all_to_all(x, axes, split_axis=0, concat_axis=0, tiled=True)


def spread(x, axes):
    n = lax.axis_size(axes)
    return exchange(jnp.broadcast_to(x[None], (n,) + x.shape), axes)


def ordered(mine, other, bit):
    first = jnp.where(bit == 0, mine, other)
    second = jnp.where(bit == 0, other, mine)
    return first, second


def x_ring(x, xh, xl):
    low = ordered(x, flip(x, ("xl",)), xl)
    high = ordered(flip(x, ("xh",)), flip(x, X), xl)
    col0 = ordered(low[0], high[0], xh)
    col1 = ordered(low[1], high[1], xh)
    return (col0[0], col1[0]), (col0[1], col1[1])


def member_parts(normed, kv, member):
    def body(at_ref, rows_ref, kv_ref, out_ref):
        out_ref[...] = lax.dot_general(
            rows_ref[...],
            kv_ref[...],
            (((0,), (0,)), ((), ())),
            preferred_element_type=jnp.float32,
        ).astype(jnp.bfloat16)

    return pl.pallas_call(
        body,
        out_shape=jax.ShapeDtypeStruct((1024, 2 * HD), jnp.bfloat16),
        grid_spec=pltpu.PrefetchScalarGridSpec(
            num_scalar_prefetch=1,
            grid=(8,),
            in_specs=[
                pl.BlockSpec((512, HD), lambda b, at: (0, b * 8 + at[0])),
                pl.BlockSpec((512, 2 * HD), lambda b, at: (0, 0)),
            ],
            out_specs=pl.BlockSpec((HD, 2 * HD), lambda b, at: (b, 0)),
        ),
        name="member_parts",
    )(member.reshape(1).astype(jnp.int32), normed, kv)


def local(hidden, cotangent, seg_ids, advantage, w_query, w_key, w_value):
    f32 = jnp.float32
    bf16 = jnp.bfloat16
    inv_width = D ** (-0.5)
    xh = lax.axis_index("xh")
    xl = lax.axis_index("xl")
    core = lax.axis_index("core")
    zl = lax.axis_index("zl")
    member = zl * 2 + core
    ring = xh * 2 + xl

    token_rows = hidden[0].astype(f32)
    normed_own = (
        token_rows * lax.rsqrt(jnp.mean(token_rows * token_rows, axis=-1, keepdims=True) + norm_eps)
    ).astype(bf16)
    normed = lax.all_gather(swap(normed_own), YZ + ("core",), axis=0, tiled=True)
    cot = swap(cotangent[0])
    seg_row = swap(seg_ids[0])
    adv_row = swap(advantage[0])
    block_len = 512

    wq = w_query.reshape(2, 64, 32, 2, HD)
    wq = lax.dynamic_index_in_dim(wq, xh, 0, keepdims=False)
    wq = lax.dynamic_index_in_dim(wq, core, 2, keepdims=False).transpose(1, 0, 2)
    wkv = jnp.stack([w_key.reshape(4, 4, 8, 8, HD), w_value.reshape(4, 4, 8, 8, HD)], axis=2)
    wkv = lax.dynamic_index_in_dim(wkv, xh * 2 + core, 0, keepdims=False)
    wkv = wkv.transpose(3, 0, 1, 2, 4).reshape(32, 16, HD)
    cut = exchange(jnp.concatenate([wq, wkv], axis=1), YZ)
    wq = cut[:, :64]
    wkv = spread(cut[:, 64:], ("zl",))

    wq = x_ring(wq, xh, xl)
    q_cols = jnp.stack([wq[h][l] for l in (0, 1) for h in (0, 1)], axis=1).reshape(D, HD)
    wkv = x_ring(wkv, xh, xl)
    wkv = jnp.stack([wkv[h][l] for l in (0, 1) for h in (0, 1)], axis=0)
    wkv = jnp.stack(ordered(wkv, flip(wkv, ("core",)), core), axis=0)
    wkv = wkv.reshape(2, 2, 2, 4, 32, 2, 8, HD).transpose(4, 1, 2, 0, 3, 6, 5, 7)
    wkv = wkv.reshape(D, 2 * HD)

    cosine_table, sine_table = angles(seg_row)
    weight_row = token_weights(seg_row, adv_row)
    grad_context = (cot.astype(f32) * weight_row[:, None]).astype(bf16)
    position = jnp.arange(block_len, dtype=jnp.int32)
    allowed = (seg_row[:, None] == seg_row[None, :]) & (position[None, :] <= position[:, None])

    def project(cols):
        return jnp.dot(normed, cols, preferred_element_type=f32) * inv_width

    queries = project(q_cols)
    keys_values = project(wkv)
    q_rot = rotate(queries, cosine_table, sine_table).astype(bf16)
    k_rot = rotate(keys_values[:, :HD], cosine_table, sine_table).astype(bf16)
    v_bf = keys_values[:, HD:].astype(bf16)

    grad_query, grad_key, grad_value = attend_back(q_rot, k_rot, v_bf, grad_context, allowed)
    scaled_q = (rotate(grad_query, cosine_table, -sine_table) * inv_width).astype(bf16)
    scaled_kv = (
        jnp.concatenate([rotate(grad_key, cosine_table, -sine_table), grad_value], -1) * inv_width
    ).astype(bf16)

    contract = (((0,), (0,)), ((), ()))
    part_q = lax.dot_general(normed, scaled_q, contract, preferred_element_type=f32)
    part_q = part_q.astype(bf16).reshape(4, 2048, HD)
    part_q, scaled_kv = lax.optimization_barrier((part_q, scaled_kv))

    def to_ring(mask, axes):
        piece = lax.dynamic_index_in_dim(part_q, ring ^ mask, 0, keepdims=False)
        return flip(piece, axes)

    sum_q = (
        lax.dynamic_index_in_dim(part_q, ring, 0, keepdims=False).astype(f32)
        + to_ring(1, ("xl",)).astype(f32)
        + to_ring(3, X).astype(f32)
        + to_ring(2, ("xh",)).astype(f32)
    )
    old_q = lax.dynamic_slice_in_dim(q_cols, ring * 2048, 2048)
    new_q = (old_q.astype(f32) - step_rate * sum_q).astype(bf16)
    near = swap(new_q)
    far = lax.ppermute(
        new_q,
        ("xh", "xl", "core"),
        [
            (h * 4 + l * 2 + c, (1 - h) * 4 + c * 2 + l)
            for h in (0, 1)
            for l in (0, 1)
            for c in (0, 1)
        ],
    )
    near_other = flip(near, ("core",))
    far_other = flip(far, ("core",))
    near = ordered(near, near_other, core)
    far = ordered(far, far_other, core)
    low = ordered(near[0], far[0], xh)
    high = ordered(near[1], far[1], xh)
    roll_q = jnp.stack([low[0], high[0], low[1], high[1]], axis=0).reshape(D, HD)

    kv_sum = exchange(scaled_kv.reshape(8, 64, 2 * HD), MEM)
    kv_sum = kv_sum.astype(f32)
    kv_sum = jnp.sum(kv_sum, axis=0).astype(bf16)
    kv_sum = spread(kv_sum, MEM).reshape(block_len, 2 * HD)
    part_kv = member_parts(normed, kv_sum, member)
    part_kv = exchange(part_kv.reshape(4, 256, 2 * HD), X).astype(f32)
    old_kv = wkv.reshape(4, 2, 8, 128, 2 * HD)
    old_kv = lax.dynamic_index_in_dim(old_kv, ring, 0, keepdims=False)
    old_kv = lax.dynamic_index_in_dim(old_kv, member, 1, keepdims=False).reshape(256, 2 * HD)
    new_kv = (old_kv.astype(f32) - step_rate * jnp.sum(part_kv, axis=0)).astype(bf16)
    new_kv = spread(new_kv, ("zl",))
    new_kv = x_ring(new_kv, xh, xl)
    new_kv = jnp.stack([new_kv[h][l] for h in (0, 1) for l in (0, 1)], axis=0)
    new_kv = jnp.stack(ordered(new_kv, flip(new_kv, ("core",)), core), axis=0)
    new_kv = new_kv.reshape(2, 4, 4, 2, 128, 2 * HD).transpose(1, 3, 2, 0, 4, 5).reshape(D, 2 * HD)
    return roll_q, new_kv[:, :HD], new_kv[:, HD:]


def solution(mesh):
    grid = Mesh(
        mesh.devices.reshape(2, 4, 2, 4, 2, 2), ("xh", "y", "zh", "zl", "xl", "core")
    )
    groups = ("xh", "core")
    in_specs = (
        P(groups, FS, None),
        P(groups, None, FS),
        P(groups, None),
        P(groups, None),
        P(FS, None),
        P(FS, None),
        P(FS, None),
    )
    out_specs = (P(None, FS), P(None, FS), P(None, FS))

    return jax.shard_map(local, mesh=grid, in_specs=in_specs, out_specs=out_specs, check_vma=False)
```

profile of v0, /device:TPU:8, one launch (start us, length us, event | category | flops | bytes accessed | tf_op | source)
XLA Modules:
  0.0 307.6 jit_solution(7486134579822520181)
XLA Ops:
  7.2 1.1 fusion.13
  8.3 1.0 fusion.14
  10.7 1.0 copy.46
  11.7 1.0 copy.47
  12.8 3.2 %reshape.101 = bf16[2,64,32,2,128]{4,3,2,1,0:T(2,128)(2,1)S(1)} reshape(bf16[128,8192]{1,0:T(8,128)(2,1)} %param.11) | data formatting | bytes 4194304 | tf_op jit(solution)/shard_map/reshape | solution.py:149
  16.1 1.2 constant_dynamic-slice_fusion.1
  17.7 27.5 %all_to_all.30 = bf16[32,80,128]{2,1,0:T(8,128)(2,1)S(1)} all-to-all(bf16[32,80,128]{2,1,0:T(8,128)(2,1)S(1)} %copy.37), channel_id=1, replica_groups=mesh['xh'=2,'y'=4,'zh'=2,'zl'=4,'xl'=2,'core'=2] {'y','zh','zl'}, dimensions={0} | all-to-all | bytes 1310720 | tf_op jit(solution)/shard_map/all_to_all | solution.py:81
  45.4 22.7 %all_to_all.31 = bf16[4,32,16,128]{3,2,1,0:T(8,128)(2,1)} all-to-all(bf16[4,32,16,128]{3,2,1,0:T(8,128)(2,1)S(1)} %broadcast_in_dim.9), channel_id=1, replica_groups=mesh['xh'=2,'y'=4,'zh'=2,'zl'=4,'xl'=2,'core'=2] {'zl'}, dimensions={0} | all-to-all | bytes 1048576 | tf_op jit(solution)/shard_map/all_to_all | solution.py:81
  68.1 3.1 collective-permute-start.6
  71.1 1.6 collective-permute-start.7
  72.8 10.3 %collective-permute-done.5 = bf16[4,32,16,128]{3,2,1,0:T(8,128)(2,1)S(1)} collective-permute-done((bf16[4,32,16,128]{3,2,1,0:T(8,128)(2,1)}, bf16[4,32,16,128]{3,2,1,0:T(8,128)(2,1)S(1)}, u32[]{:S(2)}, u32[]{:S(2)}) %collective-permute-start.5) | collective-permute-done | bytes 524320 | tf_op jit(solution)/shard_map/ppermute | solution.py:77
  83.1 12.3 %collective-permute-done.6 = bf16[4,32,16,128]{3,2,1,0:T(8,128)(2,1)S(1)} collective-permute-done((bf16[4,32,16,128]{3,2,1,0:T(8,128)(2,1)}, bf16[4,32,16,128]{3,2,1,0:T(8,128)(2,1)S(1)}, u32[]{:S(2)}, u32[]{:S(2)}) %collective-permute-start.6) | collective-permute-done | bytes 524320 | tf_op jit(solution)/shard_map/ppermute | solution.py:77
  96.1 2.1 collective-permute-done.7
  98.3 1.7 select_bitcast_fusion.11
  100.0 1.6 pad_maximum_fusion.2
  103.9 7.7 %collective-permute-start = (bf16[32,64,128]{2,1,0:T(8,128)(2,1)S(1)}, bf16[32,64,128]{2,1,0:T(8,128)(2,1)S(1)}, u32[]{:S(2)}, u32[]{:S(2)}) collective-permute-start(bf16[32,64,128]{2,1,0:T(8,128)(2,1)S(1)} %slice.64), channel_id=1, source_target_pairs={{0,2},{2,0},{1,3},{3,1},{4,6},{6,4},{5,7},{7,5},{8,10},{10,8},{9,1... | collective-permute-start | bytes 1572872 | tf_op jit(solution)/shard_map/ppermute | solution.py:77
  112.3 2.0 collective-permute-start.2
  114.6 12.2 %collective-permute-done = bf16[32,64,128]{2,1,0:T(8,128)(2,1)S(1)} collective-permute-done((bf16[32,64,128]{2,1,0:T(8,128)(2,1)S(1)}, bf16[32,64,128]{2,1,0:T(8,128)(2,1)S(1)}, u32[]{:S(2)}, u32[]{:S(2)}) %collective-permute-start) | collective-permute-done | bytes 524320 | tf_op jit(solution)/shard_map/ppermute | solution.py:77
  126.8 9.6 %collective-permute-done.1 = bf16[32,64,128]{2,1,0:T(8,128)(2,1)S(1)} collective-permute-done((bf16[32,64,128]{2,1,0:T(8,128)(2,1)S(1)}, bf16[32,64,128]{2,1,0:T(8,128)(2,1)S(1)}, u32[]{:S(2)}, u32[]{:S(2)}) %collective-permute-start.1) | collective-permute-done | bytes 524320 | tf_op jit(solution)/shard_map/ppermute | solution.py:77
  136.4 2.1 collective-permute-done.2
  139.9 1.8 broadcast_select_fusion.3
  142.9 2.4 pad_maximum_fusion
  145.3 6.4 %convolution_multiply_fusion.4 = f32[512,128]{0,1:T(8,128)S(1)} fusion(bf16[512,8192]{1,0:T(8,128)(2,1)} %all-gather.2.cloned.1.call-done.rows_ref, bf16[8192,128]{1,0:T(8,128)(2,1)S(1)} %bitcast.102), kind=kOutput, calls=%fused_computation.15 | convolution fusion | flops 1073807360 | bytes 10747904 | tf_op jit(solution)/shard_map/dot_general | solution.py:174
  151.7 4.6 %convolution_multiply_fusion.1 = f32[512,256]{0,1:T(8,128)S(1)} fusion(bf16[512,8192]{1,0:T(8,128)(2,1)S(1)} %copy-done, bf16[8192,256]{1,0:T(8,128)(2,1)} %bitcast.108), kind=kOutput, calls=%fused_computation.12 | convolution fusion | flops 2147614720 | bytes 13107200 | tf_op jit(solution)/shard_map/dot_general | solution.py:174
  160.3 2.4 convolution_convert_fusion
  162.8 12.1 %all_to_all.32 = bf16[8,64,256]{2,1,0:T(8,128)(2,1)S(1)} all-to-all(bf16[8,64,256]{2,1,0:T(8,128)(2,1)S(1)} %bitcast.116), channel_id=1, replica_groups=mesh['xh'=2,'y'=4,'zh'=2,'zl'=4,'xl'=2,'core'=2] {'zl','core'}, dimensions={0} | all-to-all | bytes 524288 | tf_op jit(solution)/shard_map/all_to_all | solution.py:81
  175.7 3.4 %all-to-all-start.3 = ((bf16[8,64,256]{2,1,0:T(8,128)(2,1)}), bf16[8,64,256]{2,1,0:T(8,128)(2,1)S(1)}, u32[]{:S(2)}, u32[]{:S(2)}) async-start(bf16[8,64,256]{2,1,0:T(8,128)(2,1)} %broadcast_in_dim.11), calls=%async_computation.3 | async-start | bytes 524288 | tf_op jit(solution)/shard_map/all_to_all | solution.py:81
  179.2 9.6 %all-to-all-done.3 = bf16[8,64,256]{2,1,0:T(8,128)(2,1)S(1)} async-done(((bf16[8,64,256]{2,1,0:T(8,128)(2,1)}), bf16[8,64,256]{2,1,0:T(8,128)(2,1)S(1)}, u32[]{:S(2)}, u32[]{:S(2)}) %all-to-all-start.3) | async-done | bytes 262176 | tf_op jit(solution)/shard_map/all_to_all | solution.py:81
  189.5 6.0 %member_parts.1 = bf16[1024,256]{1,0:T(8,128)(2,1)} custom-call(s32[1]{0:T(128)} %bitcast.37.at_ref, bf16[512,8192]{1,0:T(8,128)(2,1)} %all-gather.2.cloned.1.call-done.rows_ref, bf16[512,256]{1,0:T(8,128)(2,1)} %bitcast.113), custom_call_target="tpu_custom_call" | custom-call | tf_op jit(solution)/shard_map/member_parts/pallas_call | solution.py:112
  195.5 3.7 %all-to-all-start.4 = ((bf16[4,256,256]{2,1,0:T(8,128)(2,1)}), bf16[4,256,256]{2,1,0:T(8,128)(2,1)S(1)}, u32[]{:S(2)}, u32[]{:S(2)}) async-start(bf16[4,256,256]{2,1,0:T(8,128)(2,1)} %bitcast.110), calls=%async_computation.4 | async-start | bytes 1048576 | tf_op jit(solution)/shard_map/all_to_all | solution.py:81
  200.2 8.4 %all-to-all-done.4 = bf16[4,256,256]{2,1,0:T(8,128)(2,1)S(1)} async-done(((bf16[4,256,256]{2,1,0:T(8,128)(2,1)}), bf16[4,256,256]{2,1,0:T(8,128)(2,1)S(1)}, u32[]{:S(2)}, u32[]{:S(2)}) %all-to-all-start.4) | async-done | bytes 524320 | tf_op jit(solution)/shard_map/all_to_all | solution.py:81
  208.7 16.8 %all_to_all.33 = bf16[4,256,256]{2,1,0:T(8,128)(2,1)S(1)} all-to-all(bf16[4,256,256]{2,1,0:T(8,128)(2,1)S(1)} %broadcast_in_dim.12), channel_id=1, replica_groups=mesh['xh'=2,'y'=4,'zh'=2,'zl'=4,'xl'=2,'core'=2] {'zl'}, dimensions={0} | all-to-all | bytes 1048576 | tf_op jit(solution)/shard_map/all_to_all | solution.py:81
  226.1 2.1 collective-permute-start.19
  228.2 2.1 collective-permute-start.20
  230.2 1.2 dynamic-slice_bitcast_fusion.2
  231.4 1.2 collective-permute-start.12
  232.6 7.7 %collective-permute-done.18 = bf16[4,256,256]{2,1,0:T(8,128)(2,1)S(1)} collective-permute-done((bf16[4,256,256]{2,1,0:T(8,128)(2,1)S(1)}, bf16[4,256,256]{2,1,0:T(8,128)(2,1)S(1)}, u32[]{:S(2)}, u32[]{:S(2)}) %collective-permute-start.18) | collective-permute-done | bytes 524320 | tf_op jit(solution)/shard_map/ppermute | solution.py:77
  241.0 11.4 %collective-permute-done.19 = bf16[4,256,256]{2,1,0:T(8,128)(2,1)} collective-permute-done((bf16[4,256,256]{2,1,0:T(8,128)(2,1)S(1)}, bf16[4,256,256]{2,1,0:T(8,128)(2,1)}, u32[]{:S(2)}, u32[]{:S(2)}) %collective-permute-start.19) | collective-permute-done | bytes 524320 | tf_op jit(solution)/shard_map/ppermute | solution.py:77
  252.3 3.2 %collective-permute-done.20 = bf16[4,256,256]{2,1,0:T(8,128)(2,1)} collective-permute-done((bf16[4,256,256]{2,1,0:T(8,128)(2,1)S(1)}, bf16[4,256,256]{2,1,0:T(8,128)(2,1)}, u32[]{:S(2)}, u32[]{:S(2)}) %collective-permute-start.20) | collective-permute-done | bytes 524320 | tf_op jit(solution)/shard_map/ppermute | solution.py:77
  255.5 1.4 select_bitcast_fusion.3
  257.3 5.7 %collective-permute-done.11 = bf16[2048,128]{1,0:T(8,128)(2,1)} collective-permute-done((bf16[2048,128]{1,0:T(8,128)(2,1)}, bf16[2048,128]{1,0:T(8,128)(2,1)}, u32[]{:S(2)}, u32[]{:S(2)}) %collective-permute-start.11) | collective-permute-done | bytes 524320 | tf_op jit(solution)/shard_map/ppermute | solution.py:77
  262.9 12.1 %collective-permute-done.12 = bf16[2048,128]{1,0:T(8,128)(2,1)} collective-permute-done((bf16[2048,128]{1,0:T(8,128)(2,1)}, bf16[2048,128]{1,0:T(8,128)(2,1)}, u32[]{:S(2)}, u32[]{:S(2)}) %collective-permute-start.12) | collective-permute-done | bytes 524320 | tf_op jit(solution)/shard_map/ppermute | solution.py:77
  275.0 1.9 fusion.4
  278.0 9.9 %collective-permute-start.15 = (bf16[2048,128]{1,0:T(8,128)(2,1)S(1)}, bf16[2048,128]{1,0:T(8,128)(2,1)S(1)}, u32[]{:S(2)}, u32[]{:S(2)}) collective-permute-start(bf16[2048,128]{1,0:T(8,128)(2,1)S(1)} %collective-permute-done.14), channel_id=1, source_target_pairs={{0,1},{1,0},{2,3},{3,2},{4,5},{5,4},{6,7},{7,6},{8,9},{9,8},{10,11... | collective-permute-start | bytes 1572872 | tf_op jit(solution)/shard_map/ppermute | solution.py:77
  287.9 5.6 %collective-permute-done.16 = bf16[2048,128]{1,0:T(8,128)(2,1)S(1)} collective-permute-done((bf16[2048,128]{1,0:T(8,128)(2,1)S(1)}, bf16[2048,128]{1,0:T(8,128)(2,1)S(1)}, u32[]{:S(2)}, u32[]{:S(2)}) %collective-permute-start.16) | collective-permute-done | bytes 524320 | tf_op jit(solution)/shard_map/ppermute | solution.py:206
  293.6 1.8 collective-permute-done.17
  295.6 1.6 pad_maximum_fusion.3
  298.5 2.3 fusion.60
  (94 shorter events, 19.4 us)
Async XLA Ops:
  7.2 138.1 %all-gather.2.cloned.1.call-start = ((), (), s32[]{:S(2)}) async-start(), calls=%async_computation.6 | async-start | bytes 8519680 | tf_op jit(solution)/shard_map/all_gather | solution.py:143
  9.3 0.7 collective-permute-start.3
  10.0 0.7 copy-start.9
  68.1 15.0 %collective-permute-start.5 = (bf16[4,32,16,128]{3,2,1,0:T(8,128)(2,1)}, bf16[4,32,16,128]{3,2,1,0:T(8,128)(2,1)S(1)}, u32[]{:S(2)}, u32[]{:S(2)}) collective-permute-start(bf16[4,32,16,128]{3,2,1,0:T(8,128)(2,1)} %all_to_all.31), channel_id=1, source_target_pairs={{0,2},{2,0},{1,3},{3,1},{4,6},{6,4},{5,7},{7,5},{8,10},{10,8},{9,1... | collective-permute-start | bytes 1572872 | tf_op jit(solution)/shard_map/ppermute | solution.py:77
  68.1 27.3 %collective-permute-start.6 = (bf16[4,32,16,128]{3,2,1,0:T(8,128)(2,1)}, bf16[4,32,16,128]{3,2,1,0:T(8,128)(2,1)S(1)}, u32[]{:S(2)}, u32[]{:S(2)}) collective-permute-start(bf16[4,32,16,128]{3,2,1,0:T(8,128)(2,1)} %all_to_all.31), channel_id=1, source_target_pairs={{0,128},{128,0},{1,129},{129,1},{2,130},{130,2},{3,131},{131,3},{4... | collective-permute-start | bytes 1572872 | tf_op jit(solution)/shard_map/ppermute | solution.py:77
  71.1 27.1 %collective-permute-start.7 = (bf16[4,32,16,128]{3,2,1,0:T(8,128)(2,1)}, bf16[4,32,16,128]{3,2,1,0:T(8,128)(2,1)}, u32[]{:S(2)}, u32[]{:S(2)}) collective-permute-start(bf16[4,32,16,128]{3,2,1,0:T(8,128)(2,1)} %all_to_all.31), channel_id=1, source_target_pairs={{0,130},{2,128},{128,2},{130,0},{1,131},{3,129},{129,3},{131,1},{4... | collective-permute-start | bytes 1572872 | tf_op jit(solution)/shard_map/ppermute | solution.py:77
  83.1 12.3 %copy-start.7 = (bf16[4,32,16,128]{3,2,1,0:T(8,128)(2,1)}, bf16[4,32,16,128]{3,2,1,0:T(8,128)(2,1)S(1)}, u32[]{:S(2)}) copy-start(bf16[4,32,16,128]{3,2,1,0:T(8,128)(2,1)S(1)} %collective-permute-done.5) | copy-start | bytes 1572868
  95.3 0.8 copy-start.8
  100.0 1.6 copy-start.2
  100.0 1.6 copy-start.4
  100.0 1.6 copy-start.11
  100.0 2.3 copy-start.12
  100.0 3.0 copy-start.10
  101.6 37.4 %collective-permute-start.8 = (bf16[4,4,32,16,128]{4,3,2,1,0:T(8,128)(2,1)}, bf16[4,4,32,16,128]{4,3,2,1,0:T(8,128)(2,1)}, u32[]{:S(2)}, u32[]{:S(2)}) collective-permute-start(bf16[4,4,32,16,128]{4,3,2,1,0:T(8,128)(2,1)} %pad_maximum_fusion.2), channel_id=1, source_target_pairs={{0,1},{1,0},{2,3},{3,2},{4,5},{5,4},{6,7},{7,6},{8,9},{9,8},{10,11... | collective-permute-start | bytes 6291464 | tf_op jit(solution)/shard_map/ppermute | solution.py:77
  101.6 2.1 collective-permute-start.4
  102.3 10.0 %collective-permute-start.10 = (f32[8]{0:T(128)S(1)}, f32[8]{0:T(128)S(1)}, u32[]{:S(2)}, u32[]{:S(2)}) collective-permute-start(f32[8]{0:T(128)S(1)} %bitcast.122), channel_id=1, source_target_pairs={{0,0},{1,2},{2,1},{3,3},{4,4},{5,6},{6,5},{7,7},{8,8},{9,10},{10,9... | collective-permute-start | bytes 104 | tf_op jit(solution)/shard_map/ppermute | solution.py:72
  103.0 54.7 %collective-permute-start.9 = (bf16[512,128]{1,0:T(8,128)(2,1)S(1)}, bf16[512,128]{1,0:T(8,128)(2,1)S(1)}, u32[]{:S(2)}, u32[]{:S(2)}) collective-permute-start(bf16[512,128]{1,0:T(8,128)(2,1)S(1)} %bitcast.120), channel_id=1, source_target_pairs={{0,0},{1,2},{2,1},{3,3},{4,4},{5,6},{6,5},{7,7},{8,8},{9,10},{10,9... | collective-permute-start | bytes 393224 | tf_op jit(solution)/shard_map/ppermute | solution.py:72
  103.9 22.9 %collective-permute-start = (bf16[32,64,128]{2,1,0:T(8,128)(2,1)S(1)}, bf16[32,64,128]{2,1,0:T(8,128)(2,1)S(1)}, u32[]{:S(2)}, u32[]{:S(2)}) collective-permute-start(bf16[32,64,128]{2,1,0:T(8,128)(2,1)S(1)} %slice.64), channel_id=1, source_target_pairs={{0,2},{2,0},{1,3},{3,1},{4,6},{6,4},{5,7},{7,5},{8,10},{10,8},{9,1... | collective-permute-start | bytes 1572872 | tf_op jit(solution)/shard_map/ppermute | solution.py:77
  111.6 24.9 %collective-permute-start.1 = (bf16[32,64,128]{2,1,0:T(8,128)(2,1)S(1)}, bf16[32,64,128]{2,1,0:T(8,128)(2,1)S(1)}, u32[]{:S(2)}, u32[]{:S(2)}) collective-permute-start(bf16[32,64,128]{2,1,0:T(8,128)(2,1)S(1)} %slice.64), channel_id=1, source_target_pairs={{0,128},{128,0},{1,129},{129,1},{2,130},{130,2},{3,131},{131,3},{4... | collective-permute-start | bytes 1572872 | tf_op jit(solution)/shard_map/ppermute | solution.py:77
  112.3 26.2 %collective-permute-start.2 = (bf16[32,64,128]{2,1,0:T(8,128)(2,1)S(1)}, bf16[32,64,128]{2,1,0:T(8,128)(2,1)S(1)}, u32[]{:S(2)}, u32[]{:S(2)}) collective-permute-start(bf16[32,64,128]{2,1,0:T(8,128)(2,1)S(1)} %slice.64), channel_id=1, source_target_pairs={{0,130},{2,128},{128,2},{130,0},{1,131},{3,129},{129,3},{131,1},{4... | collective-permute-start | bytes 1572872 | tf_op jit(solution)/shard_map/ppermute | solution.py:77
  138.7 1.0 copy-start.3
  138.7 1.2 copy-start.5
  139.0 6.3 %copy-start.1 = (bf16[32,4,64,128]{3,2,1,0:T(8,128)(2,1)}, bf16[32,4,64,128]{3,2,1,0:T(8,128)(2,1)S(1)}, u32[]{:S(2)}) copy-start(bf16[32,4,64,128]{3,2,1,0:T(8,128)(2,1)S(1)} %pad_maximum_fusion.1) | copy-start | bytes 6291460
  145.3 6.4 %copy-start = (bf16[512,8192]{1,0:T(8,128)(2,1)S(1)}, bf16[512,8192]{1,0:T(8,128)(2,1)}, u32[]{:S(2)}) copy-start(bf16[512,8192]{1,0:T(8,128)(2,1)} %all-gather.2.cloned.1.call-done.rows_ref) | copy-start | bytes 25165828
  175.7 13.1 %all-to-all-start.3 = ((bf16[8,64,256]{2,1,0:T(8,128)(2,1)}), bf16[8,64,256]{2,1,0:T(8,128)(2,1)S(1)}, u32[]{:S(2)}, u32[]{:S(2)}) async-start(bf16[8,64,256]{2,1,0:T(8,128)(2,1)} %broadcast_in_dim.11), calls=%async_computation.3 | async-start | bytes 524288 | tf_op jit(solution)/shard_map/all_to_all | solution.py:81
  188.8 0.7 copy-start.6
  195.5 13.1 %all-to-all-start.4 = ((bf16[4,256,256]{2,1,0:T(8,128)(2,1)}), bf16[4,256,256]{2,1,0:T(8,128)(2,1)S(1)}, u32[]{:S(2)}, u32[]{:S(2)}) async-start(bf16[4,256,256]{2,1,0:T(8,128)(2,1)} %bitcast.110), calls=%async_computation.4 | async-start | bytes 1048576 | tf_op jit(solution)/shard_map/all_to_all | solution.py:81
  225.5 14.8 %collective-permute-start.18 = (bf16[4,256,256]{2,1,0:T(8,128)(2,1)S(1)}, bf16[4,256,256]{2,1,0:T(8,128)(2,1)S(1)}, u32[]{:S(2)}, u32[]{:S(2)}) collective-permute-start(bf16[4,256,256]{2,1,0:T(8,128)(2,1)S(1)} %all_to_all.33), channel_id=1, source_target_pairs={{0,2},{2,0},{1,3},{3,1},{4,6},{6,4},{5,7},{7,5},{8,10},{10,8},{9,1... | collective-permute-start | bytes 1572872 | tf_op jit(solution)/shard_map/ppermute | solution.py:77
  226.1 26.2 %collective-permute-start.19 = (bf16[4,256,256]{2,1,0:T(8,128)(2,1)S(1)}, bf16[4,256,256]{2,1,0:T(8,128)(2,1)}, u32[]{:S(2)}, u32[]{:S(2)}) collective-permute-start(bf16[4,256,256]{2,1,0:T(8,128)(2,1)S(1)} %all_to_all.33), channel_id=1, source_target_pairs={{0,128},{128,0},{1,129},{129,1},{2,130},{130,2},{3,131},{131,3},{4... | collective-permute-start | bytes 1572872 | tf_op jit(solution)/shard_map/ppermute | solution.py:77
  228.2 27.3 %collective-permute-start.20 = (bf16[4,256,256]{2,1,0:T(8,128)(2,1)S(1)}, bf16[4,256,256]{2,1,0:T(8,128)(2,1)}, u32[]{:S(2)}, u32[]{:S(2)}) collective-permute-start(bf16[4,256,256]{2,1,0:T(8,128)(2,1)S(1)} %all_to_all.33), channel_id=1, source_target_pairs={{0,130},{2,128},{128,2},{130,0},{1,131},{3,129},{129,3},{131,1},{4... | collective-permute-start | bytes 1572872 | tf_op jit(solution)/shard_map/ppermute | solution.py:77
  231.4 31.5 %collective-permute-start.11 = (bf16[2048,128]{1,0:T(8,128)(2,1)}, bf16[2048,128]{1,0:T(8,128)(2,1)}, u32[]{:S(2)}, u32[]{:S(2)}) collective-permute-start(bf16[2048,128]{1,0:T(8,128)(2,1)} %get-tuple-element.25), channel_id=1, source_target_pairs={{0,2},{2,0},{1,3},{3,1},{4,6},{6,4},{5,7},{7,5},{8,10},{10,8},{9,1... | collective-permute-start | bytes 1572872 | tf_op jit(solution)/shard_map/ppermute | solution.py:77
  231.4 43.6 %collective-permute-start.12 = (bf16[2048,128]{1,0:T(8,128)(2,1)}, bf16[2048,128]{1,0:T(8,128)(2,1)}, u32[]{:S(2)}, u32[]{:S(2)}) collective-permute-start(bf16[2048,128]{1,0:T(8,128)(2,1)} %get-tuple-element.27), channel_id=1, source_target_pairs={{0,130},{2,128},{128,2},{130,0},{1,131},{3,129},{129,3},{131,1},{4... | collective-permute-start | bytes 1572872 | tf_op jit(solution)/shard_map/ppermute | solution.py:77
  240.3 34.7 %collective-permute-start.13 = (bf16[2048,128]{1,0:T(8,128)(2,1)}, bf16[2048,128]{1,0:T(8,128)(2,1)}, u32[]{:S(2)}, u32[]{:S(2)}) collective-permute-start(bf16[2048,128]{1,0:T(8,128)(2,1)} %get-tuple-element.26), channel_id=1, source_target_pairs={{0,128},{128,0},{1,129},{129,1},{2,130},{130,2},{3,131},{131,3},{4... | collective-permute-start | bytes 1572872 | tf_op jit(solution)/shard_map/ppermute | solution.py:77
  257.2 40.0 %collective-permute-start.21 = (bf16[4,4,256,256]{3,2,1,0:T(8,128)(2,1)S(1)}, bf16[4,4,256,256]{3,2,1,0:T(8,128)(2,1)S(1)}, u32[]{:S(2)}, u32[]{:S(2)}) collective-permute-start(bf16[4,4,256,256]{3,2,1,0:T(8,128)(2,1)S(1)} %pad_maximum_fusion.4), channel_id=1, source_target_pairs={{0,1},{1,0},{2,3},{3,2},{4,5},{5,4},{6,7},{7,6},{8,9},{9,8},{10,11... | collective-permute-start | bytes 6291464 | tf_op jit(solution)/shard_map/ppermute | solution.py:77
  276.9 1.0 collective-permute-start.14
  277.6 15.9 %collective-permute-start.16 = (bf16[2048,128]{1,0:T(8,128)(2,1)S(1)}, bf16[2048,128]{1,0:T(8,128)(2,1)S(1)}, u32[]{:S(2)}, u32[]{:S(2)}) collective-permute-start(bf16[2048,128]{1,0:T(8,128)(2,1)S(1)} %fusion.4), channel_id=1, source_target_pairs={{0,128},{1,130},{2,129},{3,131},{128,0},{129,2},{130,1},{131,3},{4... | collective-permute-start | bytes 1572872 | tf_op jit(solution)/shard_map/ppermute | solution.py:206
  278.0 15.6 %collective-permute-start.15 = (bf16[2048,128]{1,0:T(8,128)(2,1)S(1)}, bf16[2048,128]{1,0:T(8,128)(2,1)S(1)}, u32[]{:S(2)}, u32[]{:S(2)}) collective-permute-start(bf16[2048,128]{1,0:T(8,128)(2,1)S(1)} %collective-permute-done.14), channel_id=1, source_target_pairs={{0,1},{1,0},{2,3},{3,2},{4,5},{5,4},{6,7},{7,6},{8,9},{9,8},{10,11... | collective-permute-start | bytes 1572872 | tf_op jit(solution)/shard_map/ppermute | solution.py:77
  293.5 1.9 collective-permute-start.17
Sparse Core Ops, SparseCore 0:
  10.8 91.2 all-gather.1
where the time goes:
time: 310 us; the launch traced here: 308 us
  waiting for transfers between devices  114 us (37%)
  blocking collectives  79.1 us (26%)
  starting transfers between devices  42.6 us (14%)
  other arithmetic  18.5 us (6%)
  local copies, waits for them, and re-layouts  17.2 us (6%)
  matrix products  15.4 us (5%)
  between operations  14.6 us (5%)
  Pallas kernels  6.04 us (2%)
    ppermute x16, waiting for transfers between devices, flip(): return lax.ppermute(x, axes, [(i, n - 1 - i) for i in range(n)])  90.4 us
    all_to_all x4, blocking collectives, exchange(): return lax.all_to_all(x, axes, split_axis=0, concat_axis=0, tiled=True)  79.1 us
    ppermute x16, starting transfers between devices, flip(): return lax.ppermute(x, axes, [(i, n - 1 - i) for i in range(n)])  31.8 us
    all_to_all x2, waiting for transfers between devices, exchange(): return lax.all_to_all(x, axes, split_axis=0, concat_axis=0, tiled=True)  18 us
    dot_general x2, matrix products, project(): return jnp.dot(normed, cols, preferred_element_type=f32) * inv_width  11 us
    all_to_all x2, starting transfers between devices, exchange(): return lax.all_to_all(x, axes, split_axis=0, concat_axis=0, tiled=True)  7.1 us
  transfers between devices with their start and end apart: 25, of which 15 were waited for; matrix products, arithmetic and copies ran while one was open for 12% of the time, Pallas kernels for 0%

commit v1 on v0

--- a/solution.py
+++ b/solution.py
@@ -93,36 +93,31 @@
 
 
 def x_ring(x, xh, xl):
-    low = ordered(x, flip(x, ("xl",)), xl)
-    high = ordered(flip(x, ("xh",)), flip(x, X), xl)
+    near, wrap = flip(x, ("xl",)), flip(x, X)
+    half = x.shape[0] // 2
+    far = jnp.concatenate([flip(wrap[:half], ("xl",)), flip(near[half:], X)], axis=0)
+    low = ordered(x, near, xl)
+    high = ordered(far, wrap, xl)
     col0 = ordered(low[0], high[0], xh)
     col1 = ordered(low[1], high[1], xh)
     return (col0[0], col1[0]), (col0[1], col1[1])
 
 
-def member_parts(normed, kv, member):
-    def body(at_ref, rows_ref, kv_ref, out_ref):
-        out_ref[...] = lax.dot_general(
-            rows_ref[...],
-            kv_ref[...],
-            (((0,), (0,)), ((), ())),
-            preferred_element_type=jnp.float32,
-        ).astype(jnp.bfloat16)
+def member_columns(normed, member):
+    def body(at_ref, rows_ref, out_ref):
+        out_ref[...] = rows_ref[...]
 
     return pl.pallas_call(
         body,
-        out_shape=jax.ShapeDtypeStruct((1024, 2 * HD), jnp.bfloat16),
+        out_shape=jax.ShapeDtypeStruct((512, 1024), jnp.bfloat16),
         grid_spec=pltpu.PrefetchScalarGridSpec(
             num_scalar_prefetch=1,
             grid=(8,),
-            in_specs=[
-                pl.BlockSpec((512, HD), lambda b, at: (0, b * 8 + at[0])),
-                pl.BlockSpec((512, 2 * HD), lambda b, at: (0, 0)),
-            ],
-            out_specs=pl.BlockSpec((HD, 2 * HD), lambda b, at: (b, 0)),
+            in_specs=[pl.BlockSpec((512, HD), lambda b, at: (0, b * 8 + at[0]))],
+            out_specs=pl.BlockSpec((512, HD), lambda b, at: (0, b)),
         ),
-        name="member_parts",
-    )(member.reshape(1).astype(jnp.int32), normed, kv)
+        name="member_columns",
+    )(member.reshape(1).astype(jnp.int32), normed)
 
 
 def local(hidden, cotangent, seg_ids, advantage, w_query, w_key, w_value):
@@ -149,20 +144,17 @@
     wq = w_query.reshape(2, 64, 32, 2, HD)
     wq = lax.dynamic_index_in_dim(wq, xh, 0, keepdims=False)
     wq = lax.dynamic_index_in_dim(wq, core, 2, keepdims=False).transpose(1, 0, 2)
-    wkv = jnp.stack([w_key.reshape(4, 4, 8, 8, HD), w_value.reshape(4, 4, 8, 8, HD)], axis=2)
+    wkv = jnp.stack([w_key.reshape(4, 32, 8, HD), w_value.reshape(4, 32, 8, HD)], axis=1)
     wkv = lax.dynamic_index_in_dim(wkv, xh * 2 + core, 0, keepdims=False)
-    wkv = wkv.transpose(3, 0, 1, 2, 4).reshape(32, 16, HD)
+    wkv = wkv.transpose(2, 0, 1, 3).reshape(8, 1, 64, HD)
+    wkv = jnp.broadcast_to(wkv, (8, 4, 64, HD)).reshape(32, 64, HD)
     cut = exchange(jnp.concatenate([wq, wkv], axis=1), YZ)
-    wq = cut[:, :64]
-    wkv = spread(cut[:, 64:], ("zl",))
-
-    wq = x_ring(wq, xh, xl)
-    q_cols = jnp.stack([wq[h][l] for l in (0, 1) for h in (0, 1)], axis=1).reshape(D, HD)
-    wkv = x_ring(wkv, xh, xl)
-    wkv = jnp.stack([wkv[h][l] for l in (0, 1) for h in (0, 1)], axis=0)
-    wkv = jnp.stack(ordered(wkv, flip(wkv, ("core",)), core), axis=0)
-    wkv = wkv.reshape(2, 2, 2, 4, 32, 2, 8, HD).transpose(4, 1, 2, 0, 3, 6, 5, 7)
-    wkv = wkv.reshape(D, 2 * HD)
+    cut = x_ring(cut, xh, xl)
+    order = [(h, l) for l in (0, 1) for h in (0, 1)]
+    q_cols = jnp.stack([cut[h][l][:, :64] for h, l in order], axis=1).reshape(D, HD)
+    wkv = jnp.stack([cut[h][l][:, 64:] for h, l in order], axis=1)
+    wkv = jnp.stack(ordered(wkv, flip(wkv, ("core",)), core), axis=2)
+    wkv = wkv.reshape(128, 2, 2, 32, HD).transpose(0, 1, 3, 2, 4).reshape(D, 2 * HD)
 
     cosine_table, sine_table = angles(seg_row)
     weight_row = token_weights(seg_row, adv_row)
@@ -190,16 +182,21 @@
     part_q = part_q.astype(bf16).reshape(4, 2048, HD)
     part_q, scaled_kv = lax.optimization_barrier((part_q, scaled_kv))
 
-    def to_ring(mask, axes):
-        piece = lax.dynamic_index_in_dim(part_q, ring ^ mask, 0, keepdims=False)
-        return flip(piece, axes)
-
-    sum_q = (
-        lax.dynamic_index_in_dim(part_q, ring, 0, keepdims=False).astype(f32)
-        + to_ring(1, ("xl",)).astype(f32)
-        + to_ring(3, X).astype(f32)
-        + to_ring(2, ("xh",)).astype(f32)
-    )
+    def part_for(mask):
+        return lax.dynamic_index_in_dim(part_q, ring ^ mask, 0, keepdims=False)
+
+    def add(a, b):
+        return (a.astype(f32) + b.astype(f32)).astype(bf16)
+
+    far = part_for(2)
+    first = flip(far[:1024], X)
+    second = flip(far[1024:], ("xl",))
+    near, wrap = part_for(1), part_for(3)
+    near = jnp.concatenate([add(near[:1024], first), near[1024:]], axis=0)
+    wrap = jnp.concatenate([wrap[:1024], add(wrap[1024:], second)], axis=0)
+    near = flip(near, ("xl",))
+    wrap = flip(wrap, X)
+    sum_q = part_for(0).astype(f32) + near.astype(f32) + wrap.astype(f32)
     old_q = lax.dynamic_slice_in_dim(q_cols, ring * 2048, 2048)
     new_q = (old_q.astype(f32) - step_rate * sum_q).astype(bf16)
     near = swap(new_q)
@@ -225,7 +222,9 @@
     kv_sum = kv_sum.astype(f32)
     kv_sum = jnp.sum(kv_sum, axis=0).astype(bf16)
     kv_sum = spread(kv_sum, MEM).reshape(block_len, 2 * HD)
-    part_kv = member_parts(normed, kv_sum, member)
+    part_kv = lax.dot_general(
+        member_columns(normed, member), kv_sum, contract, preferred_element_type=f32
+    ).astype(bf16)
     part_kv = exchange(part_kv.reshape(4, 256, 2 * HD), X).astype(f32)
     old_kv = wkv.reshape(4, 2, 8, 128, 2 * HD)
     old_kv = lax.dynamic_index_in_dim(old_kv, ring, 0, keepdims=False)

time: 310 us -> 289 us (0.932)
  waiting for transfers between devices: 114 us -> 84.7 us
  local copies, waits for them, and re-layouts: 17.2 us -> 36.1 us
  blocking collectives: 79.1 us -> 60.9 us
  starting transfers between devices: 42.6 us -> 49.4 us
    ppermute x16, waiting for transfers between devices: 90.4 us -> 65.9 us  [flip(): return lax.ppermute(x, axes, [(i, n - 1 - i) for i in range(n)])]
    all_to_all x4 -> x2, blocking collectives: 79.1 us -> 60.9 us  [exchange(): return lax.all_to_all(x, axes, split_axis=0, concat_axis=0, tiled=True)]
    another operation x0 -> x5, local copies, waits for them, and re-layouts: none -> 10.1 us  [the longest x1 7.61 us: local(): old_kv = wkv.reshape(4, 2, 8, 128, 2 * HD)]
    transpose x1, local copies, waits for them, and re-layouts: 0.11 us -> 6.43 us  [local(): wkv.reshape(128, 2, 2, 32, HD).transpose(0, 1, 3, 2, 4).reshape(D, 2 * HD)]
    ppermute x1, waiting for transfers between devices: 5.59 us -> 0.01 us  [local(): lax.ppermute(new_q, ('xh', 'xl', 'core'), [(h * 4 + l * 2 + c, (1 - h) *...]
    slice x2 -> x5, local copies, waits for them, and re-layouts: 0.07 us -> 3.55 us  [the longest x2 1.8 us: x_ring(): near[half:]]
    all_to_all x2 -> x3, starting transfers between devices: 7.1 us -> 10.4 us  [exchange(): return lax.all_to_all(x, axes, split_axis=0, concat_axis=0, tiled=True)]
    another operation x6 -> x4, other arithmetic: 6.67 us -> 4.09 us  [the longest x1 1.89 us: local(): jnp.stack([cut[h][l][:, :64] for h, l in order], axis=1).reshape(D, HD)]
  transfers between devices with their start and end apart: 25 -> 26, of which waited for: 15 -> 13; matrix products, arithmetic and copies ran while one was open for 12% -> 19% of each run, Pallas kernels for 0% -> 2%
where the time goes in v1:
time: 289 us; the launch traced here: 286 us
  waiting for transfers between devices  84.7 us (29%)
  blocking collectives  60.9 us (21%)
  starting transfers between devices  49.4 us (17%)
  local copies, waits for them, and re-layouts  36.1 us (12%)
  other arithmetic  18.4 us (6%)
  matrix products  16.9 us (6%)
  between operations  14.7 us (5%)
  Pallas kernels  5.19 us (2%)
    ppermute x16, waiting for transfers between devices, flip(): return lax.ppermute(x, axes, [(i, n - 1 - i) for i in range(n)])  65.9 us
    all_to_all x2, blocking collectives, exchange(): return lax.all_to_all(x, axes, split_axis=0, concat_axis=0, tiled=True)  60.9 us
    ppermute x16, starting transfers between devices, flip(): return lax.ppermute(x, axes, [(i, n - 1 - i) for i in range(n)])  32.9 us
    all_to_all x3, waiting for transfers between devices, exchange(): return lax.all_to_all(x, axes, split_axis=0, concat_axis=0, tiled=True)  18.8 us
    all_to_all x3, starting transfers between devices, exchange(): return lax.all_to_all(x, axes, split_axis=0, concat_axis=0, tiled=True)  10.4 us
    dot_general x2, matrix products, project(): return jnp.dot(normed, cols, preferred_element_type=f32) * inv_width  10 us
    another operation x1, local copies, waits for them, and re-layouts, local(): old_kv = wkv.reshape(4, 2, 8, 128, 2 * HD)  7.61 us
    transpose x1, local copies, waits for them, and re-layouts, local(): wkv.reshape(128, 2, 2, 32, HD).transpose(0, 1, 3, 2, 4).reshape(D, 2 * HD)  6.43 us
  transfers between devices with their start and end apart: 26, of which 13 were waited for; matrix products, arithmetic and copies ran while one was open for 19% of the time, Pallas kernels for 2%

profile of v1, /device:TPU:8, one launch (start us, length us, event | category | flops | bytes accessed | tf_op | source)
XLA Modules:
  0.0 286.3 jit_solution(7665287041120595273)
XLA Ops:
  7.2 1.1 fusion.20
  8.3 1.0 fusion.21
  10.7 1.0 copy.58
  11.7 1.0 copy.59
  12.9 3.2 %reshape.112 = bf16[2,64,32,2,128]{4,3,2,1,0:T(2,128)(2,1)S(1)} reshape(bf16[128,8192]{1,0:T(8,128)(2,1)} %param.11) | data formatting | bytes 4194304 | tf_op jit(solution)/shard_map/reshape | solution.py:144
  16.2 1.2 constant_dynamic-slice_fusion.1
  18.2 37.5 %all_to_all.25 = bf16[32,128,128]{2,1,0:T(8,128)(2,1)S(1)} all-to-all(bf16[32,128,128]{2,1,0:T(8,128)(2,1)S(1)} %copy.47), channel_id=1, replica_groups=mesh['xh'=2,'y'=4,'zh'=2,'zl'=4,'xl'=2,'core'=2] {'y','zh','zl'}, dimensions={0} | all-to-all | bytes 2097152 | tf_op jit(solution)/shard_map/all_to_all | solution.py:81
  55.6 7.0 %collective-permute-start.1 = (bf16[32,128,128]{2,1,0:T(8,128)(2,1)S(1)}, bf16[32,128,128]{2,1,0:T(8,128)(2,1)S(1)}, u32[]{:S(2)}, u32[]{:S(2)}) collective-permute-start(bf16[32,128,128]{2,1,0:T(8,128)(2,1)S(1)} %all_to_all.25), channel_id=1, source_target_pairs={{0,130},{2,128},{128,2},{130,0},{1,131},{3,129},{129,3},{131,1},{4... | collective-permute-start | bytes 3145736 | tf_op jit(solution)/shard_map/ppermute | solution.py:77
  62.7 22.6 %collective-permute-done.1 = bf16[32,128,128]{2,1,0:T(8,128)(2,1)S(1)} collective-permute-done((bf16[32,128,128]{2,1,0:T(8,128)(2,1)S(1)}, bf16[32,128,128]{2,1,0:T(8,128)(2,1)S(1)}, u32[]{:S(2)}, u32[]{:S(2)}) %collective-permute-start.1) | collective-permute-done | bytes 1048608 | tf_op jit(solution)/shard_map/ppermute | solution.py:77
  86.1 1.2 collective-permute-start.2
  87.3 1.0 collective-permute-done
  90.1 10.4 %collective-permute-done.2 = bf16[16,128,128]{2,1,0:T(8,128)(2,1)} collective-permute-done((bf16[16,128,128]{2,1,0:T(8,128)(2,1)}, bf16[16,128,128]{2,1,0:T(8,128)(2,1)}, u32[]{:S(2)}, u32[]{:S(2)}) %collective-permute-start.2) | collective-permute-done | bytes 524320 | tf_op jit(solution)/shard_map/ppermute | solution.py:77
  100.5 1.1 constant_dynamic-update-slice_fusion.1
  101.6 2.9 %collective-permute-done.3 = bf16[16,128,128]{2,1,0:T(8,128)(2,1)} collective-permute-done((bf16[16,128,128]{2,1,0:T(8,128)(2,1)}, bf16[16,128,128]{2,1,0:T(8,128)(2,1)}, u32[]{:S(2)}, u32[]{:S(2)}) %collective-permute-start.3) | collective-permute-done | bytes 524320 | tf_op jit(solution)/shard_map/ppermute | solution.py:77
  104.5 1.1 constant_dynamic-update-slice_fusion
  106.0 1.2 slice_bitcast_fusion.4
  107.1 1.2 slice_bitcast_fusion.6
  108.4 1.6 pad_maximum_fusion.1
  112.5 1.9 pad_maximum_fusion
  114.5 2.7 broadcast_select_fusion.3
  118.1 6.4 %copy.53 = bf16[128,2,32,2,128]{4,3,2,1,0:T(2,128)(2,1)} copy(bf16[128,2,32,2,128]{4,2,3,0,1:T(8,128)(2,1)S(1)} %maximum_bitcast_fusion) | data formatting | bytes 8388608 | tf_op jit(solution)/shard_map/transpose | solution.py:157
  124.5 7.1 %fusion.3 = f32[512,256]{0,1:T(8,128)S(1)} fusion(bf16[512,8192]{1,0:T(8,128)(2,1)} %all-gather.2.cloned.1.call-done.rows_ref, bf16[1024,8,2,128]{3,2,1,0:T(2,128)(2,1)} %bitcast.119), kind=kOutput, calls=%fused_computation.16 | convolution fusion | flops 2147614720 | bytes 13107200 | tf_op jit(solution)/shard_map/dot_general | solution.py:166
  131.6 2.9 %convolution_multiply_fusion.3 = f32[512,128]{0,1:T(8,128)S(1)} fusion(bf16[512,8192]{1,0:T(8,128)(2,1)S(1)} %copy-done, bf16[8192,128]{1,0:T(8,128)(2,1)S(1)} %bitcast.124), kind=kOutput, calls=%fused_computation.19 | convolution fusion | flops 1073807360 | bytes 10747904 | tf_op jit(solution)/shard_map/dot_general | solution.py:166
  138.7 2.4 convolution_convert_fusion
  141.3 23.5 %all_to_all.26 = bf16[8,64,256]{2,1,0:T(8,128)(2,1)S(1)} all-to-all(bf16[8,64,256]{2,1,0:T(8,128)(2,1)S(1)} %bitcast.133), channel_id=1, replica_groups=mesh['xh'=2,'y'=4,'zh'=2,'zl'=4,'xl'=2,'core'=2] {'zl','core'}, dimensions={0} | all-to-all | bytes 524288 | tf_op jit(solution)/shard_map/all_to_all | solution.py:81
  165.5 3.4 %all-to-all-start.2 = ((bf16[8,64,256]{2,1,0:T(8,128)(2,1)}), bf16[8,64,256]{2,1,0:T(8,128)(2,1)S(1)}, u32[]{:S(2)}, u32[]{:S(2)}) async-start(bf16[8,64,256]{2,1,0:T(8,128)(2,1)} %broadcast_in_dim.14), calls=%async_computation.2 | async-start | bytes 524288 | tf_op jit(solution)/shard_map/all_to_all | solution.py:81
  168.9 5.2 %member_columns.1 = bf16[512,1024]{1,0:T(8,128)(2,1)} custom-call(s32[1]{0:T(128)} %bitcast.39.at_ref, bf16[512,8192]{1,0:T(8,128)(2,1)} %all-gather.2.cloned.1.call-done.rows_ref), custom_call_target="tpu_custom_call" | custom-call | tf_op jit(solution)/shard_map/member_columns/pallas_call | solution.py:110
  174.1 4.4 %all-to-all-done.2 = bf16[8,64,256]{2,1,0:T(8,128)(2,1)S(1)} async-done(((bf16[8,64,256]{2,1,0:T(8,128)(2,1)}), bf16[8,64,256]{2,1,0:T(8,128)(2,1)S(1)}, u32[]{:S(2)}, u32[]{:S(2)}) %all-to-all-start.2) | async-done | bytes 262176 | tf_op jit(solution)/shard_map/all_to_all | solution.py:81
  178.6 2.5 convolution_convert_fusion.1
  181.1 3.5 %all-to-all-start.3 = ((bf16[4,256,256]{2,1,0:T(8,128)(2,1)}), bf16[4,256,256]{2,1,0:T(8,128)(2,1)S(1)}, u32[]{:S(2)}, u32[]{:S(2)}) async-start(bf16[4,256,256]{2,1,0:T(8,128)(2,1)} %bitcast.42), calls=%async_computation.3 | async-start | bytes 1048576 | tf_op jit(solution)/shard_map/all_to_all | solution.py:81
  184.6 7.6 %reshape_reshape.3 = bf16[4,2,8,128,256]{4,3,2,1,0:T(8,128)(2,1)} reshape(bf16[128,2,32,2,128]{4,3,2,1,0:T(2,128)(2,1)} %copy.53) | data formatting | bytes 8388608 | tf_op jit(solution)/shard_map/reshape;reshape | solution.py:229
  194.9 3.5 %all-to-all-start.4 = ((bf16[4,256,256]{2,1,0:T(8,128)(2,1)}), bf16[4,256,256]{2,1,0:T(8,128)(2,1)S(1)}, u32[]{:S(2)}, u32[]{:S(2)}) async-start(bf16[4,256,256]{2,1,0:T(8,128)(2,1)} %broadcast_in_dim.15), calls=%async_computation.4 | async-start | bytes 1048576 | tf_op jit(solution)/shard_map/all_to_all | solution.py:81
  198.4 13.5 %all-to-all-done.4 = bf16[4,256,256]{2,1,0:T(8,128)(2,1)S(1)} async-done(((bf16[4,256,256]{2,1,0:T(8,128)(2,1)}), bf16[4,256,256]{2,1,0:T(8,128)(2,1)S(1)}, u32[]{:S(2)}, u32[]{:S(2)}) %all-to-all-start.4) | async-done | bytes 524320 | tf_op jit(solution)/shard_map/all_to_all | solution.py:81
  211.9 2.9 %collective-permute-start.18 = (bf16[4,256,256]{2,1,0:T(8,128)(2,1)S(1)}, bf16[4,256,256]{2,1,0:T(8,128)(2,1)S(1)}, u32[]{:S(2)}, u32[]{:S(2)}) collective-permute-start(bf16[4,256,256]{2,1,0:T(8,128)(2,1)S(1)} %all-to-all-done.4), channel_id=1, source_target_pairs={{0,130},{2,128},{128,2},{130,0},{1,131},{3,129},{129,3},{131,1},{4... | collective-permute-start | bytes 1572872 | tf_op jit(solution)/shard_map/ppermute | solution.py:77
  216.5 1.5 collective-permute-start.17
  218.1 13.7 %collective-permute-done.9 = bf16[1024,128]{1,0:T(8,128)(2,1)} collective-permute-done((bf16[1024,128]{1,0:T(8,128)(2,1)}, bf16[1024,128]{1,0:T(8,128)(2,1)}, u32[]{:S(2)}, u32[]{:S(2)}) %collective-permute-start.9) | collective-permute-done | bytes 262176 | tf_op jit(solution)/shard_map/ppermute | solution.py:77
  231.8 1.2 fusion.17
  233.6 2.5 collective-permute-start.12
  236.1 1.0 slice.167
  237.1 1.5 collective-permute-start.20
  238.8 2.5 collective-permute-done.19
  241.3 11.0 %collective-permute-done.20 = bf16[2,256,256]{2,1,0:T(8,128)(2,1)S(1)} collective-permute-done((bf16[2,256,256]{2,1,0:T(8,128)(2,1)S(1)}, bf16[2,256,256]{2,1,0:T(8,128)(2,1)S(1)}, u32[]{:S(2)}, u32[]{:S(2)}) %collective-permute-start.20) | collective-permute-done | bytes 262176 | tf_op jit(solution)/shard_map/ppermute | solution.py:77
  252.3 1.2 select_bitcast_fusion.3
  254.0 1.4 fusion.9
  256.0 2.8 collective-permute-start.15
  258.8 13.0 %collective-permute-start.14 = (bf16[2048,128]{1,0:T(8,128)(2,1)S(1)}, bf16[2048,128]{1,0:T(8,128)(2,1)S(1)}, u32[]{:S(2)}, u32[]{:S(2)}) collective-permute-start(bf16[2048,128]{1,0:T(8,128)(2,1)S(1)} %collective-permute-done.13), channel_id=1, source_target_pairs={{0,1},{1,0},{2,3},{3,2},{4,5},{5,4},{6,7},{7,6},{8,9},{9,8},{10,11... | collective-permute-start | bytes 1572872 | tf_op jit(solution)/shard_map/ppermute | solution.py:77
  274.3 1.6 pad_maximum_fusion.2
  277.2 2.3 fusion.66
  (109 shorter events, 23.7 us)
Async XLA Ops:
  7.2 117.3 %all-gather.2.cloned.1.call-start = ((), (), s32[]{:S(2)}) async-start(), calls=%async_computation.5 | async-start | bytes 8519680 | tf_op jit(solution)/shard_map/all_gather | solution.py:138
  9.3 0.7 collective-permute-start.4
  10.0 0.7 copy-start.9
  55.6 29.6 %collective-permute-start.1 = (bf16[32,128,128]{2,1,0:T(8,128)(2,1)S(1)}, bf16[32,128,128]{2,1,0:T(8,128)(2,1)S(1)}, u32[]{:S(2)}, u32[]{:S(2)}) collective-permute-start(bf16[32,128,128]{2,1,0:T(8,128)(2,1)S(1)} %all_to_all.25), channel_id=1, source_target_pairs={{0,130},{2,128},{128,2},{130,0},{1,131},{3,129},{129,3},{131,1},{4... | collective-permute-start | bytes 3145736 | tf_op jit(solution)/shard_map/ppermute | solution.py:77
  62.7 25.6 %collective-permute-start = (bf16[32,128,128]{2,1,0:T(8,128)(2,1)S(1)}, bf16[32,128,128]{2,1,0:T(8,128)(2,1)S(1)}, u32[]{:S(2)}, u32[]{:S(2)}) collective-permute-start(bf16[32,128,128]{2,1,0:T(8,128)(2,1)S(1)} %all_to_all.25), channel_id=1, source_target_pairs={{0,2},{2,0},{1,3},{3,1},{4,6},{6,4},{5,7},{7,5},{8,10},{10,8},{9,1... | collective-permute-start | bytes 3145736 | tf_op jit(solution)/shard_map/ppermute | solution.py:77
  86.1 14.4 %collective-permute-start.2 = (bf16[16,128,128]{2,1,0:T(8,128)(2,1)}, bf16[16,128,128]{2,1,0:T(8,128)(2,1)}, u32[]{:S(2)}, u32[]{:S(2)}) collective-permute-start(bf16[16,128,128]{2,1,0:T(8,128)(2,1)} %slice.146), channel_id=1, source_target_pairs={{0,2},{2,0},{1,3},{3,1},{4,6},{6,4},{5,7},{7,5},{8,10},{10,8},{9,1... | collective-permute-start | bytes 1572872 | tf_op jit(solution)/shard_map/ppermute | solution.py:77
  89.1 15.3 %collective-permute-start.3 = (bf16[16,128,128]{2,1,0:T(8,128)(2,1)}, bf16[16,128,128]{2,1,0:T(8,128)(2,1)}, u32[]{:S(2)}, u32[]{:S(2)}) collective-permute-start(bf16[16,128,128]{2,1,0:T(8,128)(2,1)} %slice.147), channel_id=1, source_target_pairs={{0,130},{2,128},{128,2},{130,0},{1,131},{3,129},{129,3},{131,1},{4... | collective-permute-start | bytes 1572872 | tf_op jit(solution)/shard_map/ppermute | solution.py:77
  107.1 1.2 copy-start.2
  108.3 1.6 copy-start.4
  108.3 1.7 copy-start.6
  108.3 1.7 copy-start.11
  108.4 2.3 copy-start.10
  108.4 3.0 %copy-start.12 = (f32[1,8]{1,0:T(1,128)S(1)}, f32[1,8]{1,0:T(1,128)}, u32[]{:S(2)}) copy-start(f32[1,8]{1,0:T(1,128)} %param.10) | copy-start | bytes 100
  110.0 4.5 %collective-permute-start.6 = (bf16[32,4,64,128]{3,2,0,1:T(8,128)(2,1)}, bf16[32,4,64,128]{3,2,0,1:T(8,128)(2,1)}, u32[]{:S(2)}, u32[]{:S(2)}) collective-permute-start(bf16[32,4,64,128]{3,2,0,1:T(8,128)(2,1)} %pad_maximum_fusion.1), channel_id=1, source_target_pairs={{0,1},{1,0},{2,3},{3,2},{4,5},{5,4},{6,7},{7,6},{8,9},{9,8},{10,11... | collective-permute-start | bytes 6291464 | tf_op jit(solution)/shard_map/ppermute | solution.py:77
  110.0 2.0 collective-permute-start.5
  110.7 25.2 %collective-permute-start.7 = (bf16[512,128]{1,0:T(8,128)(2,1)S(1)}, bf16[512,128]{1,0:T(8,128)(2,1)S(1)}, u32[]{:S(2)}, u32[]{:S(2)}) collective-permute-start(bf16[512,128]{1,0:T(8,128)(2,1)S(1)} %bitcast.140), channel_id=1, source_target_pairs={{0,0},{1,2},{2,1},{3,3},{4,4},{5,6},{6,5},{7,7},{8,8},{9,10},{10,9... | collective-permute-start | bytes 393224 | tf_op jit(solution)/shard_map/ppermute | solution.py:72
  111.4 0.8 collective-permute-start.8
  112.5 2.0 copy-start.3
  112.5 2.0 copy-start.5
  112.5 2.0 copy-start.7
  114.4 17.2 %copy-start.1 = (bf16[32,4,64,128]{3,2,1,0:T(8,128)(2,1)}, bf16[32,4,64,128]{3,2,1,0:T(8,128)(2,1)S(1)}, u32[]{:S(2)}) copy-start(bf16[32,4,64,128]{3,2,1,0:T(8,128)(2,1)S(1)} %pad_maximum_fusion) | copy-start | bytes 6291460
  124.5 7.1 %copy-start = (bf16[512,8192]{1,0:T(8,128)(2,1)S(1)}, bf16[512,8192]{1,0:T(8,128)(2,1)}, u32[]{:S(2)}) copy-start(bf16[512,8192]{1,0:T(8,128)(2,1)} %all-gather.2.cloned.1.call-done.rows_ref) | copy-start | bytes 25165828
  165.5 13.1 %all-to-all-start.2 = ((bf16[8,64,256]{2,1,0:T(8,128)(2,1)}), bf16[8,64,256]{2,1,0:T(8,128)(2,1)S(1)}, u32[]{:S(2)}, u32[]{:S(2)}) async-start(bf16[8,64,256]{2,1,0:T(8,128)(2,1)} %broadcast_in_dim.14), calls=%async_computation.2 | async-start | bytes 524288 | tf_op jit(solution)/shard_map/all_to_all | solution.py:81
  181.1 12.8 %all-to-all-start.3 = ((bf16[4,256,256]{2,1,0:T(8,128)(2,1)}), bf16[4,256,256]{2,1,0:T(8,128)(2,1)S(1)}, u32[]{:S(2)}, u32[]{:S(2)}) async-start(bf16[4,256,256]{2,1,0:T(8,128)(2,1)} %bitcast.42), calls=%async_computation.3 | async-start | bytes 1048576 | tf_op jit(solution)/shard_map/all_to_all | solution.py:81
  194.9 17.0 %all-to-all-start.4 = ((bf16[4,256,256]{2,1,0:T(8,128)(2,1)}), bf16[4,256,256]{2,1,0:T(8,128)(2,1)S(1)}, u32[]{:S(2)}, u32[]{:S(2)}) async-start(bf16[4,256,256]{2,1,0:T(8,128)(2,1)} %broadcast_in_dim.15), calls=%async_computation.4 | async-start | bytes 1048576 | tf_op jit(solution)/shard_map/all_to_all | solution.py:81
  211.9 21.1 %collective-permute-start.18 = (bf16[4,256,256]{2,1,0:T(8,128)(2,1)S(1)}, bf16[4,256,256]{2,1,0:T(8,128)(2,1)S(1)}, u32[]{:S(2)}, u32[]{:S(2)}) collective-permute-start(bf16[4,256,256]{2,1,0:T(8,128)(2,1)S(1)} %all-to-all-done.4), channel_id=1, source_target_pairs={{0,130},{2,128},{128,2},{130,0},{1,131},{3,129},{129,3},{131,1},{4... | collective-permute-start | bytes 1572872 | tf_op jit(solution)/shard_map/ppermute | solution.py:77
  215.7 16.1 %collective-permute-start.9 = (bf16[1024,128]{1,0:T(8,128)(2,1)}, bf16[1024,128]{1,0:T(8,128)(2,1)}, u32[]{:S(2)}, u32[]{:S(2)}) collective-permute-start(bf16[1024,128]{1,0:T(8,128)(2,1)} %get-tuple-element.27), channel_id=1, source_target_pairs={{0,130},{2,128},{128,2},{130,0},{1,131},{3,129},{129,3},{131,1},{4... | collective-permute-start | bytes 786440 | tf_op jit(solution)/shard_map/ppermute | solution.py:77
  216.0 15.7 %collective-permute-start.11 = (bf16[1024,128]{1,0:T(8,128)(2,1)}, bf16[1024,128]{1,0:T(8,128)(2,1)}, u32[]{:S(2)}, u32[]{:S(2)}) collective-permute-start(bf16[1024,128]{1,0:T(8,128)(2,1)} %get-tuple-element.29), channel_id=1, source_target_pairs={{0,2},{2,0},{1,3},{3,1},{4,6},{6,4},{5,7},{7,5},{8,10},{10,8},{9,1... | collective-permute-start | bytes 786440 | tf_op jit(solution)/shard_map/ppermute | solution.py:77
  216.5 19.6 %collective-permute-start.17 = (bf16[4,256,256]{2,1,0:T(8,128)(2,1)S(1)}, bf16[4,256,256]{2,1,0:T(8,128)(2,1)}, u32[]{:S(2)}, u32[]{:S(2)}) collective-permute-start(bf16[4,256,256]{2,1,0:T(8,128)(2,1)S(1)} %all-to-all-done.4), channel_id=1, source_target_pairs={{0,2},{2,0},{1,3},{3,1},{4,6},{6,4},{5,7},{7,5},{8,10},{10,8},{9,1... | collective-permute-start | bytes 1572872 | tf_op jit(solution)/shard_map/ppermute | solution.py:77
  218.1 15.5 %copy-start.8 = (bf16[1024,128]{1,0:T(8,128)(2,1)S(1)}, bf16[1024,128]{1,0:T(8,128)(2,1)}, u32[]{:S(2)}) copy-start(bf16[1024,128]{1,0:T(8,128)(2,1)} %get-tuple-element.28) | copy-start | bytes 786436
  233.0 8.3 %collective-permute-start.19 = (bf16[2,256,256]{2,1,0:T(8,128)(2,1)S(1)}, bf16[2,256,256]{2,1,0:T(8,128)(2,1)S(1)}, u32[]{:S(2)}, u32[]{:S(2)}) collective-permute-start(bf16[2,256,256]{2,1,0:T(8,128)(2,1)S(1)} %slice.166), channel_id=1, source_target_pairs={{0,2},{2,0},{1,3},{3,1},{4,6},{6,4},{5,7},{7,5},{8,10},{10,8},{9,1... | collective-permute-start | bytes 786440 | tf_op jit(solution)/shard_map/ppermute | solution.py:77
  233.6 20.4 %collective-permute-start.12 = (bf16[2048,128]{1,0:T(8,128)(2,1)S(1)}, bf16[2048,128]{1,0:T(8,128)(2,1)S(1)}, u32[]{:S(2)}, u32[]{:S(2)}) collective-permute-start(bf16[2048,128]{1,0:T(8,128)(2,1)S(1)} %pad_maximum_fusion.6), channel_id=1, source_target_pairs={{0,130},{2,128},{128,2},{130,0},{1,131},{3,129},{129,3},{131,1},{4... | collective-permute-start | bytes 1572872 | tf_op jit(solution)/shard_map/ppermute | solution.py:77
  237.1 15.2 %collective-permute-start.20 = (bf16[2,256,256]{2,1,0:T(8,128)(2,1)S(1)}, bf16[2,256,256]{2,1,0:T(8,128)(2,1)S(1)}, u32[]{:S(2)}, u32[]{:S(2)}) collective-permute-start(bf16[2,256,256]{2,1,0:T(8,128)(2,1)S(1)} %slice.167), channel_id=1, source_target_pairs={{0,130},{2,128},{128,2},{130,0},{1,131},{3,129},{129,3},{131,1},{4... | collective-permute-start | bytes 786440 | tf_op jit(solution)/shard_map/ppermute | solution.py:77
  238.7 15.3 %collective-permute-start.10 = (bf16[2048,128]{1,0:T(8,128)(2,1)S(1)}, bf16[2048,128]{1,0:T(8,128)(2,1)S(1)}, u32[]{:S(2)}, u32[]{:S(2)}) collective-permute-start(bf16[2048,128]{1,0:T(8,128)(2,1)S(1)} %pad_maximum_fusion.5), channel_id=1, source_target_pairs={{0,2},{2,0},{1,3},{3,1},{4,6},{6,4},{5,7},{7,5},{8,10},{10,8},{9,1... | collective-permute-start | bytes 1572872 | tf_op jit(solution)/shard_map/ppermute | solution.py:77
  253.9 22.0 %collective-permute-start.21 = (bf16[4,4,256,256]{3,2,1,0:T(8,128)(2,1)S(1)}, bf16[4,4,256,256]{3,2,1,0:T(8,128)(2,1)S(1)}, u32[]{:S(2)}, u32[]{:S(2)}) collective-permute-start(bf16[4,4,256,256]{3,2,1,0:T(8,128)(2,1)S(1)} %pad_maximum_fusion.3), channel_id=1, source_target_pairs={{0,1},{1,0},{2,3},{3,2},{4,5},{5,4},{6,7},{7,6},{8,9},{9,8},{10,11... | collective-permute-start | bytes 6291464 | tf_op jit(solution)/shard_map/ppermute | solution.py:77
  255.3 3.5 %collective-permute-start.13 = (bf16[2048,128]{1,0:T(8,128)(2,1)S(1)}, bf16[2048,128]{1,0:T(8,128)(2,1)S(1)}, u32[]{:S(2)}, u32[]{:S(2)}) collective-permute-start(bf16[2048,128]{1,0:T(8,128)(2,1)S(1)} %fusion.9), channel_id=1, source_target_pairs={{0,0},{1,2},{2,1},{3,3},{4,4},{5,6},{6,5},{7,7},{8,8},{9,10},{10,9... | collective-permute-start | bytes 1572872 | tf_op jit(solution)/shard_map/ppermute | solution.py:72
  256.0 15.8 %collective-permute-start.15 = (bf16[2048,128]{1,0:T(8,128)(2,1)S(1)}, bf16[2048,128]{1,0:T(8,128)(2,1)S(1)}, u32[]{:S(2)}, u32[]{:S(2)}) collective-permute-start(bf16[2048,128]{1,0:T(8,128)(2,1)S(1)} %fusion.9), channel_id=1, source_target_pairs={{0,128},{1,130},{2,129},{3,131},{128,0},{129,2},{130,1},{131,3},{4... | collective-permute-start | bytes 1572872 | tf_op jit(solution)/shard_map/ppermute | solution.py:203
  258.8 14.5 %collective-permute-start.14 = (bf16[2048,128]{1,0:T(8,128)(2,1)S(1)}, bf16[2048,128]{1,0:T(8,128)(2,1)S(1)}, u32[]{:S(2)}, u32[]{:S(2)}) collective-permute-start(bf16[2048,128]{1,0:T(8,128)(2,1)S(1)} %collective-permute-done.13), channel_id=1, source_target_pairs={{0,1},{1,0},{2,3},{3,2},{4,5},{5,4},{6,7},{7,6},{8,9},{9,8},{10,11... | collective-permute-start | bytes 1572872 | tf_op jit(solution)/shard_map/ppermute | solution.py:77
  271.8 2.3 collective-permute-start.16
Sparse Core Ops, SparseCore 0:
  10.8 93.5 all-gather.1

commit v2 on v1

--- a/solution.py
+++ b/solution.py
@@ -92,10 +92,15 @@
     return first, second
 
 
-def x_ring(x, xh, xl):
+def ring_pieces(x):
     near, wrap = flip(x, ("xl",)), flip(x, X)
     half = x.shape[0] // 2
-    far = jnp.concatenate([flip(wrap[:half], ("xl",)), flip(near[half:], X)], axis=0)
+    return near, wrap, flip(wrap[:half], ("xl",)), flip(near[half:], X)
+
+
+def x_ring(x, xh, xl):
+    near, wrap, far_low, far_high = ring_pieces(x)
+    far = jnp.concatenate([far_low, far_high], axis=0)
     low = ordered(x, near, xl)
     high = ordered(far, wrap, xl)
     col0 = ordered(low[0], high[0], xh)
@@ -103,21 +108,91 @@
     return (col0[0], col1[0]), (col0[1], col1[1])
 
 
-def member_columns(normed, member):
-    def body(at_ref, rows_ref, out_ref):
-        out_ref[...] = rows_ref[...]
-
+def pack_columns(w_query, w_key, w_value, at):
+    def body(at_ref, q_ref, k_ref, v_ref, out_ref):
+        for j in range(32):
+            head = pl.multiple_of((2 * j + at_ref[2]) * HD, HD)
+            out_ref[j, 0:64, :] = q_ref[:, pl.ds(head, HD)]
+            key = slice(j // 4 * HD, (j // 4 + 1) * HD)
+            out_ref[j, 64:96, :] = k_ref[:, key]
+            out_ref[j, 96:128, :] = v_ref[:, key]
+
+    quarter = pl.BlockSpec((32, 8 * HD), lambda i, at: (2 * at[1] + at[2], 0))
     return pl.pallas_call(
         body,
-        out_shape=jax.ShapeDtypeStruct((512, 1024), jnp.bfloat16),
+        out_shape=jax.ShapeDtypeStruct((32, 128, HD), jnp.bfloat16),
+        grid_spec=pltpu.PrefetchScalarGridSpec(
+            num_scalar_prefetch=1,
+            grid=(1,),
+            in_specs=[pl.BlockSpec((64, D), lambda i, at: (at[1], 0)), quarter, quarter],
+            out_specs=pl.BlockSpec((32, 128, HD), lambda i, at: (0, 0, 0)),
+        ),
+        name="pack_columns",
+    )(at, w_query, w_key, w_value)
+
+
+def project(normed, pieces, others, at):
+    def body(at_ref, rows_ref, *refs):
+        mine, theirs = refs[:5], refs[5:10]
+        out_ref, wq_ref, wkv_ref, member_ref = refs[10:]
+        b = pl.program_id(0)
+        xl, xh, core = at_ref[0], at_ref[1], at_ref[2]
+        spots = ((xl, xh), (1 - xl, xh), (1 - xl, 1 - xh), (xl, 1 - xh))
+
+        def block(group, n):
+            if n < 3:
+                return group[n][...]
+            return jnp.where(b < 4, group[3][...], group[4][...])
+
+        for n, (l, h) in enumerate(spots):
+            own = block(mine, n)
+            other = block(theirs, n)
+            wq_ref[:, l, h] = own[:, :64]
+            wkv_ref[:, l, h, core, :, 0:HD] = own[:, 64:96]
+            wkv_ref[:, l, h, core, :, HD : 2 * HD] = own[:, 96:128]
+            wkv_ref[:, l, h, 1 - core, :, 0:HD] = other[:, 64:96]
+            wkv_ref[:, l, h, 1 - core, :, HD : 2 * HD] = other[:, 96:128]
+
+        rows = rows_ref[...]
+        member_ref[...] = rows_ref[:, pl.ds(pl.multiple_of(at_ref[3] * HD, HD), HD)]
+
+        @pl.when(b == 0)
+        def _():
+            out_ref[...] = jnp.zeros_like(out_ref)
+
+        out_ref[:, 0:HD] += jnp.dot(
+            rows, wq_ref[...].reshape(1024, HD), preferred_element_type=jnp.float32
+        )
+        out_ref[:, HD : 3 * HD] += jnp.dot(
+            rows, wkv_ref[...].reshape(1024, 2 * HD), preferred_element_type=jnp.float32
+        )
+
+    whole = pl.BlockSpec((4, 128, HD), lambda b, at: (b, 0, 0))
+    first = pl.BlockSpec((4, 128, HD), lambda b, at: (jnp.minimum(b, 3), 0, 0))
+    last = pl.BlockSpec((4, 128, HD), lambda b, at: (jnp.maximum(b, 4) - 4, 0, 0))
+    group = [whole, whole, whole, first, last]
+    bf16 = jnp.bfloat16
+    return pl.pallas_call(
+        body,
+        out_shape=(
+            jax.ShapeDtypeStruct((512, 3 * HD), jnp.float32),
+            jax.ShapeDtypeStruct((32, 2, 2, 64, HD), bf16),
+            jax.ShapeDtypeStruct((32, 2, 2, 2, 32, 2 * HD), bf16),
+            jax.ShapeDtypeStruct((512, 1024), bf16),
+        ),
         grid_spec=pltpu.PrefetchScalarGridSpec(
             num_scalar_prefetch=1,
             grid=(8,),
-            in_specs=[pl.BlockSpec((512, HD), lambda b, at: (0, b * 8 + at[0]))],
-            out_specs=pl.BlockSpec((512, HD), lambda b, at: (0, b)),
+            in_specs=[pl.BlockSpec((512, 1024), lambda b, at: (0, b))] + group + group,
+            out_specs=(
+                pl.BlockSpec((512, 3 * HD), lambda b, at: (0, 0)),
+                pl.BlockSpec((4, 2, 2, 64, HD), lambda b, at: (b, 0, 0, 0, 0)),
+                pl.BlockSpec((4, 2, 2, 2, 32, 2 * HD), lambda b, at: (b, 0, 0, 0, 0, 0)),
+                pl.BlockSpec((512, HD), lambda b, at: (0, b)),
+            ),
         ),
-        name="member_columns",
-    )(member.reshape(1).astype(jnp.int32), normed)
+        name="project",
+    )(at, normed, *pieces, *others)
 
 
 def local(hidden, cotangent, seg_ids, advantage, w_query, w_key, w_value):
@@ -141,20 +216,13 @@
     adv_row = swap(advantage[0])
     block_len = 512
 
-    wq = w_query.reshape(2, 64, 32, 2, HD)
-    wq = lax.dynamic_index_in_dim(wq, xh, 0, keepdims=False)
-    wq = lax.dynamic_index_in_dim(wq, core, 2, keepdims=False).transpose(1, 0, 2)
-    wkv = jnp.stack([w_key.reshape(4, 32, 8, HD), w_value.reshape(4, 32, 8, HD)], axis=1)
-    wkv = lax.dynamic_index_in_dim(wkv, xh * 2 + core, 0, keepdims=False)
-    wkv = wkv.transpose(2, 0, 1, 3).reshape(8, 1, 64, HD)
-    wkv = jnp.broadcast_to(wkv, (8, 4, 64, HD)).reshape(32, 64, HD)
-    cut = exchange(jnp.concatenate([wq, wkv], axis=1), YZ)
-    cut = x_ring(cut, xh, xl)
-    order = [(h, l) for l in (0, 1) for h in (0, 1)]
-    q_cols = jnp.stack([cut[h][l][:, :64] for h, l in order], axis=1).reshape(D, HD)
-    wkv = jnp.stack([cut[h][l][:, 64:] for h, l in order], axis=1)
-    wkv = jnp.stack(ordered(wkv, flip(wkv, ("core",)), core), axis=2)
-    wkv = wkv.reshape(128, 2, 2, 32, HD).transpose(0, 1, 3, 2, 4).reshape(D, 2 * HD)
+    at = jnp.stack([xl, xh, core, member]).astype(jnp.int32)
+    cut = exchange(pack_columns(w_query, w_key, w_value, at), YZ)
+    pieces = (cut,) + ring_pieces(cut)
+    others = tuple(flip(p, ("core",)) for p in pieces)
+    projected, q_cols, wkv, normed_m = project(normed, pieces, others, at)
+    projected = projected * inv_width
+    q_cols = q_cols.reshape(D, HD)
 
     cosine_table, sine_table = angles(seg_row)
     weight_row = token_weights(seg_row, adv_row)
@@ -162,14 +230,9 @@
     position = jnp.arange(block_len, dtype=jnp.int32)
     allowed = (seg_row[:, None] == seg_row[None, :]) & (position[None, :] <= position[:, None])
 
-    def project(cols):
-        return jnp.dot(normed, cols, preferred_element_type=f32) * inv_width
-
-    queries = project(q_cols)
-    keys_values = project(wkv)
-    q_rot = rotate(queries, cosine_table, sine_table).astype(bf16)
-    k_rot = rotate(keys_values[:, :HD], cosine_table, sine_table).astype(bf16)
-    v_bf = keys_values[:, HD:].astype(bf16)
+    q_rot = rotate(projected[:, :HD], cosine_table, sine_table).astype(bf16)
+    k_rot = rotate(projected[:, HD : 2 * HD], cosine_table, sine_table).astype(bf16)
+    v_bf = projected[:, 2 * HD :].astype(bf16)
 
     grad_query, grad_key, grad_value = attend_back(q_rot, k_rot, v_bf, grad_context, allowed)
     scaled_q = (rotate(grad_query, cosine_table, -sine_table) * inv_width).astype(bf16)
@@ -223,7 +286,7 @@
     kv_sum = jnp.sum(kv_sum, axis=0).astype(bf16)
     kv_sum = spread(kv_sum, MEM).reshape(block_len, 2 * HD)
     part_kv = lax.dot_general(
-        member_columns(normed, member), kv_sum, contract, preferred_element_type=f32
+        normed_m, kv_sum, contract, preferred_element_type=f32
     ).astype(bf16)
     part_kv = exchange(part_kv.reshape(4, 256, 2 * HD), X).astype(f32)
     old_kv = wkv.reshape(4, 2, 8, 128, 2 * HD)

time: 289 us -> 271 us (0.938)
  local copies, waits for them, and re-layouts: 36.1 us -> 9.34 us
  Pallas kernels: 5.19 us -> 16.8 us
  matrix products: 16.9 us -> 10.5 us
  starting transfers between devices: 49.4 us -> 53.6 us
    pallas_call x1 -> x2, Pallas kernels: 5.19 us -> 16.8 us  [the longest x1 13.7 us: project(): pl.pallas_call(body, out_shape=(jax.ShapeDtypeStruct((512, 3 * HD), jnp.f...]
    another operation x5 -> x0, local copies, waits for them, and re-layouts: 10.1 us -> none  [the longest x1 7.61 us: local(): old_kv = wkv.reshape(4, 2, 8, 128, 2 * HD)]
    ppermute x16 -> x20, starting transfers between devices: 32.9 us -> 43 us  [flip(): return lax.ppermute(x, axes, [(i, n - 1 - i) for i in range(n)])]
    dot_general x3 -> x1, matrix products: 12.5 us -> 2.5 us  [local(): lax.dot_general(normed_m, kv_sum, contract, preferred_element_type=f32)]
    ppermute x16 -> x20, waiting for transfers between devices: 65.9 us -> 56.1 us  [flip(): return lax.ppermute(x, axes, [(i, n - 1 - i) for i in range(n)])]
    transpose x1 -> x0, local copies, waits for them, and re-layouts: 6.43 us -> none  [local(): wkv.reshape(128, 2, 2, 32, HD).transpose(0, 1, 3, 2, 4).reshape(D, 2 * HD)]
    ppermute x1, waiting for transfers between devices: 0.01 us -> 4.33 us  [local(): lax.ppermute(new_q, ('xh', 'xl', 'core'), [(h * 4 + l * 2 + c, (1 - h) *...]
    dot_general x1, matrix products: 2.41 us -> 5.87 us  [local(): lax.dot_general(normed, scaled_q, contract, preferred_element_type=f32)]
  transfers between devices with their start and end apart: 26 -> 29, of which waited for: 13 -> 15; matrix products, arithmetic and copies ran while one was open for 19% -> 5% of each run, Pallas kernels for 2% -> 6%
where the time goes in v2:
time: 271 us; the launch traced here: 269 us
  waiting for transfers between devices  83.2 us (31%)
  blocking collectives  63.4 us (23%)
  starting transfers between devices  53.6 us (20%)
  other arithmetic  17.3 us (6%)
  Pallas kernels  16.8 us (6%)
  between operations  14.6 us (5%)
  matrix products  10.5 us (4%)
  local copies, waits for them, and re-layouts  9.34 us (3%)
    all_to_all x3, blocking collectives, exchange(): return lax.all_to_all(x, axes, split_axis=0, concat_axis=0, tiled=True)  63.4 us
    ppermute x20, waiting for transfers between devices, flip(): return lax.ppermute(x, axes, [(i, n - 1 - i) for i in range(n)])  56.1 us
    ppermute x20, starting transfers between devices, flip(): return lax.ppermute(x, axes, [(i, n - 1 - i) for i in range(n)])  43 us
    all_to_all x2, waiting for transfers between devices, exchange(): return lax.all_to_all(x, axes, split_axis=0, concat_axis=0, tiled=True)  21.9 us
    pallas_call x1, Pallas kernels, project(): pl.pallas_call(body, out_shape=(jax.ShapeDtypeStruct((512, 3 * HD), jnp.f...  13.7 us
    all_to_all x2, starting transfers between devices, exchange(): return lax.all_to_all(x, axes, split_axis=0, concat_axis=0, tiled=True)  6.94 us
    dot_general x1, matrix products, local(): lax.dot_general(normed, scaled_q, contract, preferred_element_type=f32)  5.87 us
  transfers between devices with their start and end apart: 29, of which 15 were waited for; matrix products, arithmetic and copies ran while one was open for 5% of the time, Pallas kernels for 6%

profile of v2, /device:TPU:8, one launch (start us, length us, event | category | flops | bytes accessed | tf_op | source)
XLA Modules:
  0.0 268.7 jit_solution(546560063581398869)
XLA Ops:
  7.2 1.1 fusion.31
  8.3 1.0 fusion.32
  11.3 3.1 %pack_columns.1 = bf16[32,128,128]{2,1,0:T(8,128)(2,1)} custom-call(s32[4]{0:T(128)} %pad_add_fusion.at_ref, bf16[128,8192]{1,0:T(8,128)(2,1)} %q_ref.1, bf16[128,1024]{1,0:T(8,128)(2,1)} %k_ref.1, bf16[128,1024]{1,0:T(8,128)(2,1)} %v_ref.1), custom_call_target="tpu_custom_call" | custom-call | tf_op jit(solution)/shard_map/pack_columns/pallas_call | solution.py:121
  14.3 35.9 %all_to_all.25.refs_0_ = bf16[32,128,128]{2,1,0:T(8,128)(2,1)S(1)} all-to-all(bf16[32,128,128]{2,1,0:T(8,128)(2,1)} %pack_columns.1), channel_id=1, replica_groups=mesh['xh'=2,'y'=4,'zh'=2,'zl'=4,'xl'=2,'core'=2] {'y','zh','zl'}, dimensions={0} | all-to-all | bytes 2097152 | tf_op jit(solution)/shard_map/all_to_all | solution.py:81
  50.3 8.3 %collective-permute-start.2 = (bf16[32,128,128]{2,1,0:T(8,128)(2,1)S(1)}, bf16[32,128,128]{2,1,0:T(8,128)(2,1)S(1)}, u32[]{:S(2)}, u32[]{:S(2)}) collective-permute-start(bf16[32,128,128]{2,1,0:T(8,128)(2,1)S(1)} %all_to_all.25.refs_0_), channel_id=1, source_target_pairs={{0,130},{2,128},{128,2},{130,0},{1,131},{3,129},{129,3},{131,1},{4... | collective-permute-start | bytes 3145736 | tf_op jit(solution)/shard_map/ppermute | solution.py:77
  58.6 22.5 %collective-permute-done.2.refs_2_ = bf16[32,128,128]{2,1,0:T(8,128)(2,1)S(1)} collective-permute-done((bf16[32,128,128]{2,1,0:T(8,128)(2,1)S(1)}, bf16[32,128,128]{2,1,0:T(8,128)(2,1)S(1)}, u32[]{:S(2)}, u32[]{:S(2)}) %collective-permute-start.2) | collective-permute-done | bytes 1048608 | tf_op jit(solution)/shard_map/ppermute | solution.py:77
  81.1 1.3 collective-permute-start.3
  82.4 1.7 collective-permute-done.1.refs_1_
  86.0 4.3 %collective-permute-start.5 = (bf16[32,128,128]{2,1,0:T(8,128)(2,1)S(1)}, bf16[32,128,128]{2,1,0:T(8,128)(2,1)S(1)}, u32[]{:S(2)}, u32[]{:S(2)}) collective-permute-start(bf16[32,128,128]{2,1,0:T(8,128)(2,1)S(1)} %all_to_all.25.refs_0_), channel_id=1, source_target_pairs={{0,1},{1,0},{2,3},{3,2},{4,5},{5,4},{6,7},{7,6},{8,9},{9,8},{10,11... | collective-permute-start | bytes 3145736 | tf_op jit(solution)/shard_map/ppermute | solution.py:77
  90.4 5.1 %collective-permute-start.6 = (bf16[32,128,128]{2,1,0:T(8,128)(2,1)S(1)}, bf16[32,128,128]{2,1,0:T(8,128)(2,1)S(1)}, u32[]{:S(2)}, u32[]{:S(2)}) collective-permute-start(bf16[32,128,128]{2,1,0:T(8,128)(2,1)S(1)} %collective-permute-done.1.refs_1_), channel_id=1, source_target_pairs={{0,1},{1,0},{2,3},{3,2},{4,5},{5,4},{6,7},{7,6},{8,9},{9,8},{10,11... | collective-permute-start | bytes 3145736 | tf_op jit(solution)/shard_map/ppermute | solution.py:77
  96.3 2.7 collective-permute-done.4.refs_4_
  100.1 1.0 collective-permute-done.8.refs_8_
  102.7 1.0 copy-done.11
  104.5 13.7 %project.1 = (f32[512,384]{1,0:T(8,128)}, bf16[32,2,2,64,128]{4,3,2,1,0:T(8,128)(2,1)}, bf16[32,2,2,2,32,256]{5,4,3,2,1,0:T(8,128)(2,1)}, bf16[512,1024]{1,0:T(8,128)(2,1)}) custom-call(s32[4]{0:T(128)} %pad_add_fusion.at_ref, bf16[512,8192]{1,0:T(8,128)(2,1)} %all-gather.2.cloned.1.call-done.rows_ref, bf16[32,128,128]{2,1,0:T(8,128)(2,1)} %copy-done.4, ...), custom_call_target="tpu_custom_call" | custom-call | tf_op jit(solution)/shard_map/project/pallas_call | solution.py:175
  118.3 1.2 broadcast_multiply_fusion
  119.5 1.3 fusion.38
  123.1 1.3 fusion.35
  125.2 5.9 %convolution_convert_fusion = bf16[8192,128]{1,0:T(8,128)(2,1)S(1)} fusion(bf16[512,8192]{1,0:T(8,128)(2,1)} %all-gather.2.cloned.1.call-done.rows_ref, f32[512,64]{1,0:T(8,128)S(1)} %get-tuple-element.41, f32[512,64]{1,0:T(8,128)S(1)} %get-tuple-element.42), kind=kOutput, calls=%fused_computation | convolution fusion | flops 1074987008 | bytes 10747904 | tf_op jit(solution)/shard_map/dot_general | solution.py:244
  131.2 15.3 %all_to_all.26 = bf16[8,64,256]{2,1,0:T(8,128)(2,1)S(1)} all-to-all(bf16[8,64,256]{2,1,0:T(8,128)(2,1)S(1)} %bitcast.75), channel_id=1, replica_groups=mesh['xh'=2,'y'=4,'zh'=2,'zl'=4,'xl'=2,'core'=2] {'zl','core'}, dimensions={0} | all-to-all | bytes 524288 | tf_op jit(solution)/shard_map/all_to_all | solution.py:81
  146.6 12.1 %all_to_all.27 = bf16[8,64,256]{2,1,0:T(8,128)(2,1)S(1)} all-to-all(bf16[8,64,256]{2,1,0:T(8,128)(2,1)S(1)} %broadcast_in_dim.8), channel_id=1, replica_groups=mesh['xh'=2,'y'=4,'zh'=2,'zl'=4,'xl'=2,'core'=2] {'zl','core'}, dimensions={0} | all-to-all | bytes 524288 | tf_op jit(solution)/shard_map/all_to_all | solution.py:81
  158.7 2.5 convolution_convert_fusion.1
  161.2 3.5 %all-to-all-start.3 = ((bf16[4,256,256]{2,1,0:T(8,128)(2,1)}), bf16[4,256,256]{2,1,0:T(8,128)(2,1)S(1)}, u32[]{:S(2)}, u32[]{:S(2)}) async-start(bf16[4,256,256]{2,1,0:T(8,128)(2,1)} %bitcast.27), calls=%async_computation.3 | async-start | bytes 1048576 | tf_op jit(solution)/shard_map/all_to_all | solution.py:81
  164.7 0.9 constant_dynamic-slice_fusion
  165.6 8.4 %all-to-all-done.3 = bf16[4,256,256]{2,1,0:T(8,128)(2,1)S(1)} async-done(((bf16[4,256,256]{2,1,0:T(8,128)(2,1)}), bf16[4,256,256]{2,1,0:T(8,128)(2,1)S(1)}, u32[]{:S(2)}, u32[]{:S(2)}) %all-to-all-start.3) | async-done | bytes 524320 | tf_op jit(solution)/shard_map/all_to_all | solution.py:81
  175.0 3.5 %all-to-all-start.4 = ((bf16[4,256,256]{2,1,0:T(8,128)(2,1)}), bf16[4,256,256]{2,1,0:T(8,128)(2,1)S(1)}, u32[]{:S(2)}, u32[]{:S(2)}) async-start(bf16[4,256,256]{2,1,0:T(8,128)(2,1)} %broadcast_in_dim.9), calls=%async_computation.4 | async-start | bytes 1048576 | tf_op jit(solution)/shard_map/all_to_all | solution.py:81
  178.5 13.5 %all-to-all-done.4 = bf16[4,256,256]{2,1,0:T(8,128)(2,1)S(1)} async-done(((bf16[4,256,256]{2,1,0:T(8,128)(2,1)}), bf16[4,256,256]{2,1,0:T(8,128)(2,1)S(1)}, u32[]{:S(2)}, u32[]{:S(2)}) %all-to-all-start.4) | async-done | bytes 524320 | tf_op jit(solution)/shard_map/all_to_all | solution.py:81
  192.0 1.2 collective-permute-start.22
  194.1 2.1 collective-permute-start.13
  196.1 2.0 collective-permute-start.21
  198.2 13.7 %collective-permute-done.13 = bf16[1024,128]{1,0:T(8,128)(2,1)} collective-permute-done((bf16[1024,128]{1,0:T(8,128)(2,1)}, bf16[1024,128]{1,0:T(8,128)(2,1)}, u32[]{:S(2)}, u32[]{:S(2)}) %collective-permute-start.13) | collective-permute-done | bytes 262176 | tf_op jit(solution)/shard_map/ppermute | solution.py:77
  211.9 1.2 fusion.11
  213.5 2.1 collective-permute-start.14
  215.6 1.0 slice.130
  216.6 1.3 collective-permute-start.24
  217.8 2.2 collective-permute-start.16
  220.0 2.6 collective-permute-done.23
  222.6 4.4 %collective-permute-done.24 = bf16[2,256,256]{2,1,0:T(8,128)(2,1)S(1)} collective-permute-done((bf16[2,256,256]{2,1,0:T(8,128)(2,1)S(1)}, bf16[2,256,256]{2,1,0:T(8,128)(2,1)S(1)}, u32[]{:S(2)}, u32[]{:S(2)}) %collective-permute-start.24) | collective-permute-done | bytes 262176 | tf_op jit(solution)/shard_map/ppermute | solution.py:77
  227.1 1.4 select_bitcast_fusion.3
  228.5 1.6 pad_maximum_fusion.1
  230.2 1.0 collective-permute-done.14
  231.2 3.8 %collective-permute-done.16 = bf16[2048,128]{1,0:T(8,128)(2,1)S(1)} collective-permute-done((bf16[2048,128]{1,0:T(8,128)(2,1)S(1)}, bf16[2048,128]{1,0:T(8,128)(2,1)S(1)}, u32[]{:S(2)}, u32[]{:S(2)}) %collective-permute-start.16) | collective-permute-done | bytes 524320 | tf_op jit(solution)/shard_map/ppermute | solution.py:77
  235.0 1.3 fusion.3
  237.2 11.7 %collective-permute-start.18 = (bf16[2048,128]{1,0:T(8,128)(2,1)S(1)}, bf16[2048,128]{1,0:T(8,128)(2,1)S(1)}, u32[]{:S(2)}, u32[]{:S(2)}) collective-permute-start(bf16[2048,128]{1,0:T(8,128)(2,1)S(1)} %collective-permute-done.17), channel_id=1, source_target_pairs={{0,1},{1,0},{2,3},{3,2},{4,5},{5,4},{6,7},{7,6},{8,9},{9,8},{10,11... | collective-permute-start | bytes 1572872 | tf_op jit(solution)/shard_map/ppermute | solution.py:77
  248.8 4.3 %collective-permute-done.19 = bf16[2048,128]{1,0:T(8,128)(2,1)S(1)} collective-permute-done((bf16[2048,128]{1,0:T(8,128)(2,1)S(1)}, bf16[2048,128]{1,0:T(8,128)(2,1)S(1)}, u32[]{:S(2)}, u32[]{:S(2)}) %collective-permute-start.19) | collective-permute-done | bytes 524320 | tf_op jit(solution)/shard_map/ppermute | solution.py:266
  253.2 1.9 collective-permute-done.20
  255.3 1.6 pad_maximum_fusion
  256.9 1.8 broadcast_select_fusion.1
  259.5 2.3 fusion.59
  (110 shorter events, 15.7 us)
Async XLA Ops:
  7.2 97.4 %all-gather.2.cloned.1.call-start = ((), (), s32[]{:S(2)}) async-start(), calls=%async_computation.5 | async-start | bytes 8519680 | tf_op jit(solution)/shard_map/all_gather | solution.py:213
  9.3 0.7 collective-permute-start
  14.3 70.4 %copy-start.19 = (s32[1,512]{1,0:T(1,128)S(1)}, s32[1,512]{1,0:T(1,128)}, u32[]{:S(2)}) copy-start(s32[1,512]{1,0:T(1,128)} %param.9) | copy-start | bytes 6148
  14.3 71.0 %copy-start.20 = (f32[1,8]{1,0:T(1,128)S(1)}, f32[1,8]{1,0:T(1,128)}, u32[]{:S(2)}) copy-start(f32[1,8]{1,0:T(1,128)} %param.10) | copy-start | bytes 100
  14.3 84.9 %copy-start.18 = (bf16[1,512,128]{2,1,0:T(8,128)(2,1)S(1)}, bf16[1,512,128]{2,1,0:T(8,128)(2,1)}, u32[]{:S(2)}) copy-start(bf16[1,512,128]{2,1,0:T(8,128)(2,1)} %param.8) | copy-start | bytes 393220
  50.3 54.3 %copy-start.4 = (bf16[32,128,128]{2,1,0:T(8,128)(2,1)}, bf16[32,128,128]{2,1,0:T(8,128)(2,1)S(1)}, u32[]{:S(2)}) copy-start(bf16[32,128,128]{2,1,0:T(8,128)(2,1)S(1)} %all_to_all.25.refs_0_) | copy-start | bytes 3145732
  50.3 30.8 %collective-permute-start.2 = (bf16[32,128,128]{2,1,0:T(8,128)(2,1)S(1)}, bf16[32,128,128]{2,1,0:T(8,128)(2,1)S(1)}, u32[]{:S(2)}, u32[]{:S(2)}) collective-permute-start(bf16[32,128,128]{2,1,0:T(8,128)(2,1)S(1)} %all_to_all.25.refs_0_), channel_id=1, source_target_pairs={{0,130},{2,128},{128,2},{130,0},{1,131},{3,129},{129,3},{131,1},{4... | collective-permute-start | bytes 3145736 | tf_op jit(solution)/shard_map/ppermute | solution.py:77
  58.6 25.5 %collective-permute-start.1 = (bf16[32,128,128]{2,1,0:T(8,128)(2,1)S(1)}, bf16[32,128,128]{2,1,0:T(8,128)(2,1)S(1)}, u32[]{:S(2)}, u32[]{:S(2)}) collective-permute-start(bf16[32,128,128]{2,1,0:T(8,128)(2,1)S(1)} %all_to_all.25.refs_0_), channel_id=1, source_target_pairs={{0,2},{2,0},{1,3},{3,1},{4,6},{6,4},{5,7},{7,5},{8,10},{10,8},{9,1... | collective-permute-start | bytes 3145736 | tf_op jit(solution)/shard_map/ppermute | solution.py:77
  81.1 23.5 %copy-start.5 = (bf16[32,128,128]{2,1,0:T(8,128)(2,1)}, bf16[32,128,128]{2,1,0:T(8,128)(2,1)S(1)}, u32[]{:S(2)}) copy-start(bf16[32,128,128]{2,1,0:T(8,128)(2,1)S(1)} %collective-permute-done.2.refs_2_) | copy-start | bytes 3145732
  81.1 14.5 %collective-permute-start.3 = (bf16[16,128,128]{2,1,0:T(8,128)(2,1)S(1)}, bf16[16,128,128]{2,1,0:T(8,128)(2,1)S(1)}, u32[]{:S(2)}, u32[]{:S(2)}) collective-permute-start(bf16[16,128,128]{2,1,0:T(8,128)(2,1)S(1)} %slice.117), channel_id=1, source_target_pairs={{0,2},{2,0},{1,3},{3,1},{4,6},{6,4},{5,7},{7,5},{8,10},{10,8},{9,1... | collective-permute-start | bytes 1572872 | tf_op jit(solution)/shard_map/ppermute | solution.py:77
  84.1 20.5 %copy-start.6 = (bf16[32,128,128]{2,1,0:T(8,128)(2,1)}, bf16[32,128,128]{2,1,0:T(8,128)(2,1)S(1)}, u32[]{:S(2)}) copy-start(bf16[32,128,128]{2,1,0:T(8,128)(2,1)S(1)} %collective-permute-done.1.refs_1_) | copy-start | bytes 3145732
  84.1 14.8 %collective-permute-start.4 = (bf16[16,128,128]{2,1,0:T(8,128)(2,1)S(1)}, bf16[16,128,128]{2,1,0:T(8,128)(2,1)S(1)}, u32[]{:S(2)}, u32[]{:S(2)}) collective-permute-start(bf16[16,128,128]{2,1,0:T(8,128)(2,1)S(1)} %slice.118), channel_id=1, source_target_pairs={{0,130},{2,128},{128,2},{130,0},{1,131},{3,129},{129,3},{131,1},{4... | collective-permute-start | bytes 1572872 | tf_op jit(solution)/shard_map/ppermute | solution.py:77
  84.7 10.8 %collective-permute-start.10 = (s32[512]{0:T(512)S(1)}, s32[512]{0:T(512)S(1)}, u32[]{:S(2)}, u32[]{:S(2)}) collective-permute-start(s32[512]{0:T(512)S(1)} %bitcast.80), channel_id=1, source_target_pairs={{0,0},{1,2},{2,1},{3,3},{4,4},{5,6},{6,5},{7,7},{8,8},{9,10},{10,9... | collective-permute-start | bytes 6152 | tf_op jit(solution)/shard_map/ppermute | solution.py:72
  85.4 5.0 %collective-permute-start.12 = (f32[8]{0:T(128)S(1)}, f32[8]{0:T(128)S(1)}, u32[]{:S(2)}, u32[]{:S(2)}) collective-permute-start(f32[8]{0:T(128)S(1)} %bitcast.81), channel_id=1, source_target_pairs={{0,0},{1,2},{2,1},{3,3},{4,4},{5,6},{6,5},{7,7},{8,8},{9,10},{10,9... | collective-permute-start | bytes 104 | tf_op jit(solution)/shard_map/ppermute | solution.py:72
  86.0 13.2 %collective-permute-start.5 = (bf16[32,128,128]{2,1,0:T(8,128)(2,1)S(1)}, bf16[32,128,128]{2,1,0:T(8,128)(2,1)S(1)}, u32[]{:S(2)}, u32[]{:S(2)}) collective-permute-start(bf16[32,128,128]{2,1,0:T(8,128)(2,1)S(1)} %all_to_all.25.refs_0_), channel_id=1, source_target_pairs={{0,1},{1,0},{2,3},{3,2},{4,5},{5,4},{6,7},{7,6},{8,9},{9,8},{10,11... | collective-permute-start | bytes 3145736 | tf_op jit(solution)/shard_map/ppermute | solution.py:77
  90.4 11.5 %collective-permute-start.6 = (bf16[32,128,128]{2,1,0:T(8,128)(2,1)S(1)}, bf16[32,128,128]{2,1,0:T(8,128)(2,1)S(1)}, u32[]{:S(2)}, u32[]{:S(2)}) collective-permute-start(bf16[32,128,128]{2,1,0:T(8,128)(2,1)S(1)} %collective-permute-done.1.refs_1_), channel_id=1, source_target_pairs={{0,1},{1,0},{2,3},{3,2},{4,5},{5,4},{6,7},{7,6},{8,9},{9,8},{10,11... | collective-permute-start | bytes 3145736 | tf_op jit(solution)/shard_map/ppermute | solution.py:77
  95.5 8.1 %collective-permute-start.7 = (bf16[32,128,128]{2,1,0:T(8,128)(2,1)S(1)}, bf16[32,128,128]{2,1,0:T(8,128)(2,1)}, u32[]{:S(2)}, u32[]{:S(2)}) collective-permute-start(bf16[32,128,128]{2,1,0:T(8,128)(2,1)S(1)} %collective-permute-done.2.refs_2_), channel_id=1, source_target_pairs={{0,1},{1,0},{2,3},{3,2},{4,5},{5,4},{6,7},{7,6},{8,9},{9,8},{10,11... | collective-permute-start | bytes 3145736 | tf_op jit(solution)/shard_map/ppermute | solution.py:77
  95.7 6.2 %copy-start.13 = (bf16[16,128,128]{2,1,0:T(8,128)(2,1)}, bf16[16,128,128]{2,1,0:T(8,128)(2,1)S(1)}, u32[]{:S(2)}) copy-start(bf16[16,128,128]{2,1,0:T(8,128)(2,1)S(1)} %collective-permute-done.3.refs_3_) | copy-start | bytes 1572868
  95.7 5.5 %collective-permute-start.8 = (bf16[16,128,128]{2,1,0:T(8,128)(2,1)S(1)}, bf16[16,128,128]{2,1,0:T(8,128)(2,1)S(1)}, u32[]{:S(2)}, u32[]{:S(2)}) collective-permute-start(bf16[16,128,128]{2,1,0:T(8,128)(2,1)S(1)} %collective-permute-done.3.refs_3_), channel_id=1, source_target_pairs={{0,1},{1,0},{2,3},{3,2},{4,5},{5,4},{6,7},{7,6},{8,9},{9,8},{10,11... | collective-permute-start | bytes 1572872 | tf_op jit(solution)/shard_map/ppermute | solution.py:77
  98.9 3.0 %copy-start.14 = (bf16[16,128,128]{2,1,0:T(8,128)(2,1)}, bf16[16,128,128]{2,1,0:T(8,128)(2,1)S(1)}, u32[]{:S(2)}) copy-start(bf16[16,128,128]{2,1,0:T(8,128)(2,1)S(1)} %collective-permute-done.4.refs_4_) | copy-start | bytes 1572868
  98.9 2.9 %collective-permute-start.9 = (bf16[16,128,128]{2,1,0:T(8,128)(2,1)S(1)}, bf16[16,128,128]{2,1,0:T(8,128)(2,1)S(1)}, u32[]{:S(2)}, u32[]{:S(2)}) collective-permute-start(bf16[16,128,128]{2,1,0:T(8,128)(2,1)S(1)} %collective-permute-done.4.refs_4_), channel_id=1, source_target_pairs={{0,1},{1,0},{2,3},{3,2},{4,5},{5,4},{6,7},{7,6},{8,9},{9,8},{10,11... | collective-permute-start | bytes 1572872 | tf_op jit(solution)/shard_map/ppermute | solution.py:77
  99.2 2.7 copy-start.10
  99.2 22.2 %collective-permute-start.11 = (bf16[512,128]{1,0:T(8,128)(2,1)S(1)}, bf16[512,128]{1,0:T(8,128)(2,1)S(1)}, u32[]{:S(2)}, u32[]{:S(2)}) collective-permute-start(bf16[512,128]{1,0:T(8,128)(2,1)S(1)} %bitcast.79), channel_id=1, source_target_pairs={{0,0},{1,2},{2,1},{3,3},{4,4},{5,6},{6,5},{7,7},{8,8},{9,10},{10,9... | collective-permute-start | bytes 393224 | tf_op jit(solution)/shard_map/ppermute | solution.py:72
  101.1 0.8 copy-start.15
  102.7 1.0 copy-start.11
  161.2 12.8 %all-to-all-start.3 = ((bf16[4,256,256]{2,1,0:T(8,128)(2,1)}), bf16[4,256,256]{2,1,0:T(8,128)(2,1)S(1)}, u32[]{:S(2)}, u32[]{:S(2)}) async-start(bf16[4,256,256]{2,1,0:T(8,128)(2,1)} %bitcast.27), calls=%async_computation.3 | async-start | bytes 1048576 | tf_op jit(solution)/shard_map/all_to_all | solution.py:81
  175.0 17.0 %all-to-all-start.4 = ((bf16[4,256,256]{2,1,0:T(8,128)(2,1)}), bf16[4,256,256]{2,1,0:T(8,128)(2,1)S(1)}, u32[]{:S(2)}, u32[]{:S(2)}) async-start(bf16[4,256,256]{2,1,0:T(8,128)(2,1)} %broadcast_in_dim.9), calls=%async_computation.4 | async-start | bytes 1048576 | tf_op jit(solution)/shard_map/all_to_all | solution.py:81
  192.0 21.1 %copy-start.7 = (bf16[4,256,256]{2,1,0:T(8,128)(2,1)}, bf16[4,256,256]{2,1,0:T(8,128)(2,1)S(1)}, u32[]{:S(2)}) copy-start(bf16[4,256,256]{2,1,0:T(8,128)(2,1)S(1)} %all-to-all-done.4) | copy-start | bytes 1572868
  192.0 21.1 %collective-permute-start.22 = (bf16[4,256,256]{2,1,0:T(8,128)(2,1)S(1)}, bf16[4,256,256]{2,1,0:T(8,128)(2,1)S(1)}, u32[]{:S(2)}, u32[]{:S(2)}) collective-permute-start(bf16[4,256,256]{2,1,0:T(8,128)(2,1)S(1)} %all-to-all-done.4), channel_id=1, source_target_pairs={{0,130},{2,128},{128,2},{130,0},{1,131},{3,129},{129,3},{131,1},{4... | collective-permute-start | bytes 1572872 | tf_op jit(solution)/shard_map/ppermute | solution.py:77
  194.1 17.8 %collective-permute-start.13 = (bf16[1024,128]{1,0:T(8,128)(2,1)}, bf16[1024,128]{1,0:T(8,128)(2,1)}, u32[]{:S(2)}, u32[]{:S(2)}) collective-permute-start(bf16[1024,128]{1,0:T(8,128)(2,1)} %get-tuple-element.29), channel_id=1, source_target_pairs={{0,130},{2,128},{128,2},{130,0},{1,131},{3,129},{129,3},{131,1},{4... | collective-permute-start | bytes 786440 | tf_op jit(solution)/shard_map/ppermute | solution.py:77
  196.1 15.7 %collective-permute-start.15 = (bf16[1024,128]{1,0:T(8,128)(2,1)}, bf16[1024,128]{1,0:T(8,128)(2,1)}, u32[]{:S(2)}, u32[]{:S(2)}) collective-permute-start(bf16[1024,128]{1,0:T(8,128)(2,1)} %get-tuple-element.31), channel_id=1, source_target_pairs={{0,2},{2,0},{1,3},{3,1},{4,6},{6,4},{5,7},{7,5},{8,10},{10,8},{9,1... | collective-permute-start | bytes 786440 | tf_op jit(solution)/shard_map/ppermute | solution.py:77
  196.1 19.4 %collective-permute-start.21 = (bf16[4,256,256]{2,1,0:T(8,128)(2,1)S(1)}, bf16[4,256,256]{2,1,0:T(8,128)(2,1)}, u32[]{:S(2)}, u32[]{:S(2)}) collective-permute-start(bf16[4,256,256]{2,1,0:T(8,128)(2,1)S(1)} %all-to-all-done.4), channel_id=1, source_target_pairs={{0,2},{2,0},{1,3},{3,1},{4,6},{6,4},{5,7},{7,5},{8,10},{10,8},{9,1... | collective-permute-start | bytes 1572872 | tf_op jit(solution)/shard_map/ppermute | solution.py:77
  198.2 15.3 %copy-start.12 = (bf16[1024,128]{1,0:T(8,128)(2,1)S(1)}, bf16[1024,128]{1,0:T(8,128)(2,1)}, u32[]{:S(2)}) copy-start(bf16[1024,128]{1,0:T(8,128)(2,1)} %get-tuple-element.32) | copy-start | bytes 786436
  213.1 14.0 %copy-start.9 = (bf16[4,256,256]{2,1,0:T(8,128)(2,1)}, bf16[4,256,256]{2,1,0:T(8,128)(2,1)S(1)}, u32[]{:S(2)}) copy-start(bf16[4,256,256]{2,1,0:T(8,128)(2,1)S(1)} %collective-permute-done.22) | copy-start | bytes 1572868
  213.1 9.5 %collective-permute-start.23 = (bf16[2,256,256]{2,1,0:T(8,128)(2,1)S(1)}, bf16[2,256,256]{2,1,0:T(8,128)(2,1)S(1)}, u32[]{:S(2)}, u32[]{:S(2)}) collective-permute-start(bf16[2,256,256]{2,1,0:T(8,128)(2,1)S(1)} %slice.129), channel_id=1, source_target_pairs={{0,2},{2,0},{1,3},{3,1},{4,6},{6,4},{5,7},{7,5},{8,10},{10,8},{9,1... | collective-permute-start | bytes 786440 | tf_op jit(solution)/shard_map/ppermute | solution.py:77
  213.4 13.6 %copy-start.8 = (bf16[4,256,256]{2,1,0:T(8,128)(2,1)S(1)}, bf16[4,256,256]{2,1,0:T(8,128)(2,1)}, u32[]{:S(2)}) copy-start(bf16[4,256,256]{2,1,0:T(8,128)(2,1)} %copy-done.7) | copy-start | bytes 1572868
  213.5 17.7 %collective-permute-start.14 = (bf16[2048,128]{1,0:T(8,128)(2,1)S(1)}, bf16[2048,128]{1,0:T(8,128)(2,1)S(1)}, u32[]{:S(2)}, u32[]{:S(2)}) collective-permute-start(bf16[2048,128]{1,0:T(8,128)(2,1)S(1)} %pad_maximum_fusion.2), channel_id=1, source_target_pairs={{0,2},{2,0},{1,3},{3,1},{4,6},{6,4},{5,7},{7,5},{8,10},{10,8},{9,1... | collective-permute-start | bytes 1572872 | tf_op jit(solution)/shard_map/ppermute | solution.py:77
  216.6 10.5 %collective-permute-start.24 = (bf16[2,256,256]{2,1,0:T(8,128)(2,1)S(1)}, bf16[2,256,256]{2,1,0:T(8,128)(2,1)S(1)}, u32[]{:S(2)}, u32[]{:S(2)}) collective-permute-start(bf16[2,256,256]{2,1,0:T(8,128)(2,1)S(1)} %slice.130), channel_id=1, source_target_pairs={{0,130},{2,128},{128,2},{130,0},{1,131},{3,129},{129,3},{131,1},{4... | collective-permute-start | bytes 786440 | tf_op jit(solution)/shard_map/ppermute | solution.py:77
  217.8 17.2 %collective-permute-start.16 = (bf16[2048,128]{1,0:T(8,128)(2,1)S(1)}, bf16[2048,128]{1,0:T(8,128)(2,1)S(1)}, u32[]{:S(2)}, u32[]{:S(2)}) collective-permute-start(bf16[2048,128]{1,0:T(8,128)(2,1)S(1)} %pad_maximum_fusion.3), channel_id=1, source_target_pairs={{0,130},{2,128},{128,2},{130,0},{1,131},{3,129},{129,3},{131,1},{4... | collective-permute-start | bytes 1572872 | tf_op jit(solution)/shard_map/ppermute | solution.py:77
  228.5 1.7 copy-start
  228.5 1.7 copy-start.2
  230.2 26.7 %collective-permute-start.25 = (bf16[4,4,256,256]{3,2,1,0:T(8,128)(2,1)}, bf16[4,4,256,256]{3,2,1,0:T(8,128)(2,1)}, u32[]{:S(2)}, u32[]{:S(2)}) collective-permute-start(bf16[4,4,256,256]{3,2,1,0:T(8,128)(2,1)} %pad_maximum_fusion.1), channel_id=1, source_target_pairs={{0,1},{1,0},{2,3},{3,2},{4,5},{5,4},{6,7},{7,6},{8,9},{9,8},{10,11... | collective-permute-start | bytes 6291464 | tf_op jit(solution)/shard_map/ppermute | solution.py:77
  236.4 0.8 collective-permute-start.17
  237.1 16.1 %collective-permute-start.19 = (bf16[2048,128]{1,0:T(8,128)(2,1)S(1)}, bf16[2048,128]{1,0:T(8,128)(2,1)S(1)}, u32[]{:S(2)}, u32[]{:S(2)}) collective-permute-start(bf16[2048,128]{1,0:T(8,128)(2,1)S(1)} %fusion.3), channel_id=1, source_target_pairs={{0,128},{1,130},{2,129},{3,131},{128,0},{129,2},{130,1},{131,3},{4... | collective-permute-start | bytes 1572872 | tf_op jit(solution)/shard_map/ppermute | solution.py:266
  237.2 16.0 %collective-permute-start.18 = (bf16[2048,128]{1,0:T(8,128)(2,1)S(1)}, bf16[2048,128]{1,0:T(8,128)(2,1)S(1)}, u32[]{:S(2)}, u32[]{:S(2)}) collective-permute-start(bf16[2048,128]{1,0:T(8,128)(2,1)S(1)} %collective-permute-done.17), channel_id=1, source_target_pairs={{0,1},{1,0},{2,3},{3,2},{4,5},{5,4},{6,7},{7,6},{8,9},{9,8},{10,11... | collective-permute-start | bytes 1572872 | tf_op jit(solution)/shard_map/ppermute | solution.py:77
  253.2 1.9 collective-permute-start.20
  255.3 1.6 copy-start.1
  255.3 1.6 copy-start.3
  (2 other events, 1.4 us)
Sparse Core Ops, SparseCore 0:
  10.8 93.7 all-gather.1

commit v3 on v2

--- a/solution.py
+++ b/solution.py
@@ -86,26 +86,10 @@
     return exchange(jnp.broadcast_to(x[None], (n,) + x.shape), axes)
 
 
-def ordered(mine, other, bit):
-    first = jnp.where(bit == 0, mine, other)
-    second = jnp.where(bit == 0, other, mine)
-    return first, second
-
-
 def ring_pieces(x):
     near, wrap = flip(x, ("xl",)), flip(x, X)
     half = x.shape[0] // 2
     return near, wrap, flip(wrap[:half], ("xl",)), flip(near[half:], X)
-
-
-def x_ring(x, xh, xl):
-    near, wrap, far_low, far_high = ring_pieces(x)
-    far = jnp.concatenate([far_low, far_high], axis=0)
-    low = ordered(x, near, xl)
-    high = ordered(far, wrap, xl)
-    col0 = ordered(low[0], high[0], xh)
-    col1 = ordered(low[1], high[1], xh)
-    return (col0[0], col1[0]), (col0[1], col1[1])
 
 
 def pack_columns(w_query, w_key, w_value, at):
@@ -195,6 +179,55 @@
     )(at, normed, *pieces, *others)
 
 
+def unpack(q_pieces, kv_pieces, kv_others, at):
+    def body(at_ref, *refs):
+        q_in, mine, theirs = refs[:4], refs[4:9], refs[9:14]
+        q_ref, k_ref, v_ref = refs[14:]
+        xl, xh, core = at_ref[0], at_ref[1], at_ref[2]
+        line = pl.program_id(0) % 4
+        for (h, l), piece in zip(
+            ((xh, core), (1 - xh, core), (xh, 1 - core), (1 - xh, 1 - core)), q_in
+        ):
+            q_ref[h, l] = piece[...]
+        spots = ((xl, xh), (1 - xl, xh), (1 - xl, 1 - xh), (xl, 1 - xh))
+        for group, c in ((mine, core), (theirs, 1 - core)):
+            for n, (l, h) in enumerate(spots):
+                if n < 3:
+                    piece = group[n][...]
+                else:
+                    piece = jnp.where(line < 2, group[3][...], group[4][...])
+                k_ref[h, l, 0, 0, c] = piece[0, :, 0:HD]
+                v_ref[h, l, 0, 0, c] = piece[0, :, HD : 2 * HD]
+
+    quarter = pl.BlockSpec((256, HD), lambda i, at: (i, 0))
+    whole = pl.BlockSpec((1, HD, 2 * HD), lambda i, at: (i % 4, i // 4, 0))
+    first = pl.BlockSpec((1, HD, 2 * HD), lambda i, at: (jnp.minimum(i % 4, 1), i // 4, 0))
+    last = pl.BlockSpec((1, HD, 2 * HD), lambda i, at: (jnp.maximum(i % 4, 2) - 2, i // 4, 0))
+    group = [whole, whole, whole, first, last]
+    wide = pl.BlockSpec((2, 2, 1, 1, 2, HD, HD), lambda i, at: (0, 0, i // 4, i % 4, 0, 0, 0))
+    bf16 = jnp.bfloat16
+    outs = pl.pallas_call(
+        body,
+        out_shape=(
+            jax.ShapeDtypeStruct((2, 2, 2048, HD), bf16),
+            jax.ShapeDtypeStruct((2, 2, 2, 4, 2, HD, HD), bf16),
+            jax.ShapeDtypeStruct((2, 2, 2, 4, 2, HD, HD), bf16),
+        ),
+        grid_spec=pltpu.PrefetchScalarGridSpec(
+            num_scalar_prefetch=1,
+            grid=(8,),
+            in_specs=[quarter] * 4 + group + group,
+            out_specs=(
+                pl.BlockSpec((2, 2, 256, HD), lambda i, at: (0, 0, i, 0)),
+                wide,
+                wide,
+            ),
+        ),
+        name="unpack",
+    )(at, *q_pieces, *kv_pieces, *kv_others)
+    return tuple(out.reshape(D, HD) for out in outs)
+
+
 def local(hidden, cotangent, seg_ids, advantage, w_query, w_key, w_value):
     f32 = jnp.float32
     bf16 = jnp.bfloat16
@@ -243,7 +276,6 @@
     contract = (((0,), (0,)), ((), ()))
     part_q = lax.dot_general(normed, scaled_q, contract, preferred_element_type=f32)
     part_q = part_q.astype(bf16).reshape(4, 2048, HD)
-    part_q, scaled_kv = lax.optimization_barrier((part_q, scaled_kv))
 
     def part_for(mask):
         return lax.dynamic_index_in_dim(part_q, ring ^ mask, 0, keepdims=False)
@@ -275,12 +307,6 @@
     )
     near_other = flip(near, ("core",))
     far_other = flip(far, ("core",))
-    near = ordered(near, near_other, core)
-    far = ordered(far, far_other, core)
-    low = ordered(near[0], far[0], xh)
-    high = ordered(near[1], far[1], xh)
-    roll_q = jnp.stack([low[0], high[0], low[1], high[1]], axis=0).reshape(D, HD)
-
     kv_sum = exchange(scaled_kv.reshape(8, 64, 2 * HD), MEM)
     kv_sum = kv_sum.astype(f32)
     kv_sum = jnp.sum(kv_sum, axis=0).astype(bf16)
@@ -294,11 +320,9 @@
     old_kv = lax.dynamic_index_in_dim(old_kv, member, 1, keepdims=False).reshape(256, 2 * HD)
     new_kv = (old_kv.astype(f32) - step_rate * jnp.sum(part_kv, axis=0)).astype(bf16)
     new_kv = spread(new_kv, ("zl",))
-    new_kv = x_ring(new_kv, xh, xl)
-    new_kv = jnp.stack([new_kv[h][l] for h in (0, 1) for l in (0, 1)], axis=0)
-    new_kv = jnp.stack(ordered(new_kv, flip(new_kv, ("core",)), core), axis=0)
-    new_kv = new_kv.reshape(2, 4, 4, 2, 128, 2 * HD).transpose(1, 3, 2, 0, 4, 5).reshape(D, 2 * HD)
-    return roll_q, new_kv[:, :HD], new_kv[:, HD:]
+    kv_pieces = (new_kv,) + ring_pieces(new_kv)
+    kv_others = tuple(flip(p, ("core",)) for p in kv_pieces)
+    return unpack((near, far, near_other, far_other), kv_pieces, kv_others, at)
 
 
 def solution(mesh):

time: 271 us -> 244 us (0.900)
  blocking collectives: 63.4 us -> 36 us
  waiting for transfers between devices: 83.2 us -> 63.2 us
  starting transfers between devices: 53.6 us -> 67.9 us
  Pallas kernels: 16.8 us -> 25.3 us
    all_to_all x3 -> x1, blocking collectives: 63.4 us -> 36 us  [exchange(): return lax.all_to_all(x, axes, split_axis=0, concat_axis=0, tiled=True)]
    all_to_all x2 -> x4, waiting for transfers between devices: 21.9 us -> 11.2 us  [exchange(): return lax.all_to_all(x, axes, split_axis=0, concat_axis=0, tiled=True)]
    all_to_all x2 -> x4, starting transfers between devices: 6.94 us -> 17.4 us  [exchange(): return lax.all_to_all(x, axes, split_axis=0, concat_axis=0, tiled=True)]
    pallas_call x0 -> x1, Pallas kernels: none -> 8.52 us  [unpack(): pl.pallas_call(body, out_shape=(jax.ShapeDtypeStruct((2, 2, 2048, HD), bf...]
    ppermute x20 -> x24, waiting for transfers between devices: 56.1 us -> 48.5 us  [flip(): return lax.ppermute(x, axes, [(i, n - 1 - i) for i in range(n)])]
    another operation x5 -> x1, other arithmetic: 6.12 us -> 1.28 us  [the longest x2 3.09 us: local(): new_kv = jnp.stack([new_kv[h][l] for h in (0, 1) for l in (0, 1)], axis=0)]
    ppermute x20 -> x24, starting transfers between devices: 43 us -> 44.9 us  [flip(): return lax.ppermute(x, axes, [(i, n - 1 - i) for i in range(n)])]
  transfers between devices with their start and end apart: 29 -> 35, of which waited for: 15 -> 19; matrix products, arithmetic and copies ran while one was open for 5% -> 9% of each run, Pallas kernels for 6% -> 7%
where the time goes in v3:
time: 244 us; the launch traced here: 241 us
  starting transfers between devices  67.9 us (28%)
  waiting for transfers between devices  63.2 us (26%)
  blocking collectives  36 us (15%)
  Pallas kernels  25.3 us (10%)
  other arithmetic  15.3 us (6%)
  between operations  14.4 us (6%)
  matrix products  10.5 us (4%)
  local copies, waits for them, and re-layouts  8.04 us (3%)
    ppermute x24, waiting for transfers between devices, flip(): return lax.ppermute(x, axes, [(i, n - 1 - i) for i in range(n)])  48.5 us
    ppermute x24, starting transfers between devices, flip(): return lax.ppermute(x, axes, [(i, n - 1 - i) for i in range(n)])  44.9 us
    all_to_all x1, blocking collectives, exchange(): return lax.all_to_all(x, axes, split_axis=0, concat_axis=0, tiled=True)  36 us
    all_to_all x4, starting transfers between devices, exchange(): return lax.all_to_all(x, axes, split_axis=0, concat_axis=0, tiled=True)  17.4 us
    pallas_call x1, Pallas kernels, project(): pl.pallas_call(body, out_shape=(jax.ShapeDtypeStruct((512, 3 * HD), jnp.f...  13.7 us
    all_to_all x4, waiting for transfers between devices, exchange(): return lax.all_to_all(x, axes, split_axis=0, concat_axis=0, tiled=True)  11.2 us
    pallas_call x1, Pallas kernels, unpack(): pl.pallas_call(body, out_shape=(jax.ShapeDtypeStruct((2, 2, 2048, HD), bf...  8.52 us
    dot_general x1, matrix products, local(): lax.dot_general(normed, scaled_q, contract, preferred_element_type=f32)  5.87 us
  transfers between devices with their start and end apart: 35, of which 19 were waited for; matrix products, arithmetic and copies ran while one was open for 9% of the time, Pallas kernels for 7%

profile of v3, /device:TPU:8, one launch (start us, length us, event | category | flops | bytes accessed | tf_op | source)
XLA Modules:
  0.0 240.6 jit_solution(5522669126873560652)
XLA Ops:
  7.2 1.1 fusion.31
  8.3 1.0 fusion.32
  11.3 3.1 %pack_columns.1 = bf16[32,128,128]{2,1,0:T(8,128)(2,1)} custom-call(s32[4]{0:T(128)} %pad_add_fusion.at_ref, bf16[128,8192]{1,0:T(8,128)(2,1)} %q_ref.1, bf16[128,1024]{1,0:T(8,128)(2,1)} %k_ref.1, bf16[128,1024]{1,0:T(8,128)(2,1)} %v_ref.1), custom_call_target="tpu_custom_call" | custom-call | tf_op jit(solution)/shard_map/pack_columns/pallas_call | solution.py:105
  14.4 36.0 %all_to_all.25.refs_0_ = bf16[32,128,128]{2,1,0:T(8,128)(2,1)S(1)} all-to-all(bf16[32,128,128]{2,1,0:T(8,128)(2,1)} %pack_columns.1), channel_id=1, replica_groups=mesh['xh'=2,'y'=4,'zh'=2,'zl'=4,'xl'=2,'core'=2] {'y','zh','zl'}, dimensions={0} | all-to-all | bytes 2097152 | tf_op jit(solution)/shard_map/all_to_all | solution.py:81
  50.4 8.1 %collective-permute-start.2 = (bf16[32,128,128]{2,1,0:T(8,128)(2,1)S(1)}, bf16[32,128,128]{2,1,0:T(8,128)(2,1)S(1)}, u32[]{:S(2)}, u32[]{:S(2)}) collective-permute-start(bf16[32,128,128]{2,1,0:T(8,128)(2,1)S(1)} %all_to_all.25.refs_0_), channel_id=1, source_target_pairs={{0,130},{2,128},{128,2},{130,0},{1,131},{3,129},{129,3},{131,1},{4... | collective-permute-start | bytes 3145736 | tf_op jit(solution)/shard_map/ppermute | solution.py:77
  58.5 22.5 %collective-permute-done.2.refs_2_ = bf16[32,128,128]{2,1,0:T(8,128)(2,1)S(1)} collective-permute-done((bf16[32,128,128]{2,1,0:T(8,128)(2,1)S(1)}, bf16[32,128,128]{2,1,0:T(8,128)(2,1)S(1)}, u32[]{:S(2)}, u32[]{:S(2)}) %collective-permute-start.2) | collective-permute-done | bytes 1048608 | tf_op jit(solution)/shard_map/ppermute | solution.py:77
  81.8 1.8 collective-permute-start.3
  84.0 0.9 slice.110
  84.9 1.6 collective-permute-start.4
  87.8 4.1 %collective-permute-start.5 = (bf16[32,128,128]{2,1,0:T(8,128)(2,1)S(1)}, bf16[32,128,128]{2,1,0:T(8,128)(2,1)}, u32[]{:S(2)}, u32[]{:S(2)}) collective-permute-start(bf16[32,128,128]{2,1,0:T(8,128)(2,1)S(1)} %all_to_all.25.refs_0_), channel_id=1, source_target_pairs={{0,1},{1,0},{2,3},{3,2},{4,5},{5,4},{6,7},{7,6},{8,9},{9,8},{10,11... | collective-permute-start | bytes 3145736 | tf_op jit(solution)/shard_map/ppermute | solution.py:77
  91.9 4.5 %collective-permute-start.6 = (bf16[32,128,128]{2,1,0:T(8,128)(2,1)S(1)}, bf16[32,128,128]{2,1,0:T(8,128)(2,1)}, u32[]{:S(2)}, u32[]{:S(2)}) collective-permute-start(bf16[32,128,128]{2,1,0:T(8,128)(2,1)S(1)} %collective-permute-done.1.refs_1_), channel_id=1, source_target_pairs={{0,1},{1,0},{2,3},{3,2},{4,5},{5,4},{6,7},{7,6},{8,9},{9,8},{10,11... | collective-permute-start | bytes 3145736 | tf_op jit(solution)/shard_map/ppermute | solution.py:77
  97.1 3.5 %collective-permute-done.4.refs_4_ = bf16[16,128,128]{2,1,0:T(8,128)(2,1)} collective-permute-done((bf16[16,128,128]{2,1,0:T(8,128)(2,1)}, bf16[16,128,128]{2,1,0:T(8,128)(2,1)}, u32[]{:S(2)}, u32[]{:S(2)}) %collective-permute-start.4) | collective-permute-done | bytes 524320 | tf_op jit(solution)/shard_map/ppermute | solution.py:77
  104.3 13.7 %project.1 = (f32[512,384]{1,0:T(8,128)}, bf16[32,2,2,64,128]{4,3,2,1,0:T(8,128)(2,1)}, bf16[32,2,2,2,32,256]{5,4,3,2,1,0:T(8,128)(2,1)}, bf16[512,1024]{1,0:T(8,128)(2,1)}) custom-call(s32[4]{0:T(128)} %pad_add_fusion.at_ref, bf16[512,8192]{1,0:T(8,128)(2,1)} %all-gather.2.cloned.1.call-done.rows_ref, bf16[32,128,128]{2,1,0:T(8,128)(2,1)} %copy-done, ...), custom_call_target="tpu_custom_call" | custom-call | tf_op jit(solution)/shard_map/project/pallas_call | solution.py:159
  118.1 1.2 broadcast_multiply_fusion
  119.3 1.3 fusion.38
  122.9 1.3 fusion.35
  124.6 0.9 fusion.9
  125.5 5.9 %all-to-all-start.1 = ((bf16[8,64,256]{2,1,0:T(8,128)(2,1)}), bf16[8,64,256]{2,1,0:T(8,128)(2,1)S(1)}, u32[]{:S(2)}, u32[]{:S(2)}) async-start(bf16[8,64,256]{2,1,0:T(8,128)(2,1)} %fusion.9), calls=%async_computation.1 | async-start | bytes 524288 | tf_op jit(solution)/shard_map/all_to_all | solution.py:81
  131.4 5.9 %convolution_convert_fusion = bf16[8192,128]{1,0:T(8,128)(2,1)S(1)} fusion(bf16[512,8192]{1,0:T(8,128)(2,1)} %all-gather.2.cloned.1.call-done.rows_ref, f32[512,64]{1,0:T(8,128)S(1)} %get-tuple-element.31, f32[512,64]{1,0:T(8,128)S(1)} %get-tuple-element.32), kind=kOutput, calls=%fused_computation | convolution fusion | flops 1074987008 | bytes 10747904 | tf_op jit(solution)/shard_map/dot_general | solution.py:277
  139.5 1.6 all-to-all-done.1
  141.9 3.5 %all-to-all-start.2 = ((bf16[8,64,256]{2,1,0:T(8,128)(2,1)}), bf16[8,64,256]{2,1,0:T(8,128)(2,1)S(1)}, u32[]{:S(2)}, u32[]{:S(2)}) async-start(bf16[8,64,256]{2,1,0:T(8,128)(2,1)} %broadcast_in_dim.8), calls=%async_computation.2 | async-start | bytes 524288 | tf_op jit(solution)/shard_map/all_to_all | solution.py:81
  145.4 2.8 %collective-permute-done.13 = bf16[1024,128]{1,0:T(8,128)(2,1)S(1)} collective-permute-done((bf16[1024,128]{1,0:T(8,128)(2,1)}, bf16[1024,128]{1,0:T(8,128)(2,1)S(1)}, u32[]{:S(2)}, u32[]{:S(2)}) %collective-permute-start.13) | collective-permute-done | bytes 262176 | tf_op jit(solution)/shard_map/ppermute | solution.py:77
  148.2 1.8 fusion.11
  150.0 5.1 %all-to-all-done.2 = bf16[8,64,256]{2,1,0:T(8,128)(2,1)S(1)} async-done(((bf16[8,64,256]{2,1,0:T(8,128)(2,1)}), bf16[8,64,256]{2,1,0:T(8,128)(2,1)S(1)}, u32[]{:S(2)}, u32[]{:S(2)}) %all-to-all-start.2) | async-done | bytes 262176 | tf_op jit(solution)/shard_map/all_to_all | solution.py:81
  155.1 2.5 %convolution_convert_fusion.1 = bf16[1024,256]{1,0:T(8,128)(2,1)} fusion(bf16[512,1024]{1,0:T(8,128)(2,1)} %get-tuple-element.13, bf16[512,256]{1,0:T(8,128)(2,1)S(1)} %bitcast.57), kind=kOutput, calls=%fused_computation.2 | convolution fusion | flops 268697600 | bytes 1835008 | tf_op jit(solution)/shard_map/dot_general | solution.py:314
  157.7 4.5 %all-to-all-start.3 = ((bf16[4,256,256]{2,1,0:T(8,128)(2,1)}), bf16[4,256,256]{2,1,0:T(8,128)(2,1)S(1)}, u32[]{:S(2)}, u32[]{:S(2)}) async-start(bf16[4,256,256]{2,1,0:T(8,128)(2,1)} %bitcast.56), calls=%async_computation.3 | async-start | bytes 1048576 | tf_op jit(solution)/shard_map/all_to_all | solution.py:81
  162.2 1.8 pad_maximum_fusion
  163.9 2.0 collective-permute-start.14
  166.8 2.1 collective-permute-start.16
  168.9 0.9 constant_dynamic-slice_fusion
  169.8 3.3 %all-to-all-done.3 = bf16[4,256,256]{2,1,0:T(8,128)(2,1)S(1)} async-done(((bf16[4,256,256]{2,1,0:T(8,128)(2,1)}), bf16[4,256,256]{2,1,0:T(8,128)(2,1)S(1)}, u32[]{:S(2)}, u32[]{:S(2)}) %all-to-all-start.3) | async-done | bytes 524320 | tf_op jit(solution)/shard_map/all_to_all | solution.py:81
  174.0 3.5 %all-to-all-start.4 = ((bf16[4,256,256]{2,1,0:T(8,128)(2,1)}), bf16[4,256,256]{2,1,0:T(8,128)(2,1)S(1)}, u32[]{:S(2)}, u32[]{:S(2)}) async-start(bf16[4,256,256]{2,1,0:T(8,128)(2,1)} %broadcast_in_dim.9), calls=%async_computation.4 | async-start | bytes 1048576 | tf_op jit(solution)/shard_map/all_to_all | solution.py:81
  177.5 3.6 %collective-permute-done.14 = bf16[2048,128]{1,0:T(8,128)(2,1)} collective-permute-done((bf16[2048,128]{1,0:T(8,128)(2,1)}, bf16[2048,128]{1,0:T(8,128)(2,1)}, u32[]{:S(2)}, u32[]{:S(2)}) %collective-permute-start.14) | collective-permute-done | bytes 524320 | tf_op jit(solution)/shard_map/ppermute | solution.py:77
  181.1 1.4 collective-permute-done.16
  182.5 2.3 fusion.3
  184.8 1.7 collective-permute-start.17
  186.5 1.3 collective-permute-start.18
  187.8 1.2 all-to-all-done.4.refs_4_
  189.0 1.2 collective-permute-start.22
  190.1 10.2 %collective-permute-start.19 = (bf16[2048,128]{1,0:T(8,128)(2,1)S(1)}, bf16[2048,128]{1,0:T(8,128)(2,1)S(1)}, u32[]{:S(2)}, u32[]{:S(2)}) collective-permute-start(bf16[2048,128]{1,0:T(8,128)(2,1)S(1)} %collective-permute-done.17.refs_0_), channel_id=1, source_target_pairs={{0,1},{1,0},{2,3},{3,2},{4,5},{5,4},{6,7},{7,6},{8,9},{9,8},{10,11... | collective-permute-start | bytes 1572872 | tf_op jit(solution)/shard_map/ppermute | solution.py:77
  200.4 2.6 %collective-permute-done.18.refs_1_ = bf16[2048,128]{1,0:T(8,128)(2,1)S(1)} collective-permute-done((bf16[2048,128]{1,0:T(8,128)(2,1)}, bf16[2048,128]{1,0:T(8,128)(2,1)S(1)}, u32[]{:S(2)}, u32[]{:S(2)}) %collective-permute-start.18) | collective-permute-done | bytes 524320 | tf_op jit(solution)/shard_map/ppermute | solution.py:298
  203.0 5.2 %collective-permute-start.20 = (bf16[2048,128]{1,0:T(8,128)(2,1)S(1)}, bf16[2048,128]{1,0:T(8,128)(2,1)S(1)}, u32[]{:S(2)}, u32[]{:S(2)}) collective-permute-start(bf16[2048,128]{1,0:T(8,128)(2,1)S(1)} %collective-permute-done.18.refs_1_), channel_id=1, source_target_pairs={{0,1},{1,0},{2,3},{3,2},{4,5},{5,4},{6,7},{7,6},{8,9},{9,8},{10,11... | collective-permute-start | bytes 1572872 | tf_op jit(solution)/shard_map/ppermute | solution.py:77
  208.2 6.0 %collective-permute-done.22.refs_6_ = bf16[4,256,256]{2,1,0:T(8,128)(2,1)S(1)} collective-permute-done((bf16[4,256,256]{2,1,0:T(8,128)(2,1)S(1)}, bf16[4,256,256]{2,1,0:T(8,128)(2,1)S(1)}, u32[]{:S(2)}, u32[]{:S(2)}) %collective-permute-start.22) | collective-permute-done | bytes 524320 | tf_op jit(solution)/shard_map/ppermute | solution.py:77
  214.4 1.5 collective-permute-start.24
  216.5 4.3 %collective-permute-done.23.refs_7_ = bf16[2,256,256]{2,1,0:T(8,128)(2,1)S(1)} collective-permute-done((bf16[2,256,256]{2,1,0:T(8,128)(2,1)S(1)}, bf16[2,256,256]{2,1,0:T(8,128)(2,1)S(1)}, u32[]{:S(2)}, u32[]{:S(2)}) %collective-permute-start.23) | collective-permute-done | bytes 262176 | tf_op jit(solution)/shard_map/ppermute | solution.py:77
  220.8 1.4 collective-permute-done.24.refs_8_
  222.3 1.4 collective-permute-done.29.refs_13_
  225.3 8.5 %unpack.1 = (bf16[2,2,2048,128]{3,2,1,0:T(8,128)(2,1)}, bf16[2,2,2,4,2,128,128]{6,5,4,3,2,1,0:T(8,128)(2,1)}, bf16[2,2,2,4,2,128,128]{6,5,4,3,2,1,0:T(8,128)(2,1)}) custom-call(s32[4]{0:T(128)} %pad_add_fusion.at_ref, bf16[2048,128]{1,0:T(8,128)(2,1)} %copy-done.6, bf16[2048,128]{1,0:T(8,128)(2,1)} %copy-done.7, bf16[2048,128]{1,0:T(8,128)(2,1)} %copy-done.8, ...), custom_call_target="tpu_custom_call" | custom-call | tf_op jit(solution)/shard_map/unpack/pallas_call | solution.py:209
  (110 shorter events, 18.9 us)
Async XLA Ops:
  7.2 97.2 %all-gather.2.cloned.1.call-start = ((), (), s32[]{:S(2)}) async-start(), calls=%async_computation.5 | async-start | bytes 8519680 | tf_op jit(solution)/shard_map/all_gather | solution.py:246
  9.3 0.7 collective-permute-start
  14.4 72.0 %copy-start.20 = (s32[1,512]{1,0:T(1,128)S(1)}, s32[1,512]{1,0:T(1,128)}, u32[]{:S(2)}) copy-start(s32[1,512]{1,0:T(1,128)} %param.9) | copy-start | bytes 6148
  14.4 72.7 %copy-start.21 = (f32[1,8]{1,0:T(1,128)S(1)}, f32[1,8]{1,0:T(1,128)}, u32[]{:S(2)}) copy-start(f32[1,8]{1,0:T(1,128)} %param.10) | copy-start | bytes 100
  14.4 86.5 %copy-start.19 = (bf16[1,512,128]{2,1,0:T(8,128)(2,1)S(1)}, bf16[1,512,128]{2,1,0:T(8,128)(2,1)}, u32[]{:S(2)}) copy-start(bf16[1,512,128]{2,1,0:T(8,128)(2,1)} %param.8) | copy-start | bytes 393220
  50.4 54.0 %copy-start = (bf16[32,128,128]{2,1,0:T(8,128)(2,1)}, bf16[32,128,128]{2,1,0:T(8,128)(2,1)S(1)}, u32[]{:S(2)}) copy-start(bf16[32,128,128]{2,1,0:T(8,128)(2,1)S(1)} %all_to_all.25.refs_0_) | copy-start | bytes 3145732
  50.4 30.6 %collective-permute-start.2 = (bf16[32,128,128]{2,1,0:T(8,128)(2,1)S(1)}, bf16[32,128,128]{2,1,0:T(8,128)(2,1)S(1)}, u32[]{:S(2)}, u32[]{:S(2)}) collective-permute-start(bf16[32,128,128]{2,1,0:T(8,128)(2,1)S(1)} %all_to_all.25.refs_0_), channel_id=1, source_target_pairs={{0,130},{2,128},{128,2},{130,0},{1,131},{3,129},{129,3},{131,1},{4... | collective-permute-start | bytes 3145736 | tf_op jit(solution)/shard_map/ppermute | solution.py:77
  58.5 25.5 %collective-permute-start.1 = (bf16[32,128,128]{2,1,0:T(8,128)(2,1)S(1)}, bf16[32,128,128]{2,1,0:T(8,128)(2,1)S(1)}, u32[]{:S(2)}, u32[]{:S(2)}) collective-permute-start(bf16[32,128,128]{2,1,0:T(8,128)(2,1)S(1)} %all_to_all.25.refs_0_), channel_id=1, source_target_pairs={{0,2},{2,0},{1,3},{3,1},{4,6},{6,4},{5,7},{7,5},{8,10},{10,8},{9,1... | collective-permute-start | bytes 3145736 | tf_op jit(solution)/shard_map/ppermute | solution.py:77
  80.9 23.4 %copy-start.1 = (bf16[32,128,128]{2,1,0:T(8,128)(2,1)}, bf16[32,128,128]{2,1,0:T(8,128)(2,1)S(1)}, u32[]{:S(2)}) copy-start(bf16[32,128,128]{2,1,0:T(8,128)(2,1)S(1)} %collective-permute-done.2.refs_2_) | copy-start | bytes 3145732
  81.8 14.7 %collective-permute-start.3 = (bf16[16,128,128]{2,1,0:T(8,128)(2,1)}, bf16[16,128,128]{2,1,0:T(8,128)(2,1)}, u32[]{:S(2)}, u32[]{:S(2)}) collective-permute-start(bf16[16,128,128]{2,1,0:T(8,128)(2,1)} %slice.109), channel_id=1, source_target_pairs={{0,2},{2,0},{1,3},{3,1},{4,6},{6,4},{5,7},{7,5},{8,10},{10,8},{9,1... | collective-permute-start | bytes 1572872 | tf_op jit(solution)/shard_map/ppermute | solution.py:77
  84.0 20.4 %copy-start.2 = (bf16[32,128,128]{2,1,0:T(8,128)(2,1)}, bf16[32,128,128]{2,1,0:T(8,128)(2,1)S(1)}, u32[]{:S(2)}) copy-start(bf16[32,128,128]{2,1,0:T(8,128)(2,1)S(1)} %collective-permute-done.1.refs_1_) | copy-start | bytes 3145732
  84.9 15.7 %collective-permute-start.4 = (bf16[16,128,128]{2,1,0:T(8,128)(2,1)}, bf16[16,128,128]{2,1,0:T(8,128)(2,1)}, u32[]{:S(2)}, u32[]{:S(2)}) collective-permute-start(bf16[16,128,128]{2,1,0:T(8,128)(2,1)} %slice.110), channel_id=1, source_target_pairs={{0,130},{2,128},{128,2},{130,0},{1,131},{3,129},{129,3},{131,1},{4... | collective-permute-start | bytes 1572872 | tf_op jit(solution)/shard_map/ppermute | solution.py:77
  86.4 9.9 %collective-permute-start.10 = (s32[512]{0:T(512)S(1)}, s32[512]{0:T(512)S(1)}, u32[]{:S(2)}, u32[]{:S(2)}) collective-permute-start(s32[512]{0:T(512)S(1)} %bitcast.65), channel_id=1, source_target_pairs={{0,0},{1,2},{2,1},{3,3},{4,4},{5,6},{6,5},{7,7},{8,8},{9,10},{10,9... | collective-permute-start | bytes 6152 | tf_op jit(solution)/shard_map/ppermute | solution.py:72
  87.1 4.8 %collective-permute-start.12 = (f32[8]{0:T(128)S(1)}, f32[8]{0:T(128)S(1)}, u32[]{:S(2)}, u32[]{:S(2)}) collective-permute-start(f32[8]{0:T(128)S(1)} %bitcast.66), channel_id=1, source_target_pairs={{0,0},{1,2},{2,1},{3,3},{4,4},{5,6},{6,5},{7,7},{8,8},{9,10},{10,9... | collective-permute-start | bytes 104 | tf_op jit(solution)/shard_map/ppermute | solution.py:72
  87.8 13.1 %collective-permute-start.5 = (bf16[32,128,128]{2,1,0:T(8,128)(2,1)S(1)}, bf16[32,128,128]{2,1,0:T(8,128)(2,1)}, u32[]{:S(2)}, u32[]{:S(2)}) collective-permute-start(bf16[32,128,128]{2,1,0:T(8,128)(2,1)S(1)} %all_to_all.25.refs_0_), channel_id=1, source_target_pairs={{0,1},{1,0},{2,3},{3,2},{4,5},{5,4},{6,7},{7,6},{8,9},{9,8},{10,11... | collective-permute-start | bytes 3145736 | tf_op jit(solution)/shard_map/ppermute | solution.py:77
  91.9 10.8 %collective-permute-start.6 = (bf16[32,128,128]{2,1,0:T(8,128)(2,1)S(1)}, bf16[32,128,128]{2,1,0:T(8,128)(2,1)}, u32[]{:S(2)}, u32[]{:S(2)}) collective-permute-start(bf16[32,128,128]{2,1,0:T(8,128)(2,1)S(1)} %collective-permute-done.1.refs_1_), channel_id=1, source_target_pairs={{0,1},{1,0},{2,3},{3,2},{4,5},{5,4},{6,7},{7,6},{8,9},{9,8},{10,11... | collective-permute-start | bytes 3145736 | tf_op jit(solution)/shard_map/ppermute | solution.py:77
  96.4 7.1 %collective-permute-start.7 = (bf16[32,128,128]{2,1,0:T(8,128)(2,1)S(1)}, bf16[32,128,128]{2,1,0:T(8,128)(2,1)}, u32[]{:S(2)}, u32[]{:S(2)}) collective-permute-start(bf16[32,128,128]{2,1,0:T(8,128)(2,1)S(1)} %collective-permute-done.2.refs_2_), channel_id=1, source_target_pairs={{0,1},{1,0},{2,3},{3,2},{4,5},{5,4},{6,7},{7,6},{8,9},{9,8},{10,11... | collective-permute-start | bytes 3145736 | tf_op jit(solution)/shard_map/ppermute | solution.py:77
  96.5 5.3 %collective-permute-start.8 = (bf16[16,128,128]{2,1,0:T(8,128)(2,1)}, bf16[16,128,128]{2,1,0:T(8,128)(2,1)S(1)}, u32[]{:S(2)}, u32[]{:S(2)}) collective-permute-start(bf16[16,128,128]{2,1,0:T(8,128)(2,1)} %collective-permute-done.3.refs_3_), channel_id=1, source_target_pairs={{0,1},{1,0},{2,3},{3,2},{4,5},{5,4},{6,7},{7,6},{8,9},{9,8},{10,11... | collective-permute-start | bytes 1572872 | tf_op jit(solution)/shard_map/ppermute | solution.py:77
  100.6 2.1 collective-permute-start.9
  100.9 20.4 %collective-permute-start.11 = (bf16[512,128]{1,0:T(8,128)(2,1)S(1)}, bf16[512,128]{1,0:T(8,128)(2,1)S(1)}, u32[]{:S(2)}, u32[]{:S(2)}) collective-permute-start(bf16[512,128]{1,0:T(8,128)(2,1)S(1)} %bitcast.64), channel_id=1, source_target_pairs={{0,0},{1,2},{2,1},{3,3},{4,4},{5,6},{6,5},{7,7},{8,8},{9,10},{10,9... | collective-permute-start | bytes 393224 | tf_op jit(solution)/shard_map/ppermute | solution.py:72
  125.5 15.6 %all-to-all-start.1 = ((bf16[8,64,256]{2,1,0:T(8,128)(2,1)}), bf16[8,64,256]{2,1,0:T(8,128)(2,1)S(1)}, u32[]{:S(2)}, u32[]{:S(2)}) async-start(bf16[8,64,256]{2,1,0:T(8,128)(2,1)} %fusion.9), calls=%async_computation.1 | async-start | bytes 524288 | tf_op jit(solution)/shard_map/all_to_all | solution.py:81
  138.1 10.1 %collective-permute-start.13 = (bf16[1024,128]{1,0:T(8,128)(2,1)}, bf16[1024,128]{1,0:T(8,128)(2,1)S(1)}, u32[]{:S(2)}, u32[]{:S(2)}) collective-permute-start(bf16[1024,128]{1,0:T(8,128)(2,1)} %get-tuple-element.19), channel_id=1, source_target_pairs={{0,130},{2,128},{128,2},{130,0},{1,131},{3,129},{129,3},{131,1},{4... | collective-permute-start | bytes 786440 | tf_op jit(solution)/shard_map/ppermute | solution.py:77
  138.9 9.3 %collective-permute-start.15 = (bf16[1024,128]{1,0:T(8,128)(2,1)S(1)}, bf16[1024,128]{1,0:T(8,128)(2,1)}, u32[]{:S(2)}, u32[]{:S(2)}) collective-permute-start(bf16[1024,128]{1,0:T(8,128)(2,1)S(1)} %get-tuple-element.21), channel_id=1, source_target_pairs={{0,2},{2,0},{1,3},{3,1},{4,6},{6,4},{5,7},{7,5},{8,10},{10,8},{9,1... | collective-permute-start | bytes 786440 | tf_op jit(solution)/shard_map/ppermute | solution.py:77
  141.9 13.2 %all-to-all-start.2 = ((bf16[8,64,256]{2,1,0:T(8,128)(2,1)}), bf16[8,64,256]{2,1,0:T(8,128)(2,1)S(1)}, u32[]{:S(2)}, u32[]{:S(2)}) async-start(bf16[8,64,256]{2,1,0:T(8,128)(2,1)} %broadcast_in_dim.8), calls=%async_computation.2 | async-start | bytes 524288 | tf_op jit(solution)/shard_map/all_to_all | solution.py:81
  157.7 15.4 %all-to-all-start.3 = ((bf16[4,256,256]{2,1,0:T(8,128)(2,1)}), bf16[4,256,256]{2,1,0:T(8,128)(2,1)S(1)}, u32[]{:S(2)}, u32[]{:S(2)}) async-start(bf16[4,256,256]{2,1,0:T(8,128)(2,1)} %bitcast.56), calls=%async_computation.3 | async-start | bytes 1048576 | tf_op jit(solution)/shard_map/all_to_all | solution.py:81
  163.9 17.2 %collective-permute-start.14 = (bf16[2048,128]{1,0:T(8,128)(2,1)}, bf16[2048,128]{1,0:T(8,128)(2,1)}, u32[]{:S(2)}, u32[]{:S(2)}) collective-permute-start(bf16[2048,128]{1,0:T(8,128)(2,1)} %pad_maximum_fusion), channel_id=1, source_target_pairs={{0,2},{2,0},{1,3},{3,1},{4,6},{6,4},{5,7},{7,5},{8,10},{10,8},{9,1... | collective-permute-start | bytes 1572872 | tf_op jit(solution)/shard_map/ppermute | solution.py:77
  166.8 15.7 %collective-permute-start.16 = (bf16[2048,128]{1,0:T(8,128)(2,1)}, bf16[2048,128]{1,0:T(8,128)(2,1)S(1)}, u32[]{:S(2)}, u32[]{:S(2)}) collective-permute-start(bf16[2048,128]{1,0:T(8,128)(2,1)} %pad_maximum_fusion.1), channel_id=1, source_target_pairs={{0,130},{2,128},{128,2},{130,0},{1,131},{3,129},{129,3},{131,1},{4... | collective-permute-start | bytes 1572872 | tf_op jit(solution)/shard_map/ppermute | solution.py:77
  174.0 14.9 %all-to-all-start.4 = ((bf16[4,256,256]{2,1,0:T(8,128)(2,1)}), bf16[4,256,256]{2,1,0:T(8,128)(2,1)S(1)}, u32[]{:S(2)}, u32[]{:S(2)}) async-start(bf16[4,256,256]{2,1,0:T(8,128)(2,1)} %broadcast_in_dim.9), calls=%async_computation.4 | async-start | bytes 1048576 | tf_op jit(solution)/shard_map/all_to_all | solution.py:81
  184.8 5.3 %collective-permute-start.17 = (bf16[2048,128]{1,0:T(8,128)(2,1)}, bf16[2048,128]{1,0:T(8,128)(2,1)S(1)}, u32[]{:S(2)}, u32[]{:S(2)}) collective-permute-start(bf16[2048,128]{1,0:T(8,128)(2,1)} %fusion.3), channel_id=1, source_target_pairs={{0,0},{1,2},{2,1},{3,3},{4,4},{5,6},{6,5},{7,7},{8,8},{9,10},{10,9... | collective-permute-start | bytes 1572872 | tf_op jit(solution)/shard_map/ppermute | solution.py:72
  186.5 16.5 %collective-permute-start.18 = (bf16[2048,128]{1,0:T(8,128)(2,1)}, bf16[2048,128]{1,0:T(8,128)(2,1)S(1)}, u32[]{:S(2)}, u32[]{:S(2)}) collective-permute-start(bf16[2048,128]{1,0:T(8,128)(2,1)} %fusion.3), channel_id=1, source_target_pairs={{0,128},{1,130},{2,129},{3,131},{128,0},{129,2},{130,1},{131,3},{4... | collective-permute-start | bytes 1572872 | tf_op jit(solution)/shard_map/ppermute | solution.py:298
  189.0 36.2 %copy-start.3 = (bf16[4,256,256]{2,1,0:T(8,128)(2,1)}, bf16[4,256,256]{2,1,0:T(8,128)(2,1)S(1)}, u32[]{:S(2)}) copy-start(bf16[4,256,256]{2,1,0:T(8,128)(2,1)S(1)} %all-to-all-done.4.refs_4_) | copy-start | bytes 1572868
  189.0 25.3 %collective-permute-start.22 = (bf16[4,256,256]{2,1,0:T(8,128)(2,1)S(1)}, bf16[4,256,256]{2,1,0:T(8,128)(2,1)S(1)}, u32[]{:S(2)}, u32[]{:S(2)}) collective-permute-start(bf16[4,256,256]{2,1,0:T(8,128)(2,1)S(1)} %all-to-all-done.4.refs_4_), channel_id=1, source_target_pairs={{0,130},{2,128},{128,2},{130,0},{1,131},{3,129},{129,3},{131,1},{4... | collective-permute-start | bytes 1572872 | tf_op jit(solution)/shard_map/ppermute | solution.py:77
  190.1 24.3 %collective-permute-start.21 = (bf16[4,256,256]{2,1,0:T(8,128)(2,1)S(1)}, bf16[4,256,256]{2,1,0:T(8,128)(2,1)S(1)}, u32[]{:S(2)}, u32[]{:S(2)}) collective-permute-start(bf16[4,256,256]{2,1,0:T(8,128)(2,1)S(1)} %all-to-all-done.4.refs_4_), channel_id=1, source_target_pairs={{0,2},{2,0},{1,3},{3,1},{4,6},{6,4},{5,7},{7,5},{8,10},{10,8},{9,1... | collective-permute-start | bytes 1572872 | tf_op jit(solution)/shard_map/ppermute | solution.py:77
  190.1 35.1 %copy-start.6 = (bf16[2048,128]{1,0:T(8,128)(2,1)}, bf16[2048,128]{1,0:T(8,128)(2,1)S(1)}, u32[]{:S(2)}) copy-start(bf16[2048,128]{1,0:T(8,128)(2,1)S(1)} %collective-permute-done.17.refs_0_) | copy-start | bytes 1572868
  190.1 25.8 %collective-permute-start.19 = (bf16[2048,128]{1,0:T(8,128)(2,1)S(1)}, bf16[2048,128]{1,0:T(8,128)(2,1)S(1)}, u32[]{:S(2)}, u32[]{:S(2)}) collective-permute-start(bf16[2048,128]{1,0:T(8,128)(2,1)S(1)} %collective-permute-done.17.refs_0_), channel_id=1, source_target_pairs={{0,1},{1,0},{2,3},{3,2},{4,5},{5,4},{6,7},{7,6},{8,9},{9,8},{10,11... | collective-permute-start | bytes 1572872 | tf_op jit(solution)/shard_map/ppermute | solution.py:77
  203.0 22.2 %copy-start.7 = (bf16[2048,128]{1,0:T(8,128)(2,1)}, bf16[2048,128]{1,0:T(8,128)(2,1)S(1)}, u32[]{:S(2)}) copy-start(bf16[2048,128]{1,0:T(8,128)(2,1)S(1)} %collective-permute-done.18.refs_1_) | copy-start | bytes 1572868
  203.0 12.9 %collective-permute-start.20 = (bf16[2048,128]{1,0:T(8,128)(2,1)S(1)}, bf16[2048,128]{1,0:T(8,128)(2,1)S(1)}, u32[]{:S(2)}, u32[]{:S(2)}) collective-permute-start(bf16[2048,128]{1,0:T(8,128)(2,1)S(1)} %collective-permute-done.18.refs_1_), channel_id=1, source_target_pairs={{0,1},{1,0},{2,3},{3,2},{4,5},{5,4},{6,7},{7,6},{8,9},{9,8},{10,11... | collective-permute-start | bytes 1572872 | tf_op jit(solution)/shard_map/ppermute | solution.py:77
  208.2 13.9 %collective-permute-start.25 = (bf16[4,256,256]{2,1,0:T(8,128)(2,1)S(1)}, bf16[4,256,256]{2,1,0:T(8,128)(2,1)S(1)}, u32[]{:S(2)}, u32[]{:S(2)}) collective-permute-start(bf16[4,256,256]{2,1,0:T(8,128)(2,1)S(1)} %all-to-all-done.4.refs_4_), channel_id=1, source_target_pairs={{0,1},{1,0},{2,3},{3,2},{4,5},{5,4},{6,7},{7,6},{8,9},{9,8},{10,11... | collective-permute-start | bytes 1572872 | tf_op jit(solution)/shard_map/ppermute | solution.py:77
  214.3 11.0 %copy-start.4 = (bf16[4,256,256]{2,1,0:T(8,128)(2,1)}, bf16[4,256,256]{2,1,0:T(8,128)(2,1)S(1)}, u32[]{:S(2)}) copy-start(bf16[4,256,256]{2,1,0:T(8,128)(2,1)S(1)} %collective-permute-done.22.refs_6_) | copy-start | bytes 1572868
  214.3 6.5 %collective-permute-start.23 = (bf16[2,256,256]{2,1,0:T(8,128)(2,1)S(1)}, bf16[2,256,256]{2,1,0:T(8,128)(2,1)S(1)}, u32[]{:S(2)}, u32[]{:S(2)}) collective-permute-start(bf16[2,256,256]{2,1,0:T(8,128)(2,1)S(1)} %slice.121), channel_id=1, source_target_pairs={{0,2},{2,0},{1,3},{3,1},{4,6},{6,4},{5,7},{7,5},{8,10},{10,8},{9,1... | collective-permute-start | bytes 786440 | tf_op jit(solution)/shard_map/ppermute | solution.py:77
  214.4 10.8 %copy-start.5 = (bf16[4,256,256]{2,1,0:T(8,128)(2,1)}, bf16[4,256,256]{2,1,0:T(8,128)(2,1)S(1)}, u32[]{:S(2)}) copy-start(bf16[4,256,256]{2,1,0:T(8,128)(2,1)S(1)} %collective-permute-done.21.refs_5_) | copy-start | bytes 1572868
  214.4 7.7 %collective-permute-start.24 = (bf16[2,256,256]{2,1,0:T(8,128)(2,1)S(1)}, bf16[2,256,256]{2,1,0:T(8,128)(2,1)S(1)}, u32[]{:S(2)}, u32[]{:S(2)}) collective-permute-start(bf16[2,256,256]{2,1,0:T(8,128)(2,1)S(1)} %slice.122), channel_id=1, source_target_pairs={{0,130},{2,128},{128,2},{130,0},{1,131},{3,129},{129,3},{131,1},{4... | collective-permute-start | bytes 786440 | tf_op jit(solution)/shard_map/ppermute | solution.py:77
  215.9 9.3 %copy-start.8 = (bf16[2048,128]{1,0:T(8,128)(2,1)}, bf16[2048,128]{1,0:T(8,128)(2,1)S(1)}, u32[]{:S(2)}) copy-start(bf16[2048,128]{1,0:T(8,128)(2,1)S(1)} %collective-permute-done.19.refs_2_) | copy-start | bytes 1572868
  215.9 7.8 %collective-permute-start.26 = (bf16[4,256,256]{2,1,0:T(8,128)(2,1)S(1)}, bf16[4,256,256]{2,1,0:T(8,128)(2,1)S(1)}, u32[]{:S(2)}, u32[]{:S(2)}) collective-permute-start(bf16[4,256,256]{2,1,0:T(8,128)(2,1)S(1)} %collective-permute-done.21.refs_5_), channel_id=1, source_target_pairs={{0,1},{1,0},{2,3},{3,2},{4,5},{5,4},{6,7},{7,6},{8,9},{9,8},{10,11... | collective-permute-start | bytes 1572872 | tf_op jit(solution)/shard_map/ppermute | solution.py:77
  216.0 7.8 %copy-start.9 = (bf16[2048,128]{1,0:T(8,128)(2,1)}, bf16[2048,128]{1,0:T(8,128)(2,1)S(1)}, u32[]{:S(2)}) copy-start(bf16[2048,128]{1,0:T(8,128)(2,1)S(1)} %collective-permute-done.20.refs_3_) | copy-start | bytes 1572868
  216.0 9.2 %collective-permute-start.27 = (bf16[4,256,256]{2,1,0:T(8,128)(2,1)S(1)}, bf16[4,256,256]{2,1,0:T(8,128)(2,1)}, u32[]{:S(2)}, u32[]{:S(2)}) collective-permute-start(bf16[4,256,256]{2,1,0:T(8,128)(2,1)S(1)} %collective-permute-done.22.refs_6_), channel_id=1, source_target_pairs={{0,1},{1,0},{2,3},{3,2},{4,5},{5,4},{6,7},{7,6},{8,9},{9,8},{10,11... | collective-permute-start | bytes 1572872 | tf_op jit(solution)/shard_map/ppermute | solution.py:77
  220.8 1.5 collective-permute-start.28
  222.2 1.5 collective-permute-start.29
  (9 other events, 12.8 us)
Sparse Core Ops, SparseCore 0:
  10.8 93.5 all-gather.1

commit v4 on v3

--- a/solution.py
+++ b/solution.py
@@ -126,7 +126,7 @@
         def block(group, n):
             if n < 3:
                 return group[n][...]
-            return jnp.where(b < 4, group[3][...], group[4][...])
+            return jnp.where(b < 2, group[3][...], group[4][...])
 
         for n, (l, h) in enumerate(spots):
             own = block(mine, n)
@@ -134,27 +134,36 @@
             wq_ref[:, l, h] = own[:, :64]
             wkv_ref[:, l, h, core, :, 0:HD] = own[:, 64:96]
             wkv_ref[:, l, h, core, :, HD : 2 * HD] = own[:, 96:128]
-            wkv_ref[:, l, h, 1 - core, :, 0:HD] = other[:, 64:96]
-            wkv_ref[:, l, h, 1 - core, :, HD : 2 * HD] = other[:, 96:128]
+            wkv_ref[:, l, h, 1 - core, :, 0:HD] = other[:, 0:32]
+            wkv_ref[:, l, h, 1 - core, :, HD : 2 * HD] = other[:, 32:64]
 
         rows = rows_ref[...]
-        member_ref[...] = rows_ref[:, pl.ds(pl.multiple_of(at_ref[3] * HD, HD), HD)]
+        for n in (0, 1):
+            member_ref[:, n * HD : (n + 1) * HD] = rows_ref[
+                :, pl.ds(pl.multiple_of(n * 1024 + at_ref[3] * HD, HD), HD)
+            ]
 
         @pl.when(b == 0)
         def _():
             out_ref[...] = jnp.zeros_like(out_ref)
 
         out_ref[:, 0:HD] += jnp.dot(
-            rows, wq_ref[...].reshape(1024, HD), preferred_element_type=jnp.float32
+            rows, wq_ref[...].reshape(2048, HD), preferred_element_type=jnp.float32
         )
         out_ref[:, HD : 3 * HD] += jnp.dot(
-            rows, wkv_ref[...].reshape(1024, 2 * HD), preferred_element_type=jnp.float32
+            rows, wkv_ref[...].reshape(2048, 2 * HD), preferred_element_type=jnp.float32
         )
 
-    whole = pl.BlockSpec((4, 128, HD), lambda b, at: (b, 0, 0))
-    first = pl.BlockSpec((4, 128, HD), lambda b, at: (jnp.minimum(b, 3), 0, 0))
-    last = pl.BlockSpec((4, 128, HD), lambda b, at: (jnp.maximum(b, 4) - 4, 0, 0))
-    group = [whole, whole, whole, first, last]
+        @pl.when(b == 3)
+        def _():
+            out_ref[...] *= D ** (-0.5)
+
+    def group(rows, at_row):
+        whole = pl.BlockSpec((8, rows, HD), lambda b, at: (b, at_row, 0))
+        first = pl.BlockSpec((8, rows, HD), lambda b, at: (jnp.minimum(b, 1), at_row, 0))
+        last = pl.BlockSpec((8, rows, HD), lambda b, at: (jnp.maximum(b, 2) - 2, at_row, 0))
+        return [whole, whole, whole, first, last]
+
     bf16 = jnp.bfloat16
     return pl.pallas_call(
         body,
@@ -166,13 +175,15 @@
         ),
         grid_spec=pltpu.PrefetchScalarGridSpec(
             num_scalar_prefetch=1,
-            grid=(8,),
-            in_specs=[pl.BlockSpec((512, 1024), lambda b, at: (0, b))] + group + group,
+            grid=(4,),
+            in_specs=[pl.BlockSpec((512, 2048), lambda b, at: (0, b))]
+            + group(128, 0)
+            + group(64, 1),
             out_specs=(
                 pl.BlockSpec((512, 3 * HD), lambda b, at: (0, 0)),
-                pl.BlockSpec((4, 2, 2, 64, HD), lambda b, at: (b, 0, 0, 0, 0)),
-                pl.BlockSpec((4, 2, 2, 2, 32, 2 * HD), lambda b, at: (b, 0, 0, 0, 0, 0)),
-                pl.BlockSpec((512, HD), lambda b, at: (0, b)),
+                pl.BlockSpec((8, 2, 2, 64, HD), lambda b, at: (b, 0, 0, 0, 0)),
+                pl.BlockSpec((8, 2, 2, 2, 32, 2 * HD), lambda b, at: (b, 0, 0, 0, 0, 0)),
+                pl.BlockSpec((512, 2 * HD), lambda b, at: (0, b)),
             ),
         ),
         name="project",
@@ -184,7 +195,7 @@
         q_in, mine, theirs = refs[:4], refs[4:9], refs[9:14]
         q_ref, k_ref, v_ref = refs[14:]
         xl, xh, core = at_ref[0], at_ref[1], at_ref[2]
-        line = pl.program_id(0) % 4
+        line = pl.program_id(0)
         for (h, l), piece in zip(
             ((xh, core), (1 - xh, core), (xh, 1 - core), (1 - xh, 1 - core)), q_in
         ):
@@ -196,15 +207,16 @@
                     piece = group[n][...]
                 else:
                     piece = jnp.where(line < 2, group[3][...], group[4][...])
-                k_ref[h, l, 0, 0, c] = piece[0, :, 0:HD]
-                v_ref[h, l, 0, 0, c] = piece[0, :, HD : 2 * HD]
-
-    quarter = pl.BlockSpec((256, HD), lambda i, at: (i, 0))
-    whole = pl.BlockSpec((1, HD, 2 * HD), lambda i, at: (i % 4, i // 4, 0))
-    first = pl.BlockSpec((1, HD, 2 * HD), lambda i, at: (jnp.minimum(i % 4, 1), i // 4, 0))
-    last = pl.BlockSpec((1, HD, 2 * HD), lambda i, at: (jnp.maximum(i % 4, 2) - 2, i // 4, 0))
+                for z in (0, 1):
+                    k_ref[h, l, z, 0, c] = piece[0, z * HD : (z + 1) * HD, 0:HD]
+                    v_ref[h, l, z, 0, c] = piece[0, z * HD : (z + 1) * HD, HD : 2 * HD]
+
+    quarter = pl.BlockSpec((512, HD), lambda i, at: (i, 0))
+    whole = pl.BlockSpec((1, 2 * HD, 2 * HD), lambda i, at: (i, 0, 0))
+    first = pl.BlockSpec((1, 2 * HD, 2 * HD), lambda i, at: (jnp.minimum(i, 1), 0, 0))
+    last = pl.BlockSpec((1, 2 * HD, 2 * HD), lambda i, at: (jnp.maximum(i, 2) - 2, 0, 0))
     group = [whole, whole, whole, first, last]
-    wide = pl.BlockSpec((2, 2, 1, 1, 2, HD, HD), lambda i, at: (0, 0, i // 4, i % 4, 0, 0, 0))
+    wide = pl.BlockSpec((2, 2, 2, 1, 2, HD, HD), lambda i, at: (0, 0, 0, i, 0, 0, 0))
     bf16 = jnp.bfloat16
     outs = pl.pallas_call(
         body,
@@ -215,10 +227,10 @@
         ),
         grid_spec=pltpu.PrefetchScalarGridSpec(
             num_scalar_prefetch=1,
-            grid=(8,),
+            grid=(4,),
             in_specs=[quarter] * 4 + group + group,
             out_specs=(
-                pl.BlockSpec((2, 2, 256, HD), lambda i, at: (0, 0, i, 0)),
+                pl.BlockSpec((2, 2, 512, HD), lambda i, at: (0, 0, i, 0)),
                 wide,
                 wide,
             ),
@@ -254,7 +266,6 @@
     pieces = (cut,) + ring_pieces(cut)
     others = tuple(flip(p, ("core",)) for p in pieces)
     projected, q_cols, wkv, normed_m = project(normed, pieces, others, at)
-    projected = projected * inv_width
     q_cols = q_cols.reshape(D, HD)
 
     cosine_table, sine_table = angles(seg_row)
@@ -308,13 +319,13 @@
     near_other = flip(near, ("core",))
     far_other = flip(far, ("core",))
     kv_sum = exchange(scaled_kv.reshape(8, 64, 2 * HD), MEM)
-    kv_sum = kv_sum.astype(f32)
-    kv_sum = jnp.sum(kv_sum, axis=0).astype(bf16)
+    kv_sum = jnp.sum(kv_sum.astype(f32), axis=0).astype(bf16)
     kv_sum = spread(kv_sum, MEM).reshape(block_len, 2 * HD)
     part_kv = lax.dot_general(
         normed_m, kv_sum, contract, preferred_element_type=f32
     ).astype(bf16)
-    part_kv = exchange(part_kv.reshape(4, 256, 2 * HD), X).astype(f32)
+    part_kv = exchange(part_kv.reshape(4, 256, 2 * HD), X)
+    part_kv = part_kv.astype(f32)
     old_kv = wkv.reshape(4, 2, 8, 128, 2 * HD)
     old_kv = lax.dynamic_index_in_dim(old_kv, ring, 0, keepdims=False)
     old_kv = lax.dynamic_index_in_dim(old_kv, member, 1, keepdims=False).reshape(256, 2 * HD)

time: 244 us -> 241 us (0.988)
  Pallas kernels: 25.3 us -> 22.2 us
where the time goes in v4:
time: 241 us; the launch traced here: 238 us
  starting transfers between devices  68.1 us (28%)
  waiting for transfers between devices  63 us (26%)
  blocking collectives  36 us (15%)
  Pallas kernels  22.2 us (9%)
  other arithmetic  15.2 us (6%)
  between operations  14.4 us (6%)
  matrix products  11.5 us (5%)
  local copies, waits for them, and re-layouts  8.04 us (3%)
    ppermute x24, waiting for transfers between devices, flip(): return lax.ppermute(x, axes, [(i, n - 1 - i) for i in range(n)])  48.3 us
    ppermute x24, starting transfers between devices, flip(): return lax.ppermute(x, axes, [(i, n - 1 - i) for i in range(n)])  44.9 us
    all_to_all x1, blocking collectives, exchange(): return lax.all_to_all(x, axes, split_axis=0, concat_axis=0, tiled=True)  36 us
    all_to_all x4, starting transfers between devices, exchange(): return lax.all_to_all(x, axes, split_axis=0, concat_axis=0, tiled=True)  17.4 us
    pallas_call x1, Pallas kernels, project(): pl.pallas_call(body, out_shape=(jax.ShapeDtypeStruct((512, 3 * HD), jnp.f...  12.5 us
    all_to_all x4, waiting for transfers between devices, exchange(): return lax.all_to_all(x, axes, split_axis=0, concat_axis=0, tiled=True)  11.2 us
    pallas_call x1, Pallas kernels, unpack(): pl.pallas_call(body, out_shape=(jax.ShapeDtypeStruct((2, 2, 2048, HD), bf...  6.67 us
    dot_general x1, matrix products, local(): lax.dot_general(normed, scaled_q, contract, preferred_element_type=f32)  5.87 us
  transfers between devices with their start and end apart: 35, of which 19 were waited for; matrix products, arithmetic and copies ran while one was open for 9% of the time, Pallas kernels for 7%

profile of v4, /device:TPU:8, one launch (start us, length us, event | category | flops | bytes accessed | tf_op | source)
XLA Modules:
  0.0 238.4 jit_solution(2018530760347974546)
XLA Ops:
  7.2 1.1 fusion.31
  8.3 1.0 fusion.32
  11.3 3.1 %pack_columns.1 = bf16[32,128,128]{2,1,0:T(8,128)(2,1)} custom-call(s32[4]{0:T(128)} %pad_add_fusion.at_ref, bf16[128,8192]{1,0:T(8,128)(2,1)} %q_ref.1, bf16[128,1024]{1,0:T(8,128)(2,1)} %k_ref.1, bf16[128,1024]{1,0:T(8,128)(2,1)} %v_ref.1), custom_call_target="tpu_custom_call" | custom-call | tf_op jit(solution)/shard_map/pack_columns/pallas_call | solution.py:105
  14.4 36.0 %all_to_all.25.refs_0_ = bf16[32,128,128]{2,1,0:T(8,128)(2,1)S(1)} all-to-all(bf16[32,128,128]{2,1,0:T(8,128)(2,1)} %pack_columns.1), channel_id=1, replica_groups=mesh['xh'=2,'y'=4,'zh'=2,'zl'=4,'xl'=2,'core'=2] {'y','zh','zl'}, dimensions={0} | all-to-all | bytes 2097152 | tf_op jit(solution)/shard_map/all_to_all | solution.py:81
  50.4 8.1 %collective-permute-start.2 = (bf16[32,128,128]{2,1,0:T(8,128)(2,1)S(1)}, bf16[32,128,128]{2,1,0:T(8,128)(2,1)S(1)}, u32[]{:S(2)}, u32[]{:S(2)}) collective-permute-start(bf16[32,128,128]{2,1,0:T(8,128)(2,1)S(1)} %all_to_all.25.refs_0_), channel_id=1, source_target_pairs={{0,130},{2,128},{128,2},{130,0},{1,131},{3,129},{129,3},{131,1},{4... | collective-permute-start | bytes 3145736 | tf_op jit(solution)/shard_map/ppermute | solution.py:77
  58.5 22.5 %collective-permute-done.2.refs_2_ = bf16[32,128,128]{2,1,0:T(8,128)(2,1)S(1)} collective-permute-done((bf16[32,128,128]{2,1,0:T(8,128)(2,1)S(1)}, bf16[32,128,128]{2,1,0:T(8,128)(2,1)S(1)}, u32[]{:S(2)}, u32[]{:S(2)}) %collective-permute-start.2) | collective-permute-done | bytes 1048608 | tf_op jit(solution)/shard_map/ppermute | solution.py:77
  81.8 1.8 collective-permute-start.3
  84.0 0.9 slice.110
  84.9 1.6 collective-permute-start.4
  87.8 4.1 %collective-permute-start.5 = (bf16[32,128,128]{2,1,0:T(8,128)(2,1)S(1)}, bf16[32,128,128]{2,1,0:T(8,128)(2,1)}, u32[]{:S(2)}, u32[]{:S(2)}) collective-permute-start(bf16[32,128,128]{2,1,0:T(8,128)(2,1)S(1)} %all_to_all.25.refs_0_), channel_id=1, source_target_pairs={{0,1},{1,0},{2,3},{3,2},{4,5},{5,4},{6,7},{7,6},{8,9},{9,8},{10,11... | collective-permute-start | bytes 3145736 | tf_op jit(solution)/shard_map/ppermute | solution.py:77
  91.9 4.5 %collective-permute-start.6 = (bf16[32,128,128]{2,1,0:T(8,128)(2,1)S(1)}, bf16[32,128,128]{2,1,0:T(8,128)(2,1)}, u32[]{:S(2)}, u32[]{:S(2)}) collective-permute-start(bf16[32,128,128]{2,1,0:T(8,128)(2,1)S(1)} %collective-permute-done.1.refs_1_), channel_id=1, source_target_pairs={{0,1},{1,0},{2,3},{3,2},{4,5},{5,4},{6,7},{7,6},{8,9},{9,8},{10,11... | collective-permute-start | bytes 3145736 | tf_op jit(solution)/shard_map/ppermute | solution.py:77
  97.1 3.5 %collective-permute-done.4.refs_4_ = bf16[16,128,128]{2,1,0:T(8,128)(2,1)} collective-permute-done((bf16[16,128,128]{2,1,0:T(8,128)(2,1)}, bf16[16,128,128]{2,1,0:T(8,128)(2,1)}, u32[]{:S(2)}, u32[]{:S(2)}) %collective-permute-start.4) | collective-permute-done | bytes 524320 | tf_op jit(solution)/shard_map/ppermute | solution.py:77
  104.3 12.5 %project.1 = (f32[512,384]{1,0:T(8,128)}, bf16[32,2,2,64,128]{4,3,2,1,0:T(8,128)(2,1)}, bf16[32,2,2,2,32,256]{5,4,3,2,1,0:T(8,128)(2,1)}, bf16[512,1024]{1,0:T(8,128)(2,1)}) custom-call(s32[4]{0:T(128)} %pad_add_fusion.at_ref, bf16[512,8192]{1,0:T(8,128)(2,1)} %all-gather.2.cloned.1.call-done.rows_ref, bf16[32,128,128]{2,1,0:T(8,128)(2,1)} %copy-done, ...), custom_call_target="tpu_custom_call" | custom-call | tf_op jit(solution)/shard_map/project/pallas_call | solution.py:168
  116.8 2.4 %fusion.38 = (bf16[512,64]{1,0:T(8,128)(2,1)S(1)}, bf16[512,64]{1,0:T(8,128)(2,1)S(1)}, bf16[512,64]{1,0:T(8,128)(2,1)S(1)}, bf16[512,64]{1,0:T(8,128)(2,1)S(1)}) fusion(f32[512,384]{1,0:T(8,128)} %get-tuple-element.11, f32[64]{0:T(128)S(1)} %multiply_power_fusion, f32[512]{0:T(512)S(1)} %subtract_convert_fusion), kind=kLoop, calls=%fused_computation.59 | loop fusion | flops 557056 | bytes 788736 | tf_op jit(solution)/shard_map/convert.9
  120.0 1.4 multiply_reduce_fusion
  122.5 1.3 fusion.35
  124.3 0.9 fusion.9
  125.2 5.9 %all-to-all-start.1 = ((bf16[8,64,256]{2,1,0:T(8,128)(2,1)}), bf16[8,64,256]{2,1,0:T(8,128)(2,1)S(1)}, u32[]{:S(2)}, u32[]{:S(2)}) async-start(bf16[8,64,256]{2,1,0:T(8,128)(2,1)} %fusion.9), calls=%async_computation.1 | async-start | bytes 524288 | tf_op jit(solution)/shard_map/all_to_all | solution.py:81
  131.0 5.9 %convolution_convert_fusion = bf16[8192,128]{1,0:T(8,128)(2,1)S(1)} fusion(bf16[512,8192]{1,0:T(8,128)(2,1)} %all-gather.2.cloned.1.call-done.rows_ref, f32[512,64]{1,0:T(8,128)S(1)} %get-tuple-element.31, f32[512,64]{1,0:T(8,128)S(1)} %get-tuple-element.32), kind=kOutput, calls=%fused_computation | convolution fusion | flops 1074987008 | bytes 10747904 | tf_op jit(solution)/shard_map/dot_general | solution.py:288
  139.2 1.6 all-to-all-done.1
  141.5 3.5 %all-to-all-start.2 = ((bf16[8,64,256]{2,1,0:T(8,128)(2,1)}), bf16[8,64,256]{2,1,0:T(8,128)(2,1)S(1)}, u32[]{:S(2)}, u32[]{:S(2)}) async-start(bf16[8,64,256]{2,1,0:T(8,128)(2,1)} %broadcast_in_dim.8), calls=%async_computation.2 | async-start | bytes 524288 | tf_op jit(solution)/shard_map/all_to_all | solution.py:81
  145.0 2.8 %collective-permute-done.13 = bf16[1024,128]{1,0:T(8,128)(2,1)S(1)} collective-permute-done((bf16[1024,128]{1,0:T(8,128)(2,1)}, bf16[1024,128]{1,0:T(8,128)(2,1)S(1)}, u32[]{:S(2)}, u32[]{:S(2)}) %collective-permute-start.13) | collective-permute-done | bytes 262176 | tf_op jit(solution)/shard_map/ppermute | solution.py:77
  147.8 1.8 fusion.11
  149.6 5.1 %all-to-all-done.2 = bf16[8,64,256]{2,1,0:T(8,128)(2,1)S(1)} async-done(((bf16[8,64,256]{2,1,0:T(8,128)(2,1)}), bf16[8,64,256]{2,1,0:T(8,128)(2,1)S(1)}, u32[]{:S(2)}, u32[]{:S(2)}) %all-to-all-start.2) | async-done | bytes 262176 | tf_op jit(solution)/shard_map/all_to_all | solution.py:81
  154.8 2.5 %convolution_convert_fusion.1 = bf16[1024,256]{1,0:T(8,128)(2,1)} fusion(bf16[512,1024]{1,0:T(8,128)(2,1)} %get-tuple-element.13, bf16[512,256]{1,0:T(8,128)(2,1)S(1)} %bitcast.57), kind=kOutput, calls=%fused_computation.2 | convolution fusion | flops 268697600 | bytes 1835008 | tf_op jit(solution)/shard_map/dot_general | solution.py:324
  157.3 4.5 %all-to-all-start.3 = ((bf16[4,256,256]{2,1,0:T(8,128)(2,1)}), bf16[4,256,256]{2,1,0:T(8,128)(2,1)S(1)}, u32[]{:S(2)}, u32[]{:S(2)}) async-start(bf16[4,256,256]{2,1,0:T(8,128)(2,1)} %bitcast.56), calls=%async_computation.3 | async-start | bytes 1048576 | tf_op jit(solution)/shard_map/all_to_all | solution.py:81
  161.8 1.8 pad_maximum_fusion
  163.6 2.0 collective-permute-start.14
  166.4 2.1 collective-permute-start.16
  168.5 0.9 constant_dynamic-slice_fusion
  169.4 3.3 %all-to-all-done.3 = bf16[4,256,256]{2,1,0:T(8,128)(2,1)S(1)} async-done(((bf16[4,256,256]{2,1,0:T(8,128)(2,1)}), bf16[4,256,256]{2,1,0:T(8,128)(2,1)S(1)}, u32[]{:S(2)}, u32[]{:S(2)}) %all-to-all-start.3) | async-done | bytes 524320 | tf_op jit(solution)/shard_map/all_to_all | solution.py:81
  173.6 3.5 %all-to-all-start.4 = ((bf16[4,256,256]{2,1,0:T(8,128)(2,1)}), bf16[4,256,256]{2,1,0:T(8,128)(2,1)S(1)}, u32[]{:S(2)}, u32[]{:S(2)}) async-start(bf16[4,256,256]{2,1,0:T(8,128)(2,1)} %broadcast_in_dim.9), calls=%async_computation.4 | async-start | bytes 1048576 | tf_op jit(solution)/shard_map/all_to_all | solution.py:81
  177.1 3.6 %collective-permute-done.14 = bf16[2048,128]{1,0:T(8,128)(2,1)} collective-permute-done((bf16[2048,128]{1,0:T(8,128)(2,1)}, bf16[2048,128]{1,0:T(8,128)(2,1)}, u32[]{:S(2)}, u32[]{:S(2)}) %collective-permute-start.14) | collective-permute-done | bytes 524320 | tf_op jit(solution)/shard_map/ppermute | solution.py:77
  180.7 1.4 collective-permute-done.16
  182.1 2.3 fusion.3
  184.4 1.7 collective-permute-start.17
  186.1 1.3 collective-permute-start.18
  187.4 1.2 all-to-all-done.4.refs_4_
  188.6 1.2 collective-permute-start.22
  189.8 10.2 %collective-permute-start.19 = (bf16[2048,128]{1,0:T(8,128)(2,1)S(1)}, bf16[2048,128]{1,0:T(8,128)(2,1)S(1)}, u32[]{:S(2)}, u32[]{:S(2)}) collective-permute-start(bf16[2048,128]{1,0:T(8,128)(2,1)S(1)} %collective-permute-done.17.refs_0_), channel_id=1, source_target_pairs={{0,1},{1,0},{2,3},{3,2},{4,5},{5,4},{6,7},{7,6},{8,9},{9,8},{10,11... | collective-permute-start | bytes 1572872 | tf_op jit(solution)/shard_map/ppermute | solution.py:77
  200.0 2.6 %collective-permute-done.18.refs_1_ = bf16[2048,128]{1,0:T(8,128)(2,1)S(1)} collective-permute-done((bf16[2048,128]{1,0:T(8,128)(2,1)}, bf16[2048,128]{1,0:T(8,128)(2,1)S(1)}, u32[]{:S(2)}, u32[]{:S(2)}) %collective-permute-start.18) | collective-permute-done | bytes 524320 | tf_op jit(solution)/shard_map/ppermute | solution.py:309
  202.6 5.2 %collective-permute-start.20 = (bf16[2048,128]{1,0:T(8,128)(2,1)S(1)}, bf16[2048,128]{1,0:T(8,128)(2,1)S(1)}, u32[]{:S(2)}, u32[]{:S(2)}) collective-permute-start(bf16[2048,128]{1,0:T(8,128)(2,1)S(1)} %collective-permute-done.18.refs_1_), channel_id=1, source_target_pairs={{0,1},{1,0},{2,3},{3,2},{4,5},{5,4},{6,7},{7,6},{8,9},{9,8},{10,11... | collective-permute-start | bytes 1572872 | tf_op jit(solution)/shard_map/ppermute | solution.py:77
  207.9 6.0 %collective-permute-done.22.refs_6_ = bf16[4,256,256]{2,1,0:T(8,128)(2,1)S(1)} collective-permute-done((bf16[4,256,256]{2,1,0:T(8,128)(2,1)S(1)}, bf16[4,256,256]{2,1,0:T(8,128)(2,1)S(1)}, u32[]{:S(2)}, u32[]{:S(2)}) %collective-permute-start.22) | collective-permute-done | bytes 524320 | tf_op jit(solution)/shard_map/ppermute | solution.py:77
  214.1 1.5 collective-permute-start.24
  216.1 4.3 %collective-permute-done.23.refs_7_ = bf16[2,256,256]{2,1,0:T(8,128)(2,1)S(1)} collective-permute-done((bf16[2,256,256]{2,1,0:T(8,128)(2,1)S(1)}, bf16[2,256,256]{2,1,0:T(8,128)(2,1)S(1)}, u32[]{:S(2)}, u32[]{:S(2)}) %collective-permute-start.23) | collective-permute-done | bytes 262176 | tf_op jit(solution)/shard_map/ppermute | solution.py:77
  220.4 1.4 collective-permute-done.24.refs_8_
  221.9 1.4 collective-permute-done.29.refs_13_
  224.9 6.7 %unpack.1 = (bf16[2,2,2048,128]{3,2,1,0:T(8,128)(2,1)}, bf16[2,2,2,4,2,128,128]{6,5,4,3,2,1,0:T(8,128)(2,1)}, bf16[2,2,2,4,2,128,128]{6,5,4,3,2,1,0:T(8,128)(2,1)}) custom-call(s32[4]{0:T(128)} %pad_add_fusion.at_ref, bf16[2048,128]{1,0:T(8,128)(2,1)} %copy-done.6, bf16[2048,128]{1,0:T(8,128)(2,1)} %copy-done.7, bf16[2048,128]{1,0:T(8,128)(2,1)} %copy-done.8, ...), custom_call_target="tpu_custom_call" | custom-call | tf_op jit(solution)/shard_map/unpack/pallas_call | solution.py:221
  (109 shorter events, 18.5 us)
Async XLA Ops:
  7.2 97.2 %all-gather.2.cloned.1.call-start = ((), (), s32[]{:S(2)}) async-start(), calls=%async_computation.5 | async-start | bytes 8519680 | tf_op jit(solution)/shard_map/all_gather | solution.py:258
  9.3 0.7 collective-permute-start
  14.4 72.0 %copy-start.20 = (s32[1,512]{1,0:T(1,128)S(1)}, s32[1,512]{1,0:T(1,128)}, u32[]{:S(2)}) copy-start(s32[1,512]{1,0:T(1,128)} %param.9) | copy-start | bytes 6148
  14.4 72.7 %copy-start.21 = (f32[1,8]{1,0:T(1,128)S(1)}, f32[1,8]{1,0:T(1,128)}, u32[]{:S(2)}) copy-start(f32[1,8]{1,0:T(1,128)} %param.10) | copy-start | bytes 100
  14.4 86.5 %copy-start.19 = (bf16[1,512,128]{2,1,0:T(8,128)(2,1)S(1)}, bf16[1,512,128]{2,1,0:T(8,128)(2,1)}, u32[]{:S(2)}) copy-start(bf16[1,512,128]{2,1,0:T(8,128)(2,1)} %param.8) | copy-start | bytes 393220
  50.4 54.0 %copy-start = (bf16[32,128,128]{2,1,0:T(8,128)(2,1)}, bf16[32,128,128]{2,1,0:T(8,128)(2,1)S(1)}, u32[]{:S(2)}) copy-start(bf16[32,128,128]{2,1,0:T(8,128)(2,1)S(1)} %all_to_all.25.refs_0_) | copy-start | bytes 3145732
  50.4 30.6 %collective-permute-start.2 = (bf16[32,128,128]{2,1,0:T(8,128)(2,1)S(1)}, bf16[32,128,128]{2,1,0:T(8,128)(2,1)S(1)}, u32[]{:S(2)}, u32[]{:S(2)}) collective-permute-start(bf16[32,128,128]{2,1,0:T(8,128)(2,1)S(1)} %all_to_all.25.refs_0_), channel_id=1, source_target_pairs={{0,130},{2,128},{128,2},{130,0},{1,131},{3,129},{129,3},{131,1},{4... | collective-permute-start | bytes 3145736 | tf_op jit(solution)/shard_map/ppermute | solution.py:77
  58.5 25.5 %collective-permute-start.1 = (bf16[32,128,128]{2,1,0:T(8,128)(2,1)S(1)}, bf16[32,128,128]{2,1,0:T(8,128)(2,1)S(1)}, u32[]{:S(2)}, u32[]{:S(2)}) collective-permute-start(bf16[32,128,128]{2,1,0:T(8,128)(2,1)S(1)} %all_to_all.25.refs_0_), channel_id=1, source_target_pairs={{0,2},{2,0},{1,3},{3,1},{4,6},{6,4},{5,7},{7,5},{8,10},{10,8},{9,1... | collective-permute-start | bytes 3145736 | tf_op jit(solution)/shard_map/ppermute | solution.py:77
  80.9 23.4 %copy-start.1 = (bf16[32,128,128]{2,1,0:T(8,128)(2,1)}, bf16[32,128,128]{2,1,0:T(8,128)(2,1)S(1)}, u32[]{:S(2)}) copy-start(bf16[32,128,128]{2,1,0:T(8,128)(2,1)S(1)} %collective-permute-done.2.refs_2_) | copy-start | bytes 3145732
  81.8 14.7 %collective-permute-start.3 = (bf16[16,128,128]{2,1,0:T(8,128)(2,1)}, bf16[16,128,128]{2,1,0:T(8,128)(2,1)}, u32[]{:S(2)}, u32[]{:S(2)}) collective-permute-start(bf16[16,128,128]{2,1,0:T(8,128)(2,1)} %slice.109), channel_id=1, source_target_pairs={{0,2},{2,0},{1,3},{3,1},{4,6},{6,4},{5,7},{7,5},{8,10},{10,8},{9,1... | collective-permute-start | bytes 1572872 | tf_op jit(solution)/shard_map/ppermute | solution.py:77
  84.0 20.4 %copy-start.2 = (bf16[32,128,128]{2,1,0:T(8,128)(2,1)}, bf16[32,128,128]{2,1,0:T(8,128)(2,1)S(1)}, u32[]{:S(2)}) copy-start(bf16[32,128,128]{2,1,0:T(8,128)(2,1)S(1)} %collective-permute-done.1.refs_1_) | copy-start | bytes 3145732
  84.9 15.7 %collective-permute-start.4 = (bf16[16,128,128]{2,1,0:T(8,128)(2,1)}, bf16[16,128,128]{2,1,0:T(8,128)(2,1)}, u32[]{:S(2)}, u32[]{:S(2)}) collective-permute-start(bf16[16,128,128]{2,1,0:T(8,128)(2,1)} %slice.110), channel_id=1, source_target_pairs={{0,130},{2,128},{128,2},{130,0},{1,131},{3,129},{129,3},{131,1},{4... | collective-permute-start | bytes 1572872 | tf_op jit(solution)/shard_map/ppermute | solution.py:77
  86.4 9.9 %collective-permute-start.10 = (s32[512]{0:T(512)S(1)}, s32[512]{0:T(512)S(1)}, u32[]{:S(2)}, u32[]{:S(2)}) collective-permute-start(s32[512]{0:T(512)S(1)} %bitcast.65), channel_id=1, source_target_pairs={{0,0},{1,2},{2,1},{3,3},{4,4},{5,6},{6,5},{7,7},{8,8},{9,10},{10,9... | collective-permute-start | bytes 6152 | tf_op jit(solution)/shard_map/ppermute | solution.py:72
  87.1 4.8 %collective-permute-start.12 = (f32[8]{0:T(128)S(1)}, f32[8]{0:T(128)S(1)}, u32[]{:S(2)}, u32[]{:S(2)}) collective-permute-start(f32[8]{0:T(128)S(1)} %bitcast.66), channel_id=1, source_target_pairs={{0,0},{1,2},{2,1},{3,3},{4,4},{5,6},{6,5},{7,7},{8,8},{9,10},{10,9... | collective-permute-start | bytes 104 | tf_op jit(solution)/shard_map/ppermute | solution.py:72
  87.8 13.1 %collective-permute-start.5 = (bf16[32,128,128]{2,1,0:T(8,128)(2,1)S(1)}, bf16[32,128,128]{2,1,0:T(8,128)(2,1)}, u32[]{:S(2)}, u32[]{:S(2)}) collective-permute-start(bf16[32,128,128]{2,1,0:T(8,128)(2,1)S(1)} %all_to_all.25.refs_0_), channel_id=1, source_target_pairs={{0,1},{1,0},{2,3},{3,2},{4,5},{5,4},{6,7},{7,6},{8,9},{9,8},{10,11... | collective-permute-start | bytes 3145736 | tf_op jit(solution)/shard_map/ppermute | solution.py:77
  91.9 10.8 %collective-permute-start.6 = (bf16[32,128,128]{2,1,0:T(8,128)(2,1)S(1)}, bf16[32,128,128]{2,1,0:T(8,128)(2,1)}, u32[]{:S(2)}, u32[]{:S(2)}) collective-permute-start(bf16[32,128,128]{2,1,0:T(8,128)(2,1)S(1)} %collective-permute-done.1.refs_1_), channel_id=1, source_target_pairs={{0,1},{1,0},{2,3},{3,2},{4,5},{5,4},{6,7},{7,6},{8,9},{9,8},{10,11... | collective-permute-start | bytes 3145736 | tf_op jit(solution)/shard_map/ppermute | solution.py:77
  96.4 7.1 %collective-permute-start.7 = (bf16[32,128,128]{2,1,0:T(8,128)(2,1)S(1)}, bf16[32,128,128]{2,1,0:T(8,128)(2,1)}, u32[]{:S(2)}, u32[]{:S(2)}) collective-permute-start(bf16[32,128,128]{2,1,0:T(8,128)(2,1)S(1)} %collective-permute-done.2.refs_2_), channel_id=1, source_target_pairs={{0,1},{1,0},{2,3},{3,2},{4,5},{5,4},{6,7},{7,6},{8,9},{9,8},{10,11... | collective-permute-start | bytes 3145736 | tf_op jit(solution)/shard_map/ppermute | solution.py:77
  96.5 5.3 %collective-permute-start.8 = (bf16[16,128,128]{2,1,0:T(8,128)(2,1)}, bf16[16,128,128]{2,1,0:T(8,128)(2,1)S(1)}, u32[]{:S(2)}, u32[]{:S(2)}) collective-permute-start(bf16[16,128,128]{2,1,0:T(8,128)(2,1)} %collective-permute-done.3.refs_3_), channel_id=1, source_target_pairs={{0,1},{1,0},{2,3},{3,2},{4,5},{5,4},{6,7},{7,6},{8,9},{9,8},{10,11... | collective-permute-start | bytes 1572872 | tf_op jit(solution)/shard_map/ppermute | solution.py:77
  100.6 2.1 collective-permute-start.9
  100.9 19.1 %collective-permute-start.11 = (bf16[512,128]{1,0:T(8,128)(2,1)S(1)}, bf16[512,128]{1,0:T(8,128)(2,1)S(1)}, u32[]{:S(2)}, u32[]{:S(2)}) collective-permute-start(bf16[512,128]{1,0:T(8,128)(2,1)S(1)} %bitcast.64), channel_id=1, source_target_pairs={{0,0},{1,2},{2,1},{3,3},{4,4},{5,6},{6,5},{7,7},{8,8},{9,10},{10,9... | collective-permute-start | bytes 393224 | tf_op jit(solution)/shard_map/ppermute | solution.py:72
  125.2 15.6 %all-to-all-start.1 = ((bf16[8,64,256]{2,1,0:T(8,128)(2,1)}), bf16[8,64,256]{2,1,0:T(8,128)(2,1)S(1)}, u32[]{:S(2)}, u32[]{:S(2)}) async-start(bf16[8,64,256]{2,1,0:T(8,128)(2,1)} %fusion.9), calls=%async_computation.1 | async-start | bytes 524288 | tf_op jit(solution)/shard_map/all_to_all | solution.py:81
  137.7 10.1 %collective-permute-start.13 = (bf16[1024,128]{1,0:T(8,128)(2,1)}, bf16[1024,128]{1,0:T(8,128)(2,1)S(1)}, u32[]{:S(2)}, u32[]{:S(2)}) collective-permute-start(bf16[1024,128]{1,0:T(8,128)(2,1)} %get-tuple-element.19), channel_id=1, source_target_pairs={{0,130},{2,128},{128,2},{130,0},{1,131},{3,129},{129,3},{131,1},{4... | collective-permute-start | bytes 786440 | tf_op jit(solution)/shard_map/ppermute | solution.py:77
  138.6 9.3 %collective-permute-start.15 = (bf16[1024,128]{1,0:T(8,128)(2,1)S(1)}, bf16[1024,128]{1,0:T(8,128)(2,1)}, u32[]{:S(2)}, u32[]{:S(2)}) collective-permute-start(bf16[1024,128]{1,0:T(8,128)(2,1)S(1)} %get-tuple-element.21), channel_id=1, source_target_pairs={{0,2},{2,0},{1,3},{3,1},{4,6},{6,4},{5,7},{7,5},{8,10},{10,8},{9,1... | collective-permute-start | bytes 786440 | tf_op jit(solution)/shard_map/ppermute | solution.py:77
  141.5 13.3 %all-to-all-start.2 = ((bf16[8,64,256]{2,1,0:T(8,128)(2,1)}), bf16[8,64,256]{2,1,0:T(8,128)(2,1)S(1)}, u32[]{:S(2)}, u32[]{:S(2)}) async-start(bf16[8,64,256]{2,1,0:T(8,128)(2,1)} %broadcast_in_dim.8), calls=%async_computation.2 | async-start | bytes 524288 | tf_op jit(solution)/shard_map/all_to_all | solution.py:81
  157.3 15.4 %all-to-all-start.3 = ((bf16[4,256,256]{2,1,0:T(8,128)(2,1)}), bf16[4,256,256]{2,1,0:T(8,128)(2,1)S(1)}, u32[]{:S(2)}, u32[]{:S(2)}) async-start(bf16[4,256,256]{2,1,0:T(8,128)(2,1)} %bitcast.56), calls=%async_computation.3 | async-start | bytes 1048576 | tf_op jit(solution)/shard_map/all_to_all | solution.py:81
  163.6 17.2 %collective-permute-start.14 = (bf16[2048,128]{1,0:T(8,128)(2,1)}, bf16[2048,128]{1,0:T(8,128)(2,1)}, u32[]{:S(2)}, u32[]{:S(2)}) collective-permute-start(bf16[2048,128]{1,0:T(8,128)(2,1)} %pad_maximum_fusion), channel_id=1, source_target_pairs={{0,2},{2,0},{1,3},{3,1},{4,6},{6,4},{5,7},{7,5},{8,10},{10,8},{9,1... | collective-permute-start | bytes 1572872 | tf_op jit(solution)/shard_map/ppermute | solution.py:77
  166.4 15.7 %collective-permute-start.16 = (bf16[2048,128]{1,0:T(8,128)(2,1)}, bf16[2048,128]{1,0:T(8,128)(2,1)S(1)}, u32[]{:S(2)}, u32[]{:S(2)}) collective-permute-start(bf16[2048,128]{1,0:T(8,128)(2,1)} %pad_maximum_fusion.1), channel_id=1, source_target_pairs={{0,130},{2,128},{128,2},{130,0},{1,131},{3,129},{129,3},{131,1},{4... | collective-permute-start | bytes 1572872 | tf_op jit(solution)/shard_map/ppermute | solution.py:77
  173.6 15.0 %all-to-all-start.4 = ((bf16[4,256,256]{2,1,0:T(8,128)(2,1)}), bf16[4,256,256]{2,1,0:T(8,128)(2,1)S(1)}, u32[]{:S(2)}, u32[]{:S(2)}) async-start(bf16[4,256,256]{2,1,0:T(8,128)(2,1)} %broadcast_in_dim.9), calls=%async_computation.4 | async-start | bytes 1048576 | tf_op jit(solution)/shard_map/all_to_all | solution.py:81
  184.4 5.4 %collective-permute-start.17 = (bf16[2048,128]{1,0:T(8,128)(2,1)}, bf16[2048,128]{1,0:T(8,128)(2,1)S(1)}, u32[]{:S(2)}, u32[]{:S(2)}) collective-permute-start(bf16[2048,128]{1,0:T(8,128)(2,1)} %fusion.3), channel_id=1, source_target_pairs={{0,0},{1,2},{2,1},{3,3},{4,4},{5,6},{6,5},{7,7},{8,8},{9,10},{10,9... | collective-permute-start | bytes 1572872 | tf_op jit(solution)/shard_map/ppermute | solution.py:72
  186.1 16.5 %collective-permute-start.18 = (bf16[2048,128]{1,0:T(8,128)(2,1)}, bf16[2048,128]{1,0:T(8,128)(2,1)S(1)}, u32[]{:S(2)}, u32[]{:S(2)}) collective-permute-start(bf16[2048,128]{1,0:T(8,128)(2,1)} %fusion.3), channel_id=1, source_target_pairs={{0,128},{1,130},{2,129},{3,131},{128,0},{129,2},{130,1},{131,3},{4... | collective-permute-start | bytes 1572872 | tf_op jit(solution)/shard_map/ppermute | solution.py:309
  188.6 36.2 %copy-start.3 = (bf16[4,256,256]{2,1,0:T(8,128)(2,1)}, bf16[4,256,256]{2,1,0:T(8,128)(2,1)S(1)}, u32[]{:S(2)}) copy-start(bf16[4,256,256]{2,1,0:T(8,128)(2,1)S(1)} %all-to-all-done.4.refs_4_) | copy-start | bytes 1572868
  188.6 25.3 %collective-permute-start.22 = (bf16[4,256,256]{2,1,0:T(8,128)(2,1)S(1)}, bf16[4,256,256]{2,1,0:T(8,128)(2,1)S(1)}, u32[]{:S(2)}, u32[]{:S(2)}) collective-permute-start(bf16[4,256,256]{2,1,0:T(8,128)(2,1)S(1)} %all-to-all-done.4.refs_4_), channel_id=1, source_target_pairs={{0,130},{2,128},{128,2},{130,0},{1,131},{3,129},{129,3},{131,1},{4... | collective-permute-start | bytes 1572872 | tf_op jit(solution)/shard_map/ppermute | solution.py:77
  189.8 24.2 %collective-permute-start.21 = (bf16[4,256,256]{2,1,0:T(8,128)(2,1)S(1)}, bf16[4,256,256]{2,1,0:T(8,128)(2,1)S(1)}, u32[]{:S(2)}, u32[]{:S(2)}) collective-permute-start(bf16[4,256,256]{2,1,0:T(8,128)(2,1)S(1)} %all-to-all-done.4.refs_4_), channel_id=1, source_target_pairs={{0,2},{2,0},{1,3},{3,1},{4,6},{6,4},{5,7},{7,5},{8,10},{10,8},{9,1... | collective-permute-start | bytes 1572872 | tf_op jit(solution)/shard_map/ppermute | solution.py:77
  189.8 35.1 %copy-start.6 = (bf16[2048,128]{1,0:T(8,128)(2,1)}, bf16[2048,128]{1,0:T(8,128)(2,1)S(1)}, u32[]{:S(2)}) copy-start(bf16[2048,128]{1,0:T(8,128)(2,1)S(1)} %collective-permute-done.17.refs_0_) | copy-start | bytes 1572868
  189.8 25.8 %collective-permute-start.19 = (bf16[2048,128]{1,0:T(8,128)(2,1)S(1)}, bf16[2048,128]{1,0:T(8,128)(2,1)S(1)}, u32[]{:S(2)}, u32[]{:S(2)}) collective-permute-start(bf16[2048,128]{1,0:T(8,128)(2,1)S(1)} %collective-permute-done.17.refs_0_), channel_id=1, source_target_pairs={{0,1},{1,0},{2,3},{3,2},{4,5},{5,4},{6,7},{7,6},{8,9},{9,8},{10,11... | collective-permute-start | bytes 1572872 | tf_op jit(solution)/shard_map/ppermute | solution.py:77
  202.6 22.2 %copy-start.7 = (bf16[2048,128]{1,0:T(8,128)(2,1)}, bf16[2048,128]{1,0:T(8,128)(2,1)S(1)}, u32[]{:S(2)}) copy-start(bf16[2048,128]{1,0:T(8,128)(2,1)S(1)} %collective-permute-done.18.refs_1_) | copy-start | bytes 1572868
  202.6 12.9 %collective-permute-start.20 = (bf16[2048,128]{1,0:T(8,128)(2,1)S(1)}, bf16[2048,128]{1,0:T(8,128)(2,1)S(1)}, u32[]{:S(2)}, u32[]{:S(2)}) collective-permute-start(bf16[2048,128]{1,0:T(8,128)(2,1)S(1)} %collective-permute-done.18.refs_1_), channel_id=1, source_target_pairs={{0,1},{1,0},{2,3},{3,2},{4,5},{5,4},{6,7},{7,6},{8,9},{9,8},{10,11... | collective-permute-start | bytes 1572872 | tf_op jit(solution)/shard_map/ppermute | solution.py:77
  207.9 13.9 %collective-permute-start.25 = (bf16[4,256,256]{2,1,0:T(8,128)(2,1)S(1)}, bf16[4,256,256]{2,1,0:T(8,128)(2,1)S(1)}, u32[]{:S(2)}, u32[]{:S(2)}) collective-permute-start(bf16[4,256,256]{2,1,0:T(8,128)(2,1)S(1)} %all-to-all-done.4.refs_4_), channel_id=1, source_target_pairs={{0,1},{1,0},{2,3},{3,2},{4,5},{5,4},{6,7},{7,6},{8,9},{9,8},{10,11... | collective-permute-start | bytes 1572872 | tf_op jit(solution)/shard_map/ppermute | solution.py:77
  213.9 11.0 %copy-start.4 = (bf16[4,256,256]{2,1,0:T(8,128)(2,1)}, bf16[4,256,256]{2,1,0:T(8,128)(2,1)S(1)}, u32[]{:S(2)}) copy-start(bf16[4,256,256]{2,1,0:T(8,128)(2,1)S(1)} %collective-permute-done.22.refs_6_) | copy-start | bytes 1572868
  213.9 6.5 %collective-permute-start.23 = (bf16[2,256,256]{2,1,0:T(8,128)(2,1)S(1)}, bf16[2,256,256]{2,1,0:T(8,128)(2,1)S(1)}, u32[]{:S(2)}, u32[]{:S(2)}) collective-permute-start(bf16[2,256,256]{2,1,0:T(8,128)(2,1)S(1)} %slice.117), channel_id=1, source_target_pairs={{0,2},{2,0},{1,3},{3,1},{4,6},{6,4},{5,7},{7,5},{8,10},{10,8},{9,1... | collective-permute-start | bytes 786440 | tf_op jit(solution)/shard_map/ppermute | solution.py:77
  214.0 10.8 %copy-start.5 = (bf16[4,256,256]{2,1,0:T(8,128)(2,1)}, bf16[4,256,256]{2,1,0:T(8,128)(2,1)S(1)}, u32[]{:S(2)}) copy-start(bf16[4,256,256]{2,1,0:T(8,128)(2,1)S(1)} %collective-permute-done.21.refs_5_) | copy-start | bytes 1572868
  214.1 7.7 %collective-permute-start.24 = (bf16[2,256,256]{2,1,0:T(8,128)(2,1)S(1)}, bf16[2,256,256]{2,1,0:T(8,128)(2,1)S(1)}, u32[]{:S(2)}, u32[]{:S(2)}) collective-permute-start(bf16[2,256,256]{2,1,0:T(8,128)(2,1)S(1)} %slice.118), channel_id=1, source_target_pairs={{0,130},{2,128},{128,2},{130,0},{1,131},{3,129},{129,3},{131,1},{4... | collective-permute-start | bytes 786440 | tf_op jit(solution)/shard_map/ppermute | solution.py:77
  215.6 9.3 %copy-start.8 = (bf16[2048,128]{1,0:T(8,128)(2,1)}, bf16[2048,128]{1,0:T(8,128)(2,1)S(1)}, u32[]{:S(2)}) copy-start(bf16[2048,128]{1,0:T(8,128)(2,1)S(1)} %collective-permute-done.19.refs_2_) | copy-start | bytes 1572868
  215.6 7.8 %collective-permute-start.26 = (bf16[4,256,256]{2,1,0:T(8,128)(2,1)S(1)}, bf16[4,256,256]{2,1,0:T(8,128)(2,1)S(1)}, u32[]{:S(2)}, u32[]{:S(2)}) collective-permute-start(bf16[4,256,256]{2,1,0:T(8,128)(2,1)S(1)} %collective-permute-done.21.refs_5_), channel_id=1, source_target_pairs={{0,1},{1,0},{2,3},{3,2},{4,5},{5,4},{6,7},{7,6},{8,9},{9,8},{10,11... | collective-permute-start | bytes 1572872 | tf_op jit(solution)/shard_map/ppermute | solution.py:77
  215.6 7.8 %copy-start.9 = (bf16[2048,128]{1,0:T(8,128)(2,1)}, bf16[2048,128]{1,0:T(8,128)(2,1)S(1)}, u32[]{:S(2)}) copy-start(bf16[2048,128]{1,0:T(8,128)(2,1)S(1)} %collective-permute-done.20.refs_3_) | copy-start | bytes 1572868
  215.6 9.2 %collective-permute-start.27 = (bf16[4,256,256]{2,1,0:T(8,128)(2,1)S(1)}, bf16[4,256,256]{2,1,0:T(8,128)(2,1)}, u32[]{:S(2)}, u32[]{:S(2)}) collective-permute-start(bf16[4,256,256]{2,1,0:T(8,128)(2,1)S(1)} %collective-permute-done.22.refs_6_), channel_id=1, source_target_pairs={{0,1},{1,0},{2,3},{3,2},{4,5},{5,4},{6,7},{7,6},{8,9},{9,8},{10,11... | collective-permute-start | bytes 1572872 | tf_op jit(solution)/shard_map/ppermute | solution.py:77
  220.4 1.5 collective-permute-start.28
  221.8 1.5 collective-permute-start.29
  (9 other events, 12.8 us)
Sparse Core Ops, SparseCore 0:
  10.8 93.5 all-gather.1

commit v5 on v4

--- a/solution.py
+++ b/solution.py
@@ -18,6 +18,7 @@
 MEM = ("zl", "core")
 X = ("xh", "xl")
 FS = ("y", "zh", "zl", "xl")
+Z = ("zh", "zl")
 
 
 def rotate(field, cosine_table, sine_table):
@@ -33,10 +34,9 @@
     )
 
 
-def angles(seg_row):
-    span_count = seg_row.shape[0]
+def angles(seg_row, place):
     earlier = jnp.sum((seg_row[None, :] < seg_row[:, None]).astype(jnp.int32), axis=1)
-    positions = jnp.arange(span_count, dtype=jnp.int32) - earlier
+    positions = place - earlier
     frequency = rope_base ** (-jnp.arange(HD // 2, dtype=jnp.float32) * 2.0 / HD)
     phase_grid = positions.astype(jnp.float32)[:, None] * frequency[None, :]
     return jnp.cos(phase_grid), jnp.sin(phase_grid)
@@ -77,6 +77,11 @@
     return lax.ppermute(x, axes, [(i, n - 1 - i) for i in range(n)])
 
 
+def shift(x, axes, step):
+    n = lax.axis_size(axes)
+    return lax.ppermute(x, axes, [((i + step) % n, i) for i in range(n)])
+
+
 def exchange(x, axes):
     return lax.all_to_all(x, axes, split_axis=0, concat_axis=0, tiled=True)
 
@@ -98,44 +103,44 @@
             head = pl.multiple_of((2 * j + at_ref[2]) * HD, HD)
             out_ref[j, 0:64, :] = q_ref[:, pl.ds(head, HD)]
             key = slice(j // 4 * HD, (j // 4 + 1) * HD)
-            out_ref[j, 64:96, :] = k_ref[:, key]
-            out_ref[j, 96:128, :] = v_ref[:, key]
+            part = slice(j % 2 * 16, j % 2 * 16 + 16)
+            out_ref[j, 64:80, :] = (k_ref if j % 4 < 2 else v_ref)[part, key]
 
     quarter = pl.BlockSpec((32, 8 * HD), lambda i, at: (2 * at[1] + at[2], 0))
     return pl.pallas_call(
         body,
-        out_shape=jax.ShapeDtypeStruct((32, 128, HD), jnp.bfloat16),
+        out_shape=jax.ShapeDtypeStruct((32, 80, HD), jnp.bfloat16),
         grid_spec=pltpu.PrefetchScalarGridSpec(
             num_scalar_prefetch=1,
             grid=(1,),
             in_specs=[pl.BlockSpec((64, D), lambda i, at: (at[1], 0)), quarter, quarter],
-            out_specs=pl.BlockSpec((32, 128, HD), lambda i, at: (0, 0, 0)),
+            out_specs=pl.BlockSpec((32, 80, HD), lambda i, at: (0, 0, 0)),
         ),
         name="pack_columns",
     )(at, w_query, w_key, w_value)
 
 
-def project(normed, pieces, others, at):
+def project(normed, q_pieces, kv_pieces, kv_others, at):
     def body(at_ref, rows_ref, *refs):
-        mine, theirs = refs[:5], refs[5:10]
-        out_ref, wq_ref, wkv_ref, member_ref = refs[10:]
+        q_in, mine, theirs = refs[:5], refs[5:10], refs[10:15]
+        out_ref, wq_ref, wkv_ref, member_ref = refs[15:]
         b = pl.program_id(0)
         xl, xh, core = at_ref[0], at_ref[1], at_ref[2]
         spots = ((xl, xh), (1 - xl, xh), (1 - xl, 1 - xh), (xl, 1 - xh))
 
-        def block(group, n):
+        for n, (l, h) in enumerate(spots):
             if n < 3:
-                return group[n][...]
-            return jnp.where(b < 2, group[3][...], group[4][...])
-
-        for n, (l, h) in enumerate(spots):
-            own = block(mine, n)
-            other = block(theirs, n)
-            wq_ref[:, l, h] = own[:, :64]
-            wkv_ref[:, l, h, core, :, 0:HD] = own[:, 64:96]
-            wkv_ref[:, l, h, core, :, HD : 2 * HD] = own[:, 96:128]
-            wkv_ref[:, l, h, 1 - core, :, 0:HD] = other[:, 0:32]
-            wkv_ref[:, l, h, 1 - core, :, HD : 2 * HD] = other[:, 32:64]
+                wq_ref[:, l, h] = q_in[n][...]
+            else:
+                wq_ref[:, l, h] = jnp.where(b < 2, q_in[3][...], q_in[4][...])
+            for group, c in ((mine, core), (theirs, 1 - core)):
+                for part in range(4):
+                    if n < 3:
+                        piece = group[n][part]
+                    else:
+                        piece = group[3 + part // 2][part % 2]
+                    row, col = part % 2 * 16, part // 2 * HD
+                    wkv_ref[:, l, h, c, row : row + 16, col : col + HD] = piece
 
         rows = rows_ref[...]
         for n in (0, 1):
@@ -154,16 +159,12 @@
             rows, wkv_ref[...].reshape(2048, 2 * HD), preferred_element_type=jnp.float32
         )
 
-        @pl.when(b == 3)
-        def _():
-            out_ref[...] *= D ** (-0.5)
-
-    def group(rows, at_row):
-        whole = pl.BlockSpec((8, rows, HD), lambda b, at: (b, at_row, 0))
-        first = pl.BlockSpec((8, rows, HD), lambda b, at: (jnp.minimum(b, 1), at_row, 0))
-        last = pl.BlockSpec((8, rows, HD), lambda b, at: (jnp.maximum(b, 2) - 2, at_row, 0))
-        return [whole, whole, whole, first, last]
-
+    whole = pl.BlockSpec((8, 64, HD), lambda b, at: (b, 0, 0))
+    first = pl.BlockSpec((8, 64, HD), lambda b, at: (jnp.minimum(b, 1), 0, 0))
+    last = pl.BlockSpec((8, 64, HD), lambda b, at: (jnp.maximum(b, 2) - 2, 0, 0))
+    four = pl.BlockSpec((4, 8, 16, HD), lambda b, at: (0, b, 0, 0))
+    two = pl.BlockSpec((2, 8, 16, HD), lambda b, at: (0, b, 0, 0))
+    group = [four, four, four, two, two]
     bf16 = jnp.bfloat16
     return pl.pallas_call(
         body,
@@ -176,9 +177,10 @@
         grid_spec=pltpu.PrefetchScalarGridSpec(
             num_scalar_prefetch=1,
             grid=(4,),
-            in_specs=[pl.BlockSpec((512, 2048), lambda b, at: (0, b))]
-            + group(128, 0)
-            + group(64, 1),
+            in_specs=[pl.BlockSpec((512, 2048), lambda b, at: (0, b)), whole, whole, whole]
+            + [first, last]
+            + group
+            + group,
             out_specs=(
                 pl.BlockSpec((512, 3 * HD), lambda b, at: (0, 0)),
                 pl.BlockSpec((8, 2, 2, 64, HD), lambda b, at: (b, 0, 0, 0, 0)),
@@ -187,7 +189,7 @@
             ),
         ),
         name="project",
-    )(at, normed, *pieces, *others)
+    )(at, normed, *q_pieces, *kv_pieces, *kv_others)
 
 
 def unpack(q_pieces, kv_pieces, kv_others, at):
@@ -255,24 +257,40 @@
     normed_own = (
         token_rows * lax.rsqrt(jnp.mean(token_rows * token_rows, axis=-1, keepdims=True) + norm_eps)
     ).astype(bf16)
-    normed = lax.all_gather(swap(normed_own), YZ + ("core",), axis=0, tiled=True)
-    cot = swap(cotangent[0])
-    seg_row = swap(seg_ids[0])
+    normed_own = swap(normed_own)
+    others = [shift(normed_own, ("y",), step) for step in (1, 2, 3)]
+    normed = lax.all_gather(
+        jnp.concatenate([normed_own] + others, axis=0), Z + ("core",), axis=0, tiled=True
+    )
+    y = lax.axis_index("y")
+
+    def in_order(x):
+        x = x.reshape((4, 8, 2, 8) + x.shape[1:])
+        x = lax.dynamic_slice_in_dim(jnp.concatenate([x, x], axis=0), y, 4)
+        return jnp.moveaxis(x, 0, 2).reshape((512,) + x.shape[4:])
+
+    cot = in_order(swap(cotangent[0]))
+    seg_row = in_order(swap(seg_ids[0]))
+    place = in_order(jnp.arange(512, dtype=jnp.int32))
     adv_row = swap(advantage[0])
     block_len = 512
 
     at = jnp.stack([xl, xh, core, member]).astype(jnp.int32)
-    cut = exchange(pack_columns(w_query, w_key, w_value, at), YZ)
-    pieces = (cut,) + ring_pieces(cut)
-    others = tuple(flip(p, ("core",)) for p in pieces)
-    projected, q_cols, wkv, normed_m = project(normed, pieces, others, at)
+    packed = pack_columns(w_query, w_key, w_value, at)
+    cut = exchange(packed, YZ)
+    wkv = spread(cut[:, 64:], ("zl",))
+    wq = cut[:, :64]
+    q_pieces = (wq,) + ring_pieces(wq)
+    kv_pieces = (wkv,) + ring_pieces(wkv)
+    kv_others = tuple(flip(p, ("core",)) for p in kv_pieces)
+    projected, q_cols, wkv, normed_m = project(normed, q_pieces, kv_pieces, kv_others, at)
+    projected = projected * inv_width
     q_cols = q_cols.reshape(D, HD)
 
-    cosine_table, sine_table = angles(seg_row)
+    cosine_table, sine_table = angles(seg_row, place)
     weight_row = token_weights(seg_row, adv_row)
     grad_context = (cot.astype(f32) * weight_row[:, None]).astype(bf16)
-    position = jnp.arange(block_len, dtype=jnp.int32)
-    allowed = (seg_row[:, None] == seg_row[None, :]) & (position[None, :] <= position[:, None])
+    allowed = (seg_row[:, None] == seg_row[None, :]) & (place[None, :] <= place[:, None])
 
     q_rot = rotate(projected[:, :HD], cosine_table, sine_table).astype(bf16)
     k_rot = rotate(projected[:, HD : 2 * HD], cosine_table, sine_table).astype(bf16)
@@ -324,8 +342,7 @@
     part_kv = lax.dot_general(
         normed_m, kv_sum, contract, preferred_element_type=f32
     ).astype(bf16)
-    part_kv = exchange(part_kv.reshape(4, 256, 2 * HD), X)
-    part_kv = part_kv.astype(f32)
+    part_kv = exchange(part_kv.reshape(4, 256, 2 * HD), X).astype(f32)
     old_kv = wkv.reshape(4, 2, 8, 128, 2 * HD)
     old_kv = lax.dynamic_index_in_dim(old_kv, ring, 0, keepdims=False)
     old_kv = lax.dynamic_index_in_dim(old_kv, member, 1, keepdims=False).reshape(256, 2 * HD)

time: 241 us -> 254 us (1.054)
  starting transfers between devices: 68.1 us -> 87 us
  blocking collectives: 36 us -> 28.7 us
  waiting for transfers between devices: 63 us -> 58.8 us
  other arithmetic: 15.2 us -> 19.3 us
  local copies, waits for them, and re-layouts: 8.04 us -> 10.8 us
    ppermute x24 -> x28, waiting for transfers between devices: 48.3 us -> 39.1 us  [flip(): return lax.ppermute(x, axes, [(i, n - 1 - i) for i in range(n)])]
    all_to_all x4 -> x5, starting transfers between devices: 17.4 us -> 25.6 us  [exchange(): return lax.all_to_all(x, axes, split_axis=0, concat_axis=0, tiled=True)]
    all_to_all x1, blocking collectives: 36 us -> 28.7 us  [exchange(): return lax.all_to_all(x, axes, split_axis=0, concat_axis=0, tiled=True)]
    ppermute x0 -> x3, starting transfers between devices: none -> 5 us  [shift(): return lax.ppermute(x, axes, [((i + step) % n, i) for i in range(n)])]
    ppermute x24 -> x28, starting transfers between devices: 44.9 us -> 48.7 us  [flip(): return lax.ppermute(x, axes, [(i, n - 1 - i) for i in range(n)])]
    ppermute x0 -> x3, waiting for transfers between devices: none -> 3.76 us  [shift(): return lax.ppermute(x, axes, [((i + step) % n, i) for i in range(n)])]
    all_to_all x4 -> x5, waiting for transfers between devices: 11.2 us -> 13.3 us  [exchange(): return lax.all_to_all(x, axes, split_axis=0, concat_axis=0, tiled=True)]
  transfers between devices with their start and end apart: 35 -> 43, of which waited for: 19 -> 20; matrix products, arithmetic and copies ran while one was open for 9% -> 9% of each run, Pallas kernels for 7% -> 1%
where the time goes in v5:
time: 254 us; the launch traced here: 251 us
  starting transfers between devices  87 us (34%)
  waiting for transfers between devices  58.8 us (23%)
  blocking collectives  28.7 us (11%)
  Pallas kernels  21 us (8%)
  other arithmetic  19.3 us (8%)
  between operations  14.6 us (6%)
  local copies, waits for them, and re-layouts  10.8 us (4%)
  matrix products  10.4 us (4%)
    ppermute x28, starting transfers between devices, flip(): return lax.ppermute(x, axes, [(i, n - 1 - i) for i in range(n)])  48.7 us
    ppermute x28, waiting for transfers between devices, flip(): return lax.ppermute(x, axes, [(i, n - 1 - i) for i in range(n)])  39.1 us
    all_to_all x1, blocking collectives, exchange(): return lax.all_to_all(x, axes, split_axis=0, concat_axis=0, tiled=True)  28.7 us
    all_to_all x5, starting transfers between devices, exchange(): return lax.all_to_all(x, axes, split_axis=0, concat_axis=0, tiled=True)  25.6 us
    all_to_all x5, waiting for transfers between devices, exchange(): return lax.all_to_all(x, axes, split_axis=0, concat_axis=0, tiled=True)  13.3 us
    pallas_call x1, Pallas kernels, project(): pl.pallas_call(body, out_shape=(jax.ShapeDtypeStruct((512, 3 * HD), jnp.f...  11.4 us
    pallas_call x1, Pallas kernels, unpack(): pl.pallas_call(body, out_shape=(jax.ShapeDtypeStruct((2, 2, 2048, HD), bf...  6.67 us
    ppermute x5, starting transfers between devices, swap(): return lax.ppermute(x, ('xl', 'core'), [(0, 0), (1, 2), (2, 1), (3, 3)])  6.36 us
  transfers between devices with their start and end apart: 43, of which 20 were waited for; matrix products, arithmetic and copies ran while one was open for 9% of the time, Pallas kernels for 1%

profile of v5, /device:TPU:8, one launch (start us, length us, event | category | flops | bytes accessed | tf_op | source)
XLA Modules:
  0.0 250.6 jit_solution(18353773342789977348)
XLA Ops:
  10.0 2.2 collective-permute-start.1
  13.1 1.9 collective-permute-start.3
  15.0 3.7 %collective-permute-done.2 = bf16[8,8192]{1,0:T(8,128)(2,1)S(1)} collective-permute-done((bf16[8,8192]{1,0:T(8,128)(2,1)S(1)}, bf16[8,8192]{1,0:T(8,128)(2,1)S(1)}, u32[]{:S(2)}, u32[]{:S(2)}) %collective-permute-start.2) | collective-permute-done | bytes 131104 | tf_op jit(solution)/shard_map/ppermute | solution.py:82
  20.3 2.9 %pack_columns.1 = bf16[32,80,128]{2,1,0:T(8,128)(2,1)} custom-call(s32[4]{0:T(128)} %pad_add_fusion.at_ref, bf16[128,8192]{1,0:T(8,128)(2,1)} %q_ref.1, bf16[128,1024]{1,0:T(8,128)(2,1)} %k_ref.1, bf16[128,1024]{1,0:T(8,128)(2,1)} %v_ref.1), custom_call_target="tpu_custom_call" | custom-call | tf_op jit(solution)/shard_map/pack_columns/pallas_call | solution.py:110
  23.2 28.7 %all_to_all.30 = bf16[32,80,128]{2,1,0:T(8,128)(2,1)S(1)} all-to-all(bf16[32,80,128]{2,1,0:T(8,128)(2,1)} %pack_columns.1), channel_id=1, replica_groups=mesh['xh'=2,'y'=4,'zh'=2,'zl'=4,'xl'=2,'core'=2] {'y','zh','zl'}, dimensions={0} | all-to-all | bytes 1310720 | tf_op jit(solution)/shard_map/all_to_all | solution.py:86
  52.8 8.4 %all-to-all-start.1 = ((bf16[4,32,16,128]{3,2,1,0:T(8,128)(2,1)}), bf16[4,32,16,128]{3,2,1,0:T(8,128)(2,1)S(1)}, u32[]{:S(2)}, u32[]{:S(2)}) async-start(bf16[4,32,16,128]{3,2,1,0:T(8,128)(2,1)} %broadcast_in_dim.9), calls=%async_computation.1 | async-start | bytes 1048576 | tf_op jit(solution)/shard_map/all_to_all | solution.py:86
  61.9 1.8 collective-permute-start.19
  64.7 12.8 %collective-permute-start.5 = (bf16[32,64,128]{2,1,0:T(8,128)(2,1)S(1)}, bf16[32,64,128]{2,1,0:T(8,128)(2,1)S(1)}, u32[]{:S(2)}, u32[]{:S(2)}) collective-permute-start(bf16[32,64,128]{2,1,0:T(8,128)(2,1)S(1)} %slice.125.refs_0_), channel_id=1, source_target_pairs={{0,130},{2,128},{128,2},{130,0},{1,131},{3,129},{129,3},{131,1},{4... | collective-permute-start | bytes 1572872 | tf_op jit(solution)/shard_map/ppermute | solution.py:77
  77.8 2.2 all-to-all-done.1.refs_5_
  79.9 5.7 %collective-permute-start.9 = (bf16[4,32,16,128]{3,2,1,0:T(8,128)(2,1)S(1)}, bf16[4,32,16,128]{3,2,1,0:T(8,128)(2,1)S(1)}, u32[]{:S(2)}, u32[]{:S(2)}) collective-permute-start(bf16[4,32,16,128]{3,2,1,0:T(8,128)(2,1)S(1)} %all-to-all-done.1.refs_5_), channel_id=1, source_target_pairs={{0,130},{2,128},{128,2},{130,0},{1,131},{3,129},{129,3},{131,1},{4... | collective-permute-start | bytes 1572872 | tf_op jit(solution)/shard_map/ppermute | solution.py:77
  85.7 4.6 %collective-permute-done.5.refs_2_ = bf16[32,64,128]{2,1,0:T(8,128)(2,1)S(1)} collective-permute-done((bf16[32,64,128]{2,1,0:T(8,128)(2,1)S(1)}, bf16[32,64,128]{2,1,0:T(8,128)(2,1)S(1)}, u32[]{:S(2)}, u32[]{:S(2)}) %collective-permute-start.5) | collective-permute-done | bytes 524320 | tf_op jit(solution)/shard_map/ppermute | solution.py:77
  91.0 1.5 collective-permute-start.7
  92.6 8.9 %collective-permute-done.9.refs_7_ = bf16[4,32,16,128]{3,2,1,0:T(8,128)(2,1)S(1)} collective-permute-done((bf16[4,32,16,128]{3,2,1,0:T(8,128)(2,1)S(1)}, bf16[4,32,16,128]{3,2,1,0:T(8,128)(2,1)S(1)}, u32[]{:S(2)}, u32[]{:S(2)}) %collective-permute-start.9) | collective-permute-done | bytes 524320 | tf_op jit(solution)/shard_map/ppermute | solution.py:77
  101.5 1.6 collective-permute-start.18
  106.4 1.5 collective-permute-start.12
  110.9 2.2 collective-permute-done.10.refs_8_
  113.1 1.7 collective-permute-done.11.refs_9_
  117.3 11.4 %project.1 = (f32[512,384]{1,0:T(8,128)}, bf16[32,2,2,64,128]{4,3,2,1,0:T(8,128)(2,1)}, bf16[32,2,2,2,32,256]{5,4,3,2,1,0:T(8,128)(2,1)}, bf16[512,1024]{1,0:T(8,128)(2,1)}) custom-call(s32[4]{0:T(128)} %pad_add_fusion.at_ref, bf16[512,8192]{1,0:T(8,128)(2,1)} %all-gather.2.cloned.1.call-done.rows_ref, bf16[32,64,128]{2,1,0:T(8,128)(2,1)} %copy-done.1, ...), custom_call_target="tpu_custom_call" | custom-call | tf_op jit(solution)/shard_map/project/pallas_call | solution.py:169
  129.9 1.3 fusion.38
  137.5 5.7 %all-to-all-start.2 = ((bf16[8,64,256]{2,1,0:T(8,128)(2,1)}), bf16[8,64,256]{2,1,0:T(8,128)(2,1)S(1)}, u32[]{:S(2)}, u32[]{:S(2)}) async-start(bf16[8,64,256]{2,1,0:T(8,128)(2,1)} %fusion.11), calls=%async_computation.2 | async-start | bytes 524288 | tf_op jit(solution)/shard_map/all_to_all | solution.py:86
  143.2 5.9 %convolution_convert_fusion = bf16[8192,128]{1,0:T(8,128)(2,1)S(1)} fusion(bf16[512,8192]{1,0:T(8,128)(2,1)} %all-gather.2.cloned.1.call-done.rows_ref, f32[512,64]{1,0:T(8,128)S(1)} %get-tuple-element.35, f32[512,64]{1,0:T(8,128)S(1)} %get-tuple-element.36), kind=kOutput, calls=%fused_computation | convolution fusion | flops 1074987008 | bytes 10747904 | tf_op jit(solution)/shard_map/dot_general | solution.py:306
  149.9 1.6 collective-permute-start.20
  151.5 1.5 all-to-all-done.2
  153.7 3.6 %all-to-all-start.3 = ((bf16[8,64,256]{2,1,0:T(8,128)(2,1)}), bf16[8,64,256]{2,1,0:T(8,128)(2,1)S(1)}, u32[]{:S(2)}, u32[]{:S(2)}) async-start(bf16[8,64,256]{2,1,0:T(8,128)(2,1)} %broadcast_in_dim.12), calls=%async_computation.3 | async-start | bytes 524288 | tf_op jit(solution)/shard_map/all_to_all | solution.py:86
  157.3 2.7 %collective-permute-done.20 = bf16[1024,128]{1,0:T(8,128)(2,1)S(1)} collective-permute-done((bf16[1024,128]{1,0:T(8,128)(2,1)}, bf16[1024,128]{1,0:T(8,128)(2,1)S(1)}, u32[]{:S(2)}, u32[]{:S(2)}) %collective-permute-start.20) | collective-permute-done | bytes 262176 | tf_op jit(solution)/shard_map/ppermute | solution.py:77
  160.0 1.8 fusion.13
  161.8 5.2 %all-to-all-done.3 = bf16[8,64,256]{2,1,0:T(8,128)(2,1)S(1)} async-done(((bf16[8,64,256]{2,1,0:T(8,128)(2,1)}), bf16[8,64,256]{2,1,0:T(8,128)(2,1)S(1)}, u32[]{:S(2)}, u32[]{:S(2)}) %all-to-all-start.3) | async-done | bytes 262176 | tf_op jit(solution)/shard_map/all_to_all | solution.py:86
  167.1 2.5 %convolution_convert_fusion.1 = bf16[1024,256]{1,0:T(8,128)(2,1)} fusion(bf16[512,1024]{1,0:T(8,128)(2,1)} %get-tuple-element.13, bf16[512,256]{1,0:T(8,128)(2,1)S(1)} %bitcast.87), kind=kOutput, calls=%fused_computation.2 | convolution fusion | flops 268697600 | bytes 1835008 | tf_op jit(solution)/shard_map/dot_general | solution.py:342
  169.6 4.4 %all-to-all-start.4 = ((bf16[4,256,256]{2,1,0:T(8,128)(2,1)}), bf16[4,256,256]{2,1,0:T(8,128)(2,1)S(1)}, u32[]{:S(2)}, u32[]{:S(2)}) async-start(bf16[4,256,256]{2,1,0:T(8,128)(2,1)} %bitcast.86), calls=%async_computation.4 | async-start | bytes 1048576 | tf_op jit(solution)/shard_map/all_to_all | solution.py:86
  173.9 1.8 pad_maximum_fusion.1
  175.7 2.0 collective-permute-start.21
  178.6 2.1 collective-permute-start.23
  181.6 3.3 %all-to-all-done.4 = bf16[4,256,256]{2,1,0:T(8,128)(2,1)S(1)} async-done(((bf16[4,256,256]{2,1,0:T(8,128)(2,1)}), bf16[4,256,256]{2,1,0:T(8,128)(2,1)S(1)}, u32[]{:S(2)}, u32[]{:S(2)}) %all-to-all-start.4) | async-done | bytes 524320 | tf_op jit(solution)/shard_map/all_to_all | solution.py:86
  185.8 3.5 %all-to-all-start.5 = ((bf16[4,256,256]{2,1,0:T(8,128)(2,1)}), bf16[4,256,256]{2,1,0:T(8,128)(2,1)S(1)}, u32[]{:S(2)}, u32[]{:S(2)}) async-start(bf16[4,256,256]{2,1,0:T(8,128)(2,1)} %broadcast_in_dim.13), calls=%async_computation.5 | async-start | bytes 1048576 | tf_op jit(solution)/shard_map/all_to_all | solution.py:86
  189.3 3.6 %collective-permute-done.21 = bf16[2048,128]{1,0:T(8,128)(2,1)} collective-permute-done((bf16[2048,128]{1,0:T(8,128)(2,1)}, bf16[2048,128]{1,0:T(8,128)(2,1)}, u32[]{:S(2)}, u32[]{:S(2)}) %collective-permute-start.21) | collective-permute-done | bytes 524320 | tf_op jit(solution)/shard_map/ppermute | solution.py:77
  192.9 1.4 collective-permute-done.23
  194.3 2.3 fusion.3
  196.6 1.7 collective-permute-start.24
  198.3 1.3 collective-permute-start.25
  201.9 10.2 %collective-permute-start.26 = (bf16[2048,128]{1,0:T(8,128)(2,1)S(1)}, bf16[2048,128]{1,0:T(8,128)(2,1)S(1)}, u32[]{:S(2)}, u32[]{:S(2)}) collective-permute-start(bf16[2048,128]{1,0:T(8,128)(2,1)S(1)} %collective-permute-done.24.refs_0_), channel_id=1, source_target_pairs={{0,1},{1,0},{2,3},{3,2},{4,5},{5,4},{6,7},{7,6},{8,9},{9,8},{10,11... | collective-permute-start | bytes 1572872 | tf_op jit(solution)/shard_map/ppermute | solution.py:77
  212.2 2.6 %collective-permute-done.25.refs_1_ = bf16[2048,128]{1,0:T(8,128)(2,1)S(1)} collective-permute-done((bf16[2048,128]{1,0:T(8,128)(2,1)}, bf16[2048,128]{1,0:T(8,128)(2,1)S(1)}, u32[]{:S(2)}, u32[]{:S(2)}) %collective-permute-start.25) | collective-permute-done | bytes 524320 | tf_op jit(solution)/shard_map/ppermute | solution.py:327
  214.8 5.2 %collective-permute-start.27 = (bf16[2048,128]{1,0:T(8,128)(2,1)S(1)}, bf16[2048,128]{1,0:T(8,128)(2,1)S(1)}, u32[]{:S(2)}, u32[]{:S(2)}) collective-permute-start(bf16[2048,128]{1,0:T(8,128)(2,1)S(1)} %collective-permute-done.25.refs_1_), channel_id=1, source_target_pairs={{0,1},{1,0},{2,3},{3,2},{4,5},{5,4},{6,7},{7,6},{8,9},{9,8},{10,11... | collective-permute-start | bytes 1572872 | tf_op jit(solution)/shard_map/ppermute | solution.py:77
  220.0 6.0 %collective-permute-done.29.refs_6_ = bf16[4,256,256]{2,1,0:T(8,128)(2,1)S(1)} collective-permute-done((bf16[4,256,256]{2,1,0:T(8,128)(2,1)S(1)}, bf16[4,256,256]{2,1,0:T(8,128)(2,1)S(1)}, u32[]{:S(2)}, u32[]{:S(2)}) %collective-permute-start.29) | collective-permute-done | bytes 524320 | tf_op jit(solution)/shard_map/ppermute | solution.py:77
  226.2 1.5 collective-permute-start.31
  228.2 4.3 %collective-permute-done.30.refs_7_ = bf16[2,256,256]{2,1,0:T(8,128)(2,1)S(1)} collective-permute-done((bf16[2,256,256]{2,1,0:T(8,128)(2,1)S(1)}, bf16[2,256,256]{2,1,0:T(8,128)(2,1)S(1)}, u32[]{:S(2)}, u32[]{:S(2)}) %collective-permute-start.30) | collective-permute-done | bytes 262176 | tf_op jit(solution)/shard_map/ppermute | solution.py:77
  232.6 1.4 collective-permute-done.31.refs_8_
  234.1 1.4 collective-permute-done.36.refs_13_
  237.1 6.7 %unpack.1 = (bf16[2,2,2048,128]{3,2,1,0:T(8,128)(2,1)}, bf16[2,2,2,4,2,128,128]{6,5,4,3,2,1,0:T(8,128)(2,1)}, bf16[2,2,2,4,2,128,128]{6,5,4,3,2,1,0:T(8,128)(2,1)}) custom-call(s32[4]{0:T(128)} %pad_add_fusion.at_ref, bf16[2048,128]{1,0:T(8,128)(2,1)} %copy-done.9, bf16[2048,128]{1,0:T(8,128)(2,1)} %copy-done.10, bf16[2048,128]{1,0:T(8,128)(2,1)} %copy-done.11, ...), custom_call_target="tpu_custom_call" | custom-call | tf_op jit(solution)/shard_map/unpack/pallas_call | solution.py:223
  (157 shorter events, 33.9 us)
Async XLA Ops:
  7.2 110.1 %all-gather.2.cloned.1.call-start = ((), (), s32[]{:S(2)}) async-start(), calls=%async_computation.6 | async-start | bytes 8912896 | tf_op jit(solution)/shard_map/all_gather | solution.py:262
  9.3 0.7 collective-permute-start
  10.0 5.0 %collective-permute-start.1 = (bf16[8,8192]{1,0:T(8,128)(2,1)S(1)}, bf16[8,8192]{1,0:T(8,128)(2,1)S(1)}, u32[]{:S(2)}, u32[]{:S(2)}) collective-permute-start(bf16[8,8192]{1,0:T(8,128)(2,1)S(1)} %collective-permute-done), channel_id=1, source_target_pairs={{32,0},{64,32},{96,64},{0,96},{33,1},{65,33},{97,65},{1,97},{34,2}... | collective-permute-start | bytes 393224 | tf_op jit(solution)/shard_map/ppermute | solution.py:82
  12.2 6.5 %collective-permute-start.2 = (bf16[8,8192]{1,0:T(8,128)(2,1)S(1)}, bf16[8,8192]{1,0:T(8,128)(2,1)S(1)}, u32[]{:S(2)}, u32[]{:S(2)}) collective-permute-start(bf16[8,8192]{1,0:T(8,128)(2,1)S(1)} %collective-permute-done), channel_id=1, source_target_pairs={{64,0},{96,32},{0,64},{32,96},{65,1},{97,33},{1,65},{33,97},{66,2}... | collective-permute-start | bytes 393224 | tf_op jit(solution)/shard_map/ppermute | solution.py:82
  13.1 5.6 %collective-permute-start.3 = (bf16[8,8192]{1,0:T(8,128)(2,1)S(1)}, bf16[8,8192]{1,0:T(8,128)(2,1)S(1)}, u32[]{:S(2)}, u32[]{:S(2)}) collective-permute-start(bf16[8,8192]{1,0:T(8,128)(2,1)S(1)} %collective-permute-done), channel_id=1, source_target_pairs={{96,0},{0,32},{32,64},{64,96},{97,1},{1,33},{33,65},{65,97},{98,2}... | collective-permute-start | bytes 393224 | tf_op jit(solution)/shard_map/ppermute | solution.py:82
  23.2 38.0 %copy-start.26 = (s32[1,512]{1,0:T(1,128)S(1)}, s32[1,512]{1,0:T(1,128)}, u32[]{:S(2)}) copy-start(s32[1,512]{1,0:T(1,128)} %param.9) | copy-start | bytes 6148
  52.8 27.1 %all-to-all-start.1 = ((bf16[4,32,16,128]{3,2,1,0:T(8,128)(2,1)}), bf16[4,32,16,128]{3,2,1,0:T(8,128)(2,1)S(1)}, u32[]{:S(2)}, u32[]{:S(2)}) async-start(bf16[4,32,16,128]{3,2,1,0:T(8,128)(2,1)} %broadcast_in_dim.9), calls=%async_computation.1 | async-start | bytes 1048576 | tf_op jit(solution)/shard_map/all_to_all | solution.py:86
  61.2 3.2 %collective-permute-start.17 = (s32[512]{0:T(512)S(1)}, s32[512]{0:T(512)S(1)}, u32[]{:S(2)}, u32[]{:S(2)}) collective-permute-start(s32[512]{0:T(512)S(1)} %bitcast.94), channel_id=1, source_target_pairs={{0,0},{1,2},{2,1},{3,3},{4,4},{5,6},{6,5},{7,7},{8,8},{9,10},{10,9... | collective-permute-start | bytes 6152 | tf_op jit(solution)/shard_map/ppermute | solution.py:72
  61.9 43.0 %collective-permute-start.19 = (f32[8]{0:T(128)}, f32[8]{0:T(128)}, u32[]{:S(2)}, u32[]{:S(2)}) collective-permute-start(f32[8]{0:T(128)} %bitcast.14), channel_id=1, source_target_pairs={{0,0},{1,2},{2,1},{3,3},{4,4},{5,6},{6,5},{7,7},{8,8},{9,10},{10,9... | collective-permute-start | bytes 104 | tf_op jit(solution)/shard_map/ppermute | solution.py:72
  64.7 52.5 %copy-start.1 = (bf16[32,64,128]{2,1,0:T(8,128)(2,1)}, bf16[32,64,128]{2,1,0:T(8,128)(2,1)S(1)}, u32[]{:S(2)}) copy-start(bf16[32,64,128]{2,1,0:T(8,128)(2,1)S(1)} %slice.125.refs_0_) | copy-start | bytes 1572868
  64.7 25.5 %collective-permute-start.5 = (bf16[32,64,128]{2,1,0:T(8,128)(2,1)S(1)}, bf16[32,64,128]{2,1,0:T(8,128)(2,1)S(1)}, u32[]{:S(2)}, u32[]{:S(2)}) collective-permute-start(bf16[32,64,128]{2,1,0:T(8,128)(2,1)S(1)} %slice.125.refs_0_), channel_id=1, source_target_pairs={{0,130},{2,128},{128,2},{130,0},{1,131},{3,129},{129,3},{131,1},{4... | collective-permute-start | bytes 1572872 | tf_op jit(solution)/shard_map/ppermute | solution.py:77
  77.5 13.5 %collective-permute-start.4 = (bf16[32,64,128]{2,1,0:T(8,128)(2,1)S(1)}, bf16[32,64,128]{2,1,0:T(8,128)(2,1)S(1)}, u32[]{:S(2)}, u32[]{:S(2)}) collective-permute-start(bf16[32,64,128]{2,1,0:T(8,128)(2,1)S(1)} %slice.125.refs_0_), channel_id=1, source_target_pairs={{0,2},{2,0},{1,3},{3,1},{4,6},{6,4},{5,7},{7,5},{8,10},{10,8},{9,1... | collective-permute-start | bytes 1572872 | tf_op jit(solution)/shard_map/ppermute | solution.py:77
  79.9 37.3 %copy-start = (bf16[4,32,16,128]{3,2,1,0:T(8,128)(2,1)}, bf16[4,32,16,128]{3,2,1,0:T(8,128)(2,1)S(1)}, u32[]{:S(2)}) copy-start(bf16[4,32,16,128]{3,2,1,0:T(8,128)(2,1)S(1)} %all-to-all-done.1.refs_5_) | copy-start | bytes 1572868
  79.9 21.6 %collective-permute-start.9 = (bf16[4,32,16,128]{3,2,1,0:T(8,128)(2,1)S(1)}, bf16[4,32,16,128]{3,2,1,0:T(8,128)(2,1)S(1)}, u32[]{:S(2)}, u32[]{:S(2)}) collective-permute-start(bf16[4,32,16,128]{3,2,1,0:T(8,128)(2,1)S(1)} %all-to-all-done.1.refs_5_), channel_id=1, source_target_pairs={{0,130},{2,128},{128,2},{130,0},{1,131},{3,129},{129,3},{131,1},{4... | collective-permute-start | bytes 1572872 | tf_op jit(solution)/shard_map/ppermute | solution.py:77
  85.6 17.5 %collective-permute-start.8 = (bf16[4,32,16,128]{3,2,1,0:T(8,128)(2,1)S(1)}, bf16[4,32,16,128]{3,2,1,0:T(8,128)(2,1)S(1)}, u32[]{:S(2)}, u32[]{:S(2)}) collective-permute-start(bf16[4,32,16,128]{3,2,1,0:T(8,128)(2,1)S(1)} %all-to-all-done.1.refs_5_), channel_id=1, source_target_pairs={{0,2},{2,0},{1,3},{3,1},{4,6},{6,4},{5,7},{7,5},{8,10},{10,8},{9,1... | collective-permute-start | bytes 1572872 | tf_op jit(solution)/shard_map/ppermute | solution.py:77
  90.3 17.6 %collective-permute-start.6 = (bf16[16,64,128]{2,1,0:T(8,128)(2,1)S(1)}, bf16[16,64,128]{2,1,0:T(8,128)(2,1)S(1)}, u32[]{:S(2)}, u32[]{:S(2)}) collective-permute-start(bf16[16,64,128]{2,1,0:T(8,128)(2,1)S(1)} %slice.126), channel_id=1, source_target_pairs={{0,2},{2,0},{1,3},{3,1},{4,6},{6,4},{5,7},{7,5},{8,10},{10,8},{9,1... | collective-permute-start | bytes 786440 | tf_op jit(solution)/shard_map/ppermute | solution.py:77
  91.0 17.6 %collective-permute-start.7 = (bf16[16,64,128]{2,1,0:T(8,128)(2,1)S(1)}, bf16[16,64,128]{2,1,0:T(8,128)(2,1)S(1)}, u32[]{:S(2)}, u32[]{:S(2)}) collective-permute-start(bf16[16,64,128]{2,1,0:T(8,128)(2,1)S(1)} %slice.127), channel_id=1, source_target_pairs={{0,130},{2,128},{128,2},{130,0},{1,131},{3,129},{129,3},{131,1},{4... | collective-permute-start | bytes 786440 | tf_op jit(solution)/shard_map/ppermute | solution.py:77
  101.5 4.9 %collective-permute-start.18 = (bf16[512,128]{1,0:T(8,128)(2,1)}, bf16[512,128]{1,0:T(8,128)(2,1)S(1)}, u32[]{:S(2)}, u32[]{:S(2)}) collective-permute-start(bf16[512,128]{1,0:T(8,128)(2,1)} %bitcast.10), channel_id=1, source_target_pairs={{0,0},{1,2},{2,1},{3,3},{4,4},{5,6},{6,5},{7,7},{8,8},{9,10},{10,9... | collective-permute-start | bytes 393224 | tf_op jit(solution)/shard_map/ppermute | solution.py:72
  103.1 10.0 %collective-permute-start.10 = (bf16[2,32,16,128]{3,2,1,0:T(8,128)(2,1)S(1)}, bf16[2,32,16,128]{3,2,1,0:T(8,128)(2,1)}, u32[]{:S(2)}, u32[]{:S(2)}) collective-permute-start(bf16[2,32,16,128]{3,2,1,0:T(8,128)(2,1)S(1)} %slice.129), channel_id=1, source_target_pairs={{0,2},{2,0},{1,3},{3,1},{4,6},{6,4},{5,7},{7,5},{8,10},{10,8},{9,1... | collective-permute-start | bytes 786440 | tf_op jit(solution)/shard_map/ppermute | solution.py:77
  104.9 9.9 %collective-permute-start.11 = (bf16[2,32,16,128]{3,2,1,0:T(8,128)(2,1)}, bf16[2,32,16,128]{3,2,1,0:T(8,128)(2,1)}, u32[]{:S(2)}, u32[]{:S(2)}) collective-permute-start(bf16[2,32,16,128]{3,2,1,0:T(8,128)(2,1)} %slice.130), channel_id=1, source_target_pairs={{0,130},{2,128},{128,2},{130,0},{1,131},{3,129},{129,3},{131,1},{4... | collective-permute-start | bytes 786440 | tf_op jit(solution)/shard_map/ppermute | solution.py:77
  106.4 9.4 %collective-permute-start.12 = (bf16[4,32,16,128]{3,2,1,0:T(8,128)(2,1)S(1)}, bf16[4,32,16,128]{3,2,1,0:T(8,128)(2,1)}, u32[]{:S(2)}, u32[]{:S(2)}) collective-permute-start(bf16[4,32,16,128]{3,2,1,0:T(8,128)(2,1)S(1)} %all-to-all-done.1.refs_5_), channel_id=1, source_target_pairs={{0,1},{1,0},{2,3},{3,2},{4,5},{5,4},{6,7},{7,6},{8,9},{9,8},{10,11... | collective-permute-start | bytes 1572872 | tf_op jit(solution)/shard_map/ppermute | solution.py:77
  107.9 8.6 %collective-permute-start.13 = (bf16[4,32,16,128]{3,2,1,0:T(8,128)(2,1)S(1)}, bf16[4,32,16,128]{3,2,1,0:T(8,128)(2,1)}, u32[]{:S(2)}, u32[]{:S(2)}) collective-permute-start(bf16[4,32,16,128]{3,2,1,0:T(8,128)(2,1)S(1)} %collective-permute-done.8.refs_6_), channel_id=1, source_target_pairs={{0,1},{1,0},{2,3},{3,2},{4,5},{5,4},{6,7},{7,6},{8,9},{9,8},{10,11... | collective-permute-start | bytes 1572872 | tf_op jit(solution)/shard_map/ppermute | solution.py:77
  109.3 7.9 %collective-permute-start.14 = (bf16[4,32,16,128]{3,2,1,0:T(8,128)(2,1)S(1)}, bf16[4,32,16,128]{3,2,1,0:T(8,128)(2,1)}, u32[]{:S(2)}, u32[]{:S(2)}) collective-permute-start(bf16[4,32,16,128]{3,2,1,0:T(8,128)(2,1)S(1)} %collective-permute-done.9.refs_7_), channel_id=1, source_target_pairs={{0,1},{1,0},{2,3},{3,2},{4,5},{5,4},{6,7},{7,6},{8,9},{9,8},{10,11... | collective-permute-start | bytes 1572872 | tf_op jit(solution)/shard_map/ppermute | solution.py:77
  113.1 2.7 %collective-permute-start.15 = (bf16[2,32,16,128]{3,2,1,0:T(8,128)(2,1)}, bf16[2,32,16,128]{3,2,1,0:T(8,128)(2,1)S(1)}, u32[]{:S(2)}, u32[]{:S(2)}) collective-permute-start(bf16[2,32,16,128]{3,2,1,0:T(8,128)(2,1)} %collective-permute-done.10.refs_8_), channel_id=1, source_target_pairs={{0,1},{1,0},{2,3},{3,2},{4,5},{5,4},{6,7},{7,6},{8,9},{9,8},{10,11... | collective-permute-start | bytes 786440 | tf_op jit(solution)/shard_map/ppermute | solution.py:77
  114.8 1.7 collective-permute-start.16
  137.5 15.4 %all-to-all-start.2 = ((bf16[8,64,256]{2,1,0:T(8,128)(2,1)}), bf16[8,64,256]{2,1,0:T(8,128)(2,1)S(1)}, u32[]{:S(2)}, u32[]{:S(2)}) async-start(bf16[8,64,256]{2,1,0:T(8,128)(2,1)} %fusion.11), calls=%async_computation.2 | async-start | bytes 524288 | tf_op jit(solution)/shard_map/all_to_all | solution.py:86
  149.9 10.1 %collective-permute-start.20 = (bf16[1024,128]{1,0:T(8,128)(2,1)}, bf16[1024,128]{1,0:T(8,128)(2,1)S(1)}, u32[]{:S(2)}, u32[]{:S(2)}) collective-permute-start(bf16[1024,128]{1,0:T(8,128)(2,1)} %get-tuple-element.21), channel_id=1, source_target_pairs={{0,130},{2,128},{128,2},{130,0},{1,131},{3,129},{129,3},{131,1},{4... | collective-permute-start | bytes 786440 | tf_op jit(solution)/shard_map/ppermute | solution.py:77
  151.5 8.6 %collective-permute-start.22 = (bf16[1024,128]{1,0:T(8,128)(2,1)S(1)}, bf16[1024,128]{1,0:T(8,128)(2,1)}, u32[]{:S(2)}, u32[]{:S(2)}) collective-permute-start(bf16[1024,128]{1,0:T(8,128)(2,1)S(1)} %get-tuple-element.23), channel_id=1, source_target_pairs={{0,2},{2,0},{1,3},{3,1},{4,6},{6,4},{5,7},{7,5},{8,10},{10,8},{9,1... | collective-permute-start | bytes 786440 | tf_op jit(solution)/shard_map/ppermute | solution.py:77
  153.7 13.3 %all-to-all-start.3 = ((bf16[8,64,256]{2,1,0:T(8,128)(2,1)}), bf16[8,64,256]{2,1,0:T(8,128)(2,1)S(1)}, u32[]{:S(2)}, u32[]{:S(2)}) async-start(bf16[8,64,256]{2,1,0:T(8,128)(2,1)} %broadcast_in_dim.12), calls=%async_computation.3 | async-start | bytes 524288 | tf_op jit(solution)/shard_map/all_to_all | solution.py:86
  169.6 15.3 %all-to-all-start.4 = ((bf16[4,256,256]{2,1,0:T(8,128)(2,1)}), bf16[4,256,256]{2,1,0:T(8,128)(2,1)S(1)}, u32[]{:S(2)}, u32[]{:S(2)}) async-start(bf16[4,256,256]{2,1,0:T(8,128)(2,1)} %bitcast.86), calls=%async_computation.4 | async-start | bytes 1048576 | tf_op jit(solution)/shard_map/all_to_all | solution.py:86
  175.7 17.2 %collective-permute-start.21 = (bf16[2048,128]{1,0:T(8,128)(2,1)}, bf16[2048,128]{1,0:T(8,128)(2,1)}, u32[]{:S(2)}, u32[]{:S(2)}) collective-permute-start(bf16[2048,128]{1,0:T(8,128)(2,1)} %pad_maximum_fusion.1), channel_id=1, source_target_pairs={{0,2},{2,0},{1,3},{3,1},{4,6},{6,4},{5,7},{7,5},{8,10},{10,8},{9,1... | collective-permute-start | bytes 1572872 | tf_op jit(solution)/shard_map/ppermute | solution.py:77
  178.6 15.7 %collective-permute-start.23 = (bf16[2048,128]{1,0:T(8,128)(2,1)}, bf16[2048,128]{1,0:T(8,128)(2,1)S(1)}, u32[]{:S(2)}, u32[]{:S(2)}) collective-permute-start(bf16[2048,128]{1,0:T(8,128)(2,1)} %pad_maximum_fusion.2), channel_id=1, source_target_pairs={{0,130},{2,128},{128,2},{130,0},{1,131},{3,129},{129,3},{131,1},{4... | collective-permute-start | bytes 1572872 | tf_op jit(solution)/shard_map/ppermute | solution.py:77
  185.8 15.0 %all-to-all-start.5 = ((bf16[4,256,256]{2,1,0:T(8,128)(2,1)}), bf16[4,256,256]{2,1,0:T(8,128)(2,1)S(1)}, u32[]{:S(2)}, u32[]{:S(2)}) async-start(bf16[4,256,256]{2,1,0:T(8,128)(2,1)} %broadcast_in_dim.13), calls=%async_computation.5 | async-start | bytes 1048576 | tf_op jit(solution)/shard_map/all_to_all | solution.py:86
  196.6 5.3 %collective-permute-start.24 = (bf16[2048,128]{1,0:T(8,128)(2,1)}, bf16[2048,128]{1,0:T(8,128)(2,1)S(1)}, u32[]{:S(2)}, u32[]{:S(2)}) collective-permute-start(bf16[2048,128]{1,0:T(8,128)(2,1)} %fusion.3), channel_id=1, source_target_pairs={{0,0},{1,2},{2,1},{3,3},{4,4},{5,6},{6,5},{7,7},{8,8},{9,10},{10,9... | collective-permute-start | bytes 1572872 | tf_op jit(solution)/shard_map/ppermute | solution.py:72
  198.3 16.5 %collective-permute-start.25 = (bf16[2048,128]{1,0:T(8,128)(2,1)}, bf16[2048,128]{1,0:T(8,128)(2,1)S(1)}, u32[]{:S(2)}, u32[]{:S(2)}) collective-permute-start(bf16[2048,128]{1,0:T(8,128)(2,1)} %fusion.3), channel_id=1, source_target_pairs={{0,128},{1,130},{2,129},{3,131},{128,0},{129,2},{130,1},{131,3},{4... | collective-permute-start | bytes 1572872 | tf_op jit(solution)/shard_map/ppermute | solution.py:327
  200.7 36.3 %copy-start.2 = (bf16[4,256,256]{2,1,0:T(8,128)(2,1)}, bf16[4,256,256]{2,1,0:T(8,128)(2,1)S(1)}, u32[]{:S(2)}) copy-start(bf16[4,256,256]{2,1,0:T(8,128)(2,1)S(1)} %all-to-all-done.5.refs_4_) | copy-start | bytes 1572868
  200.7 25.3 %collective-permute-start.29 = (bf16[4,256,256]{2,1,0:T(8,128)(2,1)S(1)}, bf16[4,256,256]{2,1,0:T(8,128)(2,1)S(1)}, u32[]{:S(2)}, u32[]{:S(2)}) collective-permute-start(bf16[4,256,256]{2,1,0:T(8,128)(2,1)S(1)} %all-to-all-done.5.refs_4_), channel_id=1, source_target_pairs={{0,130},{2,128},{128,2},{130,0},{1,131},{3,129},{129,3},{131,1},{4... | collective-permute-start | bytes 1572872 | tf_op jit(solution)/shard_map/ppermute | solution.py:77
  201.9 24.3 %collective-permute-start.28 = (bf16[4,256,256]{2,1,0:T(8,128)(2,1)S(1)}, bf16[4,256,256]{2,1,0:T(8,128)(2,1)S(1)}, u32[]{:S(2)}, u32[]{:S(2)}) collective-permute-start(bf16[4,256,256]{2,1,0:T(8,128)(2,1)S(1)} %all-to-all-done.5.refs_4_), channel_id=1, source_target_pairs={{0,2},{2,0},{1,3},{3,1},{4,6},{6,4},{5,7},{7,5},{8,10},{10,8},{9,1... | collective-permute-start | bytes 1572872 | tf_op jit(solution)/shard_map/ppermute | solution.py:77
  201.9 35.1 %copy-start.9 = (bf16[2048,128]{1,0:T(8,128)(2,1)}, bf16[2048,128]{1,0:T(8,128)(2,1)S(1)}, u32[]{:S(2)}) copy-start(bf16[2048,128]{1,0:T(8,128)(2,1)S(1)} %collective-permute-done.24.refs_0_) | copy-start | bytes 1572868
  201.9 25.8 %collective-permute-start.26 = (bf16[2048,128]{1,0:T(8,128)(2,1)S(1)}, bf16[2048,128]{1,0:T(8,128)(2,1)S(1)}, u32[]{:S(2)}, u32[]{:S(2)}) collective-permute-start(bf16[2048,128]{1,0:T(8,128)(2,1)S(1)} %collective-permute-done.24.refs_0_), channel_id=1, source_target_pairs={{0,1},{1,0},{2,3},{3,2},{4,5},{5,4},{6,7},{7,6},{8,9},{9,8},{10,11... | collective-permute-start | bytes 1572872 | tf_op jit(solution)/shard_map/ppermute | solution.py:77
  214.8 12.9 %collective-permute-start.27 = (bf16[2048,128]{1,0:T(8,128)(2,1)S(1)}, bf16[2048,128]{1,0:T(8,128)(2,1)S(1)}, u32[]{:S(2)}, u32[]{:S(2)}) collective-permute-start(bf16[2048,128]{1,0:T(8,128)(2,1)S(1)} %collective-permute-done.25.refs_1_), channel_id=1, source_target_pairs={{0,1},{1,0},{2,3},{3,2},{4,5},{5,4},{6,7},{7,6},{8,9},{9,8},{10,11... | collective-permute-start | bytes 1572872 | tf_op jit(solution)/shard_map/ppermute | solution.py:77
  220.0 13.9 %collective-permute-start.32 = (bf16[4,256,256]{2,1,0:T(8,128)(2,1)S(1)}, bf16[4,256,256]{2,1,0:T(8,128)(2,1)S(1)}, u32[]{:S(2)}, u32[]{:S(2)}) collective-permute-start(bf16[4,256,256]{2,1,0:T(8,128)(2,1)S(1)} %all-to-all-done.5.refs_4_), channel_id=1, source_target_pairs={{0,1},{1,0},{2,3},{3,2},{4,5},{5,4},{6,7},{7,6},{8,9},{9,8},{10,11... | collective-permute-start | bytes 1572872 | tf_op jit(solution)/shard_map/ppermute | solution.py:77
  226.1 6.5 %collective-permute-start.30 = (bf16[2,256,256]{2,1,0:T(8,128)(2,1)S(1)}, bf16[2,256,256]{2,1,0:T(8,128)(2,1)S(1)}, u32[]{:S(2)}, u32[]{:S(2)}) collective-permute-start(bf16[2,256,256]{2,1,0:T(8,128)(2,1)S(1)} %slice.141), channel_id=1, source_target_pairs={{0,2},{2,0},{1,3},{3,1},{4,6},{6,4},{5,7},{7,5},{8,10},{10,8},{9,1... | collective-permute-start | bytes 786440 | tf_op jit(solution)/shard_map/ppermute | solution.py:77
  226.2 7.7 %collective-permute-start.31 = (bf16[2,256,256]{2,1,0:T(8,128)(2,1)S(1)}, bf16[2,256,256]{2,1,0:T(8,128)(2,1)S(1)}, u32[]{:S(2)}, u32[]{:S(2)}) collective-permute-start(bf16[2,256,256]{2,1,0:T(8,128)(2,1)S(1)} %slice.142), channel_id=1, source_target_pairs={{0,130},{2,128},{128,2},{130,0},{1,131},{3,129},{129,3},{131,1},{4... | collective-permute-start | bytes 786440 | tf_op jit(solution)/shard_map/ppermute | solution.py:77
  227.7 7.8 %collective-permute-start.33 = (bf16[4,256,256]{2,1,0:T(8,128)(2,1)S(1)}, bf16[4,256,256]{2,1,0:T(8,128)(2,1)S(1)}, u32[]{:S(2)}, u32[]{:S(2)}) collective-permute-start(bf16[4,256,256]{2,1,0:T(8,128)(2,1)S(1)} %collective-permute-done.28.refs_5_), channel_id=1, source_target_pairs={{0,1},{1,0},{2,3},{3,2},{4,5},{5,4},{6,7},{7,6},{8,9},{9,8},{10,11... | collective-permute-start | bytes 1572872 | tf_op jit(solution)/shard_map/ppermute | solution.py:77
  227.8 9.2 %collective-permute-start.34 = (bf16[4,256,256]{2,1,0:T(8,128)(2,1)S(1)}, bf16[4,256,256]{2,1,0:T(8,128)(2,1)}, u32[]{:S(2)}, u32[]{:S(2)}) collective-permute-start(bf16[4,256,256]{2,1,0:T(8,128)(2,1)S(1)} %collective-permute-done.29.refs_6_), channel_id=1, source_target_pairs={{0,1},{1,0},{2,3},{3,2},{4,5},{5,4},{6,7},{7,6},{8,9},{9,8},{10,11... | collective-permute-start | bytes 1572872 | tf_op jit(solution)/shard_map/ppermute | solution.py:77
  232.6 1.5 collective-permute-start.35
  234.0 1.5 collective-permute-start.36
  (22 other events, 173.5 us)
Sparse Core Ops, SparseCore 0:
  19.7 82.7 all-gather.1

commit v6 on v2

--- a/solution.py
+++ b/solution.py
@@ -86,26 +86,10 @@
     return exchange(jnp.broadcast_to(x[None], (n,) + x.shape), axes)
 
 
-def ordered(mine, other, bit):
-    first = jnp.where(bit == 0, mine, other)
-    second = jnp.where(bit == 0, other, mine)
-    return first, second
-
-
 def ring_pieces(x):
     near, wrap = flip(x, ("xl",)), flip(x, X)
     half = x.shape[0] // 2
     return near, wrap, flip(wrap[:half], ("xl",)), flip(near[half:], X)
-
-
-def x_ring(x, xh, xl):
-    near, wrap, far_low, far_high = ring_pieces(x)
-    far = jnp.concatenate([far_low, far_high], axis=0)
-    low = ordered(x, near, xl)
-    high = ordered(far, wrap, xl)
-    col0 = ordered(low[0], high[0], xh)
-    col1 = ordered(low[1], high[1], xh)
-    return (col0[0], col1[0]), (col0[1], col1[1])
 
 
 def pack_columns(w_query, w_key, w_value, at):
@@ -142,7 +126,7 @@
         def block(group, n):
             if n < 3:
                 return group[n][...]
-            return jnp.where(b < 4, group[3][...], group[4][...])
+            return jnp.where(b < 2, group[3][...], group[4][...])
 
         for n, (l, h) in enumerate(spots):
             own = block(mine, n)
@@ -154,22 +138,25 @@
             wkv_ref[:, l, h, 1 - core, :, HD : 2 * HD] = other[:, 96:128]
 
         rows = rows_ref[...]
-        member_ref[...] = rows_ref[:, pl.ds(pl.multiple_of(at_ref[3] * HD, HD), HD)]
+        for n in (0, 1):
+            member_ref[:, n * HD : (n + 1) * HD] = rows_ref[
+                :, pl.ds(pl.multiple_of(n * 1024 + at_ref[3] * HD, HD), HD)
+            ]
 
         @pl.when(b == 0)
         def _():
             out_ref[...] = jnp.zeros_like(out_ref)
 
         out_ref[:, 0:HD] += jnp.dot(
-            rows, wq_ref[...].reshape(1024, HD), preferred_element_type=jnp.float32
+            rows, wq_ref[...].reshape(2048, HD), preferred_element_type=jnp.float32
         )
         out_ref[:, HD : 3 * HD] += jnp.dot(
-            rows, wkv_ref[...].reshape(1024, 2 * HD), preferred_element_type=jnp.float32
+            rows, wkv_ref[...].reshape(2048, 2 * HD), preferred_element_type=jnp.float32
         )
 
-    whole = pl.BlockSpec((4, 128, HD), lambda b, at: (b, 0, 0))
-    first = pl.BlockSpec((4, 128, HD), lambda b, at: (jnp.minimum(b, 3), 0, 0))
-    last = pl.BlockSpec((4, 128, HD), lambda b, at: (jnp.maximum(b, 4) - 4, 0, 0))
+    whole = pl.BlockSpec((8, 128, HD), lambda b, at: (b, 0, 0))
+    first = pl.BlockSpec((8, 128, HD), lambda b, at: (jnp.minimum(b, 1), 0, 0))
+    last = pl.BlockSpec((8, 128, HD), lambda b, at: (jnp.maximum(b, 2) - 2, 0, 0))
     group = [whole, whole, whole, first, last]
     bf16 = jnp.bfloat16
     return pl.pallas_call(
@@ -182,17 +169,104 @@
         ),
         grid_spec=pltpu.PrefetchScalarGridSpec(
             num_scalar_prefetch=1,
-            grid=(8,),
-            in_specs=[pl.BlockSpec((512, 1024), lambda b, at: (0, b))] + group + group,
+            grid=(4,),
+            in_specs=[pl.BlockSpec((512, 2048), lambda b, at: (0, b))] + group + group,
             out_specs=(
                 pl.BlockSpec((512, 3 * HD), lambda b, at: (0, 0)),
-                pl.BlockSpec((4, 2, 2, 64, HD), lambda b, at: (b, 0, 0, 0, 0)),
-                pl.BlockSpec((4, 2, 2, 2, 32, 2 * HD), lambda b, at: (b, 0, 0, 0, 0, 0)),
-                pl.BlockSpec((512, HD), lambda b, at: (0, b)),
+                pl.BlockSpec((8, 2, 2, 64, HD), lambda b, at: (b, 0, 0, 0, 0)),
+                pl.BlockSpec((8, 2, 2, 2, 32, 2 * HD), lambda b, at: (b, 0, 0, 0, 0, 0)),
+                pl.BlockSpec((512, 2 * HD), lambda b, at: (0, b)),
             ),
         ),
         name="project",
     )(at, normed, *pieces, *others)
+
+
+WIDE = jax.ShapeDtypeStruct((2, 2, 2, 4, 2, HD, HD), jnp.bfloat16)
+
+
+def unpack_query(q_pieces, at):
+    def body(at_ref, near_ref, far_ref, near_other_ref, far_other_ref, out_ref):
+        xh, core = at_ref[1], at_ref[2]
+        out_ref[xh, core] = near_ref[...]
+        out_ref[1 - xh, core] = far_ref[...]
+        out_ref[xh, 1 - core] = near_other_ref[...]
+        out_ref[1 - xh, 1 - core] = far_other_ref[...]
+
+    return pl.pallas_call(
+        body,
+        out_shape=jax.ShapeDtypeStruct((2, 2, 2048, HD), jnp.bfloat16),
+        grid_spec=pltpu.PrefetchScalarGridSpec(
+            num_scalar_prefetch=1,
+            grid=(4,),
+            in_specs=[pl.BlockSpec((512, HD), lambda i, at: (i, 0))] * 4,
+            out_specs=pl.BlockSpec((2, 2, 512, HD), lambda i, at: (0, 0, i, 0)),
+        ),
+        name="unpack_query",
+    )(at, *q_pieces)
+
+
+def unpack_near(kv_pieces, kv_others, at):
+    def body(at_ref, *refs):
+        mine, theirs = refs[:3], refs[3:6]
+        k_ref, v_ref = refs[6:]
+        core = at_ref[2]
+        for n in range(3):
+
+            @pl.when(pl.program_id(0) == n)
+            def _(n=n):
+                for group, c in ((mine, core), (theirs, 1 - core)):
+                    for line in range(4):
+                        for z in range(2):
+                            rows = slice(z * HD, (z + 1) * HD)
+                            k_ref[0, 0, z, line, c] = group[n][line, rows, 0:HD]
+                            v_ref[0, 0, z, line, c] = group[n][line, rows, HD : 2 * HD]
+
+    def spot(n, at):
+        xl, xh = at[0], at[1]
+        return (jnp.where(n == 2, 1 - xh, xh), jnp.where(n == 0, xl, 1 - xl), 0, 0, 0, 0, 0)
+
+    whole = pl.BlockSpec((4, 2 * HD, 2 * HD), lambda n, at: (0, 0, 0))
+    wide = pl.BlockSpec((1, 1, 2, 4, 2, HD, HD), spot)
+    return pl.pallas_call(
+        body,
+        out_shape=(WIDE, WIDE),
+        grid_spec=pltpu.PrefetchScalarGridSpec(
+            num_scalar_prefetch=1, grid=(3,), in_specs=[whole] * 6, out_specs=(wide, wide)
+        ),
+        name="unpack_near",
+    )(at, *kv_pieces, *kv_others)
+
+
+def unpack_far(far, far_other, keys, values, at):
+    def body(at_ref, low_ref, high_ref, low_other_ref, high_other_ref, _k, _v, k_ref, v_ref):
+        core = at_ref[2]
+        for n, group in enumerate(((low_ref, low_other_ref), (high_ref, high_other_ref))):
+
+            @pl.when(pl.program_id(0) == n)
+            def _(group=group):
+                for piece, c in zip(group, (core, 1 - core)):
+                    for line in range(2):
+                        for z in range(2):
+                            rows = slice(z * HD, (z + 1) * HD)
+                            k_ref[0, 0, z, line, c] = piece[line, rows, 0:HD]
+                            v_ref[0, 0, z, line, c] = piece[line, rows, HD : 2 * HD]
+
+    whole = pl.BlockSpec((2, 2 * HD, 2 * HD), lambda n, at: (0, 0, 0))
+    wide = pl.BlockSpec((1, 1, 2, 2, 2, HD, HD), lambda n, at: (1 - at[1], at[0], 0, n, 0, 0, 0))
+    there = pl.BlockSpec(memory_space=pl.ANY)
+    return pl.pallas_call(
+        body,
+        out_shape=(WIDE, WIDE),
+        grid_spec=pltpu.PrefetchScalarGridSpec(
+            num_scalar_prefetch=1,
+            grid=(2,),
+            in_specs=[whole] * 4 + [there, there],
+            out_specs=(wide, wide),
+        ),
+        input_output_aliases={5: 0, 6: 1},
+        name="unpack_far",
+    )(at, *far, *far_other, keys, values)
 
 
 def local(hidden, cotangent, seg_ids, advantage, w_query, w_key, w_value):
@@ -243,7 +317,6 @@
     contract = (((0,), (0,)), ((), ()))
     part_q = lax.dot_general(normed, scaled_q, contract, preferred_element_type=f32)
     part_q = part_q.astype(bf16).reshape(4, 2048, HD)
-    part_q, scaled_kv = lax.optimization_barrier((part_q, scaled_kv))
 
     def part_for(mask):
         return lax.dynamic_index_in_dim(part_q, ring ^ mask, 0, keepdims=False)
@@ -275,30 +348,28 @@
     )
     near_other = flip(near, ("core",))
     far_other = flip(far, ("core",))
-    near = ordered(near, near_other, core)
-    far = ordered(far, far_other, core)
-    low = ordered(near[0], far[0], xh)
-    high = ordered(near[1], far[1], xh)
-    roll_q = jnp.stack([low[0], high[0], low[1], high[1]], axis=0).reshape(D, HD)
-
     kv_sum = exchange(scaled_kv.reshape(8, 64, 2 * HD), MEM)
-    kv_sum = kv_sum.astype(f32)
-    kv_sum = jnp.sum(kv_sum, axis=0).astype(bf16)
+    kv_sum = jnp.sum(kv_sum.astype(f32), axis=0).astype(bf16)
     kv_sum = spread(kv_sum, MEM).reshape(block_len, 2 * HD)
     part_kv = lax.dot_general(
         normed_m, kv_sum, contract, preferred_element_type=f32
     ).astype(bf16)
-    part_kv = exchange(part_kv.reshape(4, 256, 2 * HD), X).astype(f32)
+    part_kv = exchange(part_kv.reshape(4, 256, 2 * HD), X)
+    part_kv = part_kv.astype(f32)
     old_kv = wkv.reshape(4, 2, 8, 128, 2 * HD)
     old_kv = lax.dynamic_index_in_dim(old_kv, ring, 0, keepdims=False)
     old_kv = lax.dynamic_index_in_dim(old_kv, member, 1, keepdims=False).reshape(256, 2 * HD)
     new_kv = (old_kv.astype(f32) - step_rate * jnp.sum(part_kv, axis=0)).astype(bf16)
     new_kv = spread(new_kv, ("zl",))
-    new_kv = x_ring(new_kv, xh, xl)
-    new_kv = jnp.stack([new_kv[h][l] for h in (0, 1) for l in (0, 1)], axis=0)
-    new_kv = jnp.stack(ordered(new_kv, flip(new_kv, ("core",)), core), axis=0)
-    new_kv = new_kv.reshape(2, 4, 4, 2, 128, 2 * HD).transpose(1, 3, 2, 0, 4, 5).reshape(D, 2 * HD)
-    return roll_q, new_kv[:, :HD], new_kv[:, HD:]
+    near_kv, wrap_kv = flip(new_kv, ("xl",)), flip(new_kv, X)
+    far_kv = (flip(wrap_kv[:2], ("xl",)), flip(near_kv[2:], X))
+    kv_pieces = (new_kv, near_kv, wrap_kv)
+    kv_others = tuple(flip(p, ("core",)) for p in kv_pieces)
+    far_others = tuple(flip(p, ("core",)) for p in far_kv)
+    roll_q = unpack_query((near, far, near_other, far_other), at)
+    keys, values = unpack_near(kv_pieces, kv_others, at)
+    keys, values = unpack_far(far_kv, far_others, keys, values, at)
+    return tuple(out.reshape(D, HD) for out in (roll_q, keys, values))
 
 
 def solution(mesh):

time: 271 us -> 246 us (0.908)
  blocking collectives: 63.4 us -> 35.9 us
  waiting for transfers between devices: 83.2 us -> 64.5 us
  starting transfers between devices: 53.6 us -> 67.8 us
  Pallas kernels: 16.8 us -> 27.3 us
    all_to_all x3 -> x1, blocking collectives: 63.4 us -> 35.9 us  [exchange(): return lax.all_to_all(x, axes, split_axis=0, concat_axis=0, tiled=True)]
    pallas_call x0 -> x3, Pallas kernels: none -> 12.3 us  [the longest x1 4.86 us: unpack_near(): pl.pallas_call(body, out_shape=(WIDE, WIDE), grid_spec=pltpu.PrefetchScal...]
    all_to_all x2 -> x4, waiting for transfers between devices: 21.9 us -> 11.2 us  [exchange(): return lax.all_to_all(x, axes, split_axis=0, concat_axis=0, tiled=True)]
    all_to_all x2 -> x4, starting transfers between devices: 6.94 us -> 17.3 us  [exchange(): return lax.all_to_all(x, axes, split_axis=0, concat_axis=0, tiled=True)]
    ppermute x20 -> x24, waiting for transfers between devices: 56.1 us -> 49.8 us  [flip(): return lax.ppermute(x, axes, [(i, n - 1 - i) for i in range(n)])]
    another operation x5 -> x1, other arithmetic: 6.12 us -> 1.28 us  [the longest x2 3.09 us: local(): new_kv = jnp.stack([new_kv[h][l] for h in (0, 1) for l in (0, 1)], axis=0)]
    ppermute x20 -> x24, starting transfers between devices: 43 us -> 44.6 us  [flip(): return lax.ppermute(x, axes, [(i, n - 1 - i) for i in range(n)])]
  transfers between devices with their start and end apart: 29 -> 35, of which waited for: 15 -> 17; matrix products, arithmetic and copies ran while one was open for 5% -> 9% of each run, Pallas kernels for 6% -> 10%
where the time goes in v6:
time: 246 us; the launch traced here: 243 us
  starting transfers between devices  67.8 us (28%)
  waiting for transfers between devices  64.5 us (26%)
  blocking collectives  35.9 us (15%)
  Pallas kernels  27.3 us (11%)
  other arithmetic  15.2 us (6%)
  between operations  14.4 us (6%)
  matrix products  10.5 us (4%)
  local copies, waits for them, and re-layouts  7.4 us (3%)
    ppermute x24, waiting for transfers between devices, flip(): return lax.ppermute(x, axes, [(i, n - 1 - i) for i in range(n)])  49.8 us
    ppermute x24, starting transfers between devices, flip(): return lax.ppermute(x, axes, [(i, n - 1 - i) for i in range(n)])  44.6 us
    all_to_all x1, blocking collectives, exchange(): return lax.all_to_all(x, axes, split_axis=0, concat_axis=0, tiled=True)  35.9 us
    all_to_all x4, starting transfers between devices, exchange(): return lax.all_to_all(x, axes, split_axis=0, concat_axis=0, tiled=True)  17.3 us
    pallas_call x1, Pallas kernels, project(): pl.pallas_call(body, out_shape=(jax.ShapeDtypeStruct((512, 3 * HD), jnp.f...  11.9 us
    all_to_all x4, waiting for transfers between devices, exchange(): return lax.all_to_all(x, axes, split_axis=0, concat_axis=0, tiled=True)  11.2 us
    dot_general x1, matrix products, local(): lax.dot_general(normed, scaled_q, contract, preferred_element_type=f32)  5.87 us
  transfers between devices with their start and end apart: 35, of which 17 were waited for; matrix products, arithmetic and copies ran while one was open for 9% of the time, Pallas kernels for 10%

profile of v6, /device:TPU:8, one launch (start us, length us, event | category | flops | bytes accessed | tf_op | source)
XLA Modules:
  0.0 243.0 jit_solution(17556242188335487286)
XLA Ops:
  7.2 1.1 fusion.31
  8.3 1.0 fusion.32
  11.2 3.1 %pack_columns.1 = bf16[32,128,128]{2,1,0:T(8,128)(2,1)} custom-call(s32[4]{0:T(128)} %pad_add_fusion.at_ref, bf16[128,8192]{1,0:T(8,128)(2,1)} %q_ref.1, bf16[128,1024]{1,0:T(8,128)(2,1)} %k_ref.1, bf16[128,1024]{1,0:T(8,128)(2,1)} %v_ref.1), custom_call_target="tpu_custom_call" | custom-call | tf_op jit(solution)/shard_map/pack_columns/pallas_call | solution.py:105
  14.3 35.9 %all_to_all.25.refs_0_ = bf16[32,128,128]{2,1,0:T(8,128)(2,1)S(1)} all-to-all(bf16[32,128,128]{2,1,0:T(8,128)(2,1)} %pack_columns.1), channel_id=1, replica_groups=mesh['xh'=2,'y'=4,'zh'=2,'zl'=4,'xl'=2,'core'=2] {'y','zh','zl'}, dimensions={0} | all-to-all | bytes 2097152 | tf_op jit(solution)/shard_map/all_to_all | solution.py:81
  50.3 8.2 %collective-permute-start.2 = (bf16[32,128,128]{2,1,0:T(8,128)(2,1)S(1)}, bf16[32,128,128]{2,1,0:T(8,128)(2,1)S(1)}, u32[]{:S(2)}, u32[]{:S(2)}) collective-permute-start(bf16[32,128,128]{2,1,0:T(8,128)(2,1)S(1)} %all_to_all.25.refs_0_), channel_id=1, source_target_pairs={{0,130},{2,128},{128,2},{130,0},{1,131},{3,129},{129,3},{131,1},{4... | collective-permute-start | bytes 3145736 | tf_op jit(solution)/shard_map/ppermute | solution.py:77
  58.5 22.6 %collective-permute-done.2.refs_2_ = bf16[32,128,128]{2,1,0:T(8,128)(2,1)S(1)} collective-permute-done((bf16[32,128,128]{2,1,0:T(8,128)(2,1)S(1)}, bf16[32,128,128]{2,1,0:T(8,128)(2,1)S(1)}, u32[]{:S(2)}, u32[]{:S(2)}) %collective-permute-start.2) | collective-permute-done | bytes 1048608 | tf_op jit(solution)/shard_map/ppermute | solution.py:77
  81.9 1.3 collective-permute-start.3
  84.7 1.3 collective-permute-start.4
  87.4 4.1 %collective-permute-start.5 = (bf16[32,128,128]{2,1,0:T(8,128)(2,1)S(1)}, bf16[32,128,128]{2,1,0:T(8,128)(2,1)}, u32[]{:S(2)}, u32[]{:S(2)}) collective-permute-start(bf16[32,128,128]{2,1,0:T(8,128)(2,1)S(1)} %all_to_all.25.refs_0_), channel_id=1, source_target_pairs={{0,1},{1,0},{2,3},{3,2},{4,5},{5,4},{6,7},{7,6},{8,9},{9,8},{10,11... | collective-permute-start | bytes 3145736 | tf_op jit(solution)/shard_map/ppermute | solution.py:77
  91.5 5.0 %collective-permute-start.6 = (bf16[32,128,128]{2,1,0:T(8,128)(2,1)S(1)}, bf16[32,128,128]{2,1,0:T(8,128)(2,1)}, u32[]{:S(2)}, u32[]{:S(2)}) collective-permute-start(bf16[32,128,128]{2,1,0:T(8,128)(2,1)S(1)} %collective-permute-done.1.refs_1_), channel_id=1, source_target_pairs={{0,1},{1,0},{2,3},{3,2},{4,5},{5,4},{6,7},{7,6},{8,9},{9,8},{10,11... | collective-permute-start | bytes 3145736 | tf_op jit(solution)/shard_map/ppermute | solution.py:77
  97.3 3.1 %collective-permute-done.4.refs_4_ = bf16[16,128,128]{2,1,0:T(8,128)(2,1)} collective-permute-done((bf16[16,128,128]{2,1,0:T(8,128)(2,1)}, bf16[16,128,128]{2,1,0:T(8,128)(2,1)}, u32[]{:S(2)}, u32[]{:S(2)}) %collective-permute-start.4) | collective-permute-done | bytes 524320 | tf_op jit(solution)/shard_map/ppermute | solution.py:77
  104.4 11.9 %project.1 = (f32[512,384]{1,0:T(8,128)}, bf16[32,2,2,64,128]{4,3,2,1,0:T(8,128)(2,1)}, bf16[32,2,2,2,32,256]{5,4,3,2,1,0:T(8,128)(2,1)}, bf16[512,1024]{1,0:T(8,128)(2,1)}) custom-call(s32[4]{0:T(128)} %pad_add_fusion.at_ref, bf16[512,8192]{1,0:T(8,128)(2,1)} %all-gather.2.cloned.1.call-done.rows_ref, bf16[32,128,128]{2,1,0:T(8,128)(2,1)} %copy-done, ...), custom_call_target="tpu_custom_call" | custom-call | tf_op jit(solution)/shard_map/project/pallas_call | solution.py:162
  116.3 1.2 broadcast_multiply_fusion
  117.5 1.3 fusion.38
  121.2 1.3 fusion.35
  122.9 0.9 fusion.9
  123.8 5.7 %all-to-all-start.1 = ((bf16[8,64,256]{2,1,0:T(8,128)(2,1)}), bf16[8,64,256]{2,1,0:T(8,128)(2,1)S(1)}, u32[]{:S(2)}, u32[]{:S(2)}) async-start(bf16[8,64,256]{2,1,0:T(8,128)(2,1)} %fusion.9), calls=%async_computation.1 | async-start | bytes 524288 | tf_op jit(solution)/shard_map/all_to_all | solution.py:81
  129.5 5.9 %convolution_convert_fusion = bf16[8192,128]{1,0:T(8,128)(2,1)S(1)} fusion(bf16[512,8192]{1,0:T(8,128)(2,1)} %all-gather.2.cloned.1.call-done.rows_ref, f32[512,64]{1,0:T(8,128)S(1)} %get-tuple-element.33, f32[512,64]{1,0:T(8,128)S(1)} %get-tuple-element.34), kind=kOutput, calls=%fused_computation | convolution fusion | flops 1074987008 | bytes 10747904 | tf_op jit(solution)/shard_map/dot_general | solution.py:318
  136.2 1.0 collective-permute-start.13
  137.4 1.8 all-to-all-done.1
  140.0 3.4 %all-to-all-start.2 = ((bf16[8,64,256]{2,1,0:T(8,128)(2,1)}), bf16[8,64,256]{2,1,0:T(8,128)(2,1)S(1)}, u32[]{:S(2)}, u32[]{:S(2)}) async-start(bf16[8,64,256]{2,1,0:T(8,128)(2,1)} %broadcast_in_dim.8), calls=%async_computation.2 | async-start | bytes 524288 | tf_op jit(solution)/shard_map/all_to_all | solution.py:81
  143.4 2.9 %collective-permute-done.13 = bf16[1024,128]{1,0:T(8,128)(2,1)S(1)} collective-permute-done((bf16[1024,128]{1,0:T(8,128)(2,1)}, bf16[1024,128]{1,0:T(8,128)(2,1)S(1)}, u32[]{:S(2)}, u32[]{:S(2)}) %collective-permute-start.13) | collective-permute-done | bytes 262176 | tf_op jit(solution)/shard_map/ppermute | solution.py:77
  146.3 1.8 fusion.11
  148.1 4.9 %all-to-all-done.2 = bf16[8,64,256]{2,1,0:T(8,128)(2,1)S(1)} async-done(((bf16[8,64,256]{2,1,0:T(8,128)(2,1)}), bf16[8,64,256]{2,1,0:T(8,128)(2,1)S(1)}, u32[]{:S(2)}, u32[]{:S(2)}) %all-to-all-start.2) | async-done | bytes 262176 | tf_op jit(solution)/shard_map/all_to_all | solution.py:81
  153.1 2.5 %convolution_convert_fusion.1 = bf16[1024,256]{1,0:T(8,128)(2,1)} fusion(bf16[512,1024]{1,0:T(8,128)(2,1)} %get-tuple-element.14, bf16[512,256]{1,0:T(8,128)(2,1)S(1)} %bitcast.60), kind=kOutput, calls=%fused_computation.2 | convolution fusion | flops 268697600 | bytes 1835008 | tf_op jit(solution)/shard_map/dot_general | solution.py:354
  155.6 4.7 %all-to-all-start.3 = ((bf16[4,256,256]{2,1,0:T(8,128)(2,1)}), bf16[4,256,256]{2,1,0:T(8,128)(2,1)S(1)}, u32[]{:S(2)}, u32[]{:S(2)}) async-start(bf16[4,256,256]{2,1,0:T(8,128)(2,1)} %bitcast.59), calls=%async_computation.3 | async-start | bytes 1048576 | tf_op jit(solution)/shard_map/all_to_all | solution.py:81
  160.3 1.8 pad_maximum_fusion
  162.0 2.0 collective-permute-start.14
  164.9 2.1 collective-permute-start.16
  167.9 3.3 %all-to-all-done.3 = bf16[4,256,256]{2,1,0:T(8,128)(2,1)S(1)} async-done(((bf16[4,256,256]{2,1,0:T(8,128)(2,1)}), bf16[4,256,256]{2,1,0:T(8,128)(2,1)S(1)}, u32[]{:S(2)}, u32[]{:S(2)}) %all-to-all-start.3) | async-done | bytes 524320 | tf_op jit(solution)/shard_map/all_to_all | solution.py:81
  172.1 3.5 %all-to-all-start.4 = ((bf16[4,256,256]{2,1,0:T(8,128)(2,1)}), bf16[4,256,256]{2,1,0:T(8,128)(2,1)S(1)}, u32[]{:S(2)}, u32[]{:S(2)}) async-start(bf16[4,256,256]{2,1,0:T(8,128)(2,1)} %broadcast_in_dim.9), calls=%async_computation.4 | async-start | bytes 1048576 | tf_op jit(solution)/shard_map/all_to_all | solution.py:81
  175.6 3.6 %collective-permute-done.14 = bf16[2048,128]{1,0:T(8,128)(2,1)} collective-permute-done((bf16[2048,128]{1,0:T(8,128)(2,1)}, bf16[2048,128]{1,0:T(8,128)(2,1)}, u32[]{:S(2)}, u32[]{:S(2)}) %collective-permute-start.14) | collective-permute-done | bytes 524320 | tf_op jit(solution)/shard_map/ppermute | solution.py:77
  179.2 1.4 collective-permute-done.16
  180.6 2.3 fusion.3
  182.9 1.7 collective-permute-start.17
  184.6 1.3 collective-permute-start.18
  185.9 1.2 all-to-all-done.4.refs_0_
  187.1 1.2 collective-permute-start.21
  188.3 10.2 %collective-permute-start.19 = (bf16[2048,128]{1,0:T(8,128)(2,1)S(1)}, bf16[2048,128]{1,0:T(8,128)(2,1)S(1)}, u32[]{:S(2)}, u32[]{:S(2)}) collective-permute-start(bf16[2048,128]{1,0:T(8,128)(2,1)S(1)} %collective-permute-done.17.near_ref), channel_id=1, source_target_pairs={{0,1},{1,0},{2,3},{3,2},{4,5},{5,4},{6,7},{7,6},{8,9},{9,8},{10,11... | collective-permute-start | bytes 1572872 | tf_op jit(solution)/shard_map/ppermute | solution.py:77
  198.5 2.6 %collective-permute-done.18.far_ref = bf16[2048,128]{1,0:T(8,128)(2,1)S(1)} collective-permute-done((bf16[2048,128]{1,0:T(8,128)(2,1)}, bf16[2048,128]{1,0:T(8,128)(2,1)S(1)}, u32[]{:S(2)}, u32[]{:S(2)}) %collective-permute-start.18) | collective-permute-done | bytes 524320 | tf_op jit(solution)/shard_map/ppermute | solution.py:339
  201.1 5.2 %collective-permute-start.20 = (bf16[2048,128]{1,0:T(8,128)(2,1)S(1)}, bf16[2048,128]{1,0:T(8,128)(2,1)S(1)}, u32[]{:S(2)}, u32[]{:S(2)}) collective-permute-start(bf16[2048,128]{1,0:T(8,128)(2,1)S(1)} %collective-permute-done.18.far_ref), channel_id=1, source_target_pairs={{0,1},{1,0},{2,3},{3,2},{4,5},{5,4},{6,7},{7,6},{8,9},{9,8},{10,11... | collective-permute-start | bytes 1572872 | tf_op jit(solution)/shard_map/ppermute | solution.py:77
  206.4 6.0 %collective-permute-done.21.refs_2_ = bf16[4,256,256]{2,1,0:T(8,128)(2,1)S(1)} collective-permute-done((bf16[4,256,256]{2,1,0:T(8,128)(2,1)S(1)}, bf16[4,256,256]{2,1,0:T(8,128)(2,1)S(1)}, u32[]{:S(2)}, u32[]{:S(2)}) %collective-permute-start.21) | collective-permute-done | bytes 524320 | tf_op jit(solution)/shard_map/ppermute | solution.py:77
  214.1 1.3 collective-permute-start.24
  215.4 3.5 %collective-permute-done.22.low_ref = bf16[2,256,256]{2,1,0:T(8,128)(2,1)S(1)} collective-permute-done((bf16[2,256,256]{2,1,0:T(8,128)(2,1)S(1)}, bf16[2,256,256]{2,1,0:T(8,128)(2,1)S(1)}, u32[]{:S(2)}, u32[]{:S(2)}) %collective-permute-start.22) | collective-permute-done | bytes 262176 | tf_op jit(solution)/shard_map/ppermute | solution.py:77
  218.9 4.8 %collective-permute-done.24.high_ref = bf16[2,256,256]{2,1,0:T(8,128)(2,1)} collective-permute-done((bf16[2,256,256]{2,1,0:T(8,128)(2,1)S(1)}, bf16[2,256,256]{2,1,0:T(8,128)(2,1)}, u32[]{:S(2)}, u32[]{:S(2)}) %collective-permute-start.24) | collective-permute-done | bytes 262176 | tf_op jit(solution)/shard_map/ppermute | solution.py:77
  223.7 4.5 %unpack_query.1 = bf16[2,2,2048,128]{3,2,1,0:T(8,128)(2,1)} custom-call(s32[4]{0:T(128)} %pad_add_fusion.at_ref, bf16[2048,128]{1,0:T(8,128)(2,1)} %copy-done.6, bf16[2048,128]{1,0:T(8,128)(2,1)} %copy-done.7, bf16[2048,128]{1,0:T(8,128)(2,1)} %copy-done.8, bf16[2048,128]{1,0:T(8,128)(2,1)} %copy-done.9), custom_call_target="tpu_custom_call" | custom-call | tf_op jit(solution)/shard_map/unpack_query/pallas_call | solution.py:196
  228.3 4.9 %unpack_near.1 = (bf16[2,2,2,4,2,128,128]{6,5,4,3,2,1,0:T(8,128)(2,1)}, bf16[2,2,2,4,2,128,128]{6,5,4,3,2,1,0:T(8,128)(2,1)}) custom-call(s32[4]{0:T(128)} %pad_add_fusion.at_ref, bf16[4,256,256]{2,1,0:T(8,128)(2,1)} %copy-done.3, bf16[4,256,256]{2,1,0:T(8,128)(2,1)} %copy-done.5, bf16[4,256,256]{2,1,0:T(8,128)(2,1)} %copy-done.4, ...), custom_call_target="tpu_custom_call" | custom-call | tf_op jit(solution)/shard_map/unpack_near/pallas_call | solution.py:231
  233.1 3.0 %unpack_far.1 = (bf16[2,2,2,4,2,128,128]{6,5,4,3,2,1,0:T(8,128)(2,1)}, bf16[2,2,2,4,2,128,128]{6,5,4,3,2,1,0:T(8,128)(2,1)}) custom-call(s32[4]{0:T(128)} %pad_add_fusion.at_ref, bf16[2,256,256]{2,1,0:T(8,128)(2,1)} %copy-done.12, bf16[2,256,256]{2,1,0:T(8,128)(2,1)} %collective-permute-done.24.high_ref, ...), custom_call_target="tpu_custom_call", output_to_operand_aliasing={{0}: (5, {}), {1}: (6, {})} | custom-call | tf_op jit(solution)/shard_map/unpack_far/pallas_call | solution.py:258
  (102 shorter events, 19.3 us)
Async XLA Ops:
  7.2 97.3 %all-gather.2.cloned.1.call-start = ((), (), s32[]{:S(2)}) async-start(), calls=%async_computation.5 | async-start | bytes 8519680 | tf_op jit(solution)/shard_map/all_gather | solution.py:287
  9.3 0.7 collective-permute-start
  14.3 71.7 %copy-start.15 = (s32[1,512]{1,0:T(1,128)S(1)}, s32[1,512]{1,0:T(1,128)}, u32[]{:S(2)}) copy-start(s32[1,512]{1,0:T(1,128)} %param.9) | copy-start | bytes 6148
  14.3 72.4 %copy-start.16 = (f32[1,8]{1,0:T(1,128)S(1)}, f32[1,8]{1,0:T(1,128)}, u32[]{:S(2)}) copy-start(f32[1,8]{1,0:T(1,128)} %param.10) | copy-start | bytes 100
  14.3 86.3 %copy-start.14 = (bf16[1,512,128]{2,1,0:T(8,128)(2,1)S(1)}, bf16[1,512,128]{2,1,0:T(8,128)(2,1)}, u32[]{:S(2)}) copy-start(bf16[1,512,128]{2,1,0:T(8,128)(2,1)} %param.8) | copy-start | bytes 393220
  50.3 54.2 %copy-start = (bf16[32,128,128]{2,1,0:T(8,128)(2,1)}, bf16[32,128,128]{2,1,0:T(8,128)(2,1)S(1)}, u32[]{:S(2)}) copy-start(bf16[32,128,128]{2,1,0:T(8,128)(2,1)S(1)} %all_to_all.25.refs_0_) | copy-start | bytes 3145732
  50.3 30.8 %collective-permute-start.2 = (bf16[32,128,128]{2,1,0:T(8,128)(2,1)S(1)}, bf16[32,128,128]{2,1,0:T(8,128)(2,1)S(1)}, u32[]{:S(2)}, u32[]{:S(2)}) collective-permute-start(bf16[32,128,128]{2,1,0:T(8,128)(2,1)S(1)} %all_to_all.25.refs_0_), channel_id=1, source_target_pairs={{0,130},{2,128},{128,2},{130,0},{1,131},{3,129},{129,3},{131,1},{4... | collective-permute-start | bytes 3145736 | tf_op jit(solution)/shard_map/ppermute | solution.py:77
  58.5 25.3 %collective-permute-start.1 = (bf16[32,128,128]{2,1,0:T(8,128)(2,1)S(1)}, bf16[32,128,128]{2,1,0:T(8,128)(2,1)S(1)}, u32[]{:S(2)}, u32[]{:S(2)}) collective-permute-start(bf16[32,128,128]{2,1,0:T(8,128)(2,1)S(1)} %all_to_all.25.refs_0_), channel_id=1, source_target_pairs={{0,2},{2,0},{1,3},{3,1},{4,6},{6,4},{5,7},{7,5},{8,10},{10,8},{9,1... | collective-permute-start | bytes 3145736 | tf_op jit(solution)/shard_map/ppermute | solution.py:77
  81.1 23.4 %copy-start.1 = (bf16[32,128,128]{2,1,0:T(8,128)(2,1)}, bf16[32,128,128]{2,1,0:T(8,128)(2,1)S(1)}, u32[]{:S(2)}) copy-start(bf16[32,128,128]{2,1,0:T(8,128)(2,1)S(1)} %collective-permute-done.2.refs_2_) | copy-start | bytes 3145732
  81.9 14.8 %collective-permute-start.3 = (bf16[16,128,128]{2,1,0:T(8,128)(2,1)}, bf16[16,128,128]{2,1,0:T(8,128)(2,1)}, u32[]{:S(2)}, u32[]{:S(2)}) collective-permute-start(bf16[16,128,128]{2,1,0:T(8,128)(2,1)} %slice.109), channel_id=1, source_target_pairs={{0,2},{2,0},{1,3},{3,1},{4,6},{6,4},{5,7},{7,5},{8,10},{10,8},{9,1... | collective-permute-start | bytes 1572872 | tf_op jit(solution)/shard_map/ppermute | solution.py:77
  83.8 20.6 %copy-start.2 = (bf16[32,128,128]{2,1,0:T(8,128)(2,1)}, bf16[32,128,128]{2,1,0:T(8,128)(2,1)S(1)}, u32[]{:S(2)}) copy-start(bf16[32,128,128]{2,1,0:T(8,128)(2,1)S(1)} %collective-permute-done.1.refs_1_) | copy-start | bytes 3145732
  84.7 15.6 %collective-permute-start.4 = (bf16[16,128,128]{2,1,0:T(8,128)(2,1)}, bf16[16,128,128]{2,1,0:T(8,128)(2,1)}, u32[]{:S(2)}, u32[]{:S(2)}) collective-permute-start(bf16[16,128,128]{2,1,0:T(8,128)(2,1)} %slice.110), channel_id=1, source_target_pairs={{0,130},{2,128},{128,2},{130,0},{1,131},{3,129},{129,3},{131,1},{4... | collective-permute-start | bytes 1572872 | tf_op jit(solution)/shard_map/ppermute | solution.py:77
  86.0 10.5 %collective-permute-start.10 = (s32[512]{0:T(512)S(1)}, s32[512]{0:T(512)S(1)}, u32[]{:S(2)}, u32[]{:S(2)}) collective-permute-start(s32[512]{0:T(512)S(1)} %bitcast.65), channel_id=1, source_target_pairs={{0,0},{1,2},{2,1},{3,3},{4,4},{5,6},{6,5},{7,7},{8,8},{9,10},{10,9... | collective-permute-start | bytes 6152 | tf_op jit(solution)/shard_map/ppermute | solution.py:72
  86.7 4.8 %collective-permute-start.12 = (f32[8]{0:T(128)S(1)}, f32[8]{0:T(128)S(1)}, u32[]{:S(2)}, u32[]{:S(2)}) collective-permute-start(f32[8]{0:T(128)S(1)} %bitcast.66), channel_id=1, source_target_pairs={{0,0},{1,2},{2,1},{3,3},{4,4},{5,6},{6,5},{7,7},{8,8},{9,10},{10,9... | collective-permute-start | bytes 104 | tf_op jit(solution)/shard_map/ppermute | solution.py:72
  87.4 13.3 %collective-permute-start.5 = (bf16[32,128,128]{2,1,0:T(8,128)(2,1)S(1)}, bf16[32,128,128]{2,1,0:T(8,128)(2,1)}, u32[]{:S(2)}, u32[]{:S(2)}) collective-permute-start(bf16[32,128,128]{2,1,0:T(8,128)(2,1)S(1)} %all_to_all.25.refs_0_), channel_id=1, source_target_pairs={{0,1},{1,0},{2,3},{3,2},{4,5},{5,4},{6,7},{7,6},{8,9},{9,8},{10,11... | collective-permute-start | bytes 3145736 | tf_op jit(solution)/shard_map/ppermute | solution.py:77
  91.5 11.3 %collective-permute-start.6 = (bf16[32,128,128]{2,1,0:T(8,128)(2,1)S(1)}, bf16[32,128,128]{2,1,0:T(8,128)(2,1)}, u32[]{:S(2)}, u32[]{:S(2)}) collective-permute-start(bf16[32,128,128]{2,1,0:T(8,128)(2,1)S(1)} %collective-permute-done.1.refs_1_), channel_id=1, source_target_pairs={{0,1},{1,0},{2,3},{3,2},{4,5},{5,4},{6,7},{7,6},{8,9},{9,8},{10,11... | collective-permute-start | bytes 3145736 | tf_op jit(solution)/shard_map/ppermute | solution.py:77
  96.5 7.1 %collective-permute-start.7 = (bf16[32,128,128]{2,1,0:T(8,128)(2,1)S(1)}, bf16[32,128,128]{2,1,0:T(8,128)(2,1)}, u32[]{:S(2)}, u32[]{:S(2)}) collective-permute-start(bf16[32,128,128]{2,1,0:T(8,128)(2,1)S(1)} %collective-permute-done.2.refs_2_), channel_id=1, source_target_pairs={{0,1},{1,0},{2,3},{3,2},{4,5},{5,4},{6,7},{7,6},{8,9},{9,8},{10,11... | collective-permute-start | bytes 3145736 | tf_op jit(solution)/shard_map/ppermute | solution.py:77
  96.7 5.3 %collective-permute-start.8 = (bf16[16,128,128]{2,1,0:T(8,128)(2,1)}, bf16[16,128,128]{2,1,0:T(8,128)(2,1)S(1)}, u32[]{:S(2)}, u32[]{:S(2)}) collective-permute-start(bf16[16,128,128]{2,1,0:T(8,128)(2,1)} %collective-permute-done.3.refs_3_), channel_id=1, source_target_pairs={{0,1},{1,0},{2,3},{3,2},{4,5},{5,4},{6,7},{7,6},{8,9},{9,8},{10,11... | collective-permute-start | bytes 1572872 | tf_op jit(solution)/shard_map/ppermute | solution.py:77
  100.3 2.5 %collective-permute-start.9 = (bf16[16,128,128]{2,1,0:T(8,128)(2,1)}, bf16[16,128,128]{2,1,0:T(8,128)(2,1)S(1)}, u32[]{:S(2)}, u32[]{:S(2)}) collective-permute-start(bf16[16,128,128]{2,1,0:T(8,128)(2,1)} %collective-permute-done.4.refs_4_), channel_id=1, source_target_pairs={{0,1},{1,0},{2,3},{3,2},{4,5},{5,4},{6,7},{7,6},{8,9},{9,8},{10,11... | collective-permute-start | bytes 1572872 | tf_op jit(solution)/shard_map/ppermute | solution.py:77
  100.7 18.9 %collective-permute-start.11 = (bf16[512,128]{1,0:T(8,128)(2,1)S(1)}, bf16[512,128]{1,0:T(8,128)(2,1)S(1)}, u32[]{:S(2)}, u32[]{:S(2)}) collective-permute-start(bf16[512,128]{1,0:T(8,128)(2,1)S(1)} %bitcast.64), channel_id=1, source_target_pairs={{0,0},{1,2},{2,1},{3,3},{4,4},{5,6},{6,5},{7,7},{8,8},{9,10},{10,9... | collective-permute-start | bytes 393224 | tf_op jit(solution)/shard_map/ppermute | solution.py:72
  123.8 15.5 %all-to-all-start.1 = ((bf16[8,64,256]{2,1,0:T(8,128)(2,1)}), bf16[8,64,256]{2,1,0:T(8,128)(2,1)S(1)}, u32[]{:S(2)}, u32[]{:S(2)}) async-start(bf16[8,64,256]{2,1,0:T(8,128)(2,1)} %fusion.9), calls=%async_computation.1 | async-start | bytes 524288 | tf_op jit(solution)/shard_map/all_to_all | solution.py:81
  136.2 10.1 %collective-permute-start.13 = (bf16[1024,128]{1,0:T(8,128)(2,1)}, bf16[1024,128]{1,0:T(8,128)(2,1)S(1)}, u32[]{:S(2)}, u32[]{:S(2)}) collective-permute-start(bf16[1024,128]{1,0:T(8,128)(2,1)} %get-tuple-element.21), channel_id=1, source_target_pairs={{0,130},{2,128},{128,2},{130,0},{1,131},{3,129},{129,3},{131,1},{4... | collective-permute-start | bytes 786440 | tf_op jit(solution)/shard_map/ppermute | solution.py:77
  137.2 9.2 %collective-permute-start.15 = (bf16[1024,128]{1,0:T(8,128)(2,1)S(1)}, bf16[1024,128]{1,0:T(8,128)(2,1)}, u32[]{:S(2)}, u32[]{:S(2)}) collective-permute-start(bf16[1024,128]{1,0:T(8,128)(2,1)S(1)} %get-tuple-element.23), channel_id=1, source_target_pairs={{0,2},{2,0},{1,3},{3,1},{4,6},{6,4},{5,7},{7,5},{8,10},{10,8},{9,1... | collective-permute-start | bytes 786440 | tf_op jit(solution)/shard_map/ppermute | solution.py:77
  140.0 13.1 %all-to-all-start.2 = ((bf16[8,64,256]{2,1,0:T(8,128)(2,1)}), bf16[8,64,256]{2,1,0:T(8,128)(2,1)S(1)}, u32[]{:S(2)}, u32[]{:S(2)}) async-start(bf16[8,64,256]{2,1,0:T(8,128)(2,1)} %broadcast_in_dim.8), calls=%async_computation.2 | async-start | bytes 524288 | tf_op jit(solution)/shard_map/all_to_all | solution.py:81
  155.6 15.6 %all-to-all-start.3 = ((bf16[4,256,256]{2,1,0:T(8,128)(2,1)}), bf16[4,256,256]{2,1,0:T(8,128)(2,1)S(1)}, u32[]{:S(2)}, u32[]{:S(2)}) async-start(bf16[4,256,256]{2,1,0:T(8,128)(2,1)} %bitcast.59), calls=%async_computation.3 | async-start | bytes 1048576 | tf_op jit(solution)/shard_map/all_to_all | solution.py:81
  162.0 17.2 %collective-permute-start.14 = (bf16[2048,128]{1,0:T(8,128)(2,1)}, bf16[2048,128]{1,0:T(8,128)(2,1)}, u32[]{:S(2)}, u32[]{:S(2)}) collective-permute-start(bf16[2048,128]{1,0:T(8,128)(2,1)} %pad_maximum_fusion), channel_id=1, source_target_pairs={{0,2},{2,0},{1,3},{3,1},{4,6},{6,4},{5,7},{7,5},{8,10},{10,8},{9,1... | collective-permute-start | bytes 1572872 | tf_op jit(solution)/shard_map/ppermute | solution.py:77
  164.9 15.7 %collective-permute-start.16 = (bf16[2048,128]{1,0:T(8,128)(2,1)}, bf16[2048,128]{1,0:T(8,128)(2,1)S(1)}, u32[]{:S(2)}, u32[]{:S(2)}) collective-permute-start(bf16[2048,128]{1,0:T(8,128)(2,1)} %pad_maximum_fusion.1), channel_id=1, source_target_pairs={{0,130},{2,128},{128,2},{130,0},{1,131},{3,129},{129,3},{131,1},{4... | collective-permute-start | bytes 1572872 | tf_op jit(solution)/shard_map/ppermute | solution.py:77
  172.1 15.0 %all-to-all-start.4 = ((bf16[4,256,256]{2,1,0:T(8,128)(2,1)}), bf16[4,256,256]{2,1,0:T(8,128)(2,1)S(1)}, u32[]{:S(2)}, u32[]{:S(2)}) async-start(bf16[4,256,256]{2,1,0:T(8,128)(2,1)} %broadcast_in_dim.9), calls=%async_computation.4 | async-start | bytes 1048576 | tf_op jit(solution)/shard_map/all_to_all | solution.py:81
  182.9 5.3 %collective-permute-start.17 = (bf16[2048,128]{1,0:T(8,128)(2,1)}, bf16[2048,128]{1,0:T(8,128)(2,1)S(1)}, u32[]{:S(2)}, u32[]{:S(2)}) collective-permute-start(bf16[2048,128]{1,0:T(8,128)(2,1)} %fusion.3), channel_id=1, source_target_pairs={{0,0},{1,2},{2,1},{3,3},{4,4},{5,6},{6,5},{7,7},{8,8},{9,10},{10,9... | collective-permute-start | bytes 1572872 | tf_op jit(solution)/shard_map/ppermute | solution.py:72
  184.6 16.5 %collective-permute-start.18 = (bf16[2048,128]{1,0:T(8,128)(2,1)}, bf16[2048,128]{1,0:T(8,128)(2,1)S(1)}, u32[]{:S(2)}, u32[]{:S(2)}) collective-permute-start(bf16[2048,128]{1,0:T(8,128)(2,1)} %fusion.3), channel_id=1, source_target_pairs={{0,128},{1,130},{2,129},{3,131},{128,0},{129,2},{130,1},{131,3},{4... | collective-permute-start | bytes 1572872 | tf_op jit(solution)/shard_map/ppermute | solution.py:339
  187.1 41.1 %copy-start.3 = (bf16[4,256,256]{2,1,0:T(8,128)(2,1)}, bf16[4,256,256]{2,1,0:T(8,128)(2,1)S(1)}, u32[]{:S(2)}) copy-start(bf16[4,256,256]{2,1,0:T(8,128)(2,1)S(1)} %all-to-all-done.4.refs_0_) | copy-start | bytes 1572868
  187.1 25.3 %collective-permute-start.21 = (bf16[4,256,256]{2,1,0:T(8,128)(2,1)S(1)}, bf16[4,256,256]{2,1,0:T(8,128)(2,1)S(1)}, u32[]{:S(2)}, u32[]{:S(2)}) collective-permute-start(bf16[4,256,256]{2,1,0:T(8,128)(2,1)S(1)} %all-to-all-done.4.refs_0_), channel_id=1, source_target_pairs={{0,130},{2,128},{128,2},{130,0},{1,131},{3,129},{129,3},{131,1},{4... | collective-permute-start | bytes 1572872 | tf_op jit(solution)/shard_map/ppermute | solution.py:77
  188.2 24.3 %collective-permute-start.23 = (bf16[4,256,256]{2,1,0:T(8,128)(2,1)S(1)}, bf16[4,256,256]{2,1,0:T(8,128)(2,1)S(1)}, u32[]{:S(2)}, u32[]{:S(2)}) collective-permute-start(bf16[4,256,256]{2,1,0:T(8,128)(2,1)S(1)} %all-to-all-done.4.refs_0_), channel_id=1, source_target_pairs={{0,2},{2,0},{1,3},{3,1},{4,6},{6,4},{5,7},{7,5},{8,10},{10,8},{9,1... | collective-permute-start | bytes 1572872 | tf_op jit(solution)/shard_map/ppermute | solution.py:77
  188.3 35.5 %copy-start.6 = (bf16[2048,128]{1,0:T(8,128)(2,1)}, bf16[2048,128]{1,0:T(8,128)(2,1)S(1)}, u32[]{:S(2)}) copy-start(bf16[2048,128]{1,0:T(8,128)(2,1)S(1)} %collective-permute-done.17.near_ref) | copy-start | bytes 1572868
  188.3 24.4 %collective-permute-start.19 = (bf16[2048,128]{1,0:T(8,128)(2,1)S(1)}, bf16[2048,128]{1,0:T(8,128)(2,1)S(1)}, u32[]{:S(2)}, u32[]{:S(2)}) collective-permute-start(bf16[2048,128]{1,0:T(8,128)(2,1)S(1)} %collective-permute-done.17.near_ref), channel_id=1, source_target_pairs={{0,1},{1,0},{2,3},{3,2},{4,5},{5,4},{6,7},{7,6},{8,9},{9,8},{10,11... | collective-permute-start | bytes 1572872 | tf_op jit(solution)/shard_map/ppermute | solution.py:77
  201.1 22.6 %copy-start.7 = (bf16[2048,128]{1,0:T(8,128)(2,1)}, bf16[2048,128]{1,0:T(8,128)(2,1)S(1)}, u32[]{:S(2)}) copy-start(bf16[2048,128]{1,0:T(8,128)(2,1)S(1)} %collective-permute-done.18.far_ref) | copy-start | bytes 1572868
  201.1 12.1 %collective-permute-start.20 = (bf16[2048,128]{1,0:T(8,128)(2,1)S(1)}, bf16[2048,128]{1,0:T(8,128)(2,1)S(1)}, u32[]{:S(2)}, u32[]{:S(2)}) collective-permute-start(bf16[2048,128]{1,0:T(8,128)(2,1)S(1)} %collective-permute-done.18.far_ref), channel_id=1, source_target_pairs={{0,1},{1,0},{2,3},{3,2},{4,5},{5,4},{6,7},{7,6},{8,9},{9,8},{10,11... | collective-permute-start | bytes 1572872 | tf_op jit(solution)/shard_map/ppermute | solution.py:77
  206.3 21.9 %collective-permute-start.27 = (bf16[4,256,256]{2,1,0:T(8,128)(2,1)S(1)}, bf16[4,256,256]{2,1,0:T(8,128)(2,1)}, u32[]{:S(2)}, u32[]{:S(2)}) collective-permute-start(bf16[4,256,256]{2,1,0:T(8,128)(2,1)S(1)} %all-to-all-done.4.refs_0_), channel_id=1, source_target_pairs={{0,1},{1,0},{2,3},{3,2},{4,5},{5,4},{6,7},{7,6},{8,9},{9,8},{10,11... | collective-permute-start | bytes 1572872 | tf_op jit(solution)/shard_map/ppermute | solution.py:77
  212.4 15.8 %copy-start.4 = (bf16[4,256,256]{2,1,0:T(8,128)(2,1)}, bf16[4,256,256]{2,1,0:T(8,128)(2,1)S(1)}, u32[]{:S(2)}) copy-start(bf16[4,256,256]{2,1,0:T(8,128)(2,1)S(1)} %collective-permute-done.21.refs_2_) | copy-start | bytes 1572868
  212.4 6.5 %collective-permute-start.22 = (bf16[2,256,256]{2,1,0:T(8,128)(2,1)S(1)}, bf16[2,256,256]{2,1,0:T(8,128)(2,1)S(1)}, u32[]{:S(2)}, u32[]{:S(2)}) collective-permute-start(bf16[2,256,256]{2,1,0:T(8,128)(2,1)S(1)} %slice.121), channel_id=1, source_target_pairs={{0,2},{2,0},{1,3},{3,1},{4,6},{6,4},{5,7},{7,5},{8,10},{10,8},{9,1... | collective-permute-start | bytes 786440 | tf_op jit(solution)/shard_map/ppermute | solution.py:77
  212.5 15.7 %copy-start.5 = (bf16[4,256,256]{2,1,0:T(8,128)(2,1)}, bf16[4,256,256]{2,1,0:T(8,128)(2,1)S(1)}, u32[]{:S(2)}) copy-start(bf16[4,256,256]{2,1,0:T(8,128)(2,1)S(1)} %collective-permute-done.23.refs_1_) | copy-start | bytes 1572868
  212.5 15.7 %collective-permute-start.28 = (bf16[4,256,256]{2,1,0:T(8,128)(2,1)S(1)}, bf16[4,256,256]{2,1,0:T(8,128)(2,1)}, u32[]{:S(2)}, u32[]{:S(2)}) collective-permute-start(bf16[4,256,256]{2,1,0:T(8,128)(2,1)S(1)} %collective-permute-done.23.refs_1_), channel_id=1, source_target_pairs={{0,1},{1,0},{2,3},{3,2},{4,5},{5,4},{6,7},{7,6},{8,9},{9,8},{10,11... | collective-permute-start | bytes 1572872 | tf_op jit(solution)/shard_map/ppermute | solution.py:77
  212.7 11.0 %copy-start.8 = (bf16[2048,128]{1,0:T(8,128)(2,1)}, bf16[2048,128]{1,0:T(8,128)(2,1)S(1)}, u32[]{:S(2)}) copy-start(bf16[2048,128]{1,0:T(8,128)(2,1)S(1)} %collective-permute-done.19.near_other_ref) | copy-start | bytes 1572868
  212.7 15.6 %collective-permute-start.29 = (bf16[4,256,256]{2,1,0:T(8,128)(2,1)S(1)}, bf16[4,256,256]{2,1,0:T(8,128)(2,1)}, u32[]{:S(2)}, u32[]{:S(2)}) collective-permute-start(bf16[4,256,256]{2,1,0:T(8,128)(2,1)S(1)} %collective-permute-done.21.refs_2_), channel_id=1, source_target_pairs={{0,1},{1,0},{2,3},{3,2},{4,5},{5,4},{6,7},{7,6},{8,9},{9,8},{10,11... | collective-permute-start | bytes 1572872 | tf_op jit(solution)/shard_map/ppermute | solution.py:77
  214.1 9.6 %collective-permute-start.24 = (bf16[2,256,256]{2,1,0:T(8,128)(2,1)S(1)}, bf16[2,256,256]{2,1,0:T(8,128)(2,1)}, u32[]{:S(2)}, u32[]{:S(2)}) collective-permute-start(bf16[2,256,256]{2,1,0:T(8,128)(2,1)S(1)} %slice.122), channel_id=1, source_target_pairs={{0,130},{2,128},{128,2},{130,0},{1,131},{3,129},{129,3},{131,1},{4... | collective-permute-start | bytes 786440 | tf_op jit(solution)/shard_map/ppermute | solution.py:77
  218.9 9.4 %copy-start.12 = (bf16[2,256,256]{2,1,0:T(8,128)(2,1)}, bf16[2,256,256]{2,1,0:T(8,128)(2,1)S(1)}, u32[]{:S(2)}) copy-start(bf16[2,256,256]{2,1,0:T(8,128)(2,1)S(1)} %collective-permute-done.22.low_ref) | copy-start | bytes 786436
  218.9 14.3 %collective-permute-start.25 = (bf16[2,256,256]{2,1,0:T(8,128)(2,1)S(1)}, bf16[2,256,256]{2,1,0:T(8,128)(2,1)}, u32[]{:S(2)}, u32[]{:S(2)}) collective-permute-start(bf16[2,256,256]{2,1,0:T(8,128)(2,1)S(1)} %collective-permute-done.22.low_ref), channel_id=1, source_target_pairs={{0,1},{1,0},{2,3},{3,2},{4,5},{5,4},{6,7},{7,6},{8,9},{9,8},{10,11... | collective-permute-start | bytes 786440 | tf_op jit(solution)/shard_map/ppermute | solution.py:77
  223.7 9.4 %collective-permute-start.26 = (bf16[2,256,256]{2,1,0:T(8,128)(2,1)}, bf16[2,256,256]{2,1,0:T(8,128)(2,1)}, u32[]{:S(2)}, u32[]{:S(2)}) collective-permute-start(bf16[2,256,256]{2,1,0:T(8,128)(2,1)} %collective-permute-done.24.high_ref), channel_id=1, source_target_pairs={{0,1},{1,0},{2,3},{3,2},{4,5},{5,4},{6,7},{7,6},{8,9},{9,8},{10,11... | collective-permute-start | bytes 786440 | tf_op jit(solution)/shard_map/ppermute | solution.py:77
  (4 other events, 3.1 us)
Sparse Core Ops, SparseCore 0:
  10.8 93.5 all-gather.1

commit v7 on v4

--- a/solution.py
+++ b/solution.py
@@ -134,8 +134,8 @@
             wq_ref[:, l, h] = own[:, :64]
             wkv_ref[:, l, h, core, :, 0:HD] = own[:, 64:96]
             wkv_ref[:, l, h, core, :, HD : 2 * HD] = own[:, 96:128]
-            wkv_ref[:, l, h, 1 - core, :, 0:HD] = other[:, 0:32]
-            wkv_ref[:, l, h, 1 - core, :, HD : 2 * HD] = other[:, 32:64]
+            wkv_ref[:, l, h, 1 - core, :, 0:HD] = other[:, 64:96]
+            wkv_ref[:, l, h, 1 - core, :, HD : 2 * HD] = other[:, 96:128]
 
         rows = rows_ref[...]
         for n in (0, 1):
@@ -154,16 +154,10 @@
             rows, wkv_ref[...].reshape(2048, 2 * HD), preferred_element_type=jnp.float32
         )
 
-        @pl.when(b == 3)
-        def _():
-            out_ref[...] *= D ** (-0.5)
-
-    def group(rows, at_row):
-        whole = pl.BlockSpec((8, rows, HD), lambda b, at: (b, at_row, 0))
-        first = pl.BlockSpec((8, rows, HD), lambda b, at: (jnp.minimum(b, 1), at_row, 0))
-        last = pl.BlockSpec((8, rows, HD), lambda b, at: (jnp.maximum(b, 2) - 2, at_row, 0))
-        return [whole, whole, whole, first, last]
-
+    whole = pl.BlockSpec((8, 128, HD), lambda b, at: (b, 0, 0))
+    first = pl.BlockSpec((8, 128, HD), lambda b, at: (jnp.minimum(b, 1), 0, 0))
+    last = pl.BlockSpec((8, 128, HD), lambda b, at: (jnp.maximum(b, 2) - 2, 0, 0))
+    group = [whole, whole, whole, first, last]
     bf16 = jnp.bfloat16
     return pl.pallas_call(
         body,
@@ -176,9 +170,7 @@
         grid_spec=pltpu.PrefetchScalarGridSpec(
             num_scalar_prefetch=1,
             grid=(4,),
-            in_specs=[pl.BlockSpec((512, 2048), lambda b, at: (0, b))]
-            + group(128, 0)
-            + group(64, 1),
+            in_specs=[pl.BlockSpec((512, 2048), lambda b, at: (0, b))] + group + group,
             out_specs=(
                 pl.BlockSpec((512, 3 * HD), lambda b, at: (0, 0)),
                 pl.BlockSpec((8, 2, 2, 64, HD), lambda b, at: (b, 0, 0, 0, 0)),
@@ -266,6 +258,7 @@
     pieces = (cut,) + ring_pieces(cut)
     others = tuple(flip(p, ("core",)) for p in pieces)
     projected, q_cols, wkv, normed_m = project(normed, pieces, others, at)
+    projected = projected * inv_width
     q_cols = q_cols.reshape(D, HD)
 
     cosine_table, sine_table = angles(seg_row)

time: 241 us -> 240 us (level)
  transfers between devices with their start and end apart: 35 -> 35, of which waited for: 19 -> 19; matrix products, arithmetic and copies ran while one was open for 9% -> 9% of each run, Pallas kernels for 7% -> 6%
where the time goes in v7:
time: 240 us; the launch traced here: 237 us
  starting transfers between devices  68.1 us (28%)
  waiting for transfers between devices  63 us (26%)
  blocking collectives  36 us (15%)
  Pallas kernels  21.6 us (9%)
  other arithmetic  15.3 us (6%)
  between operations  14.4 us (6%)
  matrix products  10.5 us (4%)
  local copies, waits for them, and re-layouts  8.04 us (3%)
    ppermute x24, waiting for transfers between devices, flip(): return lax.ppermute(x, axes, [(i, n - 1 - i) for i in range(n)])  48.3 us
    ppermute x24, starting transfers between devices, flip(): return lax.ppermute(x, axes, [(i, n - 1 - i) for i in range(n)])  44.9 us
    all_to_all x1, blocking collectives, exchange(): return lax.all_to_all(x, axes, split_axis=0, concat_axis=0, tiled=True)  36 us
    all_to_all x4, starting transfers between devices, exchange(): return lax.all_to_all(x, axes, split_axis=0, concat_axis=0, tiled=True)  17.4 us
    pallas_call x1, Pallas kernels, project(): pl.pallas_call(body, out_shape=(jax.ShapeDtypeStruct((512, 3 * HD), jnp.f...  11.8 us
    all_to_all x4, waiting for transfers between devices, exchange(): return lax.all_to_all(x, axes, split_axis=0, concat_axis=0, tiled=True)  11.2 us
    pallas_call x1, Pallas kernels, unpack(): pl.pallas_call(body, out_shape=(jax.ShapeDtypeStruct((2, 2, 2048, HD), bf...  6.67 us
    dot_general x1, matrix products, local(): lax.dot_general(normed, scaled_q, contract, preferred_element_type=f32)  5.88 us
  transfers between devices with their start and end apart: 35, of which 19 were waited for; matrix products, arithmetic and copies ran while one was open for 9% of the time, Pallas kernels for 6%

profile of v7, /device:TPU:8, one launch (start us, length us, event | category | flops | bytes accessed | tf_op | source)
XLA Modules:
  0.0 236.9 jit_solution(2702079327091085069)
XLA Ops:
  7.2 1.1 fusion.31
  8.3 1.0 fusion.32
  11.3 3.1 %pack_columns.1 = bf16[32,128,128]{2,1,0:T(8,128)(2,1)} custom-call(s32[4]{0:T(128)} %pad_add_fusion.at_ref, bf16[128,8192]{1,0:T(8,128)(2,1)} %q_ref.1, bf16[128,1024]{1,0:T(8,128)(2,1)} %k_ref.1, bf16[128,1024]{1,0:T(8,128)(2,1)} %v_ref.1), custom_call_target="tpu_custom_call" | custom-call | tf_op jit(solution)/shard_map/pack_columns/pallas_call | solution.py:105
  14.4 36.0 %all_to_all.25.refs_0_ = bf16[32,128,128]{2,1,0:T(8,128)(2,1)S(1)} all-to-all(bf16[32,128,128]{2,1,0:T(8,128)(2,1)} %pack_columns.1), channel_id=1, replica_groups=mesh['xh'=2,'y'=4,'zh'=2,'zl'=4,'xl'=2,'core'=2] {'y','zh','zl'}, dimensions={0} | all-to-all | bytes 2097152 | tf_op jit(solution)/shard_map/all_to_all | solution.py:81
  50.4 8.1 %collective-permute-start.2 = (bf16[32,128,128]{2,1,0:T(8,128)(2,1)S(1)}, bf16[32,128,128]{2,1,0:T(8,128)(2,1)S(1)}, u32[]{:S(2)}, u32[]{:S(2)}) collective-permute-start(bf16[32,128,128]{2,1,0:T(8,128)(2,1)S(1)} %all_to_all.25.refs_0_), channel_id=1, source_target_pairs={{0,130},{2,128},{128,2},{130,0},{1,131},{3,129},{129,3},{131,1},{4... | collective-permute-start | bytes 3145736 | tf_op jit(solution)/shard_map/ppermute | solution.py:77
  58.5 22.5 %collective-permute-done.2.refs_2_ = bf16[32,128,128]{2,1,0:T(8,128)(2,1)S(1)} collective-permute-done((bf16[32,128,128]{2,1,0:T(8,128)(2,1)S(1)}, bf16[32,128,128]{2,1,0:T(8,128)(2,1)S(1)}, u32[]{:S(2)}, u32[]{:S(2)}) %collective-permute-start.2) | collective-permute-done | bytes 1048608 | tf_op jit(solution)/shard_map/ppermute | solution.py:77
  81.8 1.8 collective-permute-start.3
  84.0 0.9 slice.110
  84.9 1.6 collective-permute-start.4
  87.8 4.1 %collective-permute-start.5 = (bf16[32,128,128]{2,1,0:T(8,128)(2,1)S(1)}, bf16[32,128,128]{2,1,0:T(8,128)(2,1)}, u32[]{:S(2)}, u32[]{:S(2)}) collective-permute-start(bf16[32,128,128]{2,1,0:T(8,128)(2,1)S(1)} %all_to_all.25.refs_0_), channel_id=1, source_target_pairs={{0,1},{1,0},{2,3},{3,2},{4,5},{5,4},{6,7},{7,6},{8,9},{9,8},{10,11... | collective-permute-start | bytes 3145736 | tf_op jit(solution)/shard_map/ppermute | solution.py:77
  91.9 4.5 %collective-permute-start.6 = (bf16[32,128,128]{2,1,0:T(8,128)(2,1)S(1)}, bf16[32,128,128]{2,1,0:T(8,128)(2,1)}, u32[]{:S(2)}, u32[]{:S(2)}) collective-permute-start(bf16[32,128,128]{2,1,0:T(8,128)(2,1)S(1)} %collective-permute-done.1.refs_1_), channel_id=1, source_target_pairs={{0,1},{1,0},{2,3},{3,2},{4,5},{5,4},{6,7},{7,6},{8,9},{9,8},{10,11... | collective-permute-start | bytes 3145736 | tf_op jit(solution)/shard_map/ppermute | solution.py:77
  97.1 3.5 %collective-permute-done.4.refs_4_ = bf16[16,128,128]{2,1,0:T(8,128)(2,1)} collective-permute-done((bf16[16,128,128]{2,1,0:T(8,128)(2,1)}, bf16[16,128,128]{2,1,0:T(8,128)(2,1)}, u32[]{:S(2)}, u32[]{:S(2)}) %collective-permute-start.4) | collective-permute-done | bytes 524320 | tf_op jit(solution)/shard_map/ppermute | solution.py:77
  104.3 11.8 %project.1 = (f32[512,384]{1,0:T(8,128)}, bf16[32,2,2,64,128]{4,3,2,1,0:T(8,128)(2,1)}, bf16[32,2,2,2,32,256]{5,4,3,2,1,0:T(8,128)(2,1)}, bf16[512,1024]{1,0:T(8,128)(2,1)}) custom-call(s32[4]{0:T(128)} %pad_add_fusion.at_ref, bf16[512,8192]{1,0:T(8,128)(2,1)} %all-gather.2.cloned.1.call-done.rows_ref, bf16[32,128,128]{2,1,0:T(8,128)(2,1)} %copy-done, ...), custom_call_target="tpu_custom_call" | custom-call | tf_op jit(solution)/shard_map/project/pallas_call | solution.py:162
  116.2 1.2 broadcast_multiply_fusion
  117.4 1.3 fusion.38
  121.0 1.3 fusion.35
  122.7 0.9 fusion.9
  123.7 5.9 %all-to-all-start.1 = ((bf16[8,64,256]{2,1,0:T(8,128)(2,1)}), bf16[8,64,256]{2,1,0:T(8,128)(2,1)S(1)}, u32[]{:S(2)}, u32[]{:S(2)}) async-start(bf16[8,64,256]{2,1,0:T(8,128)(2,1)} %fusion.9), calls=%async_computation.1 | async-start | bytes 524288 | tf_op jit(solution)/shard_map/all_to_all | solution.py:81
  129.5 5.9 %convolution_convert_fusion = bf16[8192,128]{1,0:T(8,128)(2,1)S(1)} fusion(bf16[512,8192]{1,0:T(8,128)(2,1)} %all-gather.2.cloned.1.call-done.rows_ref, f32[512,64]{1,0:T(8,128)S(1)} %get-tuple-element.31, f32[512,64]{1,0:T(8,128)S(1)} %get-tuple-element.32), kind=kOutput, calls=%fused_computation | convolution fusion | flops 1074987008 | bytes 10747904 | tf_op jit(solution)/shard_map/dot_general | solution.py:281
  137.7 1.6 all-to-all-done.1
  140.0 3.5 %all-to-all-start.2 = ((bf16[8,64,256]{2,1,0:T(8,128)(2,1)}), bf16[8,64,256]{2,1,0:T(8,128)(2,1)S(1)}, u32[]{:S(2)}, u32[]{:S(2)}) async-start(bf16[8,64,256]{2,1,0:T(8,128)(2,1)} %broadcast_in_dim.8), calls=%async_computation.2 | async-start | bytes 524288 | tf_op jit(solution)/shard_map/all_to_all | solution.py:81
  143.5 2.8 %collective-permute-done.13 = bf16[1024,128]{1,0:T(8,128)(2,1)S(1)} collective-permute-done((bf16[1024,128]{1,0:T(8,128)(2,1)}, bf16[1024,128]{1,0:T(8,128)(2,1)S(1)}, u32[]{:S(2)}, u32[]{:S(2)}) %collective-permute-start.13) | collective-permute-done | bytes 262176 | tf_op jit(solution)/shard_map/ppermute | solution.py:77
  146.3 1.8 fusion.11
  148.1 5.1 %all-to-all-done.2 = bf16[8,64,256]{2,1,0:T(8,128)(2,1)S(1)} async-done(((bf16[8,64,256]{2,1,0:T(8,128)(2,1)}), bf16[8,64,256]{2,1,0:T(8,128)(2,1)S(1)}, u32[]{:S(2)}, u32[]{:S(2)}) %all-to-all-start.2) | async-done | bytes 262176 | tf_op jit(solution)/shard_map/all_to_all | solution.py:81
  153.2 2.5 %convolution_convert_fusion.1 = bf16[1024,256]{1,0:T(8,128)(2,1)} fusion(bf16[512,1024]{1,0:T(8,128)(2,1)} %get-tuple-element.13, bf16[512,256]{1,0:T(8,128)(2,1)S(1)} %bitcast.57), kind=kOutput, calls=%fused_computation.2 | convolution fusion | flops 268697600 | bytes 1835008 | tf_op jit(solution)/shard_map/dot_general | solution.py:317
  155.8 4.5 %all-to-all-start.3 = ((bf16[4,256,256]{2,1,0:T(8,128)(2,1)}), bf16[4,256,256]{2,1,0:T(8,128)(2,1)S(1)}, u32[]{:S(2)}, u32[]{:S(2)}) async-start(bf16[4,256,256]{2,1,0:T(8,128)(2,1)} %bitcast.56), calls=%async_computation.3 | async-start | bytes 1048576 | tf_op jit(solution)/shard_map/all_to_all | solution.py:81
  160.3 1.8 pad_maximum_fusion
  162.1 2.0 collective-permute-start.14
  164.9 2.1 collective-permute-start.16
  167.0 0.9 constant_dynamic-slice_fusion
  167.9 3.3 %all-to-all-done.3 = bf16[4,256,256]{2,1,0:T(8,128)(2,1)S(1)} async-done(((bf16[4,256,256]{2,1,0:T(8,128)(2,1)}), bf16[4,256,256]{2,1,0:T(8,128)(2,1)S(1)}, u32[]{:S(2)}, u32[]{:S(2)}) %all-to-all-start.3) | async-done | bytes 524320 | tf_op jit(solution)/shard_map/all_to_all | solution.py:81
  172.1 3.5 %all-to-all-start.4 = ((bf16[4,256,256]{2,1,0:T(8,128)(2,1)}), bf16[4,256,256]{2,1,0:T(8,128)(2,1)S(1)}, u32[]{:S(2)}, u32[]{:S(2)}) async-start(bf16[4,256,256]{2,1,0:T(8,128)(2,1)} %broadcast_in_dim.9), calls=%async_computation.4 | async-start | bytes 1048576 | tf_op jit(solution)/shard_map/all_to_all | solution.py:81
  175.6 3.6 %collective-permute-done.14 = bf16[2048,128]{1,0:T(8,128)(2,1)} collective-permute-done((bf16[2048,128]{1,0:T(8,128)(2,1)}, bf16[2048,128]{1,0:T(8,128)(2,1)}, u32[]{:S(2)}, u32[]{:S(2)}) %collective-permute-start.14) | collective-permute-done | bytes 524320 | tf_op jit(solution)/shard_map/ppermute | solution.py:77
  179.2 1.4 collective-permute-done.16
  180.6 2.3 fusion.3
  182.9 1.7 collective-permute-start.17
  184.6 1.3 collective-permute-start.18
  185.9 1.2 all-to-all-done.4.refs_4_
  187.1 1.2 collective-permute-start.22
  188.3 10.2 %collective-permute-start.19 = (bf16[2048,128]{1,0:T(8,128)(2,1)S(1)}, bf16[2048,128]{1,0:T(8,128)(2,1)S(1)}, u32[]{:S(2)}, u32[]{:S(2)}) collective-permute-start(bf16[2048,128]{1,0:T(8,128)(2,1)S(1)} %collective-permute-done.17.refs_0_), channel_id=1, source_target_pairs={{0,1},{1,0},{2,3},{3,2},{4,5},{5,4},{6,7},{7,6},{8,9},{9,8},{10,11... | collective-permute-start | bytes 1572872 | tf_op jit(solution)/shard_map/ppermute | solution.py:77
  198.5 2.6 %collective-permute-done.18.refs_1_ = bf16[2048,128]{1,0:T(8,128)(2,1)S(1)} collective-permute-done((bf16[2048,128]{1,0:T(8,128)(2,1)}, bf16[2048,128]{1,0:T(8,128)(2,1)S(1)}, u32[]{:S(2)}, u32[]{:S(2)}) %collective-permute-start.18) | collective-permute-done | bytes 524320 | tf_op jit(solution)/shard_map/ppermute | solution.py:302
  201.1 5.2 %collective-permute-start.20 = (bf16[2048,128]{1,0:T(8,128)(2,1)S(1)}, bf16[2048,128]{1,0:T(8,128)(2,1)S(1)}, u32[]{:S(2)}, u32[]{:S(2)}) collective-permute-start(bf16[2048,128]{1,0:T(8,128)(2,1)S(1)} %collective-permute-done.18.refs_1_), channel_id=1, source_target_pairs={{0,1},{1,0},{2,3},{3,2},{4,5},{5,4},{6,7},{7,6},{8,9},{9,8},{10,11... | collective-permute-start | bytes 1572872 | tf_op jit(solution)/shard_map/ppermute | solution.py:77
  206.4 6.0 %collective-permute-done.22.refs_6_ = bf16[4,256,256]{2,1,0:T(8,128)(2,1)S(1)} collective-permute-done((bf16[4,256,256]{2,1,0:T(8,128)(2,1)S(1)}, bf16[4,256,256]{2,1,0:T(8,128)(2,1)S(1)}, u32[]{:S(2)}, u32[]{:S(2)}) %collective-permute-start.22) | collective-permute-done | bytes 524320 | tf_op jit(solution)/shard_map/ppermute | solution.py:77
  212.6 1.5 collective-permute-start.24
  214.6 4.3 %collective-permute-done.23.refs_7_ = bf16[2,256,256]{2,1,0:T(8,128)(2,1)S(1)} collective-permute-done((bf16[2,256,256]{2,1,0:T(8,128)(2,1)S(1)}, bf16[2,256,256]{2,1,0:T(8,128)(2,1)S(1)}, u32[]{:S(2)}, u32[]{:S(2)}) %collective-permute-start.23) | collective-permute-done | bytes 262176 | tf_op jit(solution)/shard_map/ppermute | solution.py:77
  218.9 1.4 collective-permute-done.24.refs_8_
  220.4 1.4 collective-permute-done.29.refs_13_
  223.4 6.7 %unpack.1 = (bf16[2,2,2048,128]{3,2,1,0:T(8,128)(2,1)}, bf16[2,2,2,4,2,128,128]{6,5,4,3,2,1,0:T(8,128)(2,1)}, bf16[2,2,2,4,2,128,128]{6,5,4,3,2,1,0:T(8,128)(2,1)}) custom-call(s32[4]{0:T(128)} %pad_add_fusion.at_ref, bf16[2048,128]{1,0:T(8,128)(2,1)} %copy-done.6, bf16[2048,128]{1,0:T(8,128)(2,1)} %copy-done.7, bf16[2048,128]{1,0:T(8,128)(2,1)} %copy-done.8, ...), custom_call_target="tpu_custom_call" | custom-call | tf_op jit(solution)/shard_map/unpack/pallas_call | solution.py:213
  (110 shorter events, 18.9 us)
Async XLA Ops:
  7.2 97.2 %all-gather.2.cloned.1.call-start = ((), (), s32[]{:S(2)}) async-start(), calls=%async_computation.5 | async-start | bytes 8519680 | tf_op jit(solution)/shard_map/all_gather | solution.py:250
  9.3 0.7 collective-permute-start
  14.4 72.0 %copy-start.20 = (s32[1,512]{1,0:T(1,128)S(1)}, s32[1,512]{1,0:T(1,128)}, u32[]{:S(2)}) copy-start(s32[1,512]{1,0:T(1,128)} %param.9) | copy-start | bytes 6148
  14.4 72.7 %copy-start.21 = (f32[1,8]{1,0:T(1,128)S(1)}, f32[1,8]{1,0:T(1,128)}, u32[]{:S(2)}) copy-start(f32[1,8]{1,0:T(1,128)} %param.10) | copy-start | bytes 100
  14.4 86.5 %copy-start.19 = (bf16[1,512,128]{2,1,0:T(8,128)(2,1)S(1)}, bf16[1,512,128]{2,1,0:T(8,128)(2,1)}, u32[]{:S(2)}) copy-start(bf16[1,512,128]{2,1,0:T(8,128)(2,1)} %param.8) | copy-start | bytes 393220
  50.4 54.0 %copy-start = (bf16[32,128,128]{2,1,0:T(8,128)(2,1)}, bf16[32,128,128]{2,1,0:T(8,128)(2,1)S(1)}, u32[]{:S(2)}) copy-start(bf16[32,128,128]{2,1,0:T(8,128)(2,1)S(1)} %all_to_all.25.refs_0_) | copy-start | bytes 3145732
  50.4 30.6 %collective-permute-start.2 = (bf16[32,128,128]{2,1,0:T(8,128)(2,1)S(1)}, bf16[32,128,128]{2,1,0:T(8,128)(2,1)S(1)}, u32[]{:S(2)}, u32[]{:S(2)}) collective-permute-start(bf16[32,128,128]{2,1,0:T(8,128)(2,1)S(1)} %all_to_all.25.refs_0_), channel_id=1, source_target_pairs={{0,130},{2,128},{128,2},{130,0},{1,131},{3,129},{129,3},{131,1},{4... | collective-permute-start | bytes 3145736 | tf_op jit(solution)/shard_map/ppermute | solution.py:77
  58.5 25.5 %collective-permute-start.1 = (bf16[32,128,128]{2,1,0:T(8,128)(2,1)S(1)}, bf16[32,128,128]{2,1,0:T(8,128)(2,1)S(1)}, u32[]{:S(2)}, u32[]{:S(2)}) collective-permute-start(bf16[32,128,128]{2,1,0:T(8,128)(2,1)S(1)} %all_to_all.25.refs_0_), channel_id=1, source_target_pairs={{0,2},{2,0},{1,3},{3,1},{4,6},{6,4},{5,7},{7,5},{8,10},{10,8},{9,1... | collective-permute-start | bytes 3145736 | tf_op jit(solution)/shard_map/ppermute | solution.py:77
  80.9 23.4 %copy-start.1 = (bf16[32,128,128]{2,1,0:T(8,128)(2,1)}, bf16[32,128,128]{2,1,0:T(8,128)(2,1)S(1)}, u32[]{:S(2)}) copy-start(bf16[32,128,128]{2,1,0:T(8,128)(2,1)S(1)} %collective-permute-done.2.refs_2_) | copy-start | bytes 3145732
  81.8 14.7 %collective-permute-start.3 = (bf16[16,128,128]{2,1,0:T(8,128)(2,1)}, bf16[16,128,128]{2,1,0:T(8,128)(2,1)}, u32[]{:S(2)}, u32[]{:S(2)}) collective-permute-start(bf16[16,128,128]{2,1,0:T(8,128)(2,1)} %slice.109), channel_id=1, source_target_pairs={{0,2},{2,0},{1,3},{3,1},{4,6},{6,4},{5,7},{7,5},{8,10},{10,8},{9,1... | collective-permute-start | bytes 1572872 | tf_op jit(solution)/shard_map/ppermute | solution.py:77
  84.0 20.4 %copy-start.2 = (bf16[32,128,128]{2,1,0:T(8,128)(2,1)}, bf16[32,128,128]{2,1,0:T(8,128)(2,1)S(1)}, u32[]{:S(2)}) copy-start(bf16[32,128,128]{2,1,0:T(8,128)(2,1)S(1)} %collective-permute-done.1.refs_1_) | copy-start | bytes 3145732
  84.9 15.7 %collective-permute-start.4 = (bf16[16,128,128]{2,1,0:T(8,128)(2,1)}, bf16[16,128,128]{2,1,0:T(8,128)(2,1)}, u32[]{:S(2)}, u32[]{:S(2)}) collective-permute-start(bf16[16,128,128]{2,1,0:T(8,128)(2,1)} %slice.110), channel_id=1, source_target_pairs={{0,130},{2,128},{128,2},{130,0},{1,131},{3,129},{129,3},{131,1},{4... | collective-permute-start | bytes 1572872 | tf_op jit(solution)/shard_map/ppermute | solution.py:77
  86.4 9.9 %collective-permute-start.10 = (s32[512]{0:T(512)S(1)}, s32[512]{0:T(512)S(1)}, u32[]{:S(2)}, u32[]{:S(2)}) collective-permute-start(s32[512]{0:T(512)S(1)} %bitcast.65), channel_id=1, source_target_pairs={{0,0},{1,2},{2,1},{3,3},{4,4},{5,6},{6,5},{7,7},{8,8},{9,10},{10,9... | collective-permute-start | bytes 6152 | tf_op jit(solution)/shard_map/ppermute | solution.py:72
  87.1 4.8 %collective-permute-start.12 = (f32[8]{0:T(128)S(1)}, f32[8]{0:T(128)S(1)}, u32[]{:S(2)}, u32[]{:S(2)}) collective-permute-start(f32[8]{0:T(128)S(1)} %bitcast.66), channel_id=1, source_target_pairs={{0,0},{1,2},{2,1},{3,3},{4,4},{5,6},{6,5},{7,7},{8,8},{9,10},{10,9... | collective-permute-start | bytes 104 | tf_op jit(solution)/shard_map/ppermute | solution.py:72
  87.8 13.1 %collective-permute-start.5 = (bf16[32,128,128]{2,1,0:T(8,128)(2,1)S(1)}, bf16[32,128,128]{2,1,0:T(8,128)(2,1)}, u32[]{:S(2)}, u32[]{:S(2)}) collective-permute-start(bf16[32,128,128]{2,1,0:T(8,128)(2,1)S(1)} %all_to_all.25.refs_0_), channel_id=1, source_target_pairs={{0,1},{1,0},{2,3},{3,2},{4,5},{5,4},{6,7},{7,6},{8,9},{9,8},{10,11... | collective-permute-start | bytes 3145736 | tf_op jit(solution)/shard_map/ppermute | solution.py:77
  91.9 10.8 %collective-permute-start.6 = (bf16[32,128,128]{2,1,0:T(8,128)(2,1)S(1)}, bf16[32,128,128]{2,1,0:T(8,128)(2,1)}, u32[]{:S(2)}, u32[]{:S(2)}) collective-permute-start(bf16[32,128,128]{2,1,0:T(8,128)(2,1)S(1)} %collective-permute-done.1.refs_1_), channel_id=1, source_target_pairs={{0,1},{1,0},{2,3},{3,2},{4,5},{5,4},{6,7},{7,6},{8,9},{9,8},{10,11... | collective-permute-start | bytes 3145736 | tf_op jit(solution)/shard_map/ppermute | solution.py:77
  96.4 7.1 %collective-permute-start.7 = (bf16[32,128,128]{2,1,0:T(8,128)(2,1)S(1)}, bf16[32,128,128]{2,1,0:T(8,128)(2,1)}, u32[]{:S(2)}, u32[]{:S(2)}) collective-permute-start(bf16[32,128,128]{2,1,0:T(8,128)(2,1)S(1)} %collective-permute-done.2.refs_2_), channel_id=1, source_target_pairs={{0,1},{1,0},{2,3},{3,2},{4,5},{5,4},{6,7},{7,6},{8,9},{9,8},{10,11... | collective-permute-start | bytes 3145736 | tf_op jit(solution)/shard_map/ppermute | solution.py:77
  96.5 5.3 %collective-permute-start.8 = (bf16[16,128,128]{2,1,0:T(8,128)(2,1)}, bf16[16,128,128]{2,1,0:T(8,128)(2,1)S(1)}, u32[]{:S(2)}, u32[]{:S(2)}) collective-permute-start(bf16[16,128,128]{2,1,0:T(8,128)(2,1)} %collective-permute-done.3.refs_3_), channel_id=1, source_target_pairs={{0,1},{1,0},{2,3},{3,2},{4,5},{5,4},{6,7},{7,6},{8,9},{9,8},{10,11... | collective-permute-start | bytes 1572872 | tf_op jit(solution)/shard_map/ppermute | solution.py:77
  100.6 2.1 collective-permute-start.9
  100.9 18.5 %collective-permute-start.11 = (bf16[512,128]{1,0:T(8,128)(2,1)S(1)}, bf16[512,128]{1,0:T(8,128)(2,1)S(1)}, u32[]{:S(2)}, u32[]{:S(2)}) collective-permute-start(bf16[512,128]{1,0:T(8,128)(2,1)S(1)} %bitcast.64), channel_id=1, source_target_pairs={{0,0},{1,2},{2,1},{3,3},{4,4},{5,6},{6,5},{7,7},{8,8},{9,10},{10,9... | collective-permute-start | bytes 393224 | tf_op jit(solution)/shard_map/ppermute | solution.py:72
  123.7 15.6 %all-to-all-start.1 = ((bf16[8,64,256]{2,1,0:T(8,128)(2,1)}), bf16[8,64,256]{2,1,0:T(8,128)(2,1)S(1)}, u32[]{:S(2)}, u32[]{:S(2)}) async-start(bf16[8,64,256]{2,1,0:T(8,128)(2,1)} %fusion.9), calls=%async_computation.1 | async-start | bytes 524288 | tf_op jit(solution)/shard_map/all_to_all | solution.py:81
  136.2 10.1 %collective-permute-start.13 = (bf16[1024,128]{1,0:T(8,128)(2,1)}, bf16[1024,128]{1,0:T(8,128)(2,1)S(1)}, u32[]{:S(2)}, u32[]{:S(2)}) collective-permute-start(bf16[1024,128]{1,0:T(8,128)(2,1)} %get-tuple-element.19), channel_id=1, source_target_pairs={{0,130},{2,128},{128,2},{130,0},{1,131},{3,129},{129,3},{131,1},{4... | collective-permute-start | bytes 786440 | tf_op jit(solution)/shard_map/ppermute | solution.py:77
  137.1 9.3 %collective-permute-start.15 = (bf16[1024,128]{1,0:T(8,128)(2,1)S(1)}, bf16[1024,128]{1,0:T(8,128)(2,1)}, u32[]{:S(2)}, u32[]{:S(2)}) collective-permute-start(bf16[1024,128]{1,0:T(8,128)(2,1)S(1)} %get-tuple-element.21), channel_id=1, source_target_pairs={{0,2},{2,0},{1,3},{3,1},{4,6},{6,4},{5,7},{7,5},{8,10},{10,8},{9,1... | collective-permute-start | bytes 786440 | tf_op jit(solution)/shard_map/ppermute | solution.py:77
  140.0 13.2 %all-to-all-start.2 = ((bf16[8,64,256]{2,1,0:T(8,128)(2,1)}), bf16[8,64,256]{2,1,0:T(8,128)(2,1)S(1)}, u32[]{:S(2)}, u32[]{:S(2)}) async-start(bf16[8,64,256]{2,1,0:T(8,128)(2,1)} %broadcast_in_dim.8), calls=%async_computation.2 | async-start | bytes 524288 | tf_op jit(solution)/shard_map/all_to_all | solution.py:81
  155.8 15.4 %all-to-all-start.3 = ((bf16[4,256,256]{2,1,0:T(8,128)(2,1)}), bf16[4,256,256]{2,1,0:T(8,128)(2,1)S(1)}, u32[]{:S(2)}, u32[]{:S(2)}) async-start(bf16[4,256,256]{2,1,0:T(8,128)(2,1)} %bitcast.56), calls=%async_computation.3 | async-start | bytes 1048576 | tf_op jit(solution)/shard_map/all_to_all | solution.py:81
  162.1 17.2 %collective-permute-start.14 = (bf16[2048,128]{1,0:T(8,128)(2,1)}, bf16[2048,128]{1,0:T(8,128)(2,1)}, u32[]{:S(2)}, u32[]{:S(2)}) collective-permute-start(bf16[2048,128]{1,0:T(8,128)(2,1)} %pad_maximum_fusion), channel_id=1, source_target_pairs={{0,2},{2,0},{1,3},{3,1},{4,6},{6,4},{5,7},{7,5},{8,10},{10,8},{9,1... | collective-permute-start | bytes 1572872 | tf_op jit(solution)/shard_map/ppermute | solution.py:77
  164.9 15.7 %collective-permute-start.16 = (bf16[2048,128]{1,0:T(8,128)(2,1)}, bf16[2048,128]{1,0:T(8,128)(2,1)S(1)}, u32[]{:S(2)}, u32[]{:S(2)}) collective-permute-start(bf16[2048,128]{1,0:T(8,128)(2,1)} %pad_maximum_fusion.1), channel_id=1, source_target_pairs={{0,130},{2,128},{128,2},{130,0},{1,131},{3,129},{129,3},{131,1},{4... | collective-permute-start | bytes 1572872 | tf_op jit(solution)/shard_map/ppermute | solution.py:77
  172.1 14.9 %all-to-all-start.4 = ((bf16[4,256,256]{2,1,0:T(8,128)(2,1)}), bf16[4,256,256]{2,1,0:T(8,128)(2,1)S(1)}, u32[]{:S(2)}, u32[]{:S(2)}) async-start(bf16[4,256,256]{2,1,0:T(8,128)(2,1)} %broadcast_in_dim.9), calls=%async_computation.4 | async-start | bytes 1048576 | tf_op jit(solution)/shard_map/all_to_all | solution.py:81
  182.9 5.3 %collective-permute-start.17 = (bf16[2048,128]{1,0:T(8,128)(2,1)}, bf16[2048,128]{1,0:T(8,128)(2,1)S(1)}, u32[]{:S(2)}, u32[]{:S(2)}) collective-permute-start(bf16[2048,128]{1,0:T(8,128)(2,1)} %fusion.3), channel_id=1, source_target_pairs={{0,0},{1,2},{2,1},{3,3},{4,4},{5,6},{6,5},{7,7},{8,8},{9,10},{10,9... | collective-permute-start | bytes 1572872 | tf_op jit(solution)/shard_map/ppermute | solution.py:72
  184.6 16.5 %collective-permute-start.18 = (bf16[2048,128]{1,0:T(8,128)(2,1)}, bf16[2048,128]{1,0:T(8,128)(2,1)S(1)}, u32[]{:S(2)}, u32[]{:S(2)}) collective-permute-start(bf16[2048,128]{1,0:T(8,128)(2,1)} %fusion.3), channel_id=1, source_target_pairs={{0,128},{1,130},{2,129},{3,131},{128,0},{129,2},{130,1},{131,3},{4... | collective-permute-start | bytes 1572872 | tf_op jit(solution)/shard_map/ppermute | solution.py:302
  187.1 36.2 %copy-start.3 = (bf16[4,256,256]{2,1,0:T(8,128)(2,1)}, bf16[4,256,256]{2,1,0:T(8,128)(2,1)S(1)}, u32[]{:S(2)}) copy-start(bf16[4,256,256]{2,1,0:T(8,128)(2,1)S(1)} %all-to-all-done.4.refs_4_) | copy-start | bytes 1572868
  187.1 25.3 %collective-permute-start.22 = (bf16[4,256,256]{2,1,0:T(8,128)(2,1)S(1)}, bf16[4,256,256]{2,1,0:T(8,128)(2,1)S(1)}, u32[]{:S(2)}, u32[]{:S(2)}) collective-permute-start(bf16[4,256,256]{2,1,0:T(8,128)(2,1)S(1)} %all-to-all-done.4.refs_4_), channel_id=1, source_target_pairs={{0,130},{2,128},{128,2},{130,0},{1,131},{3,129},{129,3},{131,1},{4... | collective-permute-start | bytes 1572872 | tf_op jit(solution)/shard_map/ppermute | solution.py:77
  188.3 24.3 %collective-permute-start.21 = (bf16[4,256,256]{2,1,0:T(8,128)(2,1)S(1)}, bf16[4,256,256]{2,1,0:T(8,128)(2,1)S(1)}, u32[]{:S(2)}, u32[]{:S(2)}) collective-permute-start(bf16[4,256,256]{2,1,0:T(8,128)(2,1)S(1)} %all-to-all-done.4.refs_4_), channel_id=1, source_target_pairs={{0,2},{2,0},{1,3},{3,1},{4,6},{6,4},{5,7},{7,5},{8,10},{10,8},{9,1... | collective-permute-start | bytes 1572872 | tf_op jit(solution)/shard_map/ppermute | solution.py:77
  188.3 35.1 %copy-start.6 = (bf16[2048,128]{1,0:T(8,128)(2,1)}, bf16[2048,128]{1,0:T(8,128)(2,1)S(1)}, u32[]{:S(2)}) copy-start(bf16[2048,128]{1,0:T(8,128)(2,1)S(1)} %collective-permute-done.17.refs_0_) | copy-start | bytes 1572868
  188.3 25.8 %collective-permute-start.19 = (bf16[2048,128]{1,0:T(8,128)(2,1)S(1)}, bf16[2048,128]{1,0:T(8,128)(2,1)S(1)}, u32[]{:S(2)}, u32[]{:S(2)}) collective-permute-start(bf16[2048,128]{1,0:T(8,128)(2,1)S(1)} %collective-permute-done.17.refs_0_), channel_id=1, source_target_pairs={{0,1},{1,0},{2,3},{3,2},{4,5},{5,4},{6,7},{7,6},{8,9},{9,8},{10,11... | collective-permute-start | bytes 1572872 | tf_op jit(solution)/shard_map/ppermute | solution.py:77
  201.1 22.2 %copy-start.7 = (bf16[2048,128]{1,0:T(8,128)(2,1)}, bf16[2048,128]{1,0:T(8,128)(2,1)S(1)}, u32[]{:S(2)}) copy-start(bf16[2048,128]{1,0:T(8,128)(2,1)S(1)} %collective-permute-done.18.refs_1_) | copy-start | bytes 1572868
  201.1 12.9 %collective-permute-start.20 = (bf16[2048,128]{1,0:T(8,128)(2,1)S(1)}, bf16[2048,128]{1,0:T(8,128)(2,1)S(1)}, u32[]{:S(2)}, u32[]{:S(2)}) collective-permute-start(bf16[2048,128]{1,0:T(8,128)(2,1)S(1)} %collective-permute-done.18.refs_1_), channel_id=1, source_target_pairs={{0,1},{1,0},{2,3},{3,2},{4,5},{5,4},{6,7},{7,6},{8,9},{9,8},{10,11... | collective-permute-start | bytes 1572872 | tf_op jit(solution)/shard_map/ppermute | solution.py:77
  206.4 13.9 %collective-permute-start.25 = (bf16[4,256,256]{2,1,0:T(8,128)(2,1)S(1)}, bf16[4,256,256]{2,1,0:T(8,128)(2,1)S(1)}, u32[]{:S(2)}, u32[]{:S(2)}) collective-permute-start(bf16[4,256,256]{2,1,0:T(8,128)(2,1)S(1)} %all-to-all-done.4.refs_4_), channel_id=1, source_target_pairs={{0,1},{1,0},{2,3},{3,2},{4,5},{5,4},{6,7},{7,6},{8,9},{9,8},{10,11... | collective-permute-start | bytes 1572872 | tf_op jit(solution)/shard_map/ppermute | solution.py:77
  212.4 11.0 %copy-start.4 = (bf16[4,256,256]{2,1,0:T(8,128)(2,1)}, bf16[4,256,256]{2,1,0:T(8,128)(2,1)S(1)}, u32[]{:S(2)}) copy-start(bf16[4,256,256]{2,1,0:T(8,128)(2,1)S(1)} %collective-permute-done.22.refs_6_) | copy-start | bytes 1572868
  212.4 6.5 %collective-permute-start.23 = (bf16[2,256,256]{2,1,0:T(8,128)(2,1)S(1)}, bf16[2,256,256]{2,1,0:T(8,128)(2,1)S(1)}, u32[]{:S(2)}, u32[]{:S(2)}) collective-permute-start(bf16[2,256,256]{2,1,0:T(8,128)(2,1)S(1)} %slice.121), channel_id=1, source_target_pairs={{0,2},{2,0},{1,3},{3,1},{4,6},{6,4},{5,7},{7,5},{8,10},{10,8},{9,1... | collective-permute-start | bytes 786440 | tf_op jit(solution)/shard_map/ppermute | solution.py:77
  212.5 10.8 %copy-start.5 = (bf16[4,256,256]{2,1,0:T(8,128)(2,1)}, bf16[4,256,256]{2,1,0:T(8,128)(2,1)S(1)}, u32[]{:S(2)}) copy-start(bf16[4,256,256]{2,1,0:T(8,128)(2,1)S(1)} %collective-permute-done.21.refs_5_) | copy-start | bytes 1572868
  212.6 7.7 %collective-permute-start.24 = (bf16[2,256,256]{2,1,0:T(8,128)(2,1)S(1)}, bf16[2,256,256]{2,1,0:T(8,128)(2,1)S(1)}, u32[]{:S(2)}, u32[]{:S(2)}) collective-permute-start(bf16[2,256,256]{2,1,0:T(8,128)(2,1)S(1)} %slice.122), channel_id=1, source_target_pairs={{0,130},{2,128},{128,2},{130,0},{1,131},{3,129},{129,3},{131,1},{4... | collective-permute-start | bytes 786440 | tf_op jit(solution)/shard_map/ppermute | solution.py:77
  214.1 9.3 %copy-start.8 = (bf16[2048,128]{1,0:T(8,128)(2,1)}, bf16[2048,128]{1,0:T(8,128)(2,1)S(1)}, u32[]{:S(2)}) copy-start(bf16[2048,128]{1,0:T(8,128)(2,1)S(1)} %collective-permute-done.19.refs_2_) | copy-start | bytes 1572868
  214.1 7.8 %collective-permute-start.26 = (bf16[4,256,256]{2,1,0:T(8,128)(2,1)S(1)}, bf16[4,256,256]{2,1,0:T(8,128)(2,1)S(1)}, u32[]{:S(2)}, u32[]{:S(2)}) collective-permute-start(bf16[4,256,256]{2,1,0:T(8,128)(2,1)S(1)} %collective-permute-done.21.refs_5_), channel_id=1, source_target_pairs={{0,1},{1,0},{2,3},{3,2},{4,5},{5,4},{6,7},{7,6},{8,9},{9,8},{10,11... | collective-permute-start | bytes 1572872 | tf_op jit(solution)/shard_map/ppermute | solution.py:77
  214.1 7.8 %copy-start.9 = (bf16[2048,128]{1,0:T(8,128)(2,1)}, bf16[2048,128]{1,0:T(8,128)(2,1)S(1)}, u32[]{:S(2)}) copy-start(bf16[2048,128]{1,0:T(8,128)(2,1)S(1)} %collective-permute-done.20.refs_3_) | copy-start | bytes 1572868
  214.1 9.2 %collective-permute-start.27 = (bf16[4,256,256]{2,1,0:T(8,128)(2,1)S(1)}, bf16[4,256,256]{2,1,0:T(8,128)(2,1)}, u32[]{:S(2)}, u32[]{:S(2)}) collective-permute-start(bf16[4,256,256]{2,1,0:T(8,128)(2,1)S(1)} %collective-permute-done.22.refs_6_), channel_id=1, source_target_pairs={{0,1},{1,0},{2,3},{3,2},{4,5},{5,4},{6,7},{7,6},{8,9},{9,8},{10,11... | collective-permute-start | bytes 1572872 | tf_op jit(solution)/shard_map/ppermute | solution.py:77
  218.9 1.5 collective-permute-start.28
  220.3 1.5 collective-permute-start.29
  (9 other events, 12.8 us)
Sparse Core Ops, SparseCore 0:
  10.8 93.5 all-gather.1

commit v8 on v7

--- a/solution.py
+++ b/solution.py
@@ -118,7 +118,7 @@
 def project(normed, pieces, others, at):
     def body(at_ref, rows_ref, *refs):
         mine, theirs = refs[:5], refs[5:10]
-        out_ref, wq_ref, wkv_ref, member_ref = refs[10:]
+        out_ref, w_ref, member_ref = refs[10:]
         b = pl.program_id(0)
         xl, xh, core = at_ref[0], at_ref[1], at_ref[2]
         spots = ((xl, xh), (1 - xl, xh), (1 - xl, 1 - xh), (xl, 1 - xh))
@@ -131,14 +131,14 @@
         for n, (l, h) in enumerate(spots):
             own = block(mine, n)
             other = block(theirs, n)
-            wq_ref[:, l, h] = own[:, :64]
-            wkv_ref[:, l, h, core, :, 0:HD] = own[:, 64:96]
-            wkv_ref[:, l, h, core, :, HD : 2 * HD] = own[:, 96:128]
-            wkv_ref[:, l, h, 1 - core, :, 0:HD] = other[:, 64:96]
-            wkv_ref[:, l, h, 1 - core, :, HD : 2 * HD] = other[:, 96:128]
+            w_ref[:, l, h, :, 0:HD] = own[:, :64]
+            w_ref[:, l, h, pl.ds(pl.multiple_of((core) * 32, 32), 32), HD : 2 * HD] = own[:, 64:96]
+            w_ref[:, l, h, pl.ds(pl.multiple_of((core) * 32, 32), 32), 2 * HD : 3 * HD] = own[:, 96:128]
+            w_ref[:, l, h, pl.ds(pl.multiple_of((1 - core) * 32, 32), 32), HD : 2 * HD] = other[:, 64:96]
+            w_ref[:, l, h, pl.ds(pl.multiple_of((1 - core) * 32, 32), 32), 2 * HD : 3 * HD] = other[:, 96:128]
 
         rows = rows_ref[...]
-        for n in (0, 1):
+        for n in range(2):
             member_ref[:, n * HD : (n + 1) * HD] = rows_ref[
                 :, pl.ds(pl.multiple_of(n * 1024 + at_ref[3] * HD, HD), HD)
             ]
@@ -147,11 +147,8 @@
         def _():
             out_ref[...] = jnp.zeros_like(out_ref)
 
-        out_ref[:, 0:HD] += jnp.dot(
-            rows, wq_ref[...].reshape(2048, HD), preferred_element_type=jnp.float32
-        )
-        out_ref[:, HD : 3 * HD] += jnp.dot(
-            rows, wkv_ref[...].reshape(2048, 2 * HD), preferred_element_type=jnp.float32
+        out_ref[...] += jnp.dot(
+            rows, w_ref[...].reshape(2048, 3 * HD), preferred_element_type=jnp.float32
         )
 
     whole = pl.BlockSpec((8, 128, HD), lambda b, at: (b, 0, 0))
@@ -163,8 +160,7 @@
         body,
         out_shape=(
             jax.ShapeDtypeStruct((512, 3 * HD), jnp.float32),
-            jax.ShapeDtypeStruct((32, 2, 2, 64, HD), bf16),
-            jax.ShapeDtypeStruct((32, 2, 2, 2, 32, 2 * HD), bf16),
+            jax.ShapeDtypeStruct((32, 2, 2, 64, 3 * HD), bf16),
             jax.ShapeDtypeStruct((512, 1024), bf16),
         ),
         grid_spec=pltpu.PrefetchScalarGridSpec(
@@ -173,8 +169,7 @@
             in_specs=[pl.BlockSpec((512, 2048), lambda b, at: (0, b))] + group + group,
             out_specs=(
                 pl.BlockSpec((512, 3 * HD), lambda b, at: (0, 0)),
-                pl.BlockSpec((8, 2, 2, 64, HD), lambda b, at: (b, 0, 0, 0, 0)),
-                pl.BlockSpec((8, 2, 2, 2, 32, 2 * HD), lambda b, at: (b, 0, 0, 0, 0, 0)),
+                pl.BlockSpec((8, 2, 2, 64, 3 * HD), lambda b, at: (b, 0, 0, 0, 0)),
                 pl.BlockSpec((512, 2 * HD), lambda b, at: (0, b)),
             ),
         ),
@@ -257,9 +252,9 @@
     cut = exchange(pack_columns(w_query, w_key, w_value, at), YZ)
     pieces = (cut,) + ring_pieces(cut)
     others = tuple(flip(p, ("core",)) for p in pieces)
-    projected, q_cols, wkv, normed_m = project(normed, pieces, others, at)
+    projected, columns, normed_m = project(normed, pieces, others, at)
     projected = projected * inv_width
-    q_cols = q_cols.reshape(D, HD)
+    columns = columns.reshape(D, 3 * HD)
 
     cosine_table, sine_table = angles(seg_row)
     weight_row = token_weights(seg_row, adv_row)
@@ -296,7 +291,7 @@
     near = flip(near, ("xl",))
     wrap = flip(wrap, X)
     sum_q = part_for(0).astype(f32) + near.astype(f32) + wrap.astype(f32)
-    old_q = lax.dynamic_slice_in_dim(q_cols, ring * 2048, 2048)
+    old_q = lax.dynamic_slice(columns, (ring * 2048, 0), (2048, HD))
     new_q = (old_q.astype(f32) - step_rate * sum_q).astype(bf16)
     near = swap(new_q)
     far = lax.ppermute(
@@ -317,11 +312,10 @@
     part_kv = lax.dot_general(
         normed_m, kv_sum, contract, preferred_element_type=f32
     ).astype(bf16)
-    part_kv = exchange(part_kv.reshape(4, 256, 2 * HD), X)
-    part_kv = part_kv.astype(f32)
-    old_kv = wkv.reshape(4, 2, 8, 128, 2 * HD)
-    old_kv = lax.dynamic_index_in_dim(old_kv, ring, 0, keepdims=False)
-    old_kv = lax.dynamic_index_in_dim(old_kv, member, 1, keepdims=False).reshape(256, 2 * HD)
+    part_kv = exchange(part_kv.reshape(4, 256, 2 * HD), X).astype(f32)
+    old_kv = columns.reshape(4, 2, 8, 128, 3 * HD)
+    old_kv = lax.dynamic_slice(old_kv, (ring, 0, member, 0, HD), (1, 2, 1, 128, 2 * HD))
+    old_kv = old_kv.reshape(256, 2 * HD)
     new_kv = (old_kv.astype(f32) - step_rate * jnp.sum(part_kv, axis=0)).astype(bf16)
     new_kv = spread(new_kv, ("zl",))
     kv_pieces = (new_kv,) + ring_pieces(new_kv)

time: 240 us -> 240 us (level)
  no operation moved by 1% of the time
where the time goes in v8:
time: 240 us; the launch traced here: 237 us
  starting transfers between devices  67.3 us (28%)
  waiting for transfers between devices  64 us (27%)
  blocking collectives  35.9 us (15%)
  Pallas kernels  21.7 us (9%)
  other arithmetic  15.4 us (6%)
  between operations  14.4 us (6%)
  matrix products  10.5 us (4%)
  local copies, waits for them, and re-layouts  8.03 us (3%)
    ppermute x24, waiting for transfers between devices, flip(): return lax.ppermute(x, axes, [(i, n - 1 - i) for i in range(n)])  49.7 us
    ppermute x24, starting transfers between devices, flip(): return lax.ppermute(x, axes, [(i, n - 1 - i) for i in range(n)])  44.2 us
    all_to_all x1, blocking collectives, exchange(): return lax.all_to_all(x, axes, split_axis=0, concat_axis=0, tiled=True)  35.9 us
    all_to_all x4, starting transfers between devices, exchange(): return lax.all_to_all(x, axes, split_axis=0, concat_axis=0, tiled=True)  17.3 us
    pallas_call x1, Pallas kernels, project(): pl.pallas_call(body, out_shape=(jax.ShapeDtypeStruct((512, 3 * HD), jnp.f...  12 us
    all_to_all x4, waiting for transfers between devices, exchange(): return lax.all_to_all(x, axes, split_axis=0, concat_axis=0, tiled=True)  11 us
    pallas_call x1, Pallas kernels, unpack(): pl.pallas_call(body, out_shape=(jax.ShapeDtypeStruct((2, 2, 2048, HD), bf...  6.67 us
    dot_general x1, matrix products, local(): lax.dot_general(normed, scaled_q, contract, preferred_element_type=f32)  5.87 us
  transfers between devices with their start and end apart: 35, of which 19 were waited for; matrix products, arithmetic and copies ran while one was open for 9% of the time, Pallas kernels for 6%

profile of v8, /device:TPU:8, one launch (start us, length us, event | category | flops | bytes accessed | tf_op | source)
XLA Modules:
  0.0 237.2 jit_solution(4614332244604692879)
XLA Ops:
  7.2 1.1 fusion.31
  8.3 1.0 fusion.32
  11.3 3.1 %pack_columns.1 = bf16[32,128,128]{2,1,0:T(8,128)(2,1)} custom-call(s32[4]{0:T(128)} %pad_add_fusion.at_ref, bf16[128,8192]{1,0:T(8,128)(2,1)} %q_ref.1, bf16[128,1024]{1,0:T(8,128)(2,1)} %k_ref.1, bf16[128,1024]{1,0:T(8,128)(2,1)} %v_ref.1), custom_call_target="tpu_custom_call" | custom-call | tf_op jit(solution)/shard_map/pack_columns/pallas_call | solution.py:105
  14.3 35.9 %all_to_all.25.refs_0_ = bf16[32,128,128]{2,1,0:T(8,128)(2,1)S(1)} all-to-all(bf16[32,128,128]{2,1,0:T(8,128)(2,1)} %pack_columns.1), channel_id=1, replica_groups=mesh['xh'=2,'y'=4,'zh'=2,'zl'=4,'xl'=2,'core'=2] {'y','zh','zl'}, dimensions={0} | all-to-all | bytes 2097152 | tf_op jit(solution)/shard_map/all_to_all | solution.py:81
  50.2 8.2 %collective-permute-start.2 = (bf16[32,128,128]{2,1,0:T(8,128)(2,1)S(1)}, bf16[32,128,128]{2,1,0:T(8,128)(2,1)S(1)}, u32[]{:S(2)}, u32[]{:S(2)}) collective-permute-start(bf16[32,128,128]{2,1,0:T(8,128)(2,1)S(1)} %all_to_all.25.refs_0_), channel_id=1, source_target_pairs={{0,130},{2,128},{128,2},{130,0},{1,131},{3,129},{129,3},{131,1},{4... | collective-permute-start | bytes 3145736 | tf_op jit(solution)/shard_map/ppermute | solution.py:77
  58.5 22.6 %collective-permute-done.2.refs_2_ = bf16[32,128,128]{2,1,0:T(8,128)(2,1)S(1)} collective-permute-done((bf16[32,128,128]{2,1,0:T(8,128)(2,1)S(1)}, bf16[32,128,128]{2,1,0:T(8,128)(2,1)S(1)}, u32[]{:S(2)}, u32[]{:S(2)}) %collective-permute-start.2) | collective-permute-done | bytes 1048608 | tf_op jit(solution)/shard_map/ppermute | solution.py:77
  82.7 1.4 collective-permute-done.1.refs_1_
  85.0 0.9 collective-permute-start.4
  87.3 4.1 %collective-permute-start.5 = (bf16[32,128,128]{2,1,0:T(8,128)(2,1)S(1)}, bf16[32,128,128]{2,1,0:T(8,128)(2,1)}, u32[]{:S(2)}, u32[]{:S(2)}) collective-permute-start(bf16[32,128,128]{2,1,0:T(8,128)(2,1)S(1)} %all_to_all.25.refs_0_), channel_id=1, source_target_pairs={{0,1},{1,0},{2,3},{3,2},{4,5},{5,4},{6,7},{7,6},{8,9},{9,8},{10,11... | collective-permute-start | bytes 3145736 | tf_op jit(solution)/shard_map/ppermute | solution.py:77
  91.4 5.2 %collective-permute-start.6 = (bf16[32,128,128]{2,1,0:T(8,128)(2,1)S(1)}, bf16[32,128,128]{2,1,0:T(8,128)(2,1)}, u32[]{:S(2)}, u32[]{:S(2)}) collective-permute-start(bf16[32,128,128]{2,1,0:T(8,128)(2,1)S(1)} %collective-permute-done.1.refs_1_), channel_id=1, source_target_pairs={{0,1},{1,0},{2,3},{3,2},{4,5},{5,4},{6,7},{7,6},{8,9},{9,8},{10,11... | collective-permute-start | bytes 3145736 | tf_op jit(solution)/shard_map/ppermute | solution.py:77
  97.4 2.8 %collective-permute-done.4.refs_4_ = bf16[16,128,128]{2,1,0:T(8,128)(2,1)} collective-permute-done((bf16[16,128,128]{2,1,0:T(8,128)(2,1)}, bf16[16,128,128]{2,1,0:T(8,128)(2,1)}, u32[]{:S(2)}, u32[]{:S(2)}) %collective-permute-start.4) | collective-permute-done | bytes 524320 | tf_op jit(solution)/shard_map/ppermute | solution.py:77
  104.4 12.0 %project.1 = (f32[512,384]{1,0:T(8,128)}, bf16[32,2,2,64,384]{4,3,2,1,0:T(8,128)(2,1)}, bf16[512,1024]{1,0:T(8,128)(2,1)}) custom-call(s32[4]{0:T(128)} %pad_add_fusion.at_ref, bf16[512,8192]{1,0:T(8,128)(2,1)} %all-gather.2.cloned.1.call-done.rows_ref, bf16[32,128,128]{2,1,0:T(8,128)(2,1)} %copy-done, bf16[32,128,128]{2,1,0:T(8,128)(2,1)} %copy-done.2, ...), custom_call_target="tpu_custom_call" | custom-call | tf_op jit(solution)/shard_map/project/pallas_call | solution.py:159
  116.3 1.2 broadcast_multiply_fusion
  117.5 1.3 fusion.38
  121.2 1.3 fusion.35
  122.9 0.9 fusion.9
  123.8 5.8 %all-to-all-start.1 = ((bf16[8,64,256]{2,1,0:T(8,128)(2,1)}), bf16[8,64,256]{2,1,0:T(8,128)(2,1)S(1)}, u32[]{:S(2)}, u32[]{:S(2)}) async-start(bf16[8,64,256]{2,1,0:T(8,128)(2,1)} %fusion.9), calls=%async_computation.1 | async-start | bytes 524288 | tf_op jit(solution)/shard_map/all_to_all | solution.py:81
  129.6 5.9 %convolution_convert_fusion = bf16[8192,128]{1,0:T(8,128)(2,1)S(1)} fusion(bf16[512,8192]{1,0:T(8,128)(2,1)} %all-gather.2.cloned.1.call-done.rows_ref, f32[512,64]{1,0:T(8,128)S(1)} %get-tuple-element.29, f32[512,64]{1,0:T(8,128)S(1)} %get-tuple-element.30), kind=kOutput, calls=%fused_computation | convolution fusion | flops 1074987008 | bytes 10747904 | tf_op jit(solution)/shard_map/dot_general | solution.py:276
  136.3 0.9 collective-permute-start.13
  137.5 1.8 all-to-all-done.1
  140.1 3.4 %all-to-all-start.2 = ((bf16[8,64,256]{2,1,0:T(8,128)(2,1)}), bf16[8,64,256]{2,1,0:T(8,128)(2,1)S(1)}, u32[]{:S(2)}, u32[]{:S(2)}) async-start(bf16[8,64,256]{2,1,0:T(8,128)(2,1)} %broadcast_in_dim.8), calls=%async_computation.2 | async-start | bytes 524288 | tf_op jit(solution)/shard_map/all_to_all | solution.py:81
  143.5 2.9 %collective-permute-done.13 = bf16[1024,128]{1,0:T(8,128)(2,1)S(1)} collective-permute-done((bf16[1024,128]{1,0:T(8,128)(2,1)}, bf16[1024,128]{1,0:T(8,128)(2,1)S(1)}, u32[]{:S(2)}, u32[]{:S(2)}) %collective-permute-start.13) | collective-permute-done | bytes 262176 | tf_op jit(solution)/shard_map/ppermute | solution.py:77
  146.4 1.8 fusion.11
  148.2 4.9 %all-to-all-done.2 = bf16[8,64,256]{2,1,0:T(8,128)(2,1)S(1)} async-done(((bf16[8,64,256]{2,1,0:T(8,128)(2,1)}), bf16[8,64,256]{2,1,0:T(8,128)(2,1)S(1)}, u32[]{:S(2)}, u32[]{:S(2)}) %all-to-all-start.2) | async-done | bytes 262176 | tf_op jit(solution)/shard_map/all_to_all | solution.py:81
  153.1 2.5 %convolution_convert_fusion.1 = bf16[1024,256]{1,0:T(8,128)(2,1)} fusion(bf16[512,1024]{1,0:T(8,128)(2,1)} %get-tuple-element.11, bf16[512,256]{1,0:T(8,128)(2,1)S(1)} %bitcast.57), kind=kOutput, calls=%fused_computation.2 | convolution fusion | flops 268697600 | bytes 1835008 | tf_op jit(solution)/shard_map/dot_general | solution.py:312
  155.6 4.7 %all-to-all-start.3 = ((bf16[4,256,256]{2,1,0:T(8,128)(2,1)}), bf16[4,256,256]{2,1,0:T(8,128)(2,1)S(1)}, u32[]{:S(2)}, u32[]{:S(2)}) async-start(bf16[4,256,256]{2,1,0:T(8,128)(2,1)} %bitcast.56), calls=%async_computation.3 | async-start | bytes 1048576 | tf_op jit(solution)/shard_map/all_to_all | solution.py:81
  160.3 1.8 pad_maximum_fusion
  162.1 2.0 collective-permute-start.14
  164.9 2.1 collective-permute-start.16
  167.0 0.9 constant_dynamic-slice_fusion
  167.9 3.3 %all-to-all-done.3 = bf16[4,256,256]{2,1,0:T(8,128)(2,1)S(1)} async-done(((bf16[4,256,256]{2,1,0:T(8,128)(2,1)}), bf16[4,256,256]{2,1,0:T(8,128)(2,1)S(1)}, u32[]{:S(2)}, u32[]{:S(2)}) %all-to-all-start.3) | async-done | bytes 524320 | tf_op jit(solution)/shard_map/all_to_all | solution.py:81
  172.1 3.5 %all-to-all-start.4 = ((bf16[4,256,256]{2,1,0:T(8,128)(2,1)}), bf16[4,256,256]{2,1,0:T(8,128)(2,1)S(1)}, u32[]{:S(2)}, u32[]{:S(2)}) async-start(bf16[4,256,256]{2,1,0:T(8,128)(2,1)} %broadcast_in_dim.9), calls=%async_computation.4 | async-start | bytes 1048576 | tf_op jit(solution)/shard_map/all_to_all | solution.py:81
  175.6 3.6 %collective-permute-done.14 = bf16[2048,128]{1,0:T(8,128)(2,1)} collective-permute-done((bf16[2048,128]{1,0:T(8,128)(2,1)}, bf16[2048,128]{1,0:T(8,128)(2,1)}, u32[]{:S(2)}, u32[]{:S(2)}) %collective-permute-start.14) | collective-permute-done | bytes 524320 | tf_op jit(solution)/shard_map/ppermute | solution.py:77
  179.3 1.5 collective-permute-done.16
  180.8 2.5 %fusion.3 = bf16[2048,128]{1,0:T(8,128)(2,1)} fusion(bf16[2048,128]{1,0:T(8,128)(2,1)} %collective-permute-done.16, bf16[2048,128]{1,0:T(8,128)(2,1)} %collective-permute-done.14, bf16[4,2048,128]{2,1,0:T(8,128)(2,1)S(1)} %bitcast.53, s32[]{:T(128)S(6)} %select_n.26, bf16[8192,384]{1,0:T(8,128)(2,1)} %bitcast.60, s32[]{:T(128)S(6)} %select_n.24), kind=kLoop, calls=%fused_computation.9 | loop fusion | flops 2359296 | bytes 2621448 | tf_op jit(solution)/shard_map/convert_element_type | solution.py:295
  183.2 1.7 collective-permute-start.17
  184.9 1.2 collective-permute-start.18
  186.1 1.0 all-to-all-done.4.refs_4_
  187.1 1.4 collective-permute-start.22
  188.5 10.3 %collective-permute-start.19 = (bf16[2048,128]{1,0:T(8,128)(2,1)S(1)}, bf16[2048,128]{1,0:T(8,128)(2,1)S(1)}, u32[]{:S(2)}, u32[]{:S(2)}) collective-permute-start(bf16[2048,128]{1,0:T(8,128)(2,1)S(1)} %collective-permute-done.17.refs_0_), channel_id=1, source_target_pairs={{0,1},{1,0},{2,3},{3,2},{4,5},{5,4},{6,7},{7,6},{8,9},{9,8},{10,11... | collective-permute-start | bytes 1572872 | tf_op jit(solution)/shard_map/ppermute | solution.py:77
  198.8 2.6 %collective-permute-done.18.refs_1_ = bf16[2048,128]{1,0:T(8,128)(2,1)S(1)} collective-permute-done((bf16[2048,128]{1,0:T(8,128)(2,1)}, bf16[2048,128]{1,0:T(8,128)(2,1)S(1)}, u32[]{:S(2)}, u32[]{:S(2)}) %collective-permute-start.18) | collective-permute-done | bytes 524320 | tf_op jit(solution)/shard_map/ppermute | solution.py:297
  201.4 5.2 %collective-permute-start.20 = (bf16[2048,128]{1,0:T(8,128)(2,1)S(1)}, bf16[2048,128]{1,0:T(8,128)(2,1)S(1)}, u32[]{:S(2)}, u32[]{:S(2)}) collective-permute-start(bf16[2048,128]{1,0:T(8,128)(2,1)S(1)} %collective-permute-done.18.refs_1_), channel_id=1, source_target_pairs={{0,1},{1,0},{2,3},{3,2},{4,5},{5,4},{6,7},{7,6},{8,9},{9,8},{10,11... | collective-permute-start | bytes 1572872 | tf_op jit(solution)/shard_map/ppermute | solution.py:77
  206.7 6.0 %collective-permute-done.22.refs_6_ = bf16[4,256,256]{2,1,0:T(8,128)(2,1)S(1)} collective-permute-done((bf16[4,256,256]{2,1,0:T(8,128)(2,1)S(1)}, bf16[4,256,256]{2,1,0:T(8,128)(2,1)S(1)}, u32[]{:S(2)}, u32[]{:S(2)}) %collective-permute-start.22) | collective-permute-done | bytes 524320 | tf_op jit(solution)/shard_map/ppermute | solution.py:77
  212.9 1.5 collective-permute-start.24
  214.9 4.3 %collective-permute-done.23.refs_7_ = bf16[2,256,256]{2,1,0:T(8,128)(2,1)S(1)} collective-permute-done((bf16[2,256,256]{2,1,0:T(8,128)(2,1)S(1)}, bf16[2,256,256]{2,1,0:T(8,128)(2,1)S(1)}, u32[]{:S(2)}, u32[]{:S(2)}) %collective-permute-start.23) | collective-permute-done | bytes 262176 | tf_op jit(solution)/shard_map/ppermute | solution.py:77
  219.2 1.4 collective-permute-done.24.refs_8_
  220.7 1.4 collective-permute-done.29.refs_13_
  223.7 6.7 %unpack.1 = (bf16[2,2,2048,128]{3,2,1,0:T(8,128)(2,1)}, bf16[2,2,2,4,2,128,128]{6,5,4,3,2,1,0:T(8,128)(2,1)}, bf16[2,2,2,4,2,128,128]{6,5,4,3,2,1,0:T(8,128)(2,1)}) custom-call(s32[4]{0:T(128)} %pad_add_fusion.at_ref, bf16[2048,128]{1,0:T(8,128)(2,1)} %copy-done.6, bf16[2048,128]{1,0:T(8,128)(2,1)} %copy-done.7, bf16[2048,128]{1,0:T(8,128)(2,1)} %copy-done.8, ...), custom_call_target="tpu_custom_call" | custom-call | tf_op jit(solution)/shard_map/unpack/pallas_call | solution.py:208
  (110 shorter events, 19.3 us)
Async XLA Ops:
  7.2 97.2 %all-gather.2.cloned.1.call-start = ((), (), s32[]{:S(2)}) async-start(), calls=%async_computation.5 | async-start | bytes 8519680 | tf_op jit(solution)/shard_map/all_gather | solution.py:245
  9.3 0.7 collective-permute-start
  14.3 71.6 %copy-start.20 = (s32[1,512]{1,0:T(1,128)S(1)}, s32[1,512]{1,0:T(1,128)}, u32[]{:S(2)}) copy-start(s32[1,512]{1,0:T(1,128)} %param.9) | copy-start | bytes 6148
  14.3 72.3 %copy-start.21 = (f32[1,8]{1,0:T(1,128)S(1)}, f32[1,8]{1,0:T(1,128)}, u32[]{:S(2)}) copy-start(f32[1,8]{1,0:T(1,128)} %param.10) | copy-start | bytes 100
  14.3 86.2 %copy-start.19 = (bf16[1,512,128]{2,1,0:T(8,128)(2,1)S(1)}, bf16[1,512,128]{2,1,0:T(8,128)(2,1)}, u32[]{:S(2)}) copy-start(bf16[1,512,128]{2,1,0:T(8,128)(2,1)} %param.8) | copy-start | bytes 393220
  50.2 54.1 %copy-start = (bf16[32,128,128]{2,1,0:T(8,128)(2,1)}, bf16[32,128,128]{2,1,0:T(8,128)(2,1)S(1)}, u32[]{:S(2)}) copy-start(bf16[32,128,128]{2,1,0:T(8,128)(2,1)S(1)} %all_to_all.25.refs_0_) | copy-start | bytes 3145732
  50.2 30.9 %collective-permute-start.2 = (bf16[32,128,128]{2,1,0:T(8,128)(2,1)S(1)}, bf16[32,128,128]{2,1,0:T(8,128)(2,1)S(1)}, u32[]{:S(2)}, u32[]{:S(2)}) collective-permute-start(bf16[32,128,128]{2,1,0:T(8,128)(2,1)S(1)} %all_to_all.25.refs_0_), channel_id=1, source_target_pairs={{0,130},{2,128},{128,2},{130,0},{1,131},{3,129},{129,3},{131,1},{4... | collective-permute-start | bytes 3145736 | tf_op jit(solution)/shard_map/ppermute | solution.py:77
  58.5 25.7 %collective-permute-start.1 = (bf16[32,128,128]{2,1,0:T(8,128)(2,1)S(1)}, bf16[32,128,128]{2,1,0:T(8,128)(2,1)S(1)}, u32[]{:S(2)}, u32[]{:S(2)}) collective-permute-start(bf16[32,128,128]{2,1,0:T(8,128)(2,1)S(1)} %all_to_all.25.refs_0_), channel_id=1, source_target_pairs={{0,2},{2,0},{1,3},{3,1},{4,6},{6,4},{5,7},{7,5},{8,10},{10,8},{9,1... | collective-permute-start | bytes 3145736 | tf_op jit(solution)/shard_map/ppermute | solution.py:77
  81.1 23.3 %copy-start.1 = (bf16[32,128,128]{2,1,0:T(8,128)(2,1)}, bf16[32,128,128]{2,1,0:T(8,128)(2,1)S(1)}, u32[]{:S(2)}) copy-start(bf16[32,128,128]{2,1,0:T(8,128)(2,1)S(1)} %collective-permute-done.2.refs_2_) | copy-start | bytes 3145732
  82.0 14.8 %collective-permute-start.3 = (bf16[16,128,128]{2,1,0:T(8,128)(2,1)}, bf16[16,128,128]{2,1,0:T(8,128)(2,1)}, u32[]{:S(2)}, u32[]{:S(2)}) collective-permute-start(bf16[16,128,128]{2,1,0:T(8,128)(2,1)} %slice.109), channel_id=1, source_target_pairs={{0,2},{2,0},{1,3},{3,1},{4,6},{6,4},{5,7},{7,5},{8,10},{10,8},{9,1... | collective-permute-start | bytes 1572872 | tf_op jit(solution)/shard_map/ppermute | solution.py:77
  84.1 20.2 %copy-start.2 = (bf16[32,128,128]{2,1,0:T(8,128)(2,1)}, bf16[32,128,128]{2,1,0:T(8,128)(2,1)S(1)}, u32[]{:S(2)}) copy-start(bf16[32,128,128]{2,1,0:T(8,128)(2,1)S(1)} %collective-permute-done.1.refs_1_) | copy-start | bytes 3145732
  85.0 15.2 %collective-permute-start.4 = (bf16[16,128,128]{2,1,0:T(8,128)(2,1)}, bf16[16,128,128]{2,1,0:T(8,128)(2,1)}, u32[]{:S(2)}, u32[]{:S(2)}) collective-permute-start(bf16[16,128,128]{2,1,0:T(8,128)(2,1)} %slice.110), channel_id=1, source_target_pairs={{0,130},{2,128},{128,2},{130,0},{1,131},{3,129},{129,3},{131,1},{4... | collective-permute-start | bytes 1572872 | tf_op jit(solution)/shard_map/ppermute | solution.py:77
  86.0 10.7 %collective-permute-start.10 = (s32[512]{0:T(512)S(1)}, s32[512]{0:T(512)S(1)}, u32[]{:S(2)}, u32[]{:S(2)}) collective-permute-start(s32[512]{0:T(512)S(1)} %bitcast.65), channel_id=1, source_target_pairs={{0,0},{1,2},{2,1},{3,3},{4,4},{5,6},{6,5},{7,7},{8,8},{9,10},{10,9... | collective-permute-start | bytes 6152 | tf_op jit(solution)/shard_map/ppermute | solution.py:72
  86.6 4.8 %collective-permute-start.12 = (f32[8]{0:T(128)S(1)}, f32[8]{0:T(128)S(1)}, u32[]{:S(2)}, u32[]{:S(2)}) collective-permute-start(f32[8]{0:T(128)S(1)} %bitcast.66), channel_id=1, source_target_pairs={{0,0},{1,2},{2,1},{3,3},{4,4},{5,6},{6,5},{7,7},{8,8},{9,10},{10,9... | collective-permute-start | bytes 104 | tf_op jit(solution)/shard_map/ppermute | solution.py:72
  87.3 13.2 %collective-permute-start.5 = (bf16[32,128,128]{2,1,0:T(8,128)(2,1)S(1)}, bf16[32,128,128]{2,1,0:T(8,128)(2,1)}, u32[]{:S(2)}, u32[]{:S(2)}) collective-permute-start(bf16[32,128,128]{2,1,0:T(8,128)(2,1)S(1)} %all_to_all.25.refs_0_), channel_id=1, source_target_pairs={{0,1},{1,0},{2,3},{3,2},{4,5},{5,4},{6,7},{7,6},{8,9},{9,8},{10,11... | collective-permute-start | bytes 3145736 | tf_op jit(solution)/shard_map/ppermute | solution.py:77
  91.4 11.5 %collective-permute-start.6 = (bf16[32,128,128]{2,1,0:T(8,128)(2,1)S(1)}, bf16[32,128,128]{2,1,0:T(8,128)(2,1)}, u32[]{:S(2)}, u32[]{:S(2)}) collective-permute-start(bf16[32,128,128]{2,1,0:T(8,128)(2,1)S(1)} %collective-permute-done.1.refs_1_), channel_id=1, source_target_pairs={{0,1},{1,0},{2,3},{3,2},{4,5},{5,4},{6,7},{7,6},{8,9},{9,8},{10,11... | collective-permute-start | bytes 3145736 | tf_op jit(solution)/shard_map/ppermute | solution.py:77
  96.6 7.1 %collective-permute-start.7 = (bf16[32,128,128]{2,1,0:T(8,128)(2,1)S(1)}, bf16[32,128,128]{2,1,0:T(8,128)(2,1)}, u32[]{:S(2)}, u32[]{:S(2)}) collective-permute-start(bf16[32,128,128]{2,1,0:T(8,128)(2,1)S(1)} %collective-permute-done.2.refs_2_), channel_id=1, source_target_pairs={{0,1},{1,0},{2,3},{3,2},{4,5},{5,4},{6,7},{7,6},{8,9},{9,8},{10,11... | collective-permute-start | bytes 3145736 | tf_op jit(solution)/shard_map/ppermute | solution.py:77
  96.8 5.3 %collective-permute-start.8 = (bf16[16,128,128]{2,1,0:T(8,128)(2,1)}, bf16[16,128,128]{2,1,0:T(8,128)(2,1)S(1)}, u32[]{:S(2)}, u32[]{:S(2)}) collective-permute-start(bf16[16,128,128]{2,1,0:T(8,128)(2,1)} %collective-permute-done.3.refs_3_), channel_id=1, source_target_pairs={{0,1},{1,0},{2,3},{3,2},{4,5},{5,4},{6,7},{7,6},{8,9},{9,8},{10,11... | collective-permute-start | bytes 1572872 | tf_op jit(solution)/shard_map/ppermute | solution.py:77
  100.2 2.7 %collective-permute-start.9 = (bf16[16,128,128]{2,1,0:T(8,128)(2,1)}, bf16[16,128,128]{2,1,0:T(8,128)(2,1)S(1)}, u32[]{:S(2)}, u32[]{:S(2)}) collective-permute-start(bf16[16,128,128]{2,1,0:T(8,128)(2,1)} %collective-permute-done.4.refs_4_), channel_id=1, source_target_pairs={{0,1},{1,0},{2,3},{3,2},{4,5},{5,4},{6,7},{7,6},{8,9},{9,8},{10,11... | collective-permute-start | bytes 1572872 | tf_op jit(solution)/shard_map/ppermute | solution.py:77
  100.5 19.0 %collective-permute-start.11 = (bf16[512,128]{1,0:T(8,128)(2,1)S(1)}, bf16[512,128]{1,0:T(8,128)(2,1)S(1)}, u32[]{:S(2)}, u32[]{:S(2)}) collective-permute-start(bf16[512,128]{1,0:T(8,128)(2,1)S(1)} %bitcast.64), channel_id=1, source_target_pairs={{0,0},{1,2},{2,1},{3,3},{4,4},{5,6},{6,5},{7,7},{8,8},{9,10},{10,9... | collective-permute-start | bytes 393224 | tf_op jit(solution)/shard_map/ppermute | solution.py:72
  123.8 15.5 %all-to-all-start.1 = ((bf16[8,64,256]{2,1,0:T(8,128)(2,1)}), bf16[8,64,256]{2,1,0:T(8,128)(2,1)S(1)}, u32[]{:S(2)}, u32[]{:S(2)}) async-start(bf16[8,64,256]{2,1,0:T(8,128)(2,1)} %fusion.9), calls=%async_computation.1 | async-start | bytes 524288 | tf_op jit(solution)/shard_map/all_to_all | solution.py:81
  136.3 10.1 %collective-permute-start.13 = (bf16[1024,128]{1,0:T(8,128)(2,1)}, bf16[1024,128]{1,0:T(8,128)(2,1)S(1)}, u32[]{:S(2)}, u32[]{:S(2)}) collective-permute-start(bf16[1024,128]{1,0:T(8,128)(2,1)} %get-tuple-element.17), channel_id=1, source_target_pairs={{0,130},{2,128},{128,2},{130,0},{1,131},{3,129},{129,3},{131,1},{4... | collective-permute-start | bytes 786440 | tf_op jit(solution)/shard_map/ppermute | solution.py:77
  137.2 9.2 %collective-permute-start.15 = (bf16[1024,128]{1,0:T(8,128)(2,1)S(1)}, bf16[1024,128]{1,0:T(8,128)(2,1)}, u32[]{:S(2)}, u32[]{:S(2)}) collective-permute-start(bf16[1024,128]{1,0:T(8,128)(2,1)S(1)} %get-tuple-element.19), channel_id=1, source_target_pairs={{0,2},{2,0},{1,3},{3,1},{4,6},{6,4},{5,7},{7,5},{8,10},{10,8},{9,1... | collective-permute-start | bytes 786440 | tf_op jit(solution)/shard_map/ppermute | solution.py:77
  140.1 13.1 %all-to-all-start.2 = ((bf16[8,64,256]{2,1,0:T(8,128)(2,1)}), bf16[8,64,256]{2,1,0:T(8,128)(2,1)S(1)}, u32[]{:S(2)}, u32[]{:S(2)}) async-start(bf16[8,64,256]{2,1,0:T(8,128)(2,1)} %broadcast_in_dim.8), calls=%async_computation.2 | async-start | bytes 524288 | tf_op jit(solution)/shard_map/all_to_all | solution.py:81
  155.6 15.6 %all-to-all-start.3 = ((bf16[4,256,256]{2,1,0:T(8,128)(2,1)}), bf16[4,256,256]{2,1,0:T(8,128)(2,1)S(1)}, u32[]{:S(2)}, u32[]{:S(2)}) async-start(bf16[4,256,256]{2,1,0:T(8,128)(2,1)} %bitcast.56), calls=%async_computation.3 | async-start | bytes 1048576 | tf_op jit(solution)/shard_map/all_to_all | solution.py:81
  162.1 17.2 %collective-permute-start.14 = (bf16[2048,128]{1,0:T(8,128)(2,1)}, bf16[2048,128]{1,0:T(8,128)(2,1)}, u32[]{:S(2)}, u32[]{:S(2)}) collective-permute-start(bf16[2048,128]{1,0:T(8,128)(2,1)} %pad_maximum_fusion), channel_id=1, source_target_pairs={{0,2},{2,0},{1,3},{3,1},{4,6},{6,4},{5,7},{7,5},{8,10},{10,8},{9,1... | collective-permute-start | bytes 1572872 | tf_op jit(solution)/shard_map/ppermute | solution.py:77
  164.9 15.8 %collective-permute-start.16 = (bf16[2048,128]{1,0:T(8,128)(2,1)}, bf16[2048,128]{1,0:T(8,128)(2,1)}, u32[]{:S(2)}, u32[]{:S(2)}) collective-permute-start(bf16[2048,128]{1,0:T(8,128)(2,1)} %pad_maximum_fusion.1), channel_id=1, source_target_pairs={{0,130},{2,128},{128,2},{130,0},{1,131},{3,129},{129,3},{131,1},{4... | collective-permute-start | bytes 1572872 | tf_op jit(solution)/shard_map/ppermute | solution.py:77
  172.1 14.9 %all-to-all-start.4 = ((bf16[4,256,256]{2,1,0:T(8,128)(2,1)}), bf16[4,256,256]{2,1,0:T(8,128)(2,1)S(1)}, u32[]{:S(2)}, u32[]{:S(2)}) async-start(bf16[4,256,256]{2,1,0:T(8,128)(2,1)} %broadcast_in_dim.9), calls=%async_computation.4 | async-start | bytes 1048576 | tf_op jit(solution)/shard_map/all_to_all | solution.py:81
  183.2 5.3 %collective-permute-start.17 = (bf16[2048,128]{1,0:T(8,128)(2,1)}, bf16[2048,128]{1,0:T(8,128)(2,1)S(1)}, u32[]{:S(2)}, u32[]{:S(2)}) collective-permute-start(bf16[2048,128]{1,0:T(8,128)(2,1)} %fusion.3), channel_id=1, source_target_pairs={{0,0},{1,2},{2,1},{3,3},{4,4},{5,6},{6,5},{7,7},{8,8},{9,10},{10,9... | collective-permute-start | bytes 1572872 | tf_op jit(solution)/shard_map/ppermute | solution.py:72
  184.9 16.5 %collective-permute-start.18 = (bf16[2048,128]{1,0:T(8,128)(2,1)}, bf16[2048,128]{1,0:T(8,128)(2,1)S(1)}, u32[]{:S(2)}, u32[]{:S(2)}) collective-permute-start(bf16[2048,128]{1,0:T(8,128)(2,1)} %fusion.3), channel_id=1, source_target_pairs={{0,128},{1,130},{2,129},{3,131},{128,0},{129,2},{130,1},{131,3},{4... | collective-permute-start | bytes 1572872 | tf_op jit(solution)/shard_map/ppermute | solution.py:297
  187.1 36.5 %copy-start.3 = (bf16[4,256,256]{2,1,0:T(8,128)(2,1)}, bf16[4,256,256]{2,1,0:T(8,128)(2,1)S(1)}, u32[]{:S(2)}) copy-start(bf16[4,256,256]{2,1,0:T(8,128)(2,1)S(1)} %all-to-all-done.4.refs_4_) | copy-start | bytes 1572868
  187.1 25.6 %collective-permute-start.22 = (bf16[4,256,256]{2,1,0:T(8,128)(2,1)S(1)}, bf16[4,256,256]{2,1,0:T(8,128)(2,1)S(1)}, u32[]{:S(2)}, u32[]{:S(2)}) collective-permute-start(bf16[4,256,256]{2,1,0:T(8,128)(2,1)S(1)} %all-to-all-done.4.refs_4_), channel_id=1, source_target_pairs={{0,130},{2,128},{128,2},{130,0},{1,131},{3,129},{129,3},{131,1},{4... | collective-permute-start | bytes 1572872 | tf_op jit(solution)/shard_map/ppermute | solution.py:77
  188.5 24.3 %collective-permute-start.21 = (bf16[4,256,256]{2,1,0:T(8,128)(2,1)S(1)}, bf16[4,256,256]{2,1,0:T(8,128)(2,1)S(1)}, u32[]{:S(2)}, u32[]{:S(2)}) collective-permute-start(bf16[4,256,256]{2,1,0:T(8,128)(2,1)S(1)} %all-to-all-done.4.refs_4_), channel_id=1, source_target_pairs={{0,2},{2,0},{1,3},{3,1},{4,6},{6,4},{5,7},{7,5},{8,10},{10,8},{9,1... | collective-permute-start | bytes 1572872 | tf_op jit(solution)/shard_map/ppermute | solution.py:77
  188.5 35.1 %copy-start.6 = (bf16[2048,128]{1,0:T(8,128)(2,1)}, bf16[2048,128]{1,0:T(8,128)(2,1)S(1)}, u32[]{:S(2)}) copy-start(bf16[2048,128]{1,0:T(8,128)(2,1)S(1)} %collective-permute-done.17.refs_0_) | copy-start | bytes 1572868
  188.5 25.8 %collective-permute-start.19 = (bf16[2048,128]{1,0:T(8,128)(2,1)S(1)}, bf16[2048,128]{1,0:T(8,128)(2,1)S(1)}, u32[]{:S(2)}, u32[]{:S(2)}) collective-permute-start(bf16[2048,128]{1,0:T(8,128)(2,1)S(1)} %collective-permute-done.17.refs_0_), channel_id=1, source_target_pairs={{0,1},{1,0},{2,3},{3,2},{4,5},{5,4},{6,7},{7,6},{8,9},{9,8},{10,11... | collective-permute-start | bytes 1572872 | tf_op jit(solution)/shard_map/ppermute | solution.py:77
  201.4 22.2 %copy-start.7 = (bf16[2048,128]{1,0:T(8,128)(2,1)}, bf16[2048,128]{1,0:T(8,128)(2,1)S(1)}, u32[]{:S(2)}) copy-start(bf16[2048,128]{1,0:T(8,128)(2,1)S(1)} %collective-permute-done.18.refs_1_) | copy-start | bytes 1572868
  201.4 12.9 %collective-permute-start.20 = (bf16[2048,128]{1,0:T(8,128)(2,1)S(1)}, bf16[2048,128]{1,0:T(8,128)(2,1)S(1)}, u32[]{:S(2)}, u32[]{:S(2)}) collective-permute-start(bf16[2048,128]{1,0:T(8,128)(2,1)S(1)} %collective-permute-done.18.refs_1_), channel_id=1, source_target_pairs={{0,1},{1,0},{2,3},{3,2},{4,5},{5,4},{6,7},{7,6},{8,9},{9,8},{10,11... | collective-permute-start | bytes 1572872 | tf_op jit(solution)/shard_map/ppermute | solution.py:77
  206.6 13.9 %collective-permute-start.25 = (bf16[4,256,256]{2,1,0:T(8,128)(2,1)S(1)}, bf16[4,256,256]{2,1,0:T(8,128)(2,1)S(1)}, u32[]{:S(2)}, u32[]{:S(2)}) collective-permute-start(bf16[4,256,256]{2,1,0:T(8,128)(2,1)S(1)} %all-to-all-done.4.refs_4_), channel_id=1, source_target_pairs={{0,1},{1,0},{2,3},{3,2},{4,5},{5,4},{6,7},{7,6},{8,9},{9,8},{10,11... | collective-permute-start | bytes 1572872 | tf_op jit(solution)/shard_map/ppermute | solution.py:77
  212.7 11.0 %copy-start.4 = (bf16[4,256,256]{2,1,0:T(8,128)(2,1)}, bf16[4,256,256]{2,1,0:T(8,128)(2,1)S(1)}, u32[]{:S(2)}) copy-start(bf16[4,256,256]{2,1,0:T(8,128)(2,1)S(1)} %collective-permute-done.22.refs_6_) | copy-start | bytes 1572868
  212.7 6.5 %collective-permute-start.23 = (bf16[2,256,256]{2,1,0:T(8,128)(2,1)S(1)}, bf16[2,256,256]{2,1,0:T(8,128)(2,1)S(1)}, u32[]{:S(2)}, u32[]{:S(2)}) collective-permute-start(bf16[2,256,256]{2,1,0:T(8,128)(2,1)S(1)} %slice.121), channel_id=1, source_target_pairs={{0,2},{2,0},{1,3},{3,1},{4,6},{6,4},{5,7},{7,5},{8,10},{10,8},{9,1... | collective-permute-start | bytes 786440 | tf_op jit(solution)/shard_map/ppermute | solution.py:77
  212.8 10.8 %copy-start.5 = (bf16[4,256,256]{2,1,0:T(8,128)(2,1)}, bf16[4,256,256]{2,1,0:T(8,128)(2,1)S(1)}, u32[]{:S(2)}) copy-start(bf16[4,256,256]{2,1,0:T(8,128)(2,1)S(1)} %collective-permute-done.21.refs_5_) | copy-start | bytes 1572868
  212.9 7.7 %collective-permute-start.24 = (bf16[2,256,256]{2,1,0:T(8,128)(2,1)S(1)}, bf16[2,256,256]{2,1,0:T(8,128)(2,1)S(1)}, u32[]{:S(2)}, u32[]{:S(2)}) collective-permute-start(bf16[2,256,256]{2,1,0:T(8,128)(2,1)S(1)} %slice.122), channel_id=1, source_target_pairs={{0,130},{2,128},{128,2},{130,0},{1,131},{3,129},{129,3},{131,1},{4... | collective-permute-start | bytes 786440 | tf_op jit(solution)/shard_map/ppermute | solution.py:77
  214.4 9.3 %copy-start.8 = (bf16[2048,128]{1,0:T(8,128)(2,1)}, bf16[2048,128]{1,0:T(8,128)(2,1)S(1)}, u32[]{:S(2)}) copy-start(bf16[2048,128]{1,0:T(8,128)(2,1)S(1)} %collective-permute-done.19.refs_2_) | copy-start | bytes 1572868
  214.4 7.8 %collective-permute-start.26 = (bf16[4,256,256]{2,1,0:T(8,128)(2,1)S(1)}, bf16[4,256,256]{2,1,0:T(8,128)(2,1)S(1)}, u32[]{:S(2)}, u32[]{:S(2)}) collective-permute-start(bf16[4,256,256]{2,1,0:T(8,128)(2,1)S(1)} %collective-permute-done.21.refs_5_), channel_id=1, source_target_pairs={{0,1},{1,0},{2,3},{3,2},{4,5},{5,4},{6,7},{7,6},{8,9},{9,8},{10,11... | collective-permute-start | bytes 1572872 | tf_op jit(solution)/shard_map/ppermute | solution.py:77
  214.4 7.8 %copy-start.9 = (bf16[2048,128]{1,0:T(8,128)(2,1)}, bf16[2048,128]{1,0:T(8,128)(2,1)S(1)}, u32[]{:S(2)}) copy-start(bf16[2048,128]{1,0:T(8,128)(2,1)S(1)} %collective-permute-done.20.refs_3_) | copy-start | bytes 1572868
  214.4 9.2 %collective-permute-start.27 = (bf16[4,256,256]{2,1,0:T(8,128)(2,1)S(1)}, bf16[4,256,256]{2,1,0:T(8,128)(2,1)}, u32[]{:S(2)}, u32[]{:S(2)}) collective-permute-start(bf16[4,256,256]{2,1,0:T(8,128)(2,1)S(1)} %collective-permute-done.22.refs_6_), channel_id=1, source_target_pairs={{0,1},{1,0},{2,3},{3,2},{4,5},{5,4},{6,7},{7,6},{8,9},{9,8},{10,11... | collective-permute-start | bytes 1572872 | tf_op jit(solution)/shard_map/ppermute | solution.py:77
  219.2 1.5 collective-permute-start.28
  220.6 1.5 collective-permute-start.29
  (9 other events, 12.8 us)
Sparse Core Ops, SparseCore 0:
  10.8 93.5 all-gather.1

commit v9 on v7

--- a/solution.py
+++ b/solution.py
@@ -126,7 +126,7 @@
         def block(group, n):
             if n < 3:
                 return group[n][...]
-            return jnp.where(b < 2, group[3][...], group[4][...])
+            return jnp.where(b < 1, group[3][...], group[4][...])
 
         for n, (l, h) in enumerate(spots):
             own = block(mine, n)
@@ -138,7 +138,7 @@
             wkv_ref[:, l, h, 1 - core, :, HD : 2 * HD] = other[:, 96:128]
 
         rows = rows_ref[...]
-        for n in (0, 1):
+        for n in range(4):
             member_ref[:, n * HD : (n + 1) * HD] = rows_ref[
                 :, pl.ds(pl.multiple_of(n * 1024 + at_ref[3] * HD, HD), HD)
             ]
@@ -148,15 +148,15 @@
             out_ref[...] = jnp.zeros_like(out_ref)
 
         out_ref[:, 0:HD] += jnp.dot(
-            rows, wq_ref[...].reshape(2048, HD), preferred_element_type=jnp.float32
+            rows, wq_ref[...].reshape(4096, HD), preferred_element_type=jnp.float32
         )
         out_ref[:, HD : 3 * HD] += jnp.dot(
-            rows, wkv_ref[...].reshape(2048, 2 * HD), preferred_element_type=jnp.float32
+            rows, wkv_ref[...].reshape(4096, 2 * HD), preferred_element_type=jnp.float32
         )
 
-    whole = pl.BlockSpec((8, 128, HD), lambda b, at: (b, 0, 0))
-    first = pl.BlockSpec((8, 128, HD), lambda b, at: (jnp.minimum(b, 1), 0, 0))
-    last = pl.BlockSpec((8, 128, HD), lambda b, at: (jnp.maximum(b, 2) - 2, 0, 0))
+    whole = pl.BlockSpec((16, 128, HD), lambda b, at: (b, 0, 0))
+    first = pl.BlockSpec((16, 128, HD), lambda b, at: (jnp.minimum(b, 0), 0, 0))
+    last = pl.BlockSpec((16, 128, HD), lambda b, at: (jnp.maximum(b, 1) - 1, 0, 0))
     group = [whole, whole, whole, first, last]
     bf16 = jnp.bfloat16
     return pl.pallas_call(
@@ -169,13 +169,13 @@
         ),
         grid_spec=pltpu.PrefetchScalarGridSpec(
             num_scalar_prefetch=1,
-            grid=(4,),
-            in_specs=[pl.BlockSpec((512, 2048), lambda b, at: (0, b))] + group + group,
+            grid=(2,),
+            in_specs=[pl.BlockSpec((512, 4096), lambda b, at: (0, b))] + group + group,
             out_specs=(
                 pl.BlockSpec((512, 3 * HD), lambda b, at: (0, 0)),
-                pl.BlockSpec((8, 2, 2, 64, HD), lambda b, at: (b, 0, 0, 0, 0)),
-                pl.BlockSpec((8, 2, 2, 2, 32, 2 * HD), lambda b, at: (b, 0, 0, 0, 0, 0)),
-                pl.BlockSpec((512, 2 * HD), lambda b, at: (0, b)),
+                pl.BlockSpec((16, 2, 2, 64, HD), lambda b, at: (b, 0, 0, 0, 0)),
+                pl.BlockSpec((16, 2, 2, 2, 32, 2 * HD), lambda b, at: (b, 0, 0, 0, 0, 0)),
+                pl.BlockSpec((512, 4 * HD), lambda b, at: (0, b)),
             ),
         ),
         name="project",
@@ -317,8 +317,7 @@
     part_kv = lax.dot_general(
         normed_m, kv_sum, contract, preferred_element_type=f32
     ).astype(bf16)
-    part_kv = exchange(part_kv.reshape(4, 256, 2 * HD), X)
-    part_kv = part_kv.astype(f32)
+    part_kv = exchange(part_kv.reshape(4, 256, 2 * HD), X).astype(f32)
     old_kv = wkv.reshape(4, 2, 8, 128, 2 * HD)
     old_kv = lax.dynamic_index_in_dim(old_kv, ring, 0, keepdims=False)
     old_kv = lax.dynamic_index_in_dim(old_kv, member, 1, keepdims=False).reshape(256, 2 * HD)

time: 240 us -> 241 us (level)
  transfers between devices with their start and end apart: 35 -> 35, of which waited for: 19 -> 19; matrix products, arithmetic and copies ran while one was open for 9% -> 9% of each run, Pallas kernels for 6% -> 7%
where the time goes in v9:
time: 241 us; the launch traced here: 238 us
  starting transfers between devices  68.1 us (28%)
  waiting for transfers between devices  62.9 us (26%)
  blocking collectives  36 us (15%)
  Pallas kernels  22.3 us (9%)
  other arithmetic  15.3 us (6%)
  between operations  14.4 us (6%)
  matrix products  10.5 us (4%)
  local copies, waits for them, and re-layouts  8.04 us (3%)
    ppermute x24, waiting for transfers between devices, flip(): return lax.ppermute(x, axes, [(i, n - 1 - i) for i in range(n)])  48.2 us
    ppermute x24, starting transfers between devices, flip(): return lax.ppermute(x, axes, [(i, n - 1 - i) for i in range(n)])  44.9 us
    all_to_all x1, blocking collectives, exchange(): return lax.all_to_all(x, axes, split_axis=0, concat_axis=0, tiled=True)  36 us
    all_to_all x4, starting transfers between devices, exchange(): return lax.all_to_all(x, axes, split_axis=0, concat_axis=0, tiled=True)  17.4 us
    pallas_call x1, Pallas kernels, project(): pl.pallas_call(body, out_shape=(jax.ShapeDtypeStruct((512, 3 * HD), jnp.f...  12.6 us
    all_to_all x4, waiting for transfers between devices, exchange(): return lax.all_to_all(x, axes, split_axis=0, concat_axis=0, tiled=True)  11.2 us
    pallas_call x1, Pallas kernels, unpack(): pl.pallas_call(body, out_shape=(jax.ShapeDtypeStruct((2, 2, 2048, HD), bf...  6.67 us
    dot_general x1, matrix products, local(): lax.dot_general(normed, scaled_q, contract, preferred_element_type=f32)  5.87 us
  transfers between devices with their start and end apart: 35, of which 19 were waited for; matrix products, arithmetic and copies ran while one was open for 9% of the time, Pallas kernels for 7%

profile of v9, /device:TPU:8, one launch (start us, length us, event | category | flops | bytes accessed | tf_op | source)
XLA Modules:
  0.0 237.6 jit_solution(1468247051104078505)
XLA Ops:
  7.2 1.1 fusion.31
  8.3 1.0 fusion.32
  11.3 3.1 %pack_columns.1 = bf16[32,128,128]{2,1,0:T(8,128)(2,1)} custom-call(s32[4]{0:T(128)} %pad_add_fusion.at_ref, bf16[128,8192]{1,0:T(8,128)(2,1)} %q_ref.1, bf16[128,1024]{1,0:T(8,128)(2,1)} %k_ref.1, bf16[128,1024]{1,0:T(8,128)(2,1)} %v_ref.1), custom_call_target="tpu_custom_call" | custom-call | tf_op jit(solution)/shard_map/pack_columns/pallas_call | solution.py:105
  14.4 36.0 %all_to_all.25.refs_0_ = bf16[32,128,128]{2,1,0:T(8,128)(2,1)S(1)} all-to-all(bf16[32,128,128]{2,1,0:T(8,128)(2,1)} %pack_columns.1), channel_id=1, replica_groups=mesh['xh'=2,'y'=4,'zh'=2,'zl'=4,'xl'=2,'core'=2] {'y','zh','zl'}, dimensions={0} | all-to-all | bytes 2097152 | tf_op jit(solution)/shard_map/all_to_all | solution.py:81
  50.4 8.1 %collective-permute-start.2 = (bf16[32,128,128]{2,1,0:T(8,128)(2,1)S(1)}, bf16[32,128,128]{2,1,0:T(8,128)(2,1)S(1)}, u32[]{:S(2)}, u32[]{:S(2)}) collective-permute-start(bf16[32,128,128]{2,1,0:T(8,128)(2,1)S(1)} %all_to_all.25.refs_0_), channel_id=1, source_target_pairs={{0,130},{2,128},{128,2},{130,0},{1,131},{3,129},{129,3},{131,1},{4... | collective-permute-start | bytes 3145736 | tf_op jit(solution)/shard_map/ppermute | solution.py:77
  58.5 22.5 %collective-permute-done.2.refs_2_ = bf16[32,128,128]{2,1,0:T(8,128)(2,1)S(1)} collective-permute-done((bf16[32,128,128]{2,1,0:T(8,128)(2,1)S(1)}, bf16[32,128,128]{2,1,0:T(8,128)(2,1)S(1)}, u32[]{:S(2)}, u32[]{:S(2)}) %collective-permute-start.2) | collective-permute-done | bytes 1048608 | tf_op jit(solution)/shard_map/ppermute | solution.py:77
  81.8 1.8 collective-permute-start.3
  84.0 0.9 slice.110
  84.9 1.6 collective-permute-start.4
  87.8 4.1 %collective-permute-start.5 = (bf16[32,128,128]{2,1,0:T(8,128)(2,1)S(1)}, bf16[32,128,128]{2,1,0:T(8,128)(2,1)}, u32[]{:S(2)}, u32[]{:S(2)}) collective-permute-start(bf16[32,128,128]{2,1,0:T(8,128)(2,1)S(1)} %all_to_all.25.refs_0_), channel_id=1, source_target_pairs={{0,1},{1,0},{2,3},{3,2},{4,5},{5,4},{6,7},{7,6},{8,9},{9,8},{10,11... | collective-permute-start | bytes 3145736 | tf_op jit(solution)/shard_map/ppermute | solution.py:77
  91.9 4.5 %collective-permute-start.6 = (bf16[32,128,128]{2,1,0:T(8,128)(2,1)S(1)}, bf16[32,128,128]{2,1,0:T(8,128)(2,1)}, u32[]{:S(2)}, u32[]{:S(2)}) collective-permute-start(bf16[32,128,128]{2,1,0:T(8,128)(2,1)S(1)} %collective-permute-done.1.refs_1_), channel_id=1, source_target_pairs={{0,1},{1,0},{2,3},{3,2},{4,5},{5,4},{6,7},{7,6},{8,9},{9,8},{10,11... | collective-permute-start | bytes 3145736 | tf_op jit(solution)/shard_map/ppermute | solution.py:77
  97.1 3.5 %collective-permute-done.4.refs_4_ = bf16[16,128,128]{2,1,0:T(8,128)(2,1)} collective-permute-done((bf16[16,128,128]{2,1,0:T(8,128)(2,1)}, bf16[16,128,128]{2,1,0:T(8,128)(2,1)}, u32[]{:S(2)}, u32[]{:S(2)}) %collective-permute-start.4) | collective-permute-done | bytes 524320 | tf_op jit(solution)/shard_map/ppermute | solution.py:77
  104.3 12.6 %project.1 = (f32[512,384]{1,0:T(8,128)}, bf16[32,2,2,64,128]{4,3,2,1,0:T(8,128)(2,1)}, bf16[32,2,2,2,32,256]{5,4,3,2,1,0:T(8,128)(2,1)}, bf16[512,1024]{1,0:T(8,128)(2,1)}) custom-call(s32[4]{0:T(128)} %pad_add_fusion.at_ref, bf16[512,8192]{1,0:T(8,128)(2,1)} %all-gather.2.cloned.1.call-done.rows_ref, bf16[32,128,128]{2,1,0:T(8,128)(2,1)} %copy-done, ...), custom_call_target="tpu_custom_call" | custom-call | tf_op jit(solution)/shard_map/project/pallas_call | solution.py:162
  116.9 1.2 broadcast_multiply_fusion
  118.1 1.3 fusion.38
  121.8 1.3 fusion.35
  123.5 0.9 fusion.9
  124.4 5.9 %all-to-all-start.1 = ((bf16[8,64,256]{2,1,0:T(8,128)(2,1)}), bf16[8,64,256]{2,1,0:T(8,128)(2,1)S(1)}, u32[]{:S(2)}, u32[]{:S(2)}) async-start(bf16[8,64,256]{2,1,0:T(8,128)(2,1)} %fusion.9), calls=%async_computation.1 | async-start | bytes 524288 | tf_op jit(solution)/shard_map/all_to_all | solution.py:81
  130.2 5.9 %convolution_convert_fusion = bf16[8192,128]{1,0:T(8,128)(2,1)S(1)} fusion(bf16[512,8192]{1,0:T(8,128)(2,1)} %all-gather.2.cloned.1.call-done.rows_ref, f32[512,64]{1,0:T(8,128)S(1)} %get-tuple-element.31, f32[512,64]{1,0:T(8,128)S(1)} %get-tuple-element.32), kind=kOutput, calls=%fused_computation | convolution fusion | flops 1074987008 | bytes 10747904 | tf_op jit(solution)/shard_map/dot_general | solution.py:281
  138.4 1.6 all-to-all-done.1
  140.7 3.6 %all-to-all-start.2 = ((bf16[8,64,256]{2,1,0:T(8,128)(2,1)}), bf16[8,64,256]{2,1,0:T(8,128)(2,1)S(1)}, u32[]{:S(2)}, u32[]{:S(2)}) async-start(bf16[8,64,256]{2,1,0:T(8,128)(2,1)} %broadcast_in_dim.8), calls=%async_computation.2 | async-start | bytes 524288 | tf_op jit(solution)/shard_map/all_to_all | solution.py:81
  144.4 2.7 %collective-permute-done.13 = bf16[1024,128]{1,0:T(8,128)(2,1)S(1)} collective-permute-done((bf16[1024,128]{1,0:T(8,128)(2,1)}, bf16[1024,128]{1,0:T(8,128)(2,1)S(1)}, u32[]{:S(2)}, u32[]{:S(2)}) %collective-permute-start.13) | collective-permute-done | bytes 262176 | tf_op jit(solution)/shard_map/ppermute | solution.py:77
  147.0 1.8 fusion.11
  148.8 5.1 %all-to-all-done.2 = bf16[8,64,256]{2,1,0:T(8,128)(2,1)S(1)} async-done(((bf16[8,64,256]{2,1,0:T(8,128)(2,1)}), bf16[8,64,256]{2,1,0:T(8,128)(2,1)S(1)}, u32[]{:S(2)}, u32[]{:S(2)}) %all-to-all-start.2) | async-done | bytes 262176 | tf_op jit(solution)/shard_map/all_to_all | solution.py:81
  154.0 2.5 %convolution_convert_fusion.1 = bf16[1024,256]{1,0:T(8,128)(2,1)} fusion(bf16[512,1024]{1,0:T(8,128)(2,1)} %get-tuple-element.13, bf16[512,256]{1,0:T(8,128)(2,1)S(1)} %bitcast.57), kind=kOutput, calls=%fused_computation.2 | convolution fusion | flops 268697600 | bytes 1835008 | tf_op jit(solution)/shard_map/dot_general | solution.py:317
  156.5 4.5 %all-to-all-start.3 = ((bf16[4,256,256]{2,1,0:T(8,128)(2,1)}), bf16[4,256,256]{2,1,0:T(8,128)(2,1)S(1)}, u32[]{:S(2)}, u32[]{:S(2)}) async-start(bf16[4,256,256]{2,1,0:T(8,128)(2,1)} %bitcast.56), calls=%async_computation.3 | async-start | bytes 1048576 | tf_op jit(solution)/shard_map/all_to_all | solution.py:81
  161.0 1.8 pad_maximum_fusion
  162.8 2.0 collective-permute-start.14
  165.6 2.1 collective-permute-start.16
  167.7 0.9 constant_dynamic-slice_fusion
  168.6 3.3 %all-to-all-done.3 = bf16[4,256,256]{2,1,0:T(8,128)(2,1)S(1)} async-done(((bf16[4,256,256]{2,1,0:T(8,128)(2,1)}), bf16[4,256,256]{2,1,0:T(8,128)(2,1)S(1)}, u32[]{:S(2)}, u32[]{:S(2)}) %all-to-all-start.3) | async-done | bytes 524320 | tf_op jit(solution)/shard_map/all_to_all | solution.py:81
  172.9 3.5 %all-to-all-start.4 = ((bf16[4,256,256]{2,1,0:T(8,128)(2,1)}), bf16[4,256,256]{2,1,0:T(8,128)(2,1)S(1)}, u32[]{:S(2)}, u32[]{:S(2)}) async-start(bf16[4,256,256]{2,1,0:T(8,128)(2,1)} %broadcast_in_dim.9), calls=%async_computation.4 | async-start | bytes 1048576 | tf_op jit(solution)/shard_map/all_to_all | solution.py:81
  176.3 3.6 %collective-permute-done.14 = bf16[2048,128]{1,0:T(8,128)(2,1)} collective-permute-done((bf16[2048,128]{1,0:T(8,128)(2,1)}, bf16[2048,128]{1,0:T(8,128)(2,1)}, u32[]{:S(2)}, u32[]{:S(2)}) %collective-permute-start.14) | collective-permute-done | bytes 524320 | tf_op jit(solution)/shard_map/ppermute | solution.py:77
  179.9 1.4 collective-permute-done.16
  181.3 2.3 fusion.3
  183.6 1.7 collective-permute-start.17
  185.3 1.3 collective-permute-start.18
  186.6 1.2 all-to-all-done.4.refs_4_
  187.8 1.2 collective-permute-start.22
  189.0 10.2 %collective-permute-start.19 = (bf16[2048,128]{1,0:T(8,128)(2,1)S(1)}, bf16[2048,128]{1,0:T(8,128)(2,1)S(1)}, u32[]{:S(2)}, u32[]{:S(2)}) collective-permute-start(bf16[2048,128]{1,0:T(8,128)(2,1)S(1)} %collective-permute-done.17.refs_0_), channel_id=1, source_target_pairs={{0,1},{1,0},{2,3},{3,2},{4,5},{5,4},{6,7},{7,6},{8,9},{9,8},{10,11... | collective-permute-start | bytes 1572872 | tf_op jit(solution)/shard_map/ppermute | solution.py:77
  199.2 2.6 %collective-permute-done.18.refs_1_ = bf16[2048,128]{1,0:T(8,128)(2,1)S(1)} collective-permute-done((bf16[2048,128]{1,0:T(8,128)(2,1)}, bf16[2048,128]{1,0:T(8,128)(2,1)S(1)}, u32[]{:S(2)}, u32[]{:S(2)}) %collective-permute-start.18) | collective-permute-done | bytes 524320 | tf_op jit(solution)/shard_map/ppermute | solution.py:302
  201.8 5.2 %collective-permute-start.20 = (bf16[2048,128]{1,0:T(8,128)(2,1)S(1)}, bf16[2048,128]{1,0:T(8,128)(2,1)S(1)}, u32[]{:S(2)}, u32[]{:S(2)}) collective-permute-start(bf16[2048,128]{1,0:T(8,128)(2,1)S(1)} %collective-permute-done.18.refs_1_), channel_id=1, source_target_pairs={{0,1},{1,0},{2,3},{3,2},{4,5},{5,4},{6,7},{7,6},{8,9},{9,8},{10,11... | collective-permute-start | bytes 1572872 | tf_op jit(solution)/shard_map/ppermute | solution.py:77
  207.1 6.0 %collective-permute-done.22.refs_6_ = bf16[4,256,256]{2,1,0:T(8,128)(2,1)S(1)} collective-permute-done((bf16[4,256,256]{2,1,0:T(8,128)(2,1)S(1)}, bf16[4,256,256]{2,1,0:T(8,128)(2,1)S(1)}, u32[]{:S(2)}, u32[]{:S(2)}) %collective-permute-start.22) | collective-permute-done | bytes 524320 | tf_op jit(solution)/shard_map/ppermute | solution.py:77
  213.3 1.5 collective-permute-start.24
  215.3 4.3 %collective-permute-done.23.refs_7_ = bf16[2,256,256]{2,1,0:T(8,128)(2,1)S(1)} collective-permute-done((bf16[2,256,256]{2,1,0:T(8,128)(2,1)S(1)}, bf16[2,256,256]{2,1,0:T(8,128)(2,1)S(1)}, u32[]{:S(2)}, u32[]{:S(2)}) %collective-permute-start.23) | collective-permute-done | bytes 262176 | tf_op jit(solution)/shard_map/ppermute | solution.py:77
  219.6 1.4 collective-permute-done.24.refs_8_
  221.1 1.4 collective-permute-done.29.refs_13_
  224.1 6.7 %unpack.1 = (bf16[2,2,2048,128]{3,2,1,0:T(8,128)(2,1)}, bf16[2,2,2,4,2,128,128]{6,5,4,3,2,1,0:T(8,128)(2,1)}, bf16[2,2,2,4,2,128,128]{6,5,4,3,2,1,0:T(8,128)(2,1)}) custom-call(s32[4]{0:T(128)} %pad_add_fusion.at_ref, bf16[2048,128]{1,0:T(8,128)(2,1)} %copy-done.6, bf16[2048,128]{1,0:T(8,128)(2,1)} %copy-done.7, bf16[2048,128]{1,0:T(8,128)(2,1)} %copy-done.8, ...), custom_call_target="tpu_custom_call" | custom-call | tf_op jit(solution)/shard_map/unpack/pallas_call | solution.py:213
  (110 shorter events, 18.9 us)
Async XLA Ops:
  7.2 97.2 %all-gather.2.cloned.1.call-start = ((), (), s32[]{:S(2)}) async-start(), calls=%async_computation.5 | async-start | bytes 8519680 | tf_op jit(solution)/shard_map/all_gather | solution.py:250
  9.3 0.7 collective-permute-start
  14.4 72.0 %copy-start.20 = (s32[1,512]{1,0:T(1,128)S(1)}, s32[1,512]{1,0:T(1,128)}, u32[]{:S(2)}) copy-start(s32[1,512]{1,0:T(1,128)} %param.9) | copy-start | bytes 6148
  14.4 72.7 %copy-start.21 = (f32[1,8]{1,0:T(1,128)S(1)}, f32[1,8]{1,0:T(1,128)}, u32[]{:S(2)}) copy-start(f32[1,8]{1,0:T(1,128)} %param.10) | copy-start | bytes 100
  14.4 86.5 %copy-start.19 = (bf16[1,512,128]{2,1,0:T(8,128)(2,1)S(1)}, bf16[1,512,128]{2,1,0:T(8,128)(2,1)}, u32[]{:S(2)}) copy-start(bf16[1,512,128]{2,1,0:T(8,128)(2,1)} %param.8) | copy-start | bytes 393220
  50.4 54.0 %copy-start = (bf16[32,128,128]{2,1,0:T(8,128)(2,1)}, bf16[32,128,128]{2,1,0:T(8,128)(2,1)S(1)}, u32[]{:S(2)}) copy-start(bf16[32,128,128]{2,1,0:T(8,128)(2,1)S(1)} %all_to_all.25.refs_0_) | copy-start | bytes 3145732
  50.4 30.6 %collective-permute-start.2 = (bf16[32,128,128]{2,1,0:T(8,128)(2,1)S(1)}, bf16[32,128,128]{2,1,0:T(8,128)(2,1)S(1)}, u32[]{:S(2)}, u32[]{:S(2)}) collective-permute-start(bf16[32,128,128]{2,1,0:T(8,128)(2,1)S(1)} %all_to_all.25.refs_0_), channel_id=1, source_target_pairs={{0,130},{2,128},{128,2},{130,0},{1,131},{3,129},{129,3},{131,1},{4... | collective-permute-start | bytes 3145736 | tf_op jit(solution)/shard_map/ppermute | solution.py:77
  58.5 25.5 %collective-permute-start.1 = (bf16[32,128,128]{2,1,0:T(8,128)(2,1)S(1)}, bf16[32,128,128]{2,1,0:T(8,128)(2,1)S(1)}, u32[]{:S(2)}, u32[]{:S(2)}) collective-permute-start(bf16[32,128,128]{2,1,0:T(8,128)(2,1)S(1)} %all_to_all.25.refs_0_), channel_id=1, source_target_pairs={{0,2},{2,0},{1,3},{3,1},{4,6},{6,4},{5,7},{7,5},{8,10},{10,8},{9,1... | collective-permute-start | bytes 3145736 | tf_op jit(solution)/shard_map/ppermute | solution.py:77
  80.9 23.4 %copy-start.1 = (bf16[32,128,128]{2,1,0:T(8,128)(2,1)}, bf16[32,128,128]{2,1,0:T(8,128)(2,1)S(1)}, u32[]{:S(2)}) copy-start(bf16[32,128,128]{2,1,0:T(8,128)(2,1)S(1)} %collective-permute-done.2.refs_2_) | copy-start | bytes 3145732
  81.8 14.7 %collective-permute-start.3 = (bf16[16,128,128]{2,1,0:T(8,128)(2,1)}, bf16[16,128,128]{2,1,0:T(8,128)(2,1)}, u32[]{:S(2)}, u32[]{:S(2)}) collective-permute-start(bf16[16,128,128]{2,1,0:T(8,128)(2,1)} %slice.109), channel_id=1, source_target_pairs={{0,2},{2,0},{1,3},{3,1},{4,6},{6,4},{5,7},{7,5},{8,10},{10,8},{9,1... | collective-permute-start | bytes 1572872 | tf_op jit(solution)/shard_map/ppermute | solution.py:77
  84.0 20.4 %copy-start.2 = (bf16[32,128,128]{2,1,0:T(8,128)(2,1)}, bf16[32,128,128]{2,1,0:T(8,128)(2,1)S(1)}, u32[]{:S(2)}) copy-start(bf16[32,128,128]{2,1,0:T(8,128)(2,1)S(1)} %collective-permute-done.1.refs_1_) | copy-start | bytes 3145732
  84.9 15.7 %collective-permute-start.4 = (bf16[16,128,128]{2,1,0:T(8,128)(2,1)}, bf16[16,128,128]{2,1,0:T(8,128)(2,1)}, u32[]{:S(2)}, u32[]{:S(2)}) collective-permute-start(bf16[16,128,128]{2,1,0:T(8,128)(2,1)} %slice.110), channel_id=1, source_target_pairs={{0,130},{2,128},{128,2},{130,0},{1,131},{3,129},{129,3},{131,1},{4... | collective-permute-start | bytes 1572872 | tf_op jit(solution)/shard_map/ppermute | solution.py:77
  86.4 9.9 %collective-permute-start.10 = (s32[512]{0:T(512)S(1)}, s32[512]{0:T(512)S(1)}, u32[]{:S(2)}, u32[]{:S(2)}) collective-permute-start(s32[512]{0:T(512)S(1)} %bitcast.65), channel_id=1, source_target_pairs={{0,0},{1,2},{2,1},{3,3},{4,4},{5,6},{6,5},{7,7},{8,8},{9,10},{10,9... | collective-permute-start | bytes 6152 | tf_op jit(solution)/shard_map/ppermute | solution.py:72
  87.1 4.8 %collective-permute-start.12 = (f32[8]{0:T(128)S(1)}, f32[8]{0:T(128)S(1)}, u32[]{:S(2)}, u32[]{:S(2)}) collective-permute-start(f32[8]{0:T(128)S(1)} %bitcast.66), channel_id=1, source_target_pairs={{0,0},{1,2},{2,1},{3,3},{4,4},{5,6},{6,5},{7,7},{8,8},{9,10},{10,9... | collective-permute-start | bytes 104 | tf_op jit(solution)/shard_map/ppermute | solution.py:72
  87.8 13.1 %collective-permute-start.5 = (bf16[32,128,128]{2,1,0:T(8,128)(2,1)S(1)}, bf16[32,128,128]{2,1,0:T(8,128)(2,1)}, u32[]{:S(2)}, u32[]{:S(2)}) collective-permute-start(bf16[32,128,128]{2,1,0:T(8,128)(2,1)S(1)} %all_to_all.25.refs_0_), channel_id=1, source_target_pairs={{0,1},{1,0},{2,3},{3,2},{4,5},{5,4},{6,7},{7,6},{8,9},{9,8},{10,11... | collective-permute-start | bytes 3145736 | tf_op jit(solution)/shard_map/ppermute | solution.py:77
  91.9 10.8 %collective-permute-start.6 = (bf16[32,128,128]{2,1,0:T(8,128)(2,1)S(1)}, bf16[32,128,128]{2,1,0:T(8,128)(2,1)}, u32[]{:S(2)}, u32[]{:S(2)}) collective-permute-start(bf16[32,128,128]{2,1,0:T(8,128)(2,1)S(1)} %collective-permute-done.1.refs_1_), channel_id=1, source_target_pairs={{0,1},{1,0},{2,3},{3,2},{4,5},{5,4},{6,7},{7,6},{8,9},{9,8},{10,11... | collective-permute-start | bytes 3145736 | tf_op jit(solution)/shard_map/ppermute | solution.py:77
  96.4 7.1 %collective-permute-start.7 = (bf16[32,128,128]{2,1,0:T(8,128)(2,1)S(1)}, bf16[32,128,128]{2,1,0:T(8,128)(2,1)}, u32[]{:S(2)}, u32[]{:S(2)}) collective-permute-start(bf16[32,128,128]{2,1,0:T(8,128)(2,1)S(1)} %collective-permute-done.2.refs_2_), channel_id=1, source_target_pairs={{0,1},{1,0},{2,3},{3,2},{4,5},{5,4},{6,7},{7,6},{8,9},{9,8},{10,11... | collective-permute-start | bytes 3145736 | tf_op jit(solution)/shard_map/ppermute | solution.py:77
  96.5 5.3 %collective-permute-start.8 = (bf16[16,128,128]{2,1,0:T(8,128)(2,1)}, bf16[16,128,128]{2,1,0:T(8,128)(2,1)S(1)}, u32[]{:S(2)}, u32[]{:S(2)}) collective-permute-start(bf16[16,128,128]{2,1,0:T(8,128)(2,1)} %collective-permute-done.3.refs_3_), channel_id=1, source_target_pairs={{0,1},{1,0},{2,3},{3,2},{4,5},{5,4},{6,7},{7,6},{8,9},{9,8},{10,11... | collective-permute-start | bytes 1572872 | tf_op jit(solution)/shard_map/ppermute | solution.py:77
  100.6 2.1 collective-permute-start.9
  100.9 19.3 %collective-permute-start.11 = (bf16[512,128]{1,0:T(8,128)(2,1)S(1)}, bf16[512,128]{1,0:T(8,128)(2,1)S(1)}, u32[]{:S(2)}, u32[]{:S(2)}) collective-permute-start(bf16[512,128]{1,0:T(8,128)(2,1)S(1)} %bitcast.64), channel_id=1, source_target_pairs={{0,0},{1,2},{2,1},{3,3},{4,4},{5,6},{6,5},{7,7},{8,8},{9,10},{10,9... | collective-permute-start | bytes 393224 | tf_op jit(solution)/shard_map/ppermute | solution.py:72
  124.4 15.6 %all-to-all-start.1 = ((bf16[8,64,256]{2,1,0:T(8,128)(2,1)}), bf16[8,64,256]{2,1,0:T(8,128)(2,1)S(1)}, u32[]{:S(2)}, u32[]{:S(2)}) async-start(bf16[8,64,256]{2,1,0:T(8,128)(2,1)} %fusion.9), calls=%async_computation.1 | async-start | bytes 524288 | tf_op jit(solution)/shard_map/all_to_all | solution.py:81
  136.9 10.1 %collective-permute-start.13 = (bf16[1024,128]{1,0:T(8,128)(2,1)}, bf16[1024,128]{1,0:T(8,128)(2,1)S(1)}, u32[]{:S(2)}, u32[]{:S(2)}) collective-permute-start(bf16[1024,128]{1,0:T(8,128)(2,1)} %get-tuple-element.19), channel_id=1, source_target_pairs={{0,130},{2,128},{128,2},{130,0},{1,131},{3,129},{129,3},{131,1},{4... | collective-permute-start | bytes 786440 | tf_op jit(solution)/shard_map/ppermute | solution.py:77
  137.8 9.3 %collective-permute-start.15 = (bf16[1024,128]{1,0:T(8,128)(2,1)S(1)}, bf16[1024,128]{1,0:T(8,128)(2,1)}, u32[]{:S(2)}, u32[]{:S(2)}) collective-permute-start(bf16[1024,128]{1,0:T(8,128)(2,1)S(1)} %get-tuple-element.21), channel_id=1, source_target_pairs={{0,2},{2,0},{1,3},{3,1},{4,6},{6,4},{5,7},{7,5},{8,10},{10,8},{9,1... | collective-permute-start | bytes 786440 | tf_op jit(solution)/shard_map/ppermute | solution.py:77
  140.7 13.2 %all-to-all-start.2 = ((bf16[8,64,256]{2,1,0:T(8,128)(2,1)}), bf16[8,64,256]{2,1,0:T(8,128)(2,1)S(1)}, u32[]{:S(2)}, u32[]{:S(2)}) async-start(bf16[8,64,256]{2,1,0:T(8,128)(2,1)} %broadcast_in_dim.8), calls=%async_computation.2 | async-start | bytes 524288 | tf_op jit(solution)/shard_map/all_to_all | solution.py:81
  156.5 15.4 %all-to-all-start.3 = ((bf16[4,256,256]{2,1,0:T(8,128)(2,1)}), bf16[4,256,256]{2,1,0:T(8,128)(2,1)S(1)}, u32[]{:S(2)}, u32[]{:S(2)}) async-start(bf16[4,256,256]{2,1,0:T(8,128)(2,1)} %bitcast.56), calls=%async_computation.3 | async-start | bytes 1048576 | tf_op jit(solution)/shard_map/all_to_all | solution.py:81
  162.8 17.2 %collective-permute-start.14 = (bf16[2048,128]{1,0:T(8,128)(2,1)}, bf16[2048,128]{1,0:T(8,128)(2,1)}, u32[]{:S(2)}, u32[]{:S(2)}) collective-permute-start(bf16[2048,128]{1,0:T(8,128)(2,1)} %pad_maximum_fusion), channel_id=1, source_target_pairs={{0,2},{2,0},{1,3},{3,1},{4,6},{6,4},{5,7},{7,5},{8,10},{10,8},{9,1... | collective-permute-start | bytes 1572872 | tf_op jit(solution)/shard_map/ppermute | solution.py:77
  165.6 15.7 %collective-permute-start.16 = (bf16[2048,128]{1,0:T(8,128)(2,1)}, bf16[2048,128]{1,0:T(8,128)(2,1)S(1)}, u32[]{:S(2)}, u32[]{:S(2)}) collective-permute-start(bf16[2048,128]{1,0:T(8,128)(2,1)} %pad_maximum_fusion.1), channel_id=1, source_target_pairs={{0,130},{2,128},{128,2},{130,0},{1,131},{3,129},{129,3},{131,1},{4... | collective-permute-start | bytes 1572872 | tf_op jit(solution)/shard_map/ppermute | solution.py:77
  172.9 15.0 %all-to-all-start.4 = ((bf16[4,256,256]{2,1,0:T(8,128)(2,1)}), bf16[4,256,256]{2,1,0:T(8,128)(2,1)S(1)}, u32[]{:S(2)}, u32[]{:S(2)}) async-start(bf16[4,256,256]{2,1,0:T(8,128)(2,1)} %broadcast_in_dim.9), calls=%async_computation.4 | async-start | bytes 1048576 | tf_op jit(solution)/shard_map/all_to_all | solution.py:81
  183.6 5.4 %collective-permute-start.17 = (bf16[2048,128]{1,0:T(8,128)(2,1)}, bf16[2048,128]{1,0:T(8,128)(2,1)S(1)}, u32[]{:S(2)}, u32[]{:S(2)}) collective-permute-start(bf16[2048,128]{1,0:T(8,128)(2,1)} %fusion.3), channel_id=1, source_target_pairs={{0,0},{1,2},{2,1},{3,3},{4,4},{5,6},{6,5},{7,7},{8,8},{9,10},{10,9... | collective-permute-start | bytes 1572872 | tf_op jit(solution)/shard_map/ppermute | solution.py:72
  185.3 16.5 %collective-permute-start.18 = (bf16[2048,128]{1,0:T(8,128)(2,1)}, bf16[2048,128]{1,0:T(8,128)(2,1)S(1)}, u32[]{:S(2)}, u32[]{:S(2)}) collective-permute-start(bf16[2048,128]{1,0:T(8,128)(2,1)} %fusion.3), channel_id=1, source_target_pairs={{0,128},{1,130},{2,129},{3,131},{128,0},{129,2},{130,1},{131,3},{4... | collective-permute-start | bytes 1572872 | tf_op jit(solution)/shard_map/ppermute | solution.py:302
  187.8 36.2 %copy-start.3 = (bf16[4,256,256]{2,1,0:T(8,128)(2,1)}, bf16[4,256,256]{2,1,0:T(8,128)(2,1)S(1)}, u32[]{:S(2)}) copy-start(bf16[4,256,256]{2,1,0:T(8,128)(2,1)S(1)} %all-to-all-done.4.refs_4_) | copy-start | bytes 1572868
  187.8 25.3 %collective-permute-start.22 = (bf16[4,256,256]{2,1,0:T(8,128)(2,1)S(1)}, bf16[4,256,256]{2,1,0:T(8,128)(2,1)S(1)}, u32[]{:S(2)}, u32[]{:S(2)}) collective-permute-start(bf16[4,256,256]{2,1,0:T(8,128)(2,1)S(1)} %all-to-all-done.4.refs_4_), channel_id=1, source_target_pairs={{0,130},{2,128},{128,2},{130,0},{1,131},{3,129},{129,3},{131,1},{4... | collective-permute-start | bytes 1572872 | tf_op jit(solution)/shard_map/ppermute | solution.py:77
  189.0 24.2 %collective-permute-start.21 = (bf16[4,256,256]{2,1,0:T(8,128)(2,1)S(1)}, bf16[4,256,256]{2,1,0:T(8,128)(2,1)S(1)}, u32[]{:S(2)}, u32[]{:S(2)}) collective-permute-start(bf16[4,256,256]{2,1,0:T(8,128)(2,1)S(1)} %all-to-all-done.4.refs_4_), channel_id=1, source_target_pairs={{0,2},{2,0},{1,3},{3,1},{4,6},{6,4},{5,7},{7,5},{8,10},{10,8},{9,1... | collective-permute-start | bytes 1572872 | tf_op jit(solution)/shard_map/ppermute | solution.py:77
  189.0 35.1 %copy-start.6 = (bf16[2048,128]{1,0:T(8,128)(2,1)}, bf16[2048,128]{1,0:T(8,128)(2,1)S(1)}, u32[]{:S(2)}) copy-start(bf16[2048,128]{1,0:T(8,128)(2,1)S(1)} %collective-permute-done.17.refs_0_) | copy-start | bytes 1572868
  189.0 25.8 %collective-permute-start.19 = (bf16[2048,128]{1,0:T(8,128)(2,1)S(1)}, bf16[2048,128]{1,0:T(8,128)(2,1)S(1)}, u32[]{:S(2)}, u32[]{:S(2)}) collective-permute-start(bf16[2048,128]{1,0:T(8,128)(2,1)S(1)} %collective-permute-done.17.refs_0_), channel_id=1, source_target_pairs={{0,1},{1,0},{2,3},{3,2},{4,5},{5,4},{6,7},{7,6},{8,9},{9,8},{10,11... | collective-permute-start | bytes 1572872 | tf_op jit(solution)/shard_map/ppermute | solution.py:77
  201.8 22.2 %copy-start.7 = (bf16[2048,128]{1,0:T(8,128)(2,1)}, bf16[2048,128]{1,0:T(8,128)(2,1)S(1)}, u32[]{:S(2)}) copy-start(bf16[2048,128]{1,0:T(8,128)(2,1)S(1)} %collective-permute-done.18.refs_1_) | copy-start | bytes 1572868
  201.8 12.9 %collective-permute-start.20 = (bf16[2048,128]{1,0:T(8,128)(2,1)S(1)}, bf16[2048,128]{1,0:T(8,128)(2,1)S(1)}, u32[]{:S(2)}, u32[]{:S(2)}) collective-permute-start(bf16[2048,128]{1,0:T(8,128)(2,1)S(1)} %collective-permute-done.18.refs_1_), channel_id=1, source_target_pairs={{0,1},{1,0},{2,3},{3,2},{4,5},{5,4},{6,7},{7,6},{8,9},{9,8},{10,11... | collective-permute-start | bytes 1572872 | tf_op jit(solution)/shard_map/ppermute | solution.py:77
  207.1 14.0 %collective-permute-start.25 = (bf16[4,256,256]{2,1,0:T(8,128)(2,1)S(1)}, bf16[4,256,256]{2,1,0:T(8,128)(2,1)S(1)}, u32[]{:S(2)}, u32[]{:S(2)}) collective-permute-start(bf16[4,256,256]{2,1,0:T(8,128)(2,1)S(1)} %all-to-all-done.4.refs_4_), channel_id=1, source_target_pairs={{0,1},{1,0},{2,3},{3,2},{4,5},{5,4},{6,7},{7,6},{8,9},{9,8},{10,11... | collective-permute-start | bytes 1572872 | tf_op jit(solution)/shard_map/ppermute | solution.py:77
  213.1 11.0 %copy-start.4 = (bf16[4,256,256]{2,1,0:T(8,128)(2,1)}, bf16[4,256,256]{2,1,0:T(8,128)(2,1)S(1)}, u32[]{:S(2)}) copy-start(bf16[4,256,256]{2,1,0:T(8,128)(2,1)S(1)} %collective-permute-done.22.refs_6_) | copy-start | bytes 1572868
  213.1 6.5 %collective-permute-start.23 = (bf16[2,256,256]{2,1,0:T(8,128)(2,1)S(1)}, bf16[2,256,256]{2,1,0:T(8,128)(2,1)S(1)}, u32[]{:S(2)}, u32[]{:S(2)}) collective-permute-start(bf16[2,256,256]{2,1,0:T(8,128)(2,1)S(1)} %slice.121), channel_id=1, source_target_pairs={{0,2},{2,0},{1,3},{3,1},{4,6},{6,4},{5,7},{7,5},{8,10},{10,8},{9,1... | collective-permute-start | bytes 786440 | tf_op jit(solution)/shard_map/ppermute | solution.py:77
  213.2 10.8 %copy-start.5 = (bf16[4,256,256]{2,1,0:T(8,128)(2,1)}, bf16[4,256,256]{2,1,0:T(8,128)(2,1)S(1)}, u32[]{:S(2)}) copy-start(bf16[4,256,256]{2,1,0:T(8,128)(2,1)S(1)} %collective-permute-done.21.refs_5_) | copy-start | bytes 1572868
  213.3 7.7 %collective-permute-start.24 = (bf16[2,256,256]{2,1,0:T(8,128)(2,1)S(1)}, bf16[2,256,256]{2,1,0:T(8,128)(2,1)S(1)}, u32[]{:S(2)}, u32[]{:S(2)}) collective-permute-start(bf16[2,256,256]{2,1,0:T(8,128)(2,1)S(1)} %slice.122), channel_id=1, source_target_pairs={{0,130},{2,128},{128,2},{130,0},{1,131},{3,129},{129,3},{131,1},{4... | collective-permute-start | bytes 786440 | tf_op jit(solution)/shard_map/ppermute | solution.py:77
  214.8 9.3 %copy-start.8 = (bf16[2048,128]{1,0:T(8,128)(2,1)}, bf16[2048,128]{1,0:T(8,128)(2,1)S(1)}, u32[]{:S(2)}) copy-start(bf16[2048,128]{1,0:T(8,128)(2,1)S(1)} %collective-permute-done.19.refs_2_) | copy-start | bytes 1572868
  214.8 7.8 %collective-permute-start.26 = (bf16[4,256,256]{2,1,0:T(8,128)(2,1)S(1)}, bf16[4,256,256]{2,1,0:T(8,128)(2,1)S(1)}, u32[]{:S(2)}, u32[]{:S(2)}) collective-permute-start(bf16[4,256,256]{2,1,0:T(8,128)(2,1)S(1)} %collective-permute-done.21.refs_5_), channel_id=1, source_target_pairs={{0,1},{1,0},{2,3},{3,2},{4,5},{5,4},{6,7},{7,6},{8,9},{9,8},{10,11... | collective-permute-start | bytes 1572872 | tf_op jit(solution)/shard_map/ppermute | solution.py:77
  214.8 7.8 %copy-start.9 = (bf16[2048,128]{1,0:T(8,128)(2,1)}, bf16[2048,128]{1,0:T(8,128)(2,1)S(1)}, u32[]{:S(2)}) copy-start(bf16[2048,128]{1,0:T(8,128)(2,1)S(1)} %collective-permute-done.20.refs_3_) | copy-start | bytes 1572868
  214.8 9.2 %collective-permute-start.27 = (bf16[4,256,256]{2,1,0:T(8,128)(2,1)S(1)}, bf16[4,256,256]{2,1,0:T(8,128)(2,1)}, u32[]{:S(2)}, u32[]{:S(2)}) collective-permute-start(bf16[4,256,256]{2,1,0:T(8,128)(2,1)S(1)} %collective-permute-done.22.refs_6_), channel_id=1, source_target_pairs={{0,1},{1,0},{2,3},{3,2},{4,5},{5,4},{6,7},{7,6},{8,9},{9,8},{10,11... | collective-permute-start | bytes 1572872 | tf_op jit(solution)/shard_map/ppermute | solution.py:77
  219.6 1.5 collective-permute-start.28
  221.0 1.5 collective-permute-start.29
  (9 other events, 12.8 us)
Sparse Core Ops, SparseCore 0:
  10.8 93.5 all-gather.1
